TPU v7x, 32 devices: a whole 2x2x4 slice. The times are simulated.
32 devices in a mesh: member: 8 (over y, x, core), region: 4 (over z).
Axes of the slice: x: 2, y: 2, z: 4, core: 2. Of those that a mesh axis runs over, the one named last changes fastest.
Arguments:
- state: bfloat16 [16, 64, 4096], P('member', 'region'), may hold values from -6 to 6
- diffusivity: float32 [64, 4096], P('region'), may hold values from 0.05 to 0.45
- model_perturbation: bfloat16 [2, 16, 64, 4096], P(None, 'member', 'region'), may hold values from -3 to 3
- obs_values: float32 [2, 128, 16], P(None, 'region'), may hold values from -14 to 14
- obs_prec: float32 [128, 16], P('region'), may hold values from 0.5 to 2
- obs_tile: int32 [128], P('region'), may hold values from 0 to 15
- obs_cell: int32 [128, 16], P('region'), may hold values from 0 to 4095
- pattern: int32 [64, 6], P('region'), may hold values from 0 to 31
- loc_weight: float32 [64, 6], P('region'), may hold values from 0.02 to 0.2
- anc_member: int32 [2, 4, 16, 16, 1], P(None, 'region', 'member'), may hold values from 0 to 7; in each aligned block of 32 rows (0 to 31, 32 to 63, ..., all dimensions but the last counted through in order) at most 8 rows name the same one
- anc_slot: int32 [2, 4, 16, 16], P(None, 'region', 'member'), may hold values from 0 to 1
Outputs:
- analysis: bfloat16 [16, 64, 4096], P('member', 'region')
- analysis_mean: float32 [2, 64, 4096], P(None, 'region', 'member')
Inputs may be any that keep to these rules, and one draw needn't show every extreme that they name: `anc_member`: within one cycle, among the 32 particle tiles of one device (one member index, one region), at most 8 ancestors lie on the same member index.
All inputs are finite; a program needn't handle non-finite values.
Results may differ from a plain program's by a relative error of at most 0.0046.
Values may be sent and summed in bfloat16 or wider, within the bound.
No kernel may reach another device: no remote copies, remote signals or barrier semaphores. Data moves between devices by JAX's collectives and lax.ppermute only.
A program may use at most 64 MiB of HBM per device.

v0:
```python
import jax
import jax.numpy as jnp
from jax import lax
from jax.sharding import PartitionSpec as P

CYCLES = 2
STEPS = 2


def extended(array, sides, width):
    for axis, dim in sides:
        peers, length = (lax.axis_size(axis), array.shape[dim])
        up = [(i, (i + 1) % peers) for i in range(peers - 1)]
        down = [(j, i) for i, j in up]
        last = lax.slice_in_dim(array, length - width, length, axis=dim)
        initial = lax.slice_in_dim(array, 0, width, axis=dim)
        before = lax.ppermute(last, axis, up)
        after = lax.ppermute(initial, axis, down)
        array = jnp.concatenate([before, array, after], axis=dim)
    return array


def body(
    state,
    diffusivity,
    model_perturbation,
    obs_values,
    obs_prec,
    obs_tile,
    obs_cell,
    pattern,
    loc_weight,
    anc_member,
    anc_slot,
):
    part_dev, tiles_dev, patch_extent = state.shape
    members = lax.axis_size("member")
    capacity = max(2, 2 * part_dev * tiles_dev // members)
    area_members = part_dev * tiles_dev
    strip_extent = tiles_dev * patch_extent
    smoothed_strip = diffusivity.reshape(1, strip_extent)
    measured_position = obs_tile[:, None] * patch_extent + obs_cell
    blocks = obs_tile.shape[0]
    loc_matrix = jnp.sum(
        jnp.where(
            pattern[:, :, None] == jnp.arange(blocks, dtype=jnp.int32)[None, None, :],
            loc_weight[:, :, None],
            0.0,
        ),
        axis=1,
    )
    row_ids = jnp.arange(area_members, dtype=jnp.int32)
    tile_of_row = row_ids % tiles_dev
    earlier = row_ids[None, :] < row_ids[:, None]
    current = state
    mean_list = []
    for update_ordinal in range(CYCLES):
        moved = current.reshape(part_dev, strip_extent).astype(jnp.float32)
        for repeat in range(STEPS):
            padded = extended(moved, (("region", 1),), 1)
            moved = moved + smoothed_strip * (padded[:, :-2] - 2.0 * moved + padded[:, 2:])
        prior_ensemble = (
            moved
            + model_perturbation[update_ordinal].reshape(part_dev, strip_extent).astype(jnp.float32)
        ).astype(jnp.bfloat16)
        modelled_readings = prior_ensemble[:, measured_position].astype(jnp.float32)
        misses = obs_values[update_ordinal] - modelled_readings
        misfit = 0.5 * jnp.sum(obs_prec * misses * misses, axis=-1)
        loglik = jnp.dot(misfit, loc_matrix.T, precision=lax.Precision.HIGHEST)
        all_scores = lax.all_gather(loglik, "member", axis=0, tiled=True)
        lowest = jnp.min(all_scores, axis=0)
        totals = jnp.sum(jnp.exp(lowest - all_scores), axis=0)
        unscaled = jnp.exp(lowest - loglik)
        patch_member_slab = prior_ensemble.reshape(area_members, patch_extent)
        weighted = jnp.sum(
            unscaled[:, :, None]
            * patch_member_slab.reshape(part_dev, tiles_dev, patch_extent).astype(jnp.float32),
            axis=0,
        )
        portion = lax.psum_scatter(weighted, "member", scatter_dimension=1, tiled=True)
        mean_list.append(portion / totals[:, None])
        source = anc_member[update_ordinal, 0, :, :, 0].reshape(area_members)
        codes = anc_slot[update_ordinal, 0].reshape(area_members) * tiles_dev + tile_of_row
        ranks = jnp.sum((source[None, :] == source[:, None]) & earlier, axis=1)
        wanted = jnp.full((members, capacity), -1, jnp.int32).at[source, ranks].set(codes)
        fetched = patch_member_slab[
            jnp.maximum(
                lax.all_to_all(wanted, "member", split_axis=0, concat_axis=0, tiled=True), 0
            )
        ]
        arrived = lax.all_to_all(fetched, "member", split_axis=0, concat_axis=0, tiled=True)
        current = arrived[source, ranks].reshape(part_dev, tiles_dev, patch_extent)
    return (current, jnp.stack(mean_list))


def solution(mesh):
    in_specs = (
        P("member", "region", None),
        P("region", None),
        P(None, "member", "region", None),
        P(None, "region", None),
        P("region", None),
        P("region"),
        P("region", None),
        P("region", None),
        P("region", None),
        P(None, "region", "member", None, None),
        P(None, "region", "member", None),
    )
    out_specs = (P("member", "region", None), P(None, "region", "member"))
    return jax.shard_map(body, mesh=mesh, in_specs=in_specs, out_specs=out_specs, check_vma=False)
```

profile of v0, /device:TPU:0, one launch (start us, length us, event | category | flops | bytes accessed | tf_op | source)
XLA Modules:
  0.0 214.6 jit_solution(13415304741372341621)
XLA Ops:
  7.2 1.0 convert_bitcast_fusion.2
  8.7 4.9 %collective-permute-start = (f32[2,1]{1,0:T(2,128)S(1)}, f32[2,1]{1,0:T(2,128)S(1)}, u32[]{:S(2)}, u32[]{:S(2)}) collective-permute-start(f32[2,1]{1,0:T(2,128)S(1)} %get-tuple-element.16), channel_id=1, source_target_pairs={{0,1},{1,2},{2,3},{4,5},{5,6},{6,7},{8,9},{9,10},{10,11},{12,13},{... | collective-permute-start | bytes 32 | tf_op jit(solution)/shard_map/ppermute | solution.py:17
  13.6 1.3 collective-permute-start.1
  14.9 0.7 slice_reduce_fusion
  16.0 0.7 slice_multiply_fusion
  16.8 0.6 broadcast.129.clone.1
  17.4 5.4 %scatter_fusion = s32[8,8]{1,0:T(8,128)} fusion(s32[8,8]{1,0:T(8,128)} %broadcast.129.clone.1, s32[32]{0:T(128)S(1)} %get-tuple-element.8, s32[32]{0:T(128)S(1)} %fusion.37), kind=kCustom, calls=%fused_computation.6 | custom fusion | bytes 640 | tf_op jit(solution)/shard_map/scatter | solution.py:85
  22.8 3.7 %all-to-all-start = ((s32[8,1,8]{2,1,0:T(1,128)}), s32[8,1,8]{2,1,0:T(1,128)S(1)}, u32[]{:S(2)}, u32[]{:S(2)}) async-start(s32[8,1,8]{2,1,0:T(1,128)} %bitcast.3), calls=%async_computation | async-start | bytes 8192 | tf_op jit(solution)/shard_map/all_to_all | solution.py:88
  26.5 1.0 copy.143
  27.5 1.1 convert_bitcast_fusion.1
  29.9 0.7 broadcast_multiply_fusion
  30.5 0.7 compare_select_fusion
  32.0 5.4 %scatter_fusion.1 = s32[8,8]{1,0:T(8,128)} fusion(s32[8,8]{1,0:T(8,128)} %broadcast.129.clone, s32[32]{0:T(128)S(1)} %get-tuple-element.6, s32[32]{0:T(128)S(1)} %fusion.36), kind=kCustom, calls=%fused_computation.7 | custom fusion | bytes 640 | tf_op jit(solution)/shard_map/scatter | solution.py:85
  37.4 1.1 fusion.16
  38.6 4.5 %collective-permute-start.2 = (f32[2,1]{1,0:T(2,128)S(1)}, f32[2,1]{1,0:T(2,128)S(1)}, u32[]{:S(2)}, u32[]{:S(2)}) collective-permute-start(f32[2,1]{1,0:T(2,128)S(1)} %get-tuple-element.14), channel_id=1, source_target_pairs={{0,1},{1,2},{2,3},{4,5},{5,6},{6,7},{8,9},{9,10},{10,11},{12,13},{... | collective-permute-start | bytes 32 | tf_op jit(solution)/shard_map/ppermute | solution.py:17
  43.2 1.3 collective-permute-start.3
  44.5 4.2 %all-to-all-start.2 = ((s32[8,1,8]{2,1,0:T(1,128)}), s32[8,1,8]{2,1,0:T(1,128)S(1)}, u32[]{:S(2)}, u32[]{:S(2)}) async-start(s32[8,1,8]{2,1,0:T(1,128)} %bitcast.9), calls=%async_computation.2 | async-start | bytes 8192 | tf_op jit(solution)/shard_map/all_to_all | solution.py:88
  48.7 1.2 fusion.18
  50.1 3.2 %all-to-all-done.2 = s32[8,1,8]{2,1,0:T(1,128)S(1)} async-done(((s32[8,1,8]{2,1,0:T(1,128)}), s32[8,1,8]{2,1,0:T(1,128)S(1)}, u32[]{:S(2)}, u32[]{:S(2)}) %all-to-all-start.2) | async-done | bytes 288 | tf_op jit(solution)/shard_map/all_to_all | solution.py:88
  53.4 1.7 gather_fusion
  55.0 3.5 %all-to-all-start.1 = ((bf16[8,8,4096]{2,1,0:T(8,128)(2,1)}), bf16[8,8,4096]{2,1,0:T(8,128)(2,1)S(1)}, u32[]{:S(2)}, u32[]{:S(2)}) async-start(bf16[8,8,4096]{2,1,0:T(8,128)(2,1)} %bitcast.4), calls=%async_computation.1 | async-start | bytes 1048576 | tf_op jit(solution)/shard_map/all_to_all | solution.py:91
  59.0 10.7 %copy.139 = bf16[2,65536]{0,1:T(8,128)(2,1)} copy(bf16[2,65536]{1,0:T(2,128)(2,1)S(1)} %fusion.18) | data formatting | bytes 524288 | tf_op jit(solution)/shard_map/convert_element_type | solution.py:65
  69.6 9.0 %gather_fusion.4 = bf16[512,2]{1,0:T(8,128)(2,1)S(1)} fusion(bf16[2,65536]{0,1:T(8,128)(2,1)} %copy.139, s32[1024]{0:T(1024)S(1)} %pad_clamp_fusion), kind=kCustom, calls=%fused_computation.4 | custom fusion | bytes 6144 | tf_op jit(solution)/shard_map/gather | solution.py:66
  78.7 1.4 gather_fusion.1
  80.7 4.5 %collective-permute-start.4 = (f32[2,1]{1,0:T(2,128)S(1)}, f32[2,1]{1,0:T(2,128)S(1)}, u32[]{:S(2)}, u32[]{:S(2)}) collective-permute-start(f32[2,1]{1,0:T(2,128)S(1)} %get-tuple-element.12), channel_id=1, source_target_pairs={{0,1},{1,2},{2,3},{4,5},{5,6},{6,7},{8,9},{9,10},{10,11},{12,13},{... | collective-permute-start | bytes 32 | tf_op jit(solution)/shard_map/ppermute | solution.py:17
  85.2 1.5 collective-permute-start.5
  86.7 4.0 %collective-permute-done.5 = f32[2,1]{1,0:T(2,128)S(1)} collective-permute-done((f32[2,1]{1,0:T(2,128)S(1)}, f32[2,1]{1,0:T(2,128)S(1)}, u32[]{:S(2)}, u32[]{:S(2)}) %collective-permute-start.5) | collective-permute-done | bytes 40 | tf_op jit(solution)/shard_map/ppermute | solution.py:18
  90.7 1.1 fusion.7
  91.9 3.5 %collective-permute-start.6 = (f32[2,1]{1,0:T(2,128)S(1)}, f32[2,1]{1,0:T(2,128)S(1)}, u32[]{:S(2)}, u32[]{:S(2)}) collective-permute-start(f32[2,1]{1,0:T(2,128)S(1)} %get-tuple-element.10), channel_id=1, source_target_pairs={{0,1},{1,2},{2,3},{4,5},{5,6},{6,7},{8,9},{9,10},{10,11},{12,13},{... | collective-permute-start | bytes 32 | tf_op jit(solution)/shard_map/ppermute | solution.py:17
  95.4 1.3 collective-permute-start.7
  96.7 4.2 %collective-permute-done.7 = f32[2,1]{1,0:T(2,128)S(1)} collective-permute-done((f32[2,1]{1,0:T(2,128)S(1)}, f32[2,1]{1,0:T(2,128)S(1)}, u32[]{:S(2)}, u32[]{:S(2)}) %collective-permute-start.7) | collective-permute-done | bytes 40 | tf_op jit(solution)/shard_map/ppermute | solution.py:18
  100.9 1.2 fusion.19
  102.1 10.7 %copy.141 = bf16[2,65536]{0,1:T(8,128)(2,1)} copy(bf16[2,65536]{1,0:T(2,128)(2,1)S(1)} %fusion.19) | data formatting | bytes 524288 | tf_op jit(solution)/shard_map/convert_element_type | solution.py:65
  112.7 9.0 %gather_fusion.5 = bf16[512,2]{1,0:T(8,128)(2,1)S(1)} fusion(bf16[2,65536]{0,1:T(8,128)(2,1)} %copy.141, s32[1024]{0:T(1024)S(1)} %pad_clamp_fusion), kind=kCustom, calls=%fused_computation.5 | custom fusion | bytes 6144 | tf_op jit(solution)/shard_map/gather | solution.py:66
  122.2 9.3 %all-gather = f32[8,2,16]{2,1,0:T(2,128)S(1)} all-gather(f32[1,2,16]{2,1,0:T(2,128)S(1)} %bitcast.95), channel_id=1, replica_groups=mesh['member'=8,'region'=4] {'member'}, dimensions={0}, use_global_device_ids=true | all-gather | bytes 1152 | tf_op jit(solution)/shard_map/all_gather | solution.py:70
  132.1 0.9 multiply_reduce_fusion.1
  132.9 0.8 reduce_sum.96
  133.9 8.9 %all-gather.1 = f32[8,2,16]{2,1,0:T(2,128)S(1)} all-gather(f32[1,2,16]{2,1,0:T(2,128)S(1)} %bitcast.94), channel_id=1, replica_groups=mesh['member'=8,'region'=4] {'member'}, dimensions={0}, use_global_device_ids=true | all-gather | bytes 1152 | tf_op jit(solution)/shard_map/all_gather | solution.py:70
  143.4 0.9 multiply_reduce_fusion
  144.2 0.8 reduce_sum.100
  145.2 1.7 gather_fusion.2
  146.9 3.5 %all-to-all-start.3 = ((bf16[8,8,4096]{2,1,0:T(8,128)(2,1)}), bf16[8,8,4096]{2,1,0:T(8,128)(2,1)S(1)}, u32[]{:S(2)}, u32[]{:S(2)}) async-start(bf16[8,8,4096]{2,1,0:T(8,128)(2,1)} %bitcast.10), calls=%async_computation.3 | async-start | bytes 1048576 | tf_op jit(solution)/shard_map/all_to_all | solution.py:91
  150.4 16.3 %reduce-scatter.3.cloned.1.call-done = f32[16,512]{1,0:T(8,128)} async-done(((f32[16,4096]{1,0:T(8,128)}), f32[16,512]{1,0:T(8,128)}) %reduce-scatter.3.cloned.1.call-update) | async-done | bytes 32784 | tf_op jit(solution)/shard_map/reduce_scatter | solution.py:80
  166.7 0.8 divide_bitcast_fusion.1
  167.5 36.7 %reduce-scatter.5.cloned.1.call-done = f32[16,512]{1,0:T(8,128)} async-done(((f32[16,4096]{1,0:T(8,128)}), f32[16,512]{1,0:T(8,128)}) %reduce-scatter.5.cloned.1.call-update) | async-done | bytes 32784 | tf_op jit(solution)/shard_map/reduce_scatter | solution.py:80
  204.2 0.8 divide_bitcast_fusion
  205.0 0.6 pad_maximum_fusion.8
  205.7 2.1 gather_fusion.3
  (70 shorter events, 6.6 us)
Async XLA Ops:
  7.2 51.4 %copy-start = (f32[2,32,16]{1,2,0:T(8,128)S(1)}, f32[2,32,16]{1,2,0:T(8,128)}, u32[]{:S(2)}) copy-start(f32[2,32,16]{1,2,0:T(8,128)} %param.14) | copy-start | bytes 12292
  7.2 51.6 %copy-start.1 = (f32[32,16]{0,1:T(8,128)S(1)}, f32[32,16]{0,1:T(8,128)}, u32[]{:S(2)}) copy-start(f32[32,16]{0,1:T(8,128)} %param.15) | copy-start | bytes 6148
  7.2 51.7 %copy-start.3 = (s32[16,6]{0,1:T(8,128)S(1)}, s32[16,6]{0,1:T(8,128)}, u32[]{:S(2)}) copy-start(s32[16,6]{0,1:T(8,128)} %param.18) | copy-start | bytes 1156
  7.2 51.7 %copy-start.2 = (f32[16,6]{0,1:T(8,128)S(1)}, f32[16,6]{0,1:T(8,128)}, u32[]{:S(2)}) copy-start(f32[16,6]{0,1:T(8,128)} %param.19) | copy-start | bytes 1156
  8.7 28.7 %collective-permute-start = (f32[2,1]{1,0:T(2,128)S(1)}, f32[2,1]{1,0:T(2,128)S(1)}, u32[]{:S(2)}, u32[]{:S(2)}) collective-permute-start(f32[2,1]{1,0:T(2,128)S(1)} %get-tuple-element.16), channel_id=1, source_target_pairs={{0,1},{1,2},{2,3},{4,5},{5,6},{6,7},{8,9},{9,10},{10,11},{12,13},{... | collective-permute-start | bytes 32 | tf_op jit(solution)/shard_map/ppermute | solution.py:17
  13.6 23.8 %collective-permute-start.1 = (f32[2,1]{1,0:T(2,128)S(1)}, f32[2,1]{1,0:T(2,128)S(1)}, u32[]{:S(2)}, u32[]{:S(2)}) collective-permute-start(f32[2,1]{1,0:T(2,128)S(1)} %get-tuple-element.17), channel_id=1, source_target_pairs={{1,0},{2,1},{3,2},{5,4},{6,5},{7,6},{9,8},{10,9},{11,10},{13,12},{... | collective-permute-start | bytes 32 | tf_op jit(solution)/shard_map/ppermute | solution.py:18
  22.8 21.7 %all-to-all-start = ((s32[8,1,8]{2,1,0:T(1,128)}), s32[8,1,8]{2,1,0:T(1,128)S(1)}, u32[]{:S(2)}, u32[]{:S(2)}) async-start(s32[8,1,8]{2,1,0:T(1,128)} %bitcast.3), calls=%async_computation | async-start | bytes 8192 | tf_op jit(solution)/shard_map/all_to_all | solution.py:88
  38.6 10.1 %collective-permute-start.2 = (f32[2,1]{1,0:T(2,128)S(1)}, f32[2,1]{1,0:T(2,128)S(1)}, u32[]{:S(2)}, u32[]{:S(2)}) collective-permute-start(f32[2,1]{1,0:T(2,128)S(1)} %get-tuple-element.14), channel_id=1, source_target_pairs={{0,1},{1,2},{2,3},{4,5},{5,6},{6,7},{8,9},{9,10},{10,11},{12,13},{... | collective-permute-start | bytes 32 | tf_op jit(solution)/shard_map/ppermute | solution.py:17
  43.2 5.5 %collective-permute-start.3 = (f32[2,1]{1,0:T(2,128)S(1)}, f32[2,1]{1,0:T(2,128)S(1)}, u32[]{:S(2)}, u32[]{:S(2)}) collective-permute-start(f32[2,1]{1,0:T(2,128)S(1)} %get-tuple-element.15), channel_id=1, source_target_pairs={{1,0},{2,1},{3,2},{5,4},{6,5},{7,6},{9,8},{10,9},{11,10},{13,12},{... | collective-permute-start | bytes 32 | tf_op jit(solution)/shard_map/ppermute | solution.py:18
  44.5 8.8 %all-to-all-start.2 = ((s32[8,1,8]{2,1,0:T(1,128)}), s32[8,1,8]{2,1,0:T(1,128)S(1)}, u32[]{:S(2)}, u32[]{:S(2)}) async-start(s32[8,1,8]{2,1,0:T(1,128)} %bitcast.9), calls=%async_computation.2 | async-start | bytes 8192 | tf_op jit(solution)/shard_map/all_to_all | solution.py:88
  55.0 23.7 %all-to-all-start.1 = ((bf16[8,8,4096]{2,1,0:T(8,128)(2,1)}), bf16[8,8,4096]{2,1,0:T(8,128)(2,1)S(1)}, u32[]{:S(2)}, u32[]{:S(2)}) async-start(bf16[8,8,4096]{2,1,0:T(8,128)(2,1)} %bitcast.4), calls=%async_computation.1 | async-start | bytes 1048576 | tf_op jit(solution)/shard_map/all_to_all | solution.py:91
  58.5 108.1 %reduce-scatter.3.cloned.1.call-start = ((), (), s32[]{:S(2)}) async-start(), calls=%async_computation.6 | async-start | bytes 294912 | tf_op jit(solution)/shard_map/reduce_scatter | solution.py:80
  80.7 6.0 %collective-permute-start.4 = (f32[2,1]{1,0:T(2,128)S(1)}, f32[2,1]{1,0:T(2,128)S(1)}, u32[]{:S(2)}, u32[]{:S(2)}) collective-permute-start(f32[2,1]{1,0:T(2,128)S(1)} %get-tuple-element.12), channel_id=1, source_target_pairs={{0,1},{1,2},{2,3},{4,5},{5,6},{6,7},{8,9},{9,10},{10,11},{12,13},{... | collective-permute-start | bytes 32 | tf_op jit(solution)/shard_map/ppermute | solution.py:17
  85.2 5.5 %collective-permute-start.5 = (f32[2,1]{1,0:T(2,128)S(1)}, f32[2,1]{1,0:T(2,128)S(1)}, u32[]{:S(2)}, u32[]{:S(2)}) collective-permute-start(f32[2,1]{1,0:T(2,128)S(1)} %get-tuple-element.13), channel_id=1, source_target_pairs={{1,0},{2,1},{3,2},{5,4},{6,5},{7,6},{9,8},{10,9},{11,10},{13,12},{... | collective-permute-start | bytes 32 | tf_op jit(solution)/shard_map/ppermute | solution.py:18
  91.9 4.8 %collective-permute-start.6 = (f32[2,1]{1,0:T(2,128)S(1)}, f32[2,1]{1,0:T(2,128)S(1)}, u32[]{:S(2)}, u32[]{:S(2)}) collective-permute-start(f32[2,1]{1,0:T(2,128)S(1)} %get-tuple-element.10), channel_id=1, source_target_pairs={{0,1},{1,2},{2,3},{4,5},{5,6},{6,7},{8,9},{9,10},{10,11},{12,13},{... | collective-permute-start | bytes 32 | tf_op jit(solution)/shard_map/ppermute | solution.py:17
  95.4 5.5 %collective-permute-start.7 = (f32[2,1]{1,0:T(2,128)S(1)}, f32[2,1]{1,0:T(2,128)S(1)}, u32[]{:S(2)}, u32[]{:S(2)}) collective-permute-start(f32[2,1]{1,0:T(2,128)S(1)} %get-tuple-element.11), channel_id=1, source_target_pairs={{1,0},{2,1},{3,2},{5,4},{6,5},{7,6},{9,8},{10,9},{11,10},{13,12},{... | collective-permute-start | bytes 32 | tf_op jit(solution)/shard_map/ppermute | solution.py:18
  133.7 70.5 %reduce-scatter.5.cloned.1.call-start = ((), (), s32[]{:S(2)}) async-start(), calls=%async_computation.7 | async-start | bytes 294912 | tf_op jit(solution)/shard_map/reduce_scatter | solution.py:80
  146.9 58.8 %all-to-all-start.3 = ((bf16[8,8,4096]{2,1,0:T(8,128)(2,1)}), bf16[8,8,4096]{2,1,0:T(8,128)(2,1)S(1)}, u32[]{:S(2)}, u32[]{:S(2)}) async-start(bf16[8,8,4096]{2,1,0:T(8,128)(2,1)} %bitcast.10), calls=%async_computation.3 | async-start | bytes 1048576 | tf_op jit(solution)/shard_map/all_to_all | solution.py:91
Sparse Core Ops, SparseCore 0:
  133.8 32.8 reduce-scatter.2
  170.6 33.5 reduce-scatter.4
where the time goes:
time: 216 us; the launch traced here: 215 us
  local copies, waits for them, and re-layouts  65.8 us (30%)
  waiting for transfers between devices  64.3 us (30%)
  starting transfers between devices  37.8 us (17%)
  blocking collectives  18.1 us (8%)
  between operations  14.4 us (7%)
  other arithmetic  13.8 us (6%)
    reduce_scatter x2, waiting for transfers between devices, body(): lax.psum_scatter(weighted, 'member', scatter_dimension=1, tiled=True)  53 us
    convert_element_type x2, local copies, waits for them, and re-layouts, body(): prior_ensemble = (moved + model_perturbation[update_ordinal].reshape(part...  21.3 us
    all_gather x2, blocking collectives, body(): all_scores = lax.all_gather(loglik, 'member', axis=0, tiled=True)  18.1 us
    gather x2, local copies, waits for them, and re-layouts, body(): modelled_readings = prior_ensemble[:, measured_position].astype(jnp.float32)  18 us
    ppermute x4, starting transfers between devices, extended(): before = lax.ppermute(last, axis, up)  17.5 us
    scatter x2, local copies, waits for them, and re-layouts, body(): jnp.full((members, capacity), -1, jnp.int32).at[source, ranks].set(codes)  10.8 us
    ppermute x4, waiting for transfers between devices, extended(): after = lax.ppermute(initial, axis, down)  8.13 us
    all_to_all x2, starting transfers between devices, body(): lax.all_to_all(wanted, 'member', split_axis=0, concat_axis=0, tiled=True)  7.93 us
  transfers between devices with their start and end apart: 14, of which 5 were waited for; matrix products, arithmetic and copies ran while one was open for 22% of the time, Pallas kernels for 0%

commit v1 on v0

v1 whole, which is shorter than its diff:
```python
import jax
import jax.numpy as jnp
from jax import lax
from jax.experimental import pallas as pl
from jax.experimental.pallas import tpu as pltpu
from jax.sharding import PartitionSpec as P

CYCLES = 2
STEPS = 2
LANES = 128
F32 = jnp.float32
BF16 = jnp.bfloat16
I32 = jnp.int32
PARAMS = pltpu.CompilerParams(vmem_limit_bytes=48 * 1024 * 1024)


def iota(shape, dim):
    return lax.broadcasted_iota(I32, shape, dim)


def whole_spec(shape):
    zeros = (0,) * len(shape)
    return pl.BlockSpec(shape, lambda i: zeros)


def call(kernel, outs, args, specs=None, name=None):
    specs = specs or [whole_spec(a.shape) for a in args]
    return pl.pallas_call(
        kernel,
        out_shape=[jax.ShapeDtypeStruct(s, d) for s, d in outs],
        grid=(1,),
        in_specs=specs,
        out_specs=[whole_spec(s) for s, _ in outs],
        compiler_params=PARAMS,
        name=name,
    )(*args)


def column_of(row):
    n = row.shape[1]
    square = jnp.broadcast_to(row, (n, n))
    return jnp.sum(jnp.where(iota((n, n), 0) == iota((n, n), 1), square, 0), axis=1, keepdims=True)


def make_prepare(members, capacity, parts, tiles):
    def kernel(st0, st1, df0, df1, pb0, pb1, am, slot, up, down, req, keys):
        for ref, st, df, pb, t in ((up, st1, df1, pb1, tiles - 1), (down, st0, df0, pb0, 0)):
            rows = [st[p, t:t + 1, :].astype(F32) for p in range(parts)]
            rows += [df[t:t + 1, :]]
            rows += [pb[0, p, t:t + 1, :].astype(F32) for p in range(parts)]
            for p in range(parts):
                code = am[0, p:p + 1, t:t + 1] * capacity + slot[0, p:p + 1, t:t + 1]
                rows.append(jnp.broadcast_to(code.astype(F32), (1, LANES)))
            for i, row in enumerate(rows):
                ref[i:i + 1, :] = row
            for i in range(len(rows), ref.shape[0]):
                ref[i:i + 1, :] = jnp.zeros((1, LANES), F32)
        before = (iota((tiles, tiles), 0) < iota((tiles, tiles), 1)).astype(F32)
        slots = members * capacity
        for c in range(CYCLES):
            seen = jnp.zeros((members, 1), F32)
            wanted = jnp.full((slots, 1), -1, I32)
            for p in range(parts):
                source = am[c, p:p + 1, :]
                named = (iota((members, tiles), 0) == source).astype(F32)
                earlier = seen + jnp.dot(named, before, preferred_element_type=F32)
                rank = jnp.sum(named * earlier, axis=0, keepdims=True).astype(I32)
                seen = seen + jnp.sum(named, axis=1, keepdims=True)
                key = source * capacity + rank
                code = slot[c, p:p + 1, :] * tiles + iota((1, tiles), 1)
                hit = jnp.where(iota((slots, tiles), 0) == key, code, -1)
                wanted = jnp.maximum(wanted, jnp.max(hit, axis=1, keepdims=True))
                keys[c, p * tiles:(p + 1) * tiles, :] = jnp.broadcast_to(column_of(key), (tiles, LANES))
            wide = jnp.broadcast_to(wanted, (slots, LANES))
            req[:, c * capacity:(c + 1) * capacity, :] = wide.reshape(members, capacity, LANES)

    return kernel


def widen(x, left, right):
    tiles = x.shape[0]
    row = iota((tiles, LANES), 0)
    before = jnp.where(row == 0, left, pltpu.roll(x[:, -LANES:], 1, 0))
    after = jnp.where(row == tiles - 1, right, pltpu.roll(x[:, :LANES], tiles - 1, 0))
    return jnp.concatenate([before, x, after], axis=1)


def diffuse(x, d):
    n = x.shape[1]
    for _ in range(STEPS):
        x = x + d * (pltpu.roll(x, 1, 1) - 2.0 * x + pltpu.roll(x, n - 1, 1))
    return x


def pick_rows(wanted, rows):
    m = rows.shape[0]
    n = wanted.shape[0]
    choice = (wanted[:, :m] == iota((n, m), 1)).astype(F32).astype(BF16)
    return jnp.dot(choice, rows, preferred_element_type=F32)


def send_rows(req, prior, out, first, capacity, cells):
    members = req.shape[0]
    wanted = req[:, first:first + capacity, :].reshape(members * capacity, LANES)
    sent = pick_rows(wanted, prior)
    out[:, :, :cells] = sent.reshape(members, capacity, cells).astype(BF16)


def assess(prior, obs_i, terms, pattern, weight, parts, tiles, cells):
    blocks = cells // LANES
    rows = tiles * blocks
    count = obs_i.shape[1]
    stacked = jnp.concatenate(
        [jnp.concatenate([x[:, k * LANES:(k + 1) * LANES] for k in range(blocks)], axis=0) for x in prior],
        axis=1,
    )
    choice = (iota((rows, count), 0) == obs_i[0:1, :]).astype(F32).astype(BF16)
    lines = lax.dot_general(stacked, choice, (((0,), (0,)), ((), ())), preferred_element_type=F32)
    lane = (iota((LANES, count), 0) == obs_i[1:2, :])
    prec, value, group = terms
    local = jnp.zeros((tiles, count), F32)
    for k in range(pattern.shape[1]):
        local = local + jnp.where(pattern[:, k:k + 1] == group, weight[:, k:k + 1], 0.0)
    score = []
    for p in range(parts):
        predicted = jnp.sum(jnp.where(lane, lines[p * LANES:(p + 1) * LANES, :], 0.0), axis=0, keepdims=True)
        miss = value - predicted
        term = 0.5 * (prec * miss * miss)
        score.append(jnp.sum(local * term, axis=1, keepdims=True))
    least = score[0]
    for s in score[1:]:
        least = jnp.minimum(least, s)
    scale = [jnp.exp(least - s) for s in score]
    total = scale[0]
    for s in scale[1:]:
        total = total + s
    weighted = scale[0] * prior[0].astype(F32)
    for s, x in zip(scale[1:], prior[1:]):
        weighted = weighted + s * x.astype(F32)
    return least, total, weighted


def pieces(x):
    high = x.astype(BF16).astype(F32)
    middle = (x - high).astype(BF16).astype(F32)
    low = (x - high - middle).astype(BF16).astype(F32)
    return high, middle, low


def make_first(capacity, parts, tiles, cells):
    def kernel(state, diff, pert, below, above, req, send, prior_out):
        d = widen(diff[...], below[parts:parts + 1, :], above[parts:parts + 1, :])
        edge = []
        prior = []
        for p in range(parts):
            x = widen(state[p].astype(F32), below[p:p + 1, :], above[p:p + 1, :])
            x = diffuse(x, d)
            now = (x[:, LANES:LANES + cells] + pert[0, p].astype(F32)).astype(BF16)
            prior.append(now)
            prior_out[p] = now
            q = parts + 1 + p
            low = x[0:1, :LANES] + below[q:q + 1, :]
            high = x[tiles - 1:tiles, LANES + cells:] + above[q:q + 1, :]
            edge.append(jnp.where(iota((1, LANES), 1) < LANES // 2, high, low))
        send_rows(req, jnp.concatenate(prior, axis=0), send, 0, capacity, cells)
        row = iota((capacity, LANES), 0)
        misc = jnp.zeros((capacity, LANES), F32)
        for p in range(parts):
            misc = jnp.where(row == p, edge[p], misc)
        members = send.shape[0]
        send[:, :, cells:] = jnp.broadcast_to(misc.astype(BF16)[None], (members, capacity, LANES))

    return kernel


def make_assess(parts, tiles, cells):
    def kernel(prior, obs_i, obs_f, pattern, weight, part, stats):
        terms = (obs_f[0:1, :], obs_f[1:2, :], obs_i[2:3, :])
        least, total, weighted = assess(
            [prior[p] for p in range(parts)], obs_i, terms, pattern[...], weight[...], parts, tiles, cells
        )
        part[...] = weighted.astype(BF16)
        lane = iota((tiles, LANES), 1)
        stats[...] = jnp.where(lane == 0, least, total)

    return kernel


def make_second(members, capacity, parts, tiles, cells):
    share = cells // members
    groups = tiles // capacity

    def kernel(got, keys, diff, pert, below, above, req, part1, stats1, obs_i, obs_f, pattern, weight, send):
        slots = members * capacity
        arrived = got[...].reshape(slots, cells + LANES)
        field = pick_rows(keys[0], arrived[:, :cells])
        lines = arrived[:, cells:]
        q = 2 * parts + 1
        first = pick_rows(below[q:q + parts, :].astype(I32), lines)
        last = pick_rows(above[q:q + parts, :].astype(I32), lines)
        d = widen(diff[...], below[parts:parts + 1, :], above[parts:parts + 1, :])
        prior = []
        for p in range(parts):
            x = widen(field[p * tiles:(p + 1) * tiles, :], first[p:p + 1, :], last[p:p + 1, :])
            x = diffuse(x, d)[:, LANES:LANES + cells]
            prior.append((x + pert[0, p].astype(F32)).astype(BF16))
        send_rows(req, jnp.concatenate(prior, axis=0), send, capacity, capacity, cells)
        terms = (obs_f[0:1, :], obs_f[2:3, :], obs_i[2:3, :])
        least, total, weighted = assess(prior, obs_i, terms, pattern[...], weight[...], parts, tiles, cells)
        kept = (part1[...].astype(F32), weighted)
        for c in range(CYCLES):
            for m in range(members):
                for g in range(groups):
                    at = cells + (c * groups + g) * share
                    block = kept[c][g * capacity:(g + 1) * capacity, m * share:(m + 1) * share]
                    send[m, :, at:at + share] = block.astype(BF16)
        lane = iota((capacity, LANES), 1)
        misc = jnp.zeros((capacity, LANES), F32)
        spot = 0
        for x in (stats1[:, 0:1], stats1[:, 1:2], least, total):
            for piece in pieces(x):
                for g in range(groups):
                    misc = jnp.where(lane == spot, piece[g * capacity:(g + 1) * capacity, :], misc)
                    spot += 1
        at = cells + CYCLES * groups * share
        send[:, :, at:] = jnp.broadcast_to(misc.astype(BF16)[None], (members, capacity, LANES))

    return kernel


def make_last(members, capacity, parts, tiles, cells):
    share = cells // members
    groups = tiles // capacity

    def kernel(got, keys, analysis, mean):
        slots = members * capacity
        rows = got[:, :, :cells].reshape(slots, cells)
        picked = pick_rows(keys[1], rows)
        for p in range(parts):
            analysis[p] = picked[p * tiles:(p + 1) * tiles, :].astype(BF16)
        at = cells + CYCLES * groups * share
        misc = got[:, :, at:].astype(F32)
        for c in range(CYCLES):
            for g in range(groups):
                pair = []
                for kind in range(2):
                    spot = (c * 2 + kind) * 3 * groups + g
                    x = misc[:, :, spot:spot + 1]
                    for piece in range(1, 3):
                        x = x + misc[:, :, spot + piece * groups:spot + piece * groups + 1]
                    pair.append(x)
                least, total = pair
                scale = jnp.exp(jnp.min(least, axis=0, keepdims=True) - least)
                start = cells + (c * groups + g) * share
                part = got[:, :, start:start + share].astype(F32)
                top = jnp.sum(scale * part, axis=0)
                mean[c, g * capacity:(g + 1) * capacity, :] = top / jnp.sum(scale * total, axis=0)

    return kernel


def body(
    state,
    diffusivity,
    model_perturbation,
    obs_values,
    obs_prec,
    obs_tile,
    obs_cell,
    pattern,
    loc_weight,
    anc_member,
    anc_slot,
):
    parts, tiles, cells = state.shape
    members = lax.axis_size("member")
    regions = lax.axis_size("region")
    capacity = max(2, 2 * parts * tiles // members)
    share = cells // members
    groups = tiles // capacity
    blocks, per_block = obs_cell.shape
    count = blocks * per_block
    member_of = anc_member.reshape(CYCLES, parts, tiles)
    slot_of = anc_slot.reshape(CYCLES, parts, tiles)

    ends = cells // LANES - 1

    def block(shape, at):
        lead = (0,) * (len(shape) - 1)
        return pl.BlockSpec(shape, lambda i: lead + (at,))

    up, down, req, keys = call(
        make_prepare(members, capacity, parts, tiles),
        [((8, LANES), F32), ((8, LANES), F32), ((members, CYCLES * capacity, LANES), I32), ((CYCLES, parts * tiles, LANES), I32)],
        [state, state, diffusivity, diffusivity, model_perturbation, model_perturbation, member_of, slot_of],
        [
            block((parts, tiles, LANES), 0),
            block((parts, tiles, LANES), ends),
            block((tiles, LANES), 0),
            block((tiles, LANES), ends),
            block((1, parts, tiles, LANES), 0),
            block((1, parts, tiles, LANES), ends),
            whole_spec(member_of.shape),
            whole_spec(slot_of.shape),
        ],
        name="prepare",
    )
    forward = [(i, i + 1) for i in range(regions - 1)]
    below = lax.ppermute(up, "region", forward)
    above = lax.ppermute(down, "region", [(j, i) for i, j in forward])
    asked = lax.all_to_all(req, "member", split_axis=0, concat_axis=0, tiled=True)

    cell_block = (obs_cell // LANES) * tiles + obs_tile[:, None]
    group = jnp.broadcast_to(jnp.arange(blocks, dtype=I32)[:, None], obs_cell.shape)
    obs_i = jnp.stack([cell_block, obs_cell % LANES, group]).reshape(3, count)
    obs_f = jnp.concatenate([obs_prec[None], obs_values]).reshape(1 + CYCLES, count)

    def noise_spec(c):
        return pl.BlockSpec((1, parts, tiles, cells), lambda i: (c, 0, 0, 0))

    send, prior = call(
        make_first(capacity, parts, tiles, cells),
        [((members, capacity, cells + LANES), BF16), ((parts, tiles, cells), BF16)],
        [state, diffusivity, model_perturbation, below, above, asked],
        [
            whole_spec(state.shape),
            whole_spec(diffusivity.shape),
            noise_spec(0),
            whole_spec(below.shape),
            whole_spec(above.shape),
            whole_spec(asked.shape),
        ],
        name="forecast_first",
    )
    got = lax.all_to_all(send, "member", split_axis=0, concat_axis=0, tiled=True)
    part, stats = call(
        make_assess(parts, tiles, cells),
        [((tiles, cells), BF16), ((tiles, LANES), F32)],
        [prior, obs_i, obs_f, pattern, loc_weight],
        name="assess_first",
    )
    width = cells + CYCLES * groups * share + LANES
    args = [got, keys, diffusivity, model_perturbation, below, above, asked, part, stats, obs_i, obs_f, pattern, loc_weight]
    specs = [whole_spec(a.shape) for a in args]
    specs[3] = noise_spec(1)
    (send,) = call(
        make_second(members, capacity, parts, tiles, cells),
        [((members, capacity, width), BF16)],
        args,
        specs,
        name="forecast_second",
    )
    got = lax.all_to_all(send, "member", split_axis=0, concat_axis=0, tiled=True)
    return tuple(
        call(
            make_last(members, capacity, parts, tiles, cells),
            [(state.shape, BF16), ((CYCLES, tiles, share), F32)],
            [got, keys],
            name="finish",
        )
    )


def solution(mesh):
    in_specs = (
        P("member", "region", None),
        P("region", None),
        P(None, "member", "region", None),
        P(None, "region", None),
        P("region", None),
        P("region"),
        P("region", None),
        P("region", None),
        P("region", None),
        P(None, "region", "member", None, None),
        P(None, "region", "member", None),
    )
    out_specs = (P("member", "region", None), P(None, "region", "member"))
    return jax.shard_map(body, mesh=mesh, in_specs=in_specs, out_specs=out_specs, check_vma=False)
```

time: 216 us -> 54.2 us (0.25)
  local copies, waits for them, and re-layouts: 65.8 us -> 7.58 us
  waiting for transfers between devices: 64.3 us -> 10.3 us
  starting transfers between devices: 37.8 us -> 14.3 us
  other arithmetic: 13.8 us -> 0.04 us
  between operations: 14.4 us -> 0.75 us
  Pallas kernels: 0 us -> 5.44 us
  blocking collectives: 18.1 us -> 15.1 us
    reduce_scatter x2 -> x0, waiting for transfers between devices: 53 us -> none  [body(): lax.psum_scatter(weighted, 'member', scatter_dimension=1, tiled=True)]
    gather x6 -> x0, local copies, waits for them, and re-layouts: 24.7 us -> none  [the longest x2 18 us: body(): modelled_readings = prior_ensemble[:, measured_position].astype(jnp.float32)]
    convert_element_type x3 -> x0, local copies, waits for them, and re-layouts: 21.9 us -> none  [the longest x2 21.3 us: body(): prior_ensemble = (moved + model_perturbation[update_ordinal].reshape(part...]
    all_gather x2 -> x0, blocking collectives: 18.1 us -> none  [body(): all_scores = lax.all_gather(loglik, 'member', axis=0, tiled=True)]
    ppermute x8 -> x2, starting transfers between devices: 22.8 us -> 4.76 us  [the longest x1 3.47 us: body(): below = lax.ppermute(up, 'region', forward)]
    all_to_all x0 -> x1, blocking collectives: none -> 15.1 us  [body(): lax.all_to_all(send, 'member', split_axis=0, concat_axis=0, tiled=True)]
    scatter x2 -> x0, local copies, waits for them, and re-layouts: 10.8 us -> none  [body(): jnp.full((members, capacity), -1, jnp.int32).at[source, ranks].set(codes)]
    pallas_call x0 -> x5, Pallas kernels: none -> 5.44 us  [call(): pl.pallas_call(kernel, out_shape=[jax.ShapeDtypeStruct(s, d) for s, d in...]
  transfers between devices with their start and end apart: 14 -> 4, of which waited for: 5 -> 2; matrix products, arithmetic and copies ran while one was open for 22% -> 2% of each run, Pallas kernels for 0% -> 1%
where the time goes in v1:
time: 54.2 us; the launch traced here: 53.5 us
  blocking collectives  15.1 us (28%)
  starting transfers between devices  14.3 us (26%)
  waiting for transfers between devices  10.3 us (19%)
  local copies, waits for them, and re-layouts  7.58 us (14%)
  Pallas kernels  5.44 us (10%)
  between operations  0.75 us (1%)
    all_to_all x1, blocking collectives, body(): lax.all_to_all(send, 'member', split_axis=0, concat_axis=0, tiled=True)  15.1 us
    unnamed x32, local copies, waits for them, and re-layouts  7.01 us
    all_to_all x1, waiting for transfers between devices, body(): lax.all_to_all(send, 'member', split_axis=0, concat_axis=0, tiled=True)  6.05 us
    pallas_call x5, Pallas kernels, call(): pl.pallas_call(kernel, out_shape=[jax.ShapeDtypeStruct(s, d) for s, d in...  5.44 us
    all_to_all x1, starting transfers between devices, body(): lax.all_to_all(req, 'member', split_axis=0, concat_axis=0, tiled=True)  5.17 us
    all_to_all x1, starting transfers between devices, body(): lax.all_to_all(send, 'member', split_axis=0, concat_axis=0, tiled=True)  4.33 us
    ppermute x1, waiting for transfers between devices, body(): above = lax.ppermute(down, 'region', [(j, i) for i, j in forward])  4.19 us
    ppermute x1, starting transfers between devices, body(): below = lax.ppermute(up, 'region', forward)  3.47 us
  transfers between devices with their start and end apart: 4, of which 2 were waited for; matrix products, arithmetic and copies ran while one was open for 2% of the time, Pallas kernels for 1%

profile of v1, /device:TPU:0, one launch (start us, length us, event | category | flops | bytes accessed | tf_op | source)
XLA Modules:
  0.0 53.5 jit_solution(10271480693920905293)
XLA Ops:
  0.6 0.0 copy-start.6
  0.6 0.7 %copy-done.6 = s32[2,1,2,16,1]{3,4,2,1,0:T(1,128)S(1)} copy-done((s32[2,1,2,16,1]{3,4,2,1,0:T(1,128)S(1)}, s32[2,1,2,16,1]{3,4,2,1,0:T(1,128)}, u32[]{:S(2)}) %copy-start.6) | copy-done | bytes 280
  1.3 0.0 copy-start
  1.3 1.0 %copy-done = bf16[2,2,16,4096]{3,2,1,0:T(8,128)(2,1)S(1)} copy-done((bf16[2,2,16,4096]{3,2,1,0:T(8,128)(2,1)S(1)}, bf16[2,2,16,4096]{3,2,1,0:T(8,128)(2,1)}, u32[]{:S(2)}) %copy-start) | copy-done | bytes 524312
  2.4 0.0 copy-start.2
  2.4 0.9 %copy-done.2 = f32[16,4096]{1,0:T(8,128)S(1)} copy-done((f32[16,4096]{1,0:T(8,128)S(1)}, f32[16,4096]{1,0:T(8,128)}, u32[]{:S(2)}) %copy-start.2) | copy-done | bytes 262168
  3.3 0.0 copy-start.4
  3.3 0.9 %copy-done.4 = bf16[2,16,4096]{2,1,0:T(8,128)(2,1)S(1)} copy-done((bf16[2,16,4096]{2,1,0:T(8,128)(2,1)S(1)}, bf16[2,16,4096]{2,1,0:T(8,128)(2,1)}, u32[]{:S(2)}) %copy-start.4) | copy-done | bytes 262168
  4.3 0.0 copy-start.7
  4.3 0.7 %copy-done.7 = s32[2,1,2,16]{3,2,1,0:T(2,128)S(1)} copy-done((s32[2,1,2,16]{3,2,1,0:T(2,128)S(1)}, s32[2,1,2,16]{3,2,1,0:T(2,128)}, u32[]{:S(2)}) %copy-start.7) | copy-done | bytes 280
  4.9 0.0 copy-start.1
  4.9 1.0 %prepare.1 = (f32[8,128]{1,0:T(8,128)S(1)}, f32[8,128]{1,0:T(8,128)S(1)}, s32[8,16,128]{2,1,0:T(8,128)}, s32[2,32,128]{2,1,0:T(8,128)S(1)}) custom-call(bf16[2,16,4096]{2,1,0:T(8,128)(2,1)S(1)} %copy-done.4, bf16[2,16,4096]{2,1,0:T(8,128)(2,1)S(1)} %copy-done.4, f32[16,4096]{1,0:T(8,128)S(1)} %copy-done.2, f32[16,4096]{1,0:T(8,128)S(1)} %copy-done.2, ...), custom_call_target="tpu_custom_call" | custom-call | tf_op jit(solution)/shard_map/prepare/pallas_call | solution.py:28
  5.9 5.2 %all-to-all-start = ((s32[8,16,128]{2,1,0:T(8,128)}), s32[8,16,128]{2,1,0:T(8,128)S(1)}, u32[]{:S(2)}, u32[]{:S(2)}) async-start(s32[8,16,128]{2,1,0:T(8,128)} %get-tuple-element.12), calls=%async_computation | async-start | bytes 131072 | tf_op jit(solution)/shard_map/all_to_all | solution.py:311
  11.1 3.5 %collective-permute-start = (f32[8,128]{1,0:T(8,128)S(1)}, f32[8,128]{1,0:T(8,128)S(1)}, u32[]{:S(2)}, u32[]{:S(2)}) collective-permute-start(f32[8,128]{1,0:T(8,128)S(1)} %get-tuple-element.10), channel_id=1, source_target_pairs={{0,1},{1,2},{2,3},{4,5},{5,6},{6,7},{8,9},{9,10},{10,11},{12,13},{... | collective-permute-start | bytes 12296 | tf_op jit(solution)/shard_map/ppermute | solution.py:309
  14.6 1.3 %collective-permute-start.1 = (f32[8,128]{1,0:T(8,128)S(1)}, f32[8,128]{1,0:T(8,128)S(1)}, u32[]{:S(2)}, u32[]{:S(2)}) collective-permute-start(f32[8,128]{1,0:T(8,128)S(1)} %get-tuple-element.11), channel_id=1, source_target_pairs={{1,0},{2,1},{3,2},{5,4},{6,5},{7,6},{9,8},{10,9},{11,10},{13,12},{... | collective-permute-start | bytes 12296 | tf_op jit(solution)/shard_map/ppermute | solution.py:310
  15.9 0.0 collective-permute-done.below
  15.9 4.2 %collective-permute-done.1.above = f32[8,128]{1,0:T(8,128)S(1)} collective-permute-done((f32[8,128]{1,0:T(8,128)S(1)}, f32[8,128]{1,0:T(8,128)S(1)}, u32[]{:S(2)}, u32[]{:S(2)}) %collective-permute-start.1) | collective-permute-done | bytes 4128 | tf_op jit(solution)/shard_map/ppermute | solution.py:310
  20.1 0.0 all-to-all-done.req
  20.1 0.0 copy-done.1
  20.1 0.0 copy-done.3
  20.1 0.0 copy-done.5
  20.1 1.6 %forecast_first.1 = (bf16[8,8,4224]{2,1,0:T(8,128)(2,1)}, bf16[2,16,4096]{2,1,0:T(8,128)(2,1)S(1)}) custom-call(bf16[2,16,4096]{2,1,0:T(8,128)(2,1)S(1)} %copy-done.5, f32[16,4096]{1,0:T(8,128)S(1)} %copy-done.3, bf16[2,2,16,4096]{3,2,1,0:T(8,128)(2,1)S(1)} %copy-done.1, f32[8,128]{1,0:T(8,128)S(1)} %collective-permute-done.below, ...), custom_call_target="tpu_custom_call" | custom-call | tf_op jit(solution)/shard_map/forecast_first/pallas_call | solution.py:28
  21.7 4.3 %all-to-all-start.1 = ((bf16[8,8,4224]{2,1,0:T(8,128)(2,1)}), bf16[8,8,4224]{2,1,0:T(8,128)(2,1)S(1)}, u32[]{:S(2)}, u32[]{:S(2)}) async-start(bf16[8,8,4224]{2,1,0:T(8,128)(2,1)} %get-tuple-element.13), calls=%async_computation.1 | async-start | bytes 1081344 | tf_op jit(solution)/shard_map/all_to_all | solution.py:335
  26.1 0.0 copy-done.11
  26.1 0.0 copy-start.12
  26.1 0.1 copy.25.pattern
  26.2 0.6 %copy-done.12 = f32[16,6]{0,1:T(8,128)S(1)} copy-done((f32[16,6]{0,1:T(8,128)S(1)}, f32[16,6]{0,1:T(8,128)}, u32[]{:S(2)}) %copy-start.12) | copy-done | bytes 408
  26.8 0.1 copy.26.weight
  26.9 0.6 %copy-done.9 = f32[32,16]{0,1:T(8,128)S(1)} copy-done((f32[32,16]{0,1:T(8,128)S(1)}, f32[32,16]{0,1:T(8,128)}, u32[]{:S(2)}) %copy-start.9) | copy-done | bytes 2072
  27.5 0.1 copy.23
  27.5 0.1 concatenate.9
  27.6 0.0 copy-start.10
  27.6 0.0 copy-start.13
  27.7 0.1 stack_broadcast_in_dim.8
  27.7 0.6 %copy-done.10 = s32[32,16]{0,1:T(8,128)S(1)} copy-done((s32[32,16]{0,1:T(8,128)S(1)}, s32[32,16]{0,1:T(8,128)}, u32[]{:S(2)}) %copy-start.10) | copy-done | bytes 2072
  28.3 0.0 copy-done.13
  28.4 0.1 copy.21
  28.4 0.1 stack.9
  28.5 0.1 copy.22
  28.6 0.1 stack.10
  28.7 0.6 %copy-done.8 = f32[2,32,16]{1,2,0:T(8,128)S(1)} copy-done((f32[2,32,16]{1,2,0:T(8,128)S(1)}, f32[2,32,16]{1,2,0:T(8,128)}, u32[]{:S(2)}) %copy-start.8) | copy-done | bytes 4120
  29.2 0.1 copy.24
  29.3 0.1 concatenate.10
  29.4 0.5 assess_first.1
  29.9 6.0 %all-to-all-done.1.got = bf16[8,8,4224]{2,1,0:T(8,128)(2,1)S(1)} async-done(((bf16[8,8,4224]{2,1,0:T(8,128)(2,1)}), bf16[8,8,4224]{2,1,0:T(8,128)(2,1)S(1)}, u32[]{:S(2)}, u32[]{:S(2)}) %all-to-all-start.1) | async-done | bytes 540704 | tf_op jit(solution)/shard_map/all_to_all | solution.py:335
  36.0 1.4 %forecast_second.1 = bf16[8,8,6272]{2,1,0:T(8,128)(2,1)S(1)} custom-call(bf16[8,8,4224]{2,1,0:T(8,128)(2,1)S(1)} %all-to-all-done.1.got, s32[2,32,128]{2,1,0:T(8,128)S(1)} %get-tuple-element.14.keys, f32[16,4096]{1,0:T(8,128)S(1)} %copy-done.3, bf16[2,2,16,4096]{3,2,1,0:T(8,128)(2,1)S(1)} %copy-done.1, f32[8,128]{1,0:T(8,128)S(1)} %collective-permute-done.below, ...), custom_call_target="tpu_custom_call" | custom-call | tf_op jit(solution)/shard_map/forecast_second/pallas_call | solution.py:28
  37.4 15.1 %all_to_all.15.got = bf16[8,8,6272]{2,1,0:T(8,128)(2,1)S(1)} all-to-all(bf16[8,8,6272]{2,1,0:T(8,128)(2,1)S(1)} %forecast_second.1), channel_id=1, replica_groups=mesh['member'=8,'region'=4] {'member'}, dimensions={0} | all-to-all | bytes 1605632 | tf_op jit(solution)/shard_map/all_to_all | solution.py:353
  52.5 0.9 %finish.1 = (bf16[2,16,4096]{2,1,0:T(8,128)(2,1)}, f32[2,16,512]{2,1,0:T(8,128)}) custom-call(bf16[8,8,6272]{2,1,0:T(8,128)(2,1)S(1)} %all_to_all.15.got, s32[2,32,128]{2,1,0:T(8,128)S(1)} %get-tuple-element.14.keys), custom_call_target="tpu_custom_call" | custom-call | tf_op jit(solution)/shard_map/finish/pallas_call | solution.py:28
  (9 shorter events, 0.0 us)
Async XLA Ops:
  0.6 0.7 %copy-start.6 = (s32[2,1,2,16,1]{3,4,2,1,0:T(1,128)S(1)}, s32[2,1,2,16,1]{3,4,2,1,0:T(1,128)}, u32[]{:S(2)}) copy-start(s32[2,1,2,16,1]{3,4,2,1,0:T(1,128)} %param.20) | copy-start | bytes 772
  1.3 1.0 %copy-start = (bf16[2,2,16,4096]{3,2,1,0:T(8,128)(2,1)S(1)}, bf16[2,2,16,4096]{3,2,1,0:T(8,128)(2,1)}, u32[]{:S(2)}) copy-start(bf16[2,2,16,4096]{3,2,1,0:T(8,128)(2,1)} %pert.3) | copy-start | bytes 1572868
  2.4 0.9 %copy-start.2 = (f32[16,4096]{1,0:T(8,128)S(1)}, f32[16,4096]{1,0:T(8,128)}, u32[]{:S(2)}) copy-start(f32[16,4096]{1,0:T(8,128)} %diff.3) | copy-start | bytes 786436
  3.3 0.9 %copy-start.4 = (bf16[2,16,4096]{2,1,0:T(8,128)(2,1)S(1)}, bf16[2,16,4096]{2,1,0:T(8,128)(2,1)}, u32[]{:S(2)}) copy-start(bf16[2,16,4096]{2,1,0:T(8,128)(2,1)} %state.1) | copy-start | bytes 786436
  4.3 0.7 %copy-start.7 = (s32[2,1,2,16]{3,2,1,0:T(2,128)S(1)}, s32[2,1,2,16]{3,2,1,0:T(2,128)}, u32[]{:S(2)}) copy-start(s32[2,1,2,16]{3,2,1,0:T(2,128)} %param.21) | copy-start | bytes 772
  4.9 15.2 %copy-start.1 = (bf16[2,2,16,4096]{3,2,1,0:T(8,128)(2,1)S(1)}, bf16[2,2,16,4096]{3,2,1,0:T(8,128)(2,1)}, u32[]{:S(2)}) copy-start(bf16[2,2,16,4096]{3,2,1,0:T(8,128)(2,1)} %pert.3) | copy-start | bytes 1572868
  4.9 15.2 %copy-start.3 = (f32[16,4096]{1,0:T(8,128)S(1)}, f32[16,4096]{1,0:T(8,128)}, u32[]{:S(2)}) copy-start(f32[16,4096]{1,0:T(8,128)} %diff.3) | copy-start | bytes 786436
  4.9 15.2 %copy-start.5 = (bf16[2,16,4096]{2,1,0:T(8,128)(2,1)S(1)}, bf16[2,16,4096]{2,1,0:T(8,128)(2,1)}, u32[]{:S(2)}) copy-start(bf16[2,16,4096]{2,1,0:T(8,128)(2,1)} %state.1) | copy-start | bytes 786436
  5.9 14.2 %all-to-all-start = ((s32[8,16,128]{2,1,0:T(8,128)}), s32[8,16,128]{2,1,0:T(8,128)S(1)}, u32[]{:S(2)}, u32[]{:S(2)}) async-start(s32[8,16,128]{2,1,0:T(8,128)} %get-tuple-element.12), calls=%async_computation | async-start | bytes 131072 | tf_op jit(solution)/shard_map/all_to_all | solution.py:311
  11.1 4.8 %collective-permute-start = (f32[8,128]{1,0:T(8,128)S(1)}, f32[8,128]{1,0:T(8,128)S(1)}, u32[]{:S(2)}, u32[]{:S(2)}) collective-permute-start(f32[8,128]{1,0:T(8,128)S(1)} %get-tuple-element.10), channel_id=1, source_target_pairs={{0,1},{1,2},{2,3},{4,5},{5,6},{6,7},{8,9},{9,10},{10,11},{12,13},{... | collective-permute-start | bytes 12296 | tf_op jit(solution)/shard_map/ppermute | solution.py:309
  14.6 5.5 %collective-permute-start.1 = (f32[8,128]{1,0:T(8,128)S(1)}, f32[8,128]{1,0:T(8,128)S(1)}, u32[]{:S(2)}, u32[]{:S(2)}) collective-permute-start(f32[8,128]{1,0:T(8,128)S(1)} %get-tuple-element.11), channel_id=1, source_target_pairs={{1,0},{2,1},{3,2},{5,4},{6,5},{7,6},{9,8},{10,9},{11,10},{13,12},{... | collective-permute-start | bytes 12296 | tf_op jit(solution)/shard_map/ppermute | solution.py:310
  21.7 4.3 %copy-start.11 = (s32[16,6]{0,1:T(8,128)S(1)}, s32[16,6]{0,1:T(8,128)}, u32[]{:S(2)}) copy-start(s32[16,6]{0,1:T(8,128)} %param.18) | copy-start | bytes 1156
  21.7 14.3 %all-to-all-start.1 = ((bf16[8,8,4224]{2,1,0:T(8,128)(2,1)}), bf16[8,8,4224]{2,1,0:T(8,128)(2,1)S(1)}, u32[]{:S(2)}, u32[]{:S(2)}) async-start(bf16[8,8,4224]{2,1,0:T(8,128)(2,1)} %get-tuple-element.13), calls=%async_computation.1 | async-start | bytes 1081344 | tf_op jit(solution)/shard_map/all_to_all | solution.py:335
  26.1 0.7 %copy-start.12 = (f32[16,6]{0,1:T(8,128)S(1)}, f32[16,6]{0,1:T(8,128)}, u32[]{:S(2)}) copy-start(f32[16,6]{0,1:T(8,128)} %param.19) | copy-start | bytes 1156
  26.8 0.7 %copy-start.9 = (f32[32,16]{0,1:T(8,128)S(1)}, f32[32,16]{0,1:T(8,128)}, u32[]{:S(2)}) copy-start(f32[32,16]{0,1:T(8,128)} %param.15) | copy-start | bytes 6148
  27.6 0.7 %copy-start.10 = (s32[32,16]{0,1:T(8,128)S(1)}, s32[32,16]{0,1:T(8,128)}, u32[]{:S(2)}) copy-start(s32[32,16]{0,1:T(8,128)} %param.17) | copy-start | bytes 6148
  27.6 0.7 %copy-start.13 = (s32[32]{0:T(128)S(1)}, s32[32]{0:T(128)}, u32[]{:S(2)}) copy-start(s32[32]{0:T(128)} %param.16) | copy-start | bytes 388
  28.5 0.7 %copy-start.8 = (f32[2,32,16]{1,2,0:T(8,128)S(1)}, f32[2,32,16]{1,2,0:T(8,128)}, u32[]{:S(2)}) copy-start(f32[2,32,16]{1,2,0:T(8,128)} %param.14) | copy-start | bytes 12292

commit v2 on v1

v2 whole, which is shorter than its diff:
```python
import jax
import jax.numpy as jnp
from jax import lax
from jax.experimental import pallas as pl
from jax.experimental.pallas import tpu as pltpu
from jax.sharding import PartitionSpec as P

CYCLES = 2
STEPS = 2
LANES = 128
F32 = jnp.float32
BF16 = jnp.bfloat16
I32 = jnp.int32
PARAMS = pltpu.CompilerParams(vmem_limit_bytes=48 * 1024 * 1024)


def iota(shape, dim):
    return lax.broadcasted_iota(I32, shape, dim)


def whole_spec(shape):
    zeros = (0,) * len(shape)
    return pl.BlockSpec(shape, lambda i: zeros)


def call(kernel, outs, args, specs=None, name=None):
    specs = specs or [whole_spec(a.shape) for a in args]
    return pl.pallas_call(
        kernel,
        out_shape=[jax.ShapeDtypeStruct(s, d) for s, d in outs],
        grid=(1,),
        in_specs=specs,
        out_specs=[whole_spec(s) for s, _ in outs],
        compiler_params=PARAMS,
        name=name,
    )(*args)


def column_of(row):
    n = row.shape[1]
    square = jnp.broadcast_to(row, (n, n))
    return jnp.sum(jnp.where(iota((n, n), 0) == iota((n, n), 1), square, 0), axis=1, keepdims=True)


def here():
    return lax.axis_index("region"), lax.axis_index("member")


def make_prepare(regions, members, capacity, parts, tiles):
    width = 2 * STEPS

    def kernel(st0, st1, df0, df1, pb0, pb1, am, slot, note, keys):
        r, m = here()
        lane = iota((1, LANES), 1)
        halo = []
        for st, df, pb, t in ((st1, df1, pb1, tiles - 1), (st0, df0, pb0, 0)):
            top = t > 0
            rows = [st[p, t:t + 1, :].astype(F32) for p in range(parts)]
            rows += [df[t:t + 1, :]]
            rows += [pb[0, p, t:t + 1, :].astype(F32) for p in range(parts)]
            out = jnp.zeros((1, LANES), F32)
            for i, row in enumerate(rows):
                shift = (LANES - 8 * i) % LANES if top else 8 * i
                first = LANES - 8 * i - width if top else 8 * i
                moved = pltpu.roll(row, shift, 1) if shift else row
                out = jnp.where((lane >= first) & (lane < first + width), moved, out)
            for p in range(parts):
                code = am[0, p:p + 1, t:t + 1] * capacity + slot[0, p:p + 1, t:t + 1]
                out = jnp.where(lane == (p if top else LANES - 1 - p), code.astype(F32), out)
            halo.append(out)
        before = (iota((tiles, tiles), 0) < iota((tiles, tiles), 1)).astype(F32)
        asked = jnp.full((members, LANES), -1.0, F32)
        for c in range(CYCLES):
            seen = jnp.zeros((members, 1), F32)
            for p in range(parts):
                source = am[c, p:p + 1, :]
                named = (iota((members, tiles), 0) == source).astype(F32)
                earlier = seen + jnp.dot(named, before, preferred_element_type=F32)
                rank = jnp.sum(named * earlier, axis=0, keepdims=True).astype(I32)
                seen = seen + jnp.sum(named, axis=1, keepdims=True)
                code = slot[c, p:p + 1, :] * tiles + iota((1, tiles), 1)
                spot = (iota((LANES, tiles), 0) == c * capacity + rank).astype(F32)
                asked = asked + lax.dot_general(
                    named * (code + 1).astype(F32), spot, (((1,), (1,)), ((), ())), preferred_element_type=F32
                )
                column = column_of(source * capacity + rank)
                keys[c, p * tiles:(p + 1) * tiles, :] = jnp.broadcast_to(column, (tiles, LANES))
        mine = iota((members, LANES), 0) == m
        for q in range(regions):
            edge = jnp.where(q == r + 1, halo[0], halo[1])
            note[q] = jnp.where(q == r, asked, jnp.where(mine, edge, 0.0))

    return kernel


def halo_rows(note, regions, parts):
    r, m = here()
    low = note[jnp.maximum(r - 1, 0), pl.ds(m, 1), :]
    high = note[jnp.minimum(r + 1, regions - 1), pl.ds(m, 1), :]
    low = jnp.where(r > 0, low, 0.0)
    high = jnp.where(r < regions - 1, high, 0.0)

    def field(i):
        if i == 0:
            return low, high
        return pltpu.roll(low, 8 * i, 1), pltpu.roll(high, LANES - 8 * i, 1)

    def code():
        row = iota((parts, LANES), 0)
        below = jnp.zeros((parts, LANES), I32)
        above = jnp.zeros((parts, LANES), I32)
        for p in range(parts):
            below = jnp.where(row == p, low[:, p:p + 1].astype(I32), below)
            above = jnp.where(row == p, high[:, LANES - 1 - p:LANES - p].astype(I32), above)
        return below, above

    return field, code


def widen(x, left, right):
    tiles = x.shape[0]
    row = iota((tiles, LANES), 0)
    before = jnp.where(row == 0, left, pltpu.roll(x[:, -LANES:], 1, 0))
    after = jnp.where(row == tiles - 1, right, pltpu.roll(x[:, :LANES], tiles - 1, 0))
    return jnp.concatenate([before, x, after], axis=1)


def diffuse(x, d):
    n = x.shape[1]
    for _ in range(STEPS):
        x = x + d * (pltpu.roll(x, 1, 1) - 2.0 * x + pltpu.roll(x, n - 1, 1))
    return x


def pick_rows(wanted, rows):
    m = rows.shape[0]
    n = wanted.shape[0]
    choice = (wanted[:, :m] == iota((n, m), 1)).astype(F32).astype(BF16)
    return jnp.dot(choice, rows, preferred_element_type=F32)


def send_rows(note, prior, out, cycle, capacity, cells):
    r, _ = here()
    asked = note[r]
    members = asked.shape[0]
    slots = members * capacity
    spread = jnp.broadcast_to(asked[:, None, :], (members, capacity, LANES)).reshape(slots, LANES)
    mine = iota((slots, LANES), 1) == cycle * capacity + iota((slots, LANES), 0) % capacity
    wanted = jnp.sum(jnp.where(mine, spread, 0.0), axis=1, keepdims=True).astype(I32)
    sent = pick_rows(jnp.broadcast_to(wanted, (slots, LANES)), prior)
    out[:, :, :cells] = sent.reshape(members, capacity, cells).astype(BF16)


def make_observe(blocks, per_block, tiles, near):
    count = blocks * per_block

    def kernel(tile, cell, prec, value, pattern, weight, where, terms, local):
        def line(x):
            wide = jnp.concatenate([x] * per_block, axis=1)
            own = iota((per_block, count), 1) // blocks == iota((per_block, count), 0)
            return jnp.sum(jnp.where(own, wide, 0), axis=0, keepdims=True)

        at = line(cell[...])
        row = (at // LANES) * tiles + jnp.concatenate([tile[...]] * per_block, axis=1)
        pick = iota((2, count), 0) == 0
        where[...] = jnp.where(pick, row, at % LANES)
        terms[0:1, :] = line(prec[...])
        for c in range(CYCLES):
            terms[c + 1:c + 2, :] = line(value[c])
        group = iota((tiles, count), 1) % blocks
        total = jnp.zeros((tiles, count), F32)
        for k in range(near):
            total = total + jnp.where(column_of(pattern[k:k + 1, :]) == group, column_of(weight[k:k + 1, :]), 0.0)
        local[...] = total

    return kernel


def assess(prior, where, prec, value, local, parts, tiles, cells):
    blocks = cells // LANES
    rows = tiles * blocks
    count = where.shape[1]
    stacked = jnp.concatenate(
        [jnp.concatenate([x[:, k * LANES:(k + 1) * LANES] for k in range(blocks)], axis=0) for x in prior],
        axis=1,
    )
    choice = (iota((rows, count), 0) == where[0:1, :]).astype(F32).astype(BF16)
    lines = lax.dot_general(stacked, choice, (((0,), (0,)), ((), ())), preferred_element_type=F32)
    lane = iota((LANES, count), 0) == where[1:2, :]
    score = []
    for p in range(parts):
        predicted = jnp.sum(jnp.where(lane, lines[p * LANES:(p + 1) * LANES, :], 0.0), axis=0, keepdims=True)
        miss = value - predicted
        term = 0.5 * (prec * miss * miss)
        score.append(jnp.sum(local * term, axis=1, keepdims=True))
    least = score[0]
    for s in score[1:]:
        least = jnp.minimum(least, s)
    scale = [jnp.exp(least - s) for s in score]
    total = scale[0]
    for s in scale[1:]:
        total = total + s
    weighted = scale[0] * prior[0].astype(F32)
    for s, x in zip(scale[1:], prior[1:]):
        weighted = weighted + s * x.astype(F32)
    return least, total, weighted


def pieces(x):
    high = x.astype(BF16).astype(F32)
    middle = (x - high).astype(BF16).astype(F32)
    low = (x - high - middle).astype(BF16).astype(F32)
    return high, middle, low


def pack_mean(out, at, least, total, weighted):
    members, capacity, _ = out.shape
    tiles, cells = weighted.shape
    share = cells // members
    groups = tiles // capacity
    weighted = weighted.astype(BF16)
    for g in range(groups):
        rows = weighted[g * capacity:(g + 1) * capacity, :]
        for m in range(members):
            out[m, :, at + g * share:at + (g + 1) * share] = rows[:, m * share:(m + 1) * share]
    lane = iota((capacity, LANES), 1)
    misc = jnp.zeros((capacity, LANES), F32)
    spot = 0
    for x in (least, total):
        for piece in pieces(x):
            for g in range(groups):
                misc = jnp.where(lane == spot, piece[g * capacity:(g + 1) * capacity, :], misc)
                spot += 1
    out[:, :, at + groups * share:at + groups * share + LANES] = jnp.broadcast_to(misc.astype(BF16)[None], (members, capacity, LANES))


def unpack_mean(got, at, tiles, share):
    _, capacity, _ = got.shape
    groups = tiles // capacity
    misc = got[:, :, at + groups * share:at + groups * share + LANES].astype(F32)
    means = []
    for g in range(groups):
        pair = []
        for kind in range(2):
            spot = [(kind * 3 + piece) * groups + g for piece in range(3)]
            high, middle, low = [misc[:, :, i:i + 1] for i in spot]
            pair.append(high + middle + low)
        least, total = pair
        scale = jnp.exp(jnp.min(least, axis=0, keepdims=True) - least)
        part = got[:, :, at + g * share:at + (g + 1) * share].astype(F32)
        means.append(jnp.sum(scale * part, axis=0) / jnp.sum(scale * total, axis=0))
    return means


def make_first(regions, capacity, parts, tiles, cells):
    def kernel(state, diff, pert, note, send, prior_out):
        field, _ = halo_rows(note, regions, parts)
        d = widen(diff[...], *field(parts))
        edge = []
        prior = []
        for p in range(parts):
            x = widen(state[p].astype(F32), *field(p))
            x = diffuse(x, d)
            now = (x[:, LANES:LANES + cells] + pert[0, p].astype(F32)).astype(BF16)
            prior.append(now)
            prior_out[p] = now
            low, high = field(parts + 1 + p)
            low = low + x[0:1, :LANES]
            high = high + x[tiles - 1:tiles, LANES + cells:]
            edge.append(jnp.where(iota((1, LANES), 1) < LANES // 2, high, low))
        send_rows(note, jnp.concatenate(prior, axis=0), send, 0, capacity, cells)
        row = iota((capacity, LANES), 0)
        misc = jnp.zeros((capacity, LANES), F32)
        for p in range(parts):
            misc = jnp.where(row == p, edge[p], misc)
        members = send.shape[0]
        send[:, :, cells:] = jnp.broadcast_to(misc.astype(BF16)[None], (members, capacity, LANES))

    return kernel


def make_assess(parts, tiles, cells):
    def kernel(prior, where, terms, local, out):
        pack_mean(
            out,
            0,
            *assess(
                [prior[p] for p in range(parts)],
                where[...], terms[0:1, :], terms[1:2, :], local[...], parts, tiles, cells,
            ),
        )

    return kernel


def make_second(regions, capacity, parts, tiles, cells):
    def kernel(got, keys, diff, pert, note, where, terms, local, part, send):
        slots = got.shape[0] * capacity
        arrived = got[...].reshape(slots, cells + LANES)
        moved = pick_rows(keys[0], arrived[:, :cells])
        lines = arrived[:, cells:]
        field, code = halo_rows(note, regions, parts)
        first, last = [pick_rows(x, lines) for x in code()]
        d = widen(diff[...], *field(parts))
        prior = []
        for p in range(parts):
            x = widen(moved[p * tiles:(p + 1) * tiles, :], first[p:p + 1, :], last[p:p + 1, :])
            x = diffuse(x, d)[:, LANES:LANES + cells]
            prior.append((x + pert[0, p].astype(F32)).astype(BF16))
        send_rows(note, jnp.concatenate(prior, axis=0), send, 1, capacity, cells)
        extra = part.shape[2]
        send[:, :, cells:cells + extra] = part[...]
        pack_mean(
            send,
            cells + extra,
            *assess(prior, where[...], terms[0:1, :], terms[2:3, :], local[...], parts, tiles, cells),
        )

    return kernel


def make_last(capacity, parts, tiles, cells):
    def kernel(got, keys, analysis, mean):
        slots = got.shape[0] * capacity
        rows = got[:, :, :cells].reshape(slots, cells)
        picked = pick_rows(keys[1], rows)
        for p in range(parts):
            analysis[p] = picked[p * tiles:(p + 1) * tiles, :].astype(BF16)
        share = mean.shape[2]
        extra = tiles // capacity * share + LANES
        for c in range(CYCLES):
            for g, x in enumerate(unpack_mean(got, cells + c * extra, tiles, share)):
                mean[c, g * capacity:(g + 1) * capacity, :] = x

    return kernel


def body(
    state,
    diffusivity,
    model_perturbation,
    obs_values,
    obs_prec,
    obs_tile,
    obs_cell,
    pattern,
    loc_weight,
    anc_member,
    anc_slot,
):
    parts, tiles, cells = state.shape
    members = lax.axis_size("member")
    regions = lax.axis_size("region")
    capacity = max(2, 2 * parts * tiles // members)
    share = cells // members
    groups = tiles // capacity
    blocks, per_block = obs_cell.shape
    count = blocks * per_block
    member_of = anc_member.reshape(CYCLES, parts, tiles)
    slot_of = anc_slot.reshape(CYCLES, parts, tiles)
    near = pattern.shape[1]
    ends = cells // LANES - 1

    def block(shape, at):
        lead = (0,) * (len(shape) - 1)
        return pl.BlockSpec(shape, lambda i: lead + (at,))

    edges = [state, state, diffusivity, diffusivity, model_perturbation, model_perturbation, member_of, slot_of]
    note, keys = call(
        make_prepare(regions, members, capacity, parts, tiles),
        [((regions, members, LANES), F32), ((CYCLES, parts * tiles, LANES), I32)],
        [pltpu.with_memory_space_constraint(x, pltpu.HBM) for x in edges],
        [
            block((parts, tiles, LANES), 0),
            block((parts, tiles, LANES), ends),
            block((tiles, LANES), 0),
            block((tiles, LANES), ends),
            block((1, parts, tiles, LANES), 0),
            block((1, parts, tiles, LANES), ends),
            whole_spec(member_of.shape),
            whole_spec(slot_of.shape),
        ],
        name="prepare",
    )
    note = lax.all_to_all(
        note.reshape(regions * members, LANES), ("region", "member"), split_axis=0, concat_axis=0, tiled=True
    ).reshape(regions, members, LANES)

    where, terms, local = call(
        make_observe(blocks, per_block, tiles, near),
        [((2, count), I32), ((1 + CYCLES, count), F32), ((tiles, count), F32)],
        [obs_tile[None, :], obs_cell.T, obs_prec.T, jnp.swapaxes(obs_values, 1, 2), pattern.T, loc_weight.T],
        name="observe",
    )

    def noise_spec(c):
        return pl.BlockSpec((1, parts, tiles, cells), lambda i: (c, 0, 0, 0))

    args = [state, diffusivity, model_perturbation, note]
    specs = [whole_spec(a.shape) for a in args]
    specs[2] = noise_spec(0)
    send, prior = call(
        make_first(regions, capacity, parts, tiles, cells),
        [((members, capacity, cells + LANES), BF16), ((parts, tiles, cells), BF16)],
        args,
        specs,
        name="forecast_first",
    )
    got = lax.all_to_all(send, "member", split_axis=0, concat_axis=0, tiled=True)
    extra = groups * share + LANES
    (part,) = call(
        make_assess(parts, tiles, cells),
        [((members, capacity, extra), BF16)],
        [prior, where, terms, local],
        name="assess_first",
    )
    args = [got, keys, diffusivity, model_perturbation, note, where, terms, local, part]
    specs = [whole_spec(a.shape) for a in args]
    specs[3] = noise_spec(1)
    (send,) = call(
        make_second(regions, capacity, parts, tiles, cells),
        [((members, capacity, cells + CYCLES * extra), BF16)],
        args,
        specs,
        name="forecast_second",
    )
    got = lax.all_to_all(send, "member", split_axis=0, concat_axis=0, tiled=True)
    return tuple(
        call(
            make_last(capacity, parts, tiles, cells),
            [(state.shape, BF16), ((CYCLES, tiles, share), F32)],
            [got, keys],
            name="finish",
        )
    )


def solution(mesh):
    in_specs = (
        P("member", "region", None),
        P("region", None),
        P(None, "member", "region", None),
        P(None, "region", None),
        P("region", None),
        P("region"),
        P("region", None),
        P("region", None),
        P("region", None),
        P(None, "region", "member", None, None),
        P(None, "region", "member", None),
    )
    out_specs = (P("member", "region", None), P(None, "region", "member"))
    return jax.shard_map(body, mesh=mesh, in_specs=in_specs, out_specs=out_specs, check_vma=False)
```

time: 54.2 us -> 49.6 us (0.915)
  blocking collectives: 15.1 us -> 29.5 us
  starting transfers between devices: 14.3 us -> 3.68 us
  local copies, waits for them, and re-layouts: 7.58 us -> 0.67 us
  waiting for transfers between devices: 10.3 us -> 8.46 us
  Pallas kernels: 5.44 us -> 6.15 us
    all_to_all x0 -> x1, blocking collectives: none -> 14.3 us  [body(): lax.all_to_all(note.reshape(regions * members, LANES), ('region', 'member...]
    unnamed x32 -> x18, local copies, waits for them, and re-layouts: 7.01 us -> 0.67 us
    all_to_all x1 -> x0, starting transfers between devices: 5.17 us -> none  [body(): lax.all_to_all(req, 'member', split_axis=0, concat_axis=0, tiled=True)]
    ppermute x2 -> x0, starting transfers between devices: 4.76 us -> none  [the longest x1 3.47 us: body(): below = lax.ppermute(up, 'region', forward)]
    ppermute x2 -> x0, waiting for transfers between devices: 4.2 us -> none  [the longest x1 4.19 us: body(): above = lax.ppermute(down, 'region', [(j, i) for i, j in forward])]
    all_to_all x1, waiting for transfers between devices: 6.05 us -> 8.46 us  [body(): lax.all_to_all(send, 'member', split_axis=0, concat_axis=0, tiled=True)]
    pallas_call x5 -> x6, Pallas kernels: 5.44 us -> 6.15 us  [call(): pl.pallas_call(kernel, out_shape=[jax.ShapeDtypeStruct(s, d) for s, d in...]
    all_to_all x1, starting transfers between devices: 4.33 us -> 3.68 us  [body(): lax.all_to_all(send, 'member', split_axis=0, concat_axis=0, tiled=True)]
  transfers between devices with their start and end apart: 4 -> 1, of which waited for: 2 -> 1; matrix products, arithmetic and copies ran while one was open for 2% -> 0% of each run, Pallas kernels for 1% -> 1%
where the time goes in v2:
time: 49.6 us; the launch traced here: 49.3 us
  blocking collectives  29.5 us (59%)
  waiting for transfers between devices  8.46 us (17%)
  Pallas kernels  6.15 us (12%)
  starting transfers between devices  3.68 us (7%)
  between operations  0.74 us (1%)
  local copies, waits for them, and re-layouts  0.67 us (1%)
    all_to_all x1, blocking collectives, body(): lax.all_to_all(send, 'member', split_axis=0, concat_axis=0, tiled=True)  15.3 us
    all_to_all x1, blocking collectives, body(): lax.all_to_all(note.reshape(regions * members, LANES), ('region', 'member...  14.3 us
    all_to_all x1, waiting for transfers between devices, body(): lax.all_to_all(send, 'member', split_axis=0, concat_axis=0, tiled=True)  8.46 us
    pallas_call x6, Pallas kernels, call(): pl.pallas_call(kernel, out_shape=[jax.ShapeDtypeStruct(s, d) for s, d in...  6.15 us
    all_to_all x1, starting transfers between devices, body(): lax.all_to_all(send, 'member', split_axis=0, concat_axis=0, tiled=True)  3.68 us
  transfers between devices with their start and end apart: 1, of which 1 were waited for; matrix products, arithmetic and copies ran while one was open for 0% of the time, Pallas kernels for 1%

profile of v2, /device:TPU:0, one launch (start us, length us, event | category | flops | bytes accessed | tf_op | source)
XLA Modules:
  0.0 49.3 jit_solution(13927975131401687839)
XLA Ops:
  0.6 0.0 copy-start
  0.6 0.0 copy-start.1
  0.7 0.0 copy-start.2
  0.7 1.4 %prepare.1 = (f32[4,8,128]{2,1,0:T(8,128)S(1)}, s32[2,32,128]{2,1,0:T(8,128)S(1)}) custom-call(bf16[2,16,4096]{2,1,0:T(8,128)(2,1)} %state.1, bf16[2,16,4096]{2,1,0:T(8,128)(2,1)} %state.1, f32[16,4096]{1,0:T(8,128)} %diff.3, f32[16,4096]{1,0:T(8,128)} %diff.3, bf16[2,2,16,4096]{3,2,1,0:T(8,128)(2,1)} %pert.3, bf16[2,2,16,4096]{3,2,1,0:T(8,128)(2,1)} %pert.3, ...), custom_call_target="tpu_custom_call" | custom-call | tf_op jit(solution)/shard_map/prepare/pallas_call | solution.py:28
  2.0 14.3 %all_to_all.19 = f32[32,1,128]{2,1,0:T(1,128)S(1)} all-to-all(f32[32,1,128]{2,1,0:T(1,128)S(1)} %bitcast.14), channel_id=1, replica_groups=mesh['member'=8,'region'=4] {'region','member'}, dimensions={0} | all-to-all | bytes 32768 | tf_op jit(solution)/shard_map/all_to_all | solution.py:385
  16.3 0.0 copy-done
  16.3 0.0 copy-done.1
  16.3 0.0 copy-done.2
  16.3 1.7 %forecast_first.1 = (bf16[8,8,4224]{2,1,0:T(8,128)(2,1)}, bf16[2,16,4096]{2,1,0:T(8,128)(2,1)S(1)}) custom-call(bf16[2,16,4096]{2,1,0:T(8,128)(2,1)S(1)} %copy-done.2, f32[16,4096]{1,0:T(8,128)S(1)} %copy-done.1, bf16[2,2,16,4096]{3,2,1,0:T(8,128)(2,1)S(1)} %copy-done, f32[4,8,128]{2,1,0:T(8,128)S(1)} %bitcast.12), custom_call_target="tpu_custom_call" | custom-call | tf_op jit(solution)/shard_map/forecast_first/pallas_call | solution.py:28
  18.0 0.0 copy-start.3
  18.0 0.0 copy-start.5
  18.0 0.0 copy-start.6
  18.0 0.0 copy-start.7
  18.0 3.7 %all-to-all-start.1 = ((bf16[8,8,4224]{2,1,0:T(8,128)(2,1)}), bf16[8,8,4224]{2,1,0:T(8,128)(2,1)S(1)}, u32[]{:S(2)}, u32[]{:S(2)}) async-start(bf16[8,8,4224]{2,1,0:T(8,128)(2,1)} %get-tuple-element.10), calls=%async_computation.1 | async-start | bytes 1081344 | tf_op jit(solution)/shard_map/all_to_all | solution.py:409
  21.7 0.0 copy-start.4
  21.7 0.0 copy-start.8
  21.8 0.0 copy-done.3
  21.8 0.0 copy-done.5
  21.8 0.0 copy-done.6
  21.8 0.0 copy-done.7
  21.8 0.6 %copy-done.4 = s32[32,16]{0,1:T(8,128)S(1)} copy-done((s32[32,16]{0,1:T(8,128)S(1)}, s32[32,16]{0,1:T(8,128)}, u32[]{:S(2)}) %copy-start.4) | copy-done | bytes 2072
  22.4 0.0 copy-done.8
  22.4 0.2 observe.1
  22.6 0.5 assess_first.1.part
  23.1 8.5 %all-to-all-done.1.got = bf16[8,8,4224]{2,1,0:T(8,128)(2,1)S(1)} async-done(((bf16[8,8,4224]{2,1,0:T(8,128)(2,1)}), bf16[8,8,4224]{2,1,0:T(8,128)(2,1)S(1)}, u32[]{:S(2)}, u32[]{:S(2)}) %all-to-all-start.1) | async-done | bytes 540704 | tf_op jit(solution)/shard_map/all_to_all | solution.py:409
  31.6 1.4 %forecast_second.1 = bf16[8,8,6400]{2,1,0:T(8,128)(2,1)S(1)} custom-call(bf16[8,8,4224]{2,1,0:T(8,128)(2,1)S(1)} %all-to-all-done.1.got, s32[2,32,128]{2,1,0:T(8,128)S(1)} %get-tuple-element.11.keys, f32[16,4096]{1,0:T(8,128)S(1)} %copy-done.1, bf16[2,2,16,4096]{3,2,1,0:T(8,128)(2,1)S(1)} %copy-done, f32[4,8,128]{2,1,0:T(8,128)S(1)} %bitcast.13, ...), custom_call_target="tpu_custom_call" | custom-call | tf_op jit(solution)/shard_map/forecast_second/pallas_call | solution.py:28
  33.0 15.3 %all_to_all.20.got = bf16[8,8,6400]{2,1,0:T(8,128)(2,1)S(1)} all-to-all(bf16[8,8,6400]{2,1,0:T(8,128)(2,1)S(1)} %forecast_second.1), channel_id=1, replica_groups=mesh['member'=8,'region'=4] {'member'}, dimensions={0} | all-to-all | bytes 1638400 | tf_op jit(solution)/shard_map/all_to_all | solution.py:427
  48.3 0.9 %finish.1 = (bf16[2,16,4096]{2,1,0:T(8,128)(2,1)}, f32[2,16,512]{2,1,0:T(8,128)}) custom-call(bf16[8,8,6400]{2,1,0:T(8,128)(2,1)S(1)} %all_to_all.20.got, s32[2,32,128]{2,1,0:T(8,128)S(1)} %get-tuple-element.11.keys), custom_call_target="tpu_custom_call" | custom-call | tf_op jit(solution)/shard_map/finish/pallas_call | solution.py:28
Async XLA Ops:
  0.6 15.7 %copy-start = (bf16[2,2,16,4096]{3,2,1,0:T(8,128)(2,1)S(1)}, bf16[2,2,16,4096]{3,2,1,0:T(8,128)(2,1)}, u32[]{:S(2)}) copy-start(bf16[2,2,16,4096]{3,2,1,0:T(8,128)(2,1)} %pert.3) | copy-start | bytes 1572868
  0.6 15.6 %copy-start.1 = (f32[16,4096]{1,0:T(8,128)S(1)}, f32[16,4096]{1,0:T(8,128)}, u32[]{:S(2)}) copy-start(f32[16,4096]{1,0:T(8,128)} %diff.3) | copy-start | bytes 786436
  0.7 15.6 %copy-start.2 = (bf16[2,16,4096]{2,1,0:T(8,128)(2,1)S(1)}, bf16[2,16,4096]{2,1,0:T(8,128)(2,1)}, u32[]{:S(2)}) copy-start(bf16[2,16,4096]{2,1,0:T(8,128)(2,1)} %state.1) | copy-start | bytes 786436
  18.0 3.7 %copy-start.3 = (f32[2,32,16]{1,2,0:T(8,128)S(1)}, f32[2,32,16]{1,2,0:T(8,128)}, u32[]{:S(2)}) copy-start(f32[2,32,16]{1,2,0:T(8,128)} %param.14) | copy-start | bytes 12292
  18.0 3.7 %copy-start.5 = (f32[32,16]{0,1:T(8,128)S(1)}, f32[32,16]{0,1:T(8,128)}, u32[]{:S(2)}) copy-start(f32[32,16]{0,1:T(8,128)} %param.15) | copy-start | bytes 6148
  18.0 3.7 %copy-start.6 = (s32[16,6]{0,1:T(8,128)S(1)}, s32[16,6]{0,1:T(8,128)}, u32[]{:S(2)}) copy-start(s32[16,6]{0,1:T(8,128)} %param.18) | copy-start | bytes 1156
  18.0 3.7 %copy-start.7 = (f32[16,6]{0,1:T(8,128)S(1)}, f32[16,6]{0,1:T(8,128)}, u32[]{:S(2)}) copy-start(f32[16,6]{0,1:T(8,128)} %param.19) | copy-start | bytes 1156
  18.0 13.5 %all-to-all-start.1 = ((bf16[8,8,4224]{2,1,0:T(8,128)(2,1)}), bf16[8,8,4224]{2,1,0:T(8,128)(2,1)S(1)}, u32[]{:S(2)}, u32[]{:S(2)}) async-start(bf16[8,8,4224]{2,1,0:T(8,128)(2,1)} %get-tuple-element.10), calls=%async_computation.1 | async-start | bytes 1081344 | tf_op jit(solution)/shard_map/all_to_all | solution.py:409
  21.7 0.7 %copy-start.4 = (s32[32,16]{0,1:T(8,128)S(1)}, s32[32,16]{0,1:T(8,128)}, u32[]{:S(2)}) copy-start(s32[32,16]{0,1:T(8,128)} %param.17) | copy-start | bytes 6148
  21.7 0.7 %copy-start.8 = (s32[32]{0:T(128)S(1)}, s32[32]{0:T(128)}, u32[]{:S(2)}) copy-start(s32[32]{0:T(128)} %param.16) | copy-start | bytes 388

commit v3 on v2

--- a/solution.py
+++ b/solution.py
@@ -43,33 +43,36 @@
 
 
 def here():
-    return lax.axis_index("region"), lax.axis_index("member")
-
-
-def make_prepare(regions, members, capacity, parts, tiles):
+    return lax.axis_index("member")
+
+
+EDGE_AT = 32
+STRIDE = 8
+
+
+def make_prepare(members, capacity, parts, tiles):
     width = 2 * STEPS
 
-    def kernel(st0, st1, df0, df1, pb0, pb1, am, slot, note, keys):
-        r, m = here()
+    def kernel(st0, st1, df0, df1, pb0, pb1, am, slot, note, trail, keys):
         lane = iota((1, LANES), 1)
-        halo = []
-        for st, df, pb, t in ((st1, df1, pb1, tiles - 1), (st0, df0, pb0, 0)):
-            top = t > 0
-            rows = [st[p, t:t + 1, :].astype(F32) for p in range(parts)]
-            rows += [df[t:t + 1, :]]
-            rows += [pb[0, p, t:t + 1, :].astype(F32) for p in range(parts)]
-            out = jnp.zeros((1, LANES), F32)
-            for i, row in enumerate(rows):
-                shift = (LANES - 8 * i) % LANES if top else 8 * i
-                first = LANES - 8 * i - width if top else 8 * i
-                moved = pltpu.roll(row, shift, 1) if shift else row
-                out = jnp.where((lane >= first) & (lane < first + width), moved, out)
-            for p in range(parts):
-                code = am[0, p:p + 1, t:t + 1] * capacity + slot[0, p:p + 1, t:t + 1]
-                out = jnp.where(lane == (p if top else LANES - 1 - p), code.astype(F32), out)
-            halo.append(out)
+        last = tiles - 1
+        trail[...] = jnp.zeros(trail.shape, F32)
+        trail[0:1, :] = df1[last:last + 1, :]
+        trail[1:2, :] = df0[0:1, :]
+        edge = jnp.zeros((1, LANES), F32)
+        for p in range(parts):
+            for i, t in enumerate((last, 0)):
+                code = slot[0, p:p + 1, t:t + 1] * members + am[0, p:p + 1, t:t + 1]
+                row = 2 + i * parts + p
+                trail[row:row + 1, :] = jnp.broadcast_to(code.astype(F32), (1, LANES))
+            fields = (st1[p, last:last + 1, :], st0[p, 0:1, :], pb1[0, p, last:last + 1, :], pb0[0, p, 0:1, :])
+            for i, x in enumerate(fields):
+                to = EDGE_AT + STRIDE * (4 * p + i)
+                start = 0 if i % 2 else LANES - width
+                moved = pltpu.roll(x.astype(F32), (to - start) % LANES, 1)
+                edge = jnp.where((lane >= to) & (lane < to + width), moved, edge)
         before = (iota((tiles, tiles), 0) < iota((tiles, tiles), 1)).astype(F32)
-        asked = jnp.full((members, LANES), -1.0, F32)
+        asked = jnp.zeros((members, LANES), F32)
         for c in range(CYCLES):
             seen = jnp.zeros((members, 1), F32)
             for p in range(parts):
@@ -85,36 +88,35 @@
                 )
                 column = column_of(source * capacity + rank)
                 keys[c, p * tiles:(p + 1) * tiles, :] = jnp.broadcast_to(column, (tiles, LANES))
-        mine = iota((members, LANES), 0) == m
-        for q in range(regions):
-            edge = jnp.where(q == r + 1, halo[0], halo[1])
-            note[q] = jnp.where(q == r, asked, jnp.where(mine, edge, 0.0))
-
-    return kernel
-
-
-def halo_rows(note, regions, parts):
-    r, m = here()
-    low = note[jnp.maximum(r - 1, 0), pl.ds(m, 1), :]
-    high = note[jnp.minimum(r + 1, regions - 1), pl.ds(m, 1), :]
-    low = jnp.where(r > 0, low, 0.0)
-    high = jnp.where(r < regions - 1, high, 0.0)
-
-    def field(i):
-        if i == 0:
-            return low, high
-        return pltpu.roll(low, 8 * i, 1), pltpu.roll(high, LANES - 8 * i, 1)
-
-    def code():
-        row = iota((parts, LANES), 0)
-        below = jnp.zeros((parts, LANES), I32)
-        above = jnp.zeros((parts, LANES), I32)
-        for p in range(parts):
-            below = jnp.where(row == p, low[:, p:p + 1].astype(I32), below)
-            above = jnp.where(row == p, high[:, LANES - 1 - p:LANES - p].astype(I32), above)
-        return below, above
-
-    return field, code
+        note[...] = jnp.where(iota((members, LANES), 1) < EDGE_AT, asked - 1.0, edge)
+
+    return kernel
+
+
+def edge_windows(own, below, above, members, parts):
+    width = 2 * STEPS
+
+    def field(note, p, i):
+        at = EDGE_AT + STRIDE * (4 * p + i)
+        start = 0 if i % 2 else LANES - width
+        return pltpu.roll(note[:members, :], (start - at) % LANES, 1)
+
+    low, high = [], []
+    for out, before, after in ((low, below, own), (high, own, above)):
+        d = jnp.concatenate([before[members:members + 1, :], after[members + 1:members + 2, :]], axis=1)
+        for p in range(parts):
+            x = jnp.concatenate([field(before, p, 0), field(after, p, 1)], axis=1)
+            x = diffuse(x, d) + jnp.concatenate([field(before, p, 2), field(after, p, 3)], axis=1)
+            out.append(x.astype(BF16).astype(F32))
+    return jnp.concatenate(low, axis=0), jnp.concatenate(high, axis=0)
+
+
+def patch(x, first, last):
+    tiles = x.shape[0]
+    row, lane = iota((tiles, LANES), 0), iota((tiles, LANES), 1)
+    head = jnp.where((row == 0) & (lane < STEPS), first, x[:, :LANES])
+    tail = jnp.where((row == tiles - 1) & (lane >= LANES - STEPS), last, x[:, -LANES:])
+    return jnp.concatenate([head, x[:, LANES:-LANES], tail], axis=1)
 
 
 def widen(x, left, right):
@@ -139,9 +141,7 @@
     return jnp.dot(choice, rows, preferred_element_type=F32)
 
 
-def send_rows(note, prior, out, cycle, capacity, cells):
-    r, _ = here()
-    asked = note[r]
+def send_rows(asked, prior, out, cycle, capacity, cells):
     members = asked.shape[0]
     slots = members * capacity
     spread = jnp.broadcast_to(asked[:, None, :], (members, capacity, LANES)).reshape(slots, LANES)
@@ -252,62 +252,69 @@
     return means
 
 
-def make_first(regions, capacity, parts, tiles, cells):
-    def kernel(state, diff, pert, note, send, prior_out):
-        field, _ = halo_rows(note, regions, parts)
-        d = widen(diff[...], *field(parts))
-        edge = []
+def make_first(parts, tiles, cells):
+    def kernel(state, diff, pert, prior):
+        nothing = jnp.zeros((1, LANES), F32)
+        d = widen(diff[...], nothing, nothing)
+        for p in range(parts):
+            x = diffuse(widen(state[p].astype(F32), nothing, nothing), d)
+            now = x[:, LANES:LANES + cells] + pert[0, p].astype(F32)
+            prior[p * tiles:(p + 1) * tiles, :] = now.astype(BF16)
+
+    return kernel
+
+
+def make_send(capacity, cells):
+    def kernel(prior, note, trail, send, message):
+        members = note.shape[0]
+        send_rows(note[...], prior[...], send, 0, capacity, cells)
+        message[:members, :] = note[...]
+        message[members:, :] = trail[...]
+
+    return kernel
+
+
+def make_assess(members, parts, tiles, cells):
+    def kernel(prior, own, below, above, where, terms, local, part, low_out, high_out):
+        low, high = edge_windows(own[...], below[...], above[...], members, parts)
+        low_out[...] = low
+        high_out[...] = high
+        m = here()
+        fixed = []
+        for p in range(parts):
+            mine = iota(low.shape, 0) == p * members + m
+            start = jnp.sum(jnp.where(mine, low, 0.0), axis=0, keepdims=True)
+            end = jnp.sum(jnp.where(mine, high, 0.0), axis=0, keepdims=True)
+            x = patch(prior[p * tiles:(p + 1) * tiles, :].astype(F32), start[:, LANES:], end[:, :LANES])
+            fixed.append(x.astype(BF16))
+        pack_mean(
+            part,
+            0,
+            *assess(fixed, where[...], terms[0:1, :], terms[1:2, :], local[...], parts, tiles, cells),
+        )
+
+    return kernel
+
+
+def make_second(members, capacity, parts, tiles, cells):
+    def kernel(got, keys, diff, pert, own, below, above, low, high, where, terms, local, part, send):
+        arrived = got[...].reshape(members * capacity, cells)
+        moved = pick_rows(keys[0], arrived)
+        at = members + 2
+        mine = own[at:at + 2 * parts, :].astype(I32)
+        codes = jnp.concatenate([mine[parts:], below[at:at + parts, :].astype(I32)], axis=0)
+        start = pick_rows(codes, low[...].astype(BF16))
+        codes = jnp.concatenate([mine[:parts], above[at + parts:at + 2 * parts, :].astype(I32)], axis=0)
+        end = pick_rows(codes, high[...].astype(BF16))
+        d = widen(diff[...], below[members:members + 1, :], above[members + 1:members + 2, :])
         prior = []
         for p in range(parts):
-            x = widen(state[p].astype(F32), *field(p))
-            x = diffuse(x, d)
-            now = (x[:, LANES:LANES + cells] + pert[0, p].astype(F32)).astype(BF16)
-            prior.append(now)
-            prior_out[p] = now
-            low, high = field(parts + 1 + p)
-            low = low + x[0:1, :LANES]
-            high = high + x[tiles - 1:tiles, LANES + cells:]
-            edge.append(jnp.where(iota((1, LANES), 1) < LANES // 2, high, low))
-        send_rows(note, jnp.concatenate(prior, axis=0), send, 0, capacity, cells)
-        row = iota((capacity, LANES), 0)
-        misc = jnp.zeros((capacity, LANES), F32)
-        for p in range(parts):
-            misc = jnp.where(row == p, edge[p], misc)
-        members = send.shape[0]
-        send[:, :, cells:] = jnp.broadcast_to(misc.astype(BF16)[None], (members, capacity, LANES))
-
-    return kernel
-
-
-def make_assess(parts, tiles, cells):
-    def kernel(prior, where, terms, local, out):
-        pack_mean(
-            out,
-            0,
-            *assess(
-                [prior[p] for p in range(parts)],
-                where[...], terms[0:1, :], terms[1:2, :], local[...], parts, tiles, cells,
-            ),
-        )
-
-    return kernel
-
-
-def make_second(regions, capacity, parts, tiles, cells):
-    def kernel(got, keys, diff, pert, note, where, terms, local, part, send):
-        slots = got.shape[0] * capacity
-        arrived = got[...].reshape(slots, cells + LANES)
-        moved = pick_rows(keys[0], arrived[:, :cells])
-        lines = arrived[:, cells:]
-        field, code = halo_rows(note, regions, parts)
-        first, last = [pick_rows(x, lines) for x in code()]
-        d = widen(diff[...], *field(parts))
-        prior = []
-        for p in range(parts):
-            x = widen(moved[p * tiles:(p + 1) * tiles, :], first[p:p + 1, :], last[p:p + 1, :])
+            x = patch(moved[p * tiles:(p + 1) * tiles, :], start[p:p + 1, LANES:], end[p:p + 1, :LANES])
+            q = parts + p
+            x = widen(x, start[q:q + 1, :LANES], end[q:q + 1, LANES:])
             x = diffuse(x, d)[:, LANES:LANES + cells]
             prior.append((x + pert[0, p].astype(F32)).astype(BF16))
-        send_rows(note, jnp.concatenate(prior, axis=0), send, 1, capacity, cells)
+        send_rows(own[:members, :], jnp.concatenate(prior, axis=0), send, 1, capacity, cells)
         extra = part.shape[2]
         send[:, :, cells:cells + extra] = part[...]
         pack_mean(
@@ -366,9 +373,9 @@
         return pl.BlockSpec(shape, lambda i: lead + (at,))
 
     edges = [state, state, diffusivity, diffusivity, model_perturbation, model_perturbation, member_of, slot_of]
-    note, keys = call(
-        make_prepare(regions, members, capacity, parts, tiles),
-        [((regions, members, LANES), F32), ((CYCLES, parts * tiles, LANES), I32)],
+    note, trail, keys = call(
+        make_prepare(members, capacity, parts, tiles),
+        [((members, LANES), F32), ((8, LANES), F32), ((CYCLES, parts * tiles, LANES), I32)],
         [pltpu.with_memory_space_constraint(x, pltpu.HBM) for x in edges],
         [
             block((parts, tiles, LANES), 0),
@@ -382,9 +389,7 @@
         ],
         name="prepare",
     )
-    note = lax.all_to_all(
-        note.reshape(regions * members, LANES), ("region", "member"), split_axis=0, concat_axis=0, tiled=True
-    ).reshape(regions, members, LANES)
+    note = lax.all_to_all(note, "member", split_axis=0, concat_axis=0, tiled=True)
 
     where, terms, local = call(
         make_observe(blocks, per_block, tiles, near),
@@ -396,29 +401,35 @@
     def noise_spec(c):
         return pl.BlockSpec((1, parts, tiles, cells), lambda i: (c, 0, 0, 0))
 
-    args = [state, diffusivity, model_perturbation, note]
+    args = [state, diffusivity, model_perturbation]
     specs = [whole_spec(a.shape) for a in args]
     specs[2] = noise_spec(0)
-    send, prior = call(
-        make_first(regions, capacity, parts, tiles, cells),
-        [((members, capacity, cells + LANES), BF16), ((parts, tiles, cells), BF16)],
-        args,
-        specs,
-        name="forecast_first",
+    (prior,) = call(
+        make_first(parts, tiles, cells), [((parts * tiles, cells), BF16)], args, specs, name="forecast_first"
+    )
+    send, message = call(
+        make_send(capacity, cells),
+        [((members, capacity, cells), BF16), ((members + trail.shape[0], LANES), F32)],
+        [prior, note, trail],
+        name="send_first",
     )
     got = lax.all_to_all(send, "member", split_axis=0, concat_axis=0, tiled=True)
+    forward = [(i, i + 1) for i in range(regions - 1)]
+    below = lax.ppermute(message, "region", forward)
+    above = lax.ppermute(message, "region", [(j, i) for i, j in forward])
     extra = groups * share + LANES
-    (part,) = call(
-        make_assess(parts, tiles, cells),
-        [((members, capacity, extra), BF16)],
-        [prior, where, terms, local],
+    window = ((parts * members, 2 * LANES), F32)
+    part, low, high = call(
+        make_assess(members, parts, tiles, cells),
+        [((members, capacity, extra), BF16), window, window],
+        [prior, message, below, above, where, terms, local],
         name="assess_first",
     )
-    args = [got, keys, diffusivity, model_perturbation, note, where, terms, local, part]
+    args = [got, keys, diffusivity, model_perturbation, message, below, above, low, high, where, terms, local, part]
     specs = [whole_spec(a.shape) for a in args]
     specs[3] = noise_spec(1)
     (send,) = call(
-        make_second(regions, capacity, parts, tiles, cells),
+        make_second(members, capacity, parts, tiles, cells),
         [((members, capacity, cells + CYCLES * extra), BF16)],
         args,
         specs,

time: 49.6 us -> 44.9 us (0.905)
  blocking collectives: 29.5 us -> 15.3 us
  starting transfers between devices: 3.68 us -> 14.6 us
  waiting for transfers between devices: 8.46 us -> 6.03 us
  Pallas kernels: 6.15 us -> 7.01 us
    all_to_all x1 -> x0, blocking collectives: 14.3 us -> none  [body(): lax.all_to_all(note.reshape(regions * members, LANES), ('region', 'member...]
    all_to_all x1, waiting for transfers between devices: 8.46 us -> 1.62 us  [body(): lax.all_to_all(send, 'member', split_axis=0, concat_axis=0, tiled=True)]
    ppermute x0 -> x2, starting transfers between devices: none -> 5.84 us  [the longest x1 4.55 us: body(): below = lax.ppermute(message, 'region', forward)]
    all_to_all x0 -> x1, starting transfers between devices: none -> 5.17 us  [body(): lax.all_to_all(note, 'member', split_axis=0, concat_axis=0, tiled=True)]
    all_to_all x0 -> x1, waiting for transfers between devices: none -> 3.94 us  [body(): lax.all_to_all(note, 'member', split_axis=0, concat_axis=0, tiled=True)]
    pallas_call x6 -> x7, Pallas kernels: 6.15 us -> 7.01 us  [call(): pl.pallas_call(kernel, out_shape=[jax.ShapeDtypeStruct(s, d) for s, d in...]
  transfers between devices with their start and end apart: 1 -> 4, of which waited for: 1 -> 3; matrix products, arithmetic and copies ran while one was open for 0% -> 0% of each run, Pallas kernels for 1% -> 4%
where the time goes in v3:
time: 44.9 us; the launch traced here: 44.5 us
  blocking collectives  15.3 us (34%)
  starting transfers between devices  14.6 us (33%)
  Pallas kernels  7.01 us (16%)
  waiting for transfers between devices  6.03 us (13%)
  between operations  0.8 us (2%)
  local copies, waits for them, and re-layouts  0.67 us (1%)
    all_to_all x1, blocking collectives, body(): lax.all_to_all(send, 'member', split_axis=0, concat_axis=0, tiled=True)  15.3 us
    pallas_call x7, Pallas kernels, call(): pl.pallas_call(kernel, out_shape=[jax.ShapeDtypeStruct(s, d) for s, d in...  7.01 us
    all_to_all x1, starting transfers between devices, body(): lax.all_to_all(note, 'member', split_axis=0, concat_axis=0, tiled=True)  5.17 us
    ppermute x1, starting transfers between devices, body(): below = lax.ppermute(message, 'region', forward)  4.55 us
    all_to_all x1, waiting for transfers between devices, body(): lax.all_to_all(note, 'member', split_axis=0, concat_axis=0, tiled=True)  3.94 us
    all_to_all x1, starting transfers between devices, body(): lax.all_to_all(send, 'member', split_axis=0, concat_axis=0, tiled=True)  3.62 us
    all_to_all x1, waiting for transfers between devices, body(): lax.all_to_all(send, 'member', split_axis=0, concat_axis=0, tiled=True)  1.62 us
    ppermute x1, starting transfers between devices, body(): above = lax.ppermute(message, 'region', [(j, i) for i, j in forward])  1.29 us
  transfers between devices with their start and end apart: 4, of which 3 were waited for; matrix products, arithmetic and copies ran while one was open for 0% of the time, Pallas kernels for 4%

profile of v3, /device:TPU:0, one launch (start us, length us, event | category | flops | bytes accessed | tf_op | source)
XLA Modules:
  0.0 44.5 jit_solution(13007084768350879856)
XLA Ops:
  0.6 0.0 copy-start
  0.6 0.0 copy-start.1
  0.7 0.0 copy-start.2
  0.7 1.9 %prepare.1 = (f32[8,128]{1,0:T(8,128)}, f32[8,128]{1,0:T(8,128)S(1)}, s32[2,32,128]{2,1,0:T(8,128)S(1)}) custom-call(bf16[2,16,4096]{2,1,0:T(8,128)(2,1)} %st1.1, bf16[2,16,4096]{2,1,0:T(8,128)(2,1)} %st1.1, f32[16,4096]{1,0:T(8,128)} %diff.3, f32[16,4096]{1,0:T(8,128)} %diff.3, bf16[2,2,16,4096]{3,2,1,0:T(8,128)(2,1)} %pert.3, ...), custom_call_target="tpu_custom_call" | custom-call | tf_op jit(solution)/shard_map/prepare/pallas_call | solution.py:28
  2.6 5.2 %all-to-all-start = ((f32[8,1,128]{2,1,0:T(1,128)}), f32[8,1,128]{2,1,0:T(1,128)S(1)}, u32[]{:S(2)}, u32[]{:S(2)}) async-start(f32[8,1,128]{2,1,0:T(1,128)} %bitcast.3), calls=%async_computation | async-start | bytes 8192 | tf_op jit(solution)/shard_map/all_to_all | solution.py:392
  7.7 0.0 copy-done
  7.7 0.0 copy-done.1
  7.8 0.0 copy-done.2
  7.8 0.6 %forecast_first.1.prior = bf16[32,4096]{1,0:T(8,128)(2,1)S(1)} custom-call(bf16[2,16,4096]{2,1,0:T(8,128)(2,1)S(1)} %copy-done.2, f32[16,4096]{1,0:T(8,128)S(1)} %copy-done.1, bf16[2,2,16,4096]{3,2,1,0:T(8,128)(2,1)S(1)} %copy-done), custom_call_target="tpu_custom_call" | custom-call | tf_op jit(solution)/shard_map/forecast_first/pallas_call | solution.py:28
  8.4 3.9 %all-to-all-done = f32[8,1,128]{2,1,0:T(1,128)S(1)} async-done(((f32[8,1,128]{2,1,0:T(1,128)}), f32[8,1,128]{2,1,0:T(1,128)S(1)}, u32[]{:S(2)}, u32[]{:S(2)}) %all-to-all-start) | async-done | bytes 4128 | tf_op jit(solution)/shard_map/all_to_all | solution.py:392
  12.3 1.2 %send_first.1 = (bf16[8,8,4096]{2,1,0:T(8,128)(2,1)}, f32[16,128]{1,0:T(8,128)S(1)}) custom-call(bf16[32,4096]{1,0:T(8,128)(2,1)S(1)} %forecast_first.1.prior, f32[8,128]{1,0:T(8,128)S(1)} %bitcast.12, f32[8,128]{1,0:T(8,128)S(1)} %get-tuple-element.14.trail), custom_call_target="tpu_custom_call" | custom-call | tf_op jit(solution)/shard_map/send_first/pallas_call | solution.py:28
  13.5 0.0 copy-start.3
  13.5 0.0 copy-start.5
  13.5 0.0 copy-start.7
  13.5 3.6 %all-to-all-start.1 = ((bf16[8,8,4096]{2,1,0:T(8,128)(2,1)}), bf16[8,8,4096]{2,1,0:T(8,128)(2,1)S(1)}, u32[]{:S(2)}, u32[]{:S(2)}) async-start(bf16[8,8,4096]{2,1,0:T(8,128)(2,1)} %get-tuple-element.15), calls=%async_computation.1 | async-start | bytes 1048576 | tf_op jit(solution)/shard_map/all_to_all | solution.py:416
  17.1 0.0 copy-start.4
  17.1 1.3 %collective-permute-start.1 = (f32[16,128]{1,0:T(8,128)S(1)}, f32[16,128]{1,0:T(8,128)S(1)}, u32[]{:S(2)}, u32[]{:S(2)}) collective-permute-start(f32[16,128]{1,0:T(8,128)S(1)} %get-tuple-element.17.own), channel_id=1, source_target_pairs={{1,0},{2,1},{3,2},{5,4},{6,5},{7,6},{9,8},{10,9},{11,10},{13,12},{... | collective-permute-start | bytes 24584 | tf_op jit(solution)/shard_map/ppermute | solution.py:419
  18.4 4.5 %collective-permute-start = (f32[16,128]{1,0:T(8,128)S(1)}, f32[16,128]{1,0:T(8,128)S(1)}, u32[]{:S(2)}, u32[]{:S(2)}) collective-permute-start(f32[16,128]{1,0:T(8,128)S(1)} %get-tuple-element.17.own), channel_id=1, source_target_pairs={{0,1},{1,2},{2,3},{4,5},{5,6},{6,7},{8,9},{9,10},{10,11},{12,13},{... | collective-permute-start | bytes 24584 | tf_op jit(solution)/shard_map/ppermute | solution.py:418
  23.0 0.0 copy-start.6
  23.0 0.0 copy-start.8
  23.0 0.0 copy-done.3
  23.0 0.0 copy-done.5
  23.0 0.0 copy-done.7
  23.0 0.0 copy-done.4
  23.0 0.6 %copy-done.6 = s32[16,6]{0,1:T(8,128)S(1)} copy-done((s32[16,6]{0,1:T(8,128)S(1)}, s32[16,6]{0,1:T(8,128)}, u32[]{:S(2)}) %copy-start.6) | copy-done | bytes 408
  23.7 0.0 copy-done.8
  23.7 0.2 observe.1
  23.9 0.0 collective-permute-done.1.above
  23.9 0.5 %collective-permute-done.below = f32[16,128]{1,0:T(8,128)S(1)} collective-permute-done((f32[16,128]{1,0:T(8,128)S(1)}, f32[16,128]{1,0:T(8,128)S(1)}, u32[]{:S(2)}, u32[]{:S(2)}) %collective-permute-start) | collective-permute-done | bytes 8224 | tf_op jit(solution)/shard_map/ppermute | solution.py:418
  24.3 0.8 %assess_first.1 = (bf16[8,8,1152]{2,1,0:T(8,128)(2,1)S(1)}, f32[16,256]{1,0:T(8,128)S(1)}, f32[16,256]{1,0:T(8,128)S(1)}) custom-call(bf16[32,4096]{1,0:T(8,128)(2,1)S(1)} %forecast_first.1.prior, f32[16,128]{1,0:T(8,128)S(1)} %get-tuple-element.17.own, f32[16,128]{1,0:T(8,128)S(1)} %collective-permute-done.below, ...), custom_call_target="tpu_custom_call" | custom-call | tf_op jit(solution)/shard_map/assess_first/pallas_call | solution.py:28
  25.2 1.6 %all-to-all-done.1.got = bf16[8,8,4096]{2,1,0:T(8,128)(2,1)S(1)} async-done(((bf16[8,8,4096]{2,1,0:T(8,128)(2,1)}), bf16[8,8,4096]{2,1,0:T(8,128)(2,1)S(1)}, u32[]{:S(2)}, u32[]{:S(2)}) %all-to-all-start.1) | async-done | bytes 524320 | tf_op jit(solution)/shard_map/all_to_all | solution.py:416
  26.8 1.4 %forecast_second.1 = bf16[8,8,6400]{2,1,0:T(8,128)(2,1)S(1)} custom-call(bf16[8,8,4096]{2,1,0:T(8,128)(2,1)S(1)} %all-to-all-done.1.got, s32[2,32,128]{2,1,0:T(8,128)S(1)} %get-tuple-element.16.keys, f32[16,4096]{1,0:T(8,128)S(1)} %copy-done.1, bf16[2,2,16,4096]{3,2,1,0:T(8,128)(2,1)S(1)} %copy-done, f32[16,128]{1,0:T(8,128)S(1)} %get-tuple-element.17.own, ...), custom_call_target="tpu_custom_call" | custom-call | tf_op jit(solution)/shard_map/forecast_second/pallas_call | solution.py:28
  28.2 15.3 %all_to_all.21.got = bf16[8,8,6400]{2,1,0:T(8,128)(2,1)S(1)} all-to-all(bf16[8,8,6400]{2,1,0:T(8,128)(2,1)S(1)} %forecast_second.1), channel_id=1, replica_groups=mesh['member'=8,'region'=4] {'member'}, dimensions={0} | all-to-all | bytes 1638400 | tf_op jit(solution)/shard_map/all_to_all | solution.py:438
  43.5 0.9 %finish.1 = (bf16[2,16,4096]{2,1,0:T(8,128)(2,1)}, f32[2,16,512]{2,1,0:T(8,128)}) custom-call(bf16[8,8,6400]{2,1,0:T(8,128)(2,1)S(1)} %all_to_all.21.got, s32[2,32,128]{2,1,0:T(8,128)S(1)} %get-tuple-element.16.keys), custom_call_target="tpu_custom_call" | custom-call | tf_op jit(solution)/shard_map/finish/pallas_call | solution.py:28
Async XLA Ops:
  0.6 7.1 %copy-start = (bf16[2,2,16,4096]{3,2,1,0:T(8,128)(2,1)S(1)}, bf16[2,2,16,4096]{3,2,1,0:T(8,128)(2,1)}, u32[]{:S(2)}) copy-start(bf16[2,2,16,4096]{3,2,1,0:T(8,128)(2,1)} %pert.3) | copy-start | bytes 1572868
  0.6 7.1 %copy-start.1 = (f32[16,4096]{1,0:T(8,128)S(1)}, f32[16,4096]{1,0:T(8,128)}, u32[]{:S(2)}) copy-start(f32[16,4096]{1,0:T(8,128)} %diff.3) | copy-start | bytes 786436
  0.7 7.1 %copy-start.2 = (bf16[2,16,4096]{2,1,0:T(8,128)(2,1)S(1)}, bf16[2,16,4096]{2,1,0:T(8,128)(2,1)}, u32[]{:S(2)}) copy-start(bf16[2,16,4096]{2,1,0:T(8,128)(2,1)} %st1.1) | copy-start | bytes 786436
  2.6 9.8 %all-to-all-start = ((f32[8,1,128]{2,1,0:T(1,128)}), f32[8,1,128]{2,1,0:T(1,128)S(1)}, u32[]{:S(2)}, u32[]{:S(2)}) async-start(f32[8,1,128]{2,1,0:T(1,128)} %bitcast.3), calls=%async_computation | async-start | bytes 8192 | tf_op jit(solution)/shard_map/all_to_all | solution.py:392
  13.5 9.5 %copy-start.3 = (f32[2,32,16]{1,2,0:T(8,128)S(1)}, f32[2,32,16]{1,2,0:T(8,128)}, u32[]{:S(2)}) copy-start(f32[2,32,16]{1,2,0:T(8,128)} %param.14) | copy-start | bytes 12292
  13.5 9.5 %copy-start.5 = (f32[32,16]{0,1:T(8,128)S(1)}, f32[32,16]{0,1:T(8,128)}, u32[]{:S(2)}) copy-start(f32[32,16]{0,1:T(8,128)} %param.15) | copy-start | bytes 6148
  13.5 9.5 %copy-start.7 = (f32[16,6]{0,1:T(8,128)S(1)}, f32[16,6]{0,1:T(8,128)}, u32[]{:S(2)}) copy-start(f32[16,6]{0,1:T(8,128)} %param.19) | copy-start | bytes 1156
  13.5 13.3 %all-to-all-start.1 = ((bf16[8,8,4096]{2,1,0:T(8,128)(2,1)}), bf16[8,8,4096]{2,1,0:T(8,128)(2,1)S(1)}, u32[]{:S(2)}, u32[]{:S(2)}) async-start(bf16[8,8,4096]{2,1,0:T(8,128)(2,1)} %get-tuple-element.15), calls=%async_computation.1 | async-start | bytes 1048576 | tf_op jit(solution)/shard_map/all_to_all | solution.py:416
  17.1 5.9 %copy-start.4 = (s32[32,16]{0,1:T(8,128)S(1)}, s32[32,16]{0,1:T(8,128)}, u32[]{:S(2)}) copy-start(s32[32,16]{0,1:T(8,128)} %param.17) | copy-start | bytes 6148
  17.1 6.7 %collective-permute-start.1 = (f32[16,128]{1,0:T(8,128)S(1)}, f32[16,128]{1,0:T(8,128)S(1)}, u32[]{:S(2)}, u32[]{:S(2)}) collective-permute-start(f32[16,128]{1,0:T(8,128)S(1)} %get-tuple-element.17.own), channel_id=1, source_target_pairs={{1,0},{2,1},{3,2},{5,4},{6,5},{7,6},{9,8},{10,9},{11,10},{13,12},{... | collective-permute-start | bytes 24584 | tf_op jit(solution)/shard_map/ppermute | solution.py:419
  18.4 5.9 %collective-permute-start = (f32[16,128]{1,0:T(8,128)S(1)}, f32[16,128]{1,0:T(8,128)S(1)}, u32[]{:S(2)}, u32[]{:S(2)}) collective-permute-start(f32[16,128]{1,0:T(8,128)S(1)} %get-tuple-element.17.own), channel_id=1, source_target_pairs={{0,1},{1,2},{2,3},{4,5},{5,6},{6,7},{8,9},{9,10},{10,11},{12,13},{... | collective-permute-start | bytes 24584 | tf_op jit(solution)/shard_map/ppermute | solution.py:418
  23.0 0.7 %copy-start.6 = (s32[16,6]{0,1:T(8,128)S(1)}, s32[16,6]{0,1:T(8,128)}, u32[]{:S(2)}) copy-start(s32[16,6]{0,1:T(8,128)} %param.18) | copy-start | bytes 1156
  23.0 0.7 %copy-start.8 = (s32[32]{0:T(128)S(1)}, s32[32]{0:T(128)}, u32[]{:S(2)}) copy-start(s32[32]{0:T(128)} %param.16) | copy-start | bytes 388

commit v4 on v3

v4 whole, which is shorter than its diff:
```python
import jax
import jax.numpy as jnp
from jax import lax
from jax.experimental import pallas as pl
from jax.experimental.pallas import tpu as pltpu
from jax.sharding import PartitionSpec as P

CYCLES = 2
STEPS = 2
LANES = 128
F32 = jnp.float32
BF16 = jnp.bfloat16
I32 = jnp.int32
PARAMS = pltpu.CompilerParams(vmem_limit_bytes=48 * 1024 * 1024)


def iota(shape, dim):
    return lax.broadcasted_iota(I32, shape, dim)


def whole_spec(shape):
    zeros = (0,) * len(shape)
    return pl.BlockSpec(shape, lambda i: zeros)


def call(kernel, outs, args, specs=None, scratch=(), name=None):
    specs = specs or [whole_spec(a.shape) for a in args]
    return pl.pallas_call(
        kernel,
        out_shape=[jax.ShapeDtypeStruct(s, d) for s, d in outs],
        grid=(1,),
        in_specs=specs,
        out_specs=[whole_spec(s) for s, _ in outs],
        scratch_shapes=[pltpu.VMEM(s, d) for s, d in scratch],
        compiler_params=PARAMS,
        name=name,
    )(*args)


def column_of(row):
    n = row.shape[1]
    square = jnp.broadcast_to(row, (n, n))
    return jnp.sum(jnp.where(iota((n, n), 0) == iota((n, n), 1), square, 0), axis=1, keepdims=True)


def here():
    return lax.axis_index("member")


EDGE_AT = 32
STRIDE = 8


def padded(pairs):
    return max(8, pairs)


def make_prepare(members, capacity, parts, tiles):
    width = 2 * STEPS
    pairs = members // 2
    rows = parts * tiles

    def kernel(st0, st1, df0, df1, pb0, pb1, am, slot, *outs):
        notes, trail, keys = outs[:pairs], outs[pairs], outs[pairs + 1]
        m = here()
        lane = iota((1, LANES), 1)
        last = tiles - 1
        trail[...] = jnp.zeros(trail.shape, F32)
        trail[0:1, :] = df1[last:last + 1, :]
        trail[1:2, :] = df0[0:1, :]
        edge = jnp.zeros((1, LANES), F32)
        for p in range(parts):
            for i, t in enumerate((last, 0)):
                source = am[0, p:p + 1, t:t + 1] ^ m
                code = (slot[0, p:p + 1, t:t + 1] * 2 + source % 2) * padded(pairs) + source // 2
                row = 2 + i * parts + p
                trail[row:row + 1, :] = jnp.broadcast_to(code.astype(F32), (1, LANES))
            fields = (st1[p, last:last + 1, :], st0[p, 0:1, :], pb1[0, p, last:last + 1, :], pb0[0, p, 0:1, :])
            for i, x in enumerate(fields):
                to = EDGE_AT + STRIDE * (4 * p + i)
                start = 0 if i % 2 else LANES - width
                moved = pltpu.roll(x.astype(F32), (to - start) % LANES, 1)
                edge = jnp.where((lane >= to) & (lane < to + width), moved, edge)
        before = (iota((tiles, tiles), 0) < iota((tiles, tiles), 1)).astype(F32)
        asked = jnp.zeros((pairs, LANES), F32)
        for c in range(CYCLES):
            seen = jnp.zeros((members, 1), F32)
            for p in range(parts):
                source = am[c, p:p + 1, :] ^ m
                named = (iota((members, tiles), 0) == source).astype(F32)
                earlier = seen + jnp.dot(named, before, preferred_element_type=F32)
                rank = jnp.sum(named * earlier, axis=0, keepdims=True).astype(I32)
                seen = seen + jnp.sum(named, axis=1, keepdims=True)
                half = source % 2
                code = half * rows + slot[c, p:p + 1, :] * tiles + iota((1, tiles), 1)
                spot = (iota((LANES, tiles), 0) == (2 * c + half) * capacity + rank).astype(F32)
                pair = jnp.where(iota((pairs, tiles), 0) == source // 2, (code + 1).astype(F32), 0.0)
                asked = asked + lax.dot_general(pair, spot, (((1,), (1,)), ((), ())), preferred_element_type=F32)
                column = column_of(source * capacity + rank)
                keys[c, p * tiles:(p + 1) * tiles, :] = jnp.broadcast_to(column, (tiles, LANES))
        for k in range(pairs):
            notes[k][...] = jnp.where(lane < EDGE_AT, asked[k:k + 1, :] - 1.0, edge)

    return kernel


def edge_windows(own, below, above, size, parts):
    width = 2 * STEPS

    def field(note, p, i):
        at = EDGE_AT + STRIDE * (4 * p + i)
        start = 0 if i % 2 else LANES - width
        both = jnp.concatenate([note[:size, :], note[size + 8:, :]], axis=0)
        return pltpu.roll(both, (start - at) % LANES, 1)

    low, high = [], []
    for out, before, after in ((low, below, own), (high, own, above)):
        d = jnp.concatenate([before[size:size + 1, :], after[size + 1:size + 2, :]], axis=1)
        for p in range(parts):
            x = jnp.concatenate([field(before, p, 0), field(after, p, 1)], axis=1)
            x = diffuse(x, d) + jnp.concatenate([field(before, p, 2), field(after, p, 3)], axis=1)
            out.append(x.astype(BF16).astype(F32))
    return jnp.concatenate(low, axis=0), jnp.concatenate(high, axis=0)


def patch(x, first, last):
    tiles = x.shape[0]
    row, lane = iota((tiles, LANES), 0), iota((tiles, LANES), 1)
    head = jnp.where((row == 0) & (lane < STEPS), first, x[:, :LANES])
    tail = jnp.where((row == tiles - 1) & (lane >= LANES - STEPS), last, x[:, -LANES:])
    return jnp.concatenate([head, x[:, LANES:-LANES], tail], axis=1)


def widen(x, left, right):
    tiles = x.shape[0]
    row = iota((tiles, LANES), 0)
    before = jnp.where(row == 0, left, pltpu.roll(x[:, -LANES:], 1, 0))
    after = jnp.where(row == tiles - 1, right, pltpu.roll(x[:, :LANES], tiles - 1, 0))
    return jnp.concatenate([before, x, after], axis=1)


def diffuse(x, d):
    n = x.shape[1]
    for _ in range(STEPS):
        x = x + d * (pltpu.roll(x, 1, 1) - 2.0 * x + pltpu.roll(x, n - 1, 1))
    return x


def pick_rows(wanted, rows):
    m = rows.shape[0]
    n = wanted.shape[0]
    choice = (wanted[:, :m] == iota((n, m), 1)).astype(F32).astype(BF16)
    return jnp.dot(choice, rows, preferred_element_type=F32)


def requested(notes, prior, cycle, rows):
    pairs = len(notes)
    total = pairs * rows
    asked = jnp.concatenate(notes, axis=0)
    spread = jnp.broadcast_to(asked[:, None, :], (pairs, rows, LANES)).reshape(total, LANES)
    mine = iota((total, LANES), 1) == cycle * rows + iota((total, LANES), 0) % rows
    wanted = jnp.sum(jnp.where(mine, spread, 0.0), axis=1, keepdims=True).astype(I32)
    return pick_rows(jnp.broadcast_to(wanted, (total, LANES)), prior)


def make_observe(blocks, per_block, tiles, near):
    count = blocks * per_block

    def kernel(tile, cell, prec, value, pattern, weight, where, terms, local):
        def line(x):
            wide = jnp.concatenate([x] * per_block, axis=1)
            own = iota((per_block, count), 1) // blocks == iota((per_block, count), 0)
            return jnp.sum(jnp.where(own, wide, 0), axis=0, keepdims=True)

        at = line(cell[...])
        row = (at // LANES) * tiles + jnp.concatenate([tile[...]] * per_block, axis=1)
        pick = iota((2, count), 0) == 0
        where[...] = jnp.where(pick, row, at % LANES)
        terms[0:1, :] = line(prec[...])
        for c in range(CYCLES):
            terms[c + 1:c + 2, :] = line(value[c])
        group = iota((tiles, count), 1) % blocks
        total = jnp.zeros((tiles, count), F32)
        for k in range(near):
            total = total + jnp.where(column_of(pattern[k:k + 1, :]) == group, column_of(weight[k:k + 1, :]), 0.0)
        local[...] = total

    return kernel


def assess(prior, where, prec, value, local, parts, tiles, cells):
    blocks = cells // LANES
    rows = tiles * blocks
    count = where.shape[1]
    stacked = jnp.concatenate(
        [jnp.concatenate([x[:, k * LANES:(k + 1) * LANES] for k in range(blocks)], axis=0) for x in prior],
        axis=1,
    )
    choice = (iota((rows, count), 0) == where[0:1, :]).astype(F32).astype(BF16)
    lines = lax.dot_general(stacked, choice, (((0,), (0,)), ((), ())), preferred_element_type=F32)
    lane = iota((LANES, count), 0) == where[1:2, :]
    score = []
    for p in range(parts):
        predicted = jnp.sum(jnp.where(lane, lines[p * LANES:(p + 1) * LANES, :], 0.0), axis=0, keepdims=True)
        miss = value - predicted
        term = 0.5 * (prec * miss * miss)
        score.append(jnp.sum(local * term, axis=1, keepdims=True))
    least = score[0]
    for s in score[1:]:
        least = jnp.minimum(least, s)
    scale = [jnp.exp(least - s) for s in score]
    total = scale[0]
    for s in scale[1:]:
        total = total + s
    weighted = scale[0] * prior[0].astype(F32)
    for s, x in zip(scale[1:], prior[1:]):
        weighted = weighted + s * x.astype(F32)
    return least, total, weighted


def pieces(x):
    high = x.astype(BF16).astype(F32)
    middle = (x - high).astype(BF16).astype(F32)
    low = (x - high - middle).astype(BF16).astype(F32)
    return high, middle, low


def share_of(ref, member, share):
    if share % LANES == 0:
        return ref[:, pl.ds(pl.multiple_of(member * share, LANES), share)]
    return pltpu.roll(ref[...], ref.shape[1] - member * share, 1)[:, :share]


def pack_mean(outs, at, least, total, sums, share):
    rows = outs[0].shape[0]
    tiles = sums.shape[0]
    groups = tiles // rows
    m = here()
    lane = iota((rows, LANES), 1)
    misc = jnp.zeros((rows, LANES), F32)
    spot = 0
    for x in (least, total):
        for piece in pieces(x):
            for g in range(groups):
                misc = jnp.where(lane == spot, piece[g * rows:(g + 1) * rows, :], misc)
                spot += 1
    end = at + groups * share
    for k, out in enumerate(outs):
        block = share_of(sums, m ^ (2 * k), share)
        for g in range(groups):
            out[:, at + g * share:at + (g + 1) * share] = block[g * rows:(g + 1) * rows, :].astype(BF16)
        out[:, end:end + LANES] = misc.astype(BF16)


def unpack_mean(got, at, tiles, share):
    rows = got[0].shape[0]
    groups = tiles // rows
    end = at + groups * share
    misc = [x[:, end:end + LANES].astype(F32) for x in got]
    means = []
    for g in range(groups):
        stats = []
        for x in misc:
            pair = []
            for kind in range(2):
                spot = [(kind * 3 + piece) * groups + g for piece in range(3)]
                high, middle, low = [x[:, i:i + 1] for i in spot]
                pair.append(high + middle + low)
            stats.append(pair)
        lowest = stats[0][0]
        for least, _ in stats[1:]:
            lowest = jnp.minimum(lowest, least)
        top, bottom = 0.0, 0.0
        for x, (least, total) in zip(got, stats):
            scale = jnp.exp(lowest - least)
            top = top + scale * x[:, at + g * share:at + (g + 1) * share].astype(F32)
            bottom = bottom + scale * total
        means.append(top / bottom)
    return means


def make_first(parts, tiles, cells):
    def kernel(state, diff, pert, after, prior):
        nothing = jnp.zeros((1, LANES), F32)
        d = widen(diff[...], nothing, nothing)
        for p in range(parts):
            x = diffuse(widen(state[p].astype(F32), nothing, nothing), d)
            now = x[:, LANES:LANES + cells] + pert[0, p].astype(F32)
            prior[p * tiles:(p + 1) * tiles, :] = now.astype(BF16)

    return kernel


def make_send(pairs, rows):
    def kernel(own, other, trail, *refs):
        notes, sends, half = refs[:pairs], refs[pairs:2 * pairs], refs[2 * pairs]
        prior = jnp.concatenate([own[...], other[...]], axis=0)
        sent = requested([x[...] for x in notes], prior, 0, rows)
        for k in range(pairs):
            sends[k][...] = sent[k * rows:(k + 1) * rows, :].astype(BF16)
        size = padded(pairs)
        half[...] = jnp.zeros(half.shape, F32)
        for k in range(pairs):
            half[k:k + 1, :] = notes[k][...]
        half[size:, :] = trail[...]

    return kernel


def make_assess(pairs, parts, tiles, cells, share):
    size = padded(pairs)

    def kernel(own, other, message, below, above, where, terms, local, *refs):
        outs, low_out, high_out, sums = refs[:pairs], refs[pairs], refs[pairs + 1], refs[pairs + 2]
        low, high = edge_windows(message[...], below[...], above[...], size, parts)
        low_out[...] = low.astype(BF16)
        high_out[...] = high.astype(BF16)
        fixed = []
        for h, prior in enumerate((own, other)):
            for p in range(parts):
                row = (2 * p + h) * size
                x = prior[p * tiles:(p + 1) * tiles, :].astype(F32)
                x = patch(x, low[row:row + 1, LANES:], high[row:row + 1, :LANES])
                fixed.append(x.astype(BF16))
        least, total, weighted = assess(
            fixed, where[...], terms[0:1, :], terms[1:2, :], local[...], 2 * parts, tiles, cells
        )
        sums[...] = weighted
        pack_mean(outs, 0, least, total, sums, share)

    return kernel


def make_second(pairs, parts, tiles, cells):
    size = padded(pairs)

    def kernel(keys, diff, pert, message, below, above, low, high, *refs):
        got, prior = refs[:pairs], refs[pairs]
        arrived = jnp.concatenate([x[...] for x in got], axis=0)
        moved = pick_rows(keys[0], arrived)
        at = size + 2
        mine = message[at:at + 2 * parts, :].astype(I32)
        codes = jnp.concatenate([mine[parts:], below[at:at + parts, :].astype(I32)], axis=0)
        start = pick_rows(codes, low[...])
        codes = jnp.concatenate([mine[:parts], above[at + parts:at + 2 * parts, :].astype(I32)], axis=0)
        end = pick_rows(codes, high[...])
        d = widen(diff[...], below[size:size + 1, :], above[size + 1:size + 2, :])
        for p in range(parts):
            x = patch(moved[p * tiles:(p + 1) * tiles, :], start[p:p + 1, LANES:], end[p:p + 1, :LANES])
            q = parts + p
            x = widen(x, start[q:q + 1, :LANES], end[q:q + 1, LANES:])
            x = diffuse(x, d)[:, LANES:LANES + cells]
            prior[p * tiles:(p + 1) * tiles, :] = (x + pert[0, p].astype(F32)).astype(BF16)

    return kernel


def make_send_second(pairs, rows, parts, tiles, cells, share):
    def kernel(own, other, where, terms, local, *refs):
        notes, kept, outs, sums = refs[:pairs], refs[pairs:2 * pairs], refs[2 * pairs:3 * pairs], refs[3 * pairs]
        prior = jnp.concatenate([own[...], other[...]], axis=0)
        sent = requested([x[...] for x in notes], prior, 1, rows)
        extra = kept[0].shape[1]
        for k in range(pairs):
            outs[k][:, :cells] = sent[k * rows:(k + 1) * rows, :].astype(BF16)
            outs[k][:, cells:cells + extra] = kept[k][...]
        least, total, weighted = assess(
            [x[p * tiles:(p + 1) * tiles, :] for x in (own, other) for p in range(parts)],
            where[...], terms[0:1, :], terms[2:3, :], local[...], 2 * parts, tiles, cells,
        )
        sums[...] = weighted
        pack_mean(outs, cells + extra, least, total, sums, share)

    return kernel


def make_last(pairs, rows, parts, tiles, cells):
    def kernel(keys, *refs):
        got, analysis, mean = refs[:pairs], refs[pairs], refs[pairs + 1]
        arrived = jnp.concatenate([x[:, :cells] for x in got], axis=0)
        picked = pick_rows(keys[1], arrived)
        for p in range(parts):
            analysis[p] = picked[p * tiles:(p + 1) * tiles, :].astype(BF16)
        share = mean.shape[2]
        extra = tiles // rows * share + LANES
        for c in range(CYCLES):
            for g, x in enumerate(unpack_mean(got, cells + c * extra, tiles, share)):
                mean[c, g * rows:(g + 1) * rows, :] = x

    return kernel


def body(
    state,
    diffusivity,
    model_perturbation,
    obs_values,
    obs_prec,
    obs_tile,
    obs_cell,
    pattern,
    loc_weight,
    anc_member,
    anc_slot,
):
    parts, tiles, cells = state.shape
    members = lax.axis_size("member")
    regions = lax.axis_size("region")
    capacity = max(2, 2 * parts * tiles // members)
    share = cells // members
    pairs = members // 2
    rows = 2 * capacity
    extra = tiles // rows * share + LANES
    blocks, per_block = obs_cell.shape
    count = blocks * per_block
    member_of = anc_member.reshape(CYCLES, parts, tiles)
    slot_of = anc_slot.reshape(CYCLES, parts, tiles)
    near = pattern.shape[1]
    ends = cells // LANES - 1

    def block(shape, at):
        lead = (0,) * (len(shape) - 1)
        return pl.BlockSpec(shape, lambda i: lead + (at,))

    edges = [state, state, diffusivity, diffusivity, model_perturbation, model_perturbation, member_of, slot_of]
    *notes, trail, keys = call(
        make_prepare(members, capacity, parts, tiles),
        [((1, LANES), F32)] * pairs + [((8, LANES), F32), ((CYCLES, parts * tiles, LANES), I32)],
        [pltpu.with_memory_space_constraint(x, pltpu.HBM) for x in edges],
        [
            block((parts, tiles, LANES), 0),
            block((parts, tiles, LANES), ends),
            block((tiles, LANES), 0),
            block((tiles, LANES), ends),
            block((1, parts, tiles, LANES), 0),
            block((1, parts, tiles, LANES), ends),
            whole_spec(member_of.shape),
            whole_spec(slot_of.shape),
        ],
        name="prepare",
    )

    def trade(x, k):
        return lax.ppermute(x, "member", [(i, i ^ k) for i in range(members)])

    notes = notes[:1] + [trade(notes[k], 2 * k) for k in range(1, pairs)]

    where, terms, local = call(
        make_observe(blocks, per_block, tiles, near),
        [((2, count), I32), ((1 + CYCLES, count), F32), ((tiles, count), F32)],
        [obs_tile[None, :], obs_cell.T, obs_prec.T, jnp.swapaxes(obs_values, 1, 2), pattern.T, loc_weight.T],
        name="observe",
    )

    def noise_spec(c):
        return pl.BlockSpec((1, parts, tiles, cells), lambda i: (c, 0, 0, 0))

    args = [state, diffusivity, model_perturbation, trail]
    specs = [whole_spec(a.shape) for a in args]
    specs[2] = noise_spec(0)
    (prior,) = call(
        make_first(parts, tiles, cells), [((parts * tiles, cells), BF16)], args, specs, name="forecast_first"
    )
    other = trade(prior, 1)
    size = padded(pairs)
    *sends, half = call(
        make_send(pairs, rows),
        [((rows, cells), BF16)] * pairs + [((size + trail.shape[0], LANES), F32)],
        [prior, other, trail, *notes],
        name="send_first",
    )
    got = [sends[0]] + [trade(sends[k], 2 * k) for k in range(1, pairs)]
    message = jnp.concatenate([half, trade(half, 1)[:size]], axis=0)
    forward = [(i, i + 1) for i in range(regions - 1)]
    below = lax.ppermute(message, "region", forward)
    above = lax.ppermute(message, "region", [(j, i) for i, j in forward])
    window = ((parts * 2 * size, 2 * LANES), BF16)
    sums = [((tiles, cells), F32)]
    *kept, low, high = call(
        make_assess(pairs, parts, tiles, cells, share),
        [((rows, extra), BF16)] * pairs + [window, window],
        [prior, other, message, below, above, where, terms, local],
        scratch=sums,
        name="assess_first",
    )
    args = [keys, diffusivity, model_perturbation, message, below, above, low, high, *got]
    specs = [whole_spec(a.shape) for a in args]
    specs[2] = noise_spec(1)
    (prior,) = call(
        make_second(pairs, parts, tiles, cells),
        [((parts * tiles, cells), BF16)],
        args,
        specs,
        name="forecast_second",
    )
    sends = call(
        make_send_second(pairs, rows, parts, tiles, cells, share),
        [((rows, cells + CYCLES * extra), BF16)] * pairs,
        [prior, trade(prior, 1), where, terms, local, *notes, *kept],
        scratch=sums,
        name="send_second",
    )
    got = [sends[0]] + [trade(sends[k], 2 * k) for k in range(1, pairs)]
    return tuple(
        call(
            make_last(pairs, rows, parts, tiles, cells),
            [(state.shape, BF16), ((CYCLES, tiles, share), F32)],
            [keys, *got],
            name="finish",
        )
    )


def solution(mesh):
    in_specs = (
        P("member", "region", None),
        P("region", None),
        P(None, "member", "region", None),
        P(None, "region", None),
        P("region", None),
        P("region"),
        P("region", None),
        P("region", None),
        P("region", None),
        P(None, "region", "member", None, None),
        P(None, "region", "member", None),
    )
    out_specs = (P("member", "region", None), P(None, "region", "member"))
    return jax.shard_map(body, mesh=mesh, in_specs=in_specs, out_specs=out_specs, check_vma=False)
```

time: 44.9 us -> 39.2 us (0.87)
  blocking collectives: 15.3 us -> 0 us
  waiting for transfers between devices: 6.03 us -> 13.3 us
  starting transfers between devices: 14.6 us -> 17.8 us
  Pallas kernels: 7.01 us -> 6.2 us
    all_to_all x1 -> x0, blocking collectives: 15.3 us -> none  [body(): lax.all_to_all(send, 'member', split_axis=0, concat_axis=0, tiled=True)]
    ppermute x0 -> x12, waiting for transfers between devices: none -> 12.8 us  [trade(): return lax.ppermute(x, 'member', [(i, i ^ k) for i in range(members)])]
    ppermute x0 -> x12, starting transfers between devices: none -> 11.9 us  [trade(): return lax.ppermute(x, 'member', [(i, i ^ k) for i in range(members)])]
    all_to_all x2 -> x0, starting transfers between devices: 8.79 us -> none  [the longest x1 5.17 us: body(): lax.all_to_all(note, 'member', split_axis=0, concat_axis=0, tiled=True)]
    all_to_all x2 -> x0, waiting for transfers between devices: 5.57 us -> none  [the longest x1 3.94 us: body(): lax.all_to_all(note, 'member', split_axis=0, concat_axis=0, tiled=True)]
    pallas_call x7 -> x8, Pallas kernels: 7.01 us -> 6.2 us  [call(): pl.pallas_call(kernel, out_shape=[jax.ShapeDtypeStruct(s, d) for s, d in...]
  transfers between devices with their start and end apart: 4 -> 14, of which waited for: 3 -> 6; matrix products, arithmetic and copies ran while one was open for 0% -> 0% of each run, Pallas kernels for 4% -> 3%
where the time goes in v4:
time: 39.2 us; the launch traced here: 38.9 us
  starting transfers between devices  17.8 us (45%)
  waiting for transfers between devices  13.3 us (34%)
  Pallas kernels  6.2 us (16%)
  between operations  0.89 us (2%)
  local copies, waits for them, and re-layouts  0.65 us (2%)
    ppermute x12, waiting for transfers between devices, trade(): return lax.ppermute(x, 'member', [(i, i ^ k) for i in range(members)])  12.8 us
    ppermute x12, starting transfers between devices, trade(): return lax.ppermute(x, 'member', [(i, i ^ k) for i in range(members)])  11.9 us
    pallas_call x8, Pallas kernels, call(): pl.pallas_call(kernel, out_shape=[jax.ShapeDtypeStruct(s, d) for s, d in...  6.2 us
    ppermute x1, starting transfers between devices, body(): below = lax.ppermute(message, 'region', forward)  4.55 us
    ppermute x1, starting transfers between devices, body(): above = lax.ppermute(message, 'region', [(j, i) for i, j in forward])  1.42 us
  transfers between devices with their start and end apart: 14, of which 6 were waited for; matrix products, arithmetic and copies ran while one was open for 0% of the time, Pallas kernels for 3%

profile of v4, /device:TPU:0, one launch (start us, length us, event | category | flops | bytes accessed | tf_op | source)
XLA Modules:
  0.0 38.9 jit_solution(1481504225869215987)
XLA Ops:
  0.6 0.0 copy-start
  0.6 0.0 copy-start.1
  0.7 0.0 copy-start.2
  0.7 1.3 %prepare.1 = (f32[1,128]{1,0:T(1,128)S(1)}, f32[1,128]{1,0:T(1,128)S(1)}, f32[1,128]{1,0:T(1,128)S(1)}, f32[1,128]{1,0:T(1,128)S(1)}, f32[8,128]{1,0:T(8,128)S(1)}, /*index=5*/s32[2,32,128]{2,1,0:T(8,128)S(1)}) custom-call(bf16[2,16,4096]{2,1,0:T(8,128)(2,1)} %state.1, bf16[2,16,4096]{2,1,0:T(8,128)(2,1)} %state.1, f32[16,4096]{1,0:T(8,128)} %diff.3, ...), custom_call_target="tpu_custom_call" | custom-call | tf_op jit(solution)/shard_map/prepare/pallas_call | solution.py:28
  2.0 0.0 copy-done
  2.0 0.0 copy-done.1
  2.0 0.0 copy-done.2
  2.0 0.6 %forecast_first.1.own = bf16[32,4096]{1,0:T(8,128)(2,1)S(1)} custom-call(bf16[2,16,4096]{2,1,0:T(8,128)(2,1)S(1)} %copy-done.2, f32[16,4096]{1,0:T(8,128)S(1)} %copy-done.1, bf16[2,2,16,4096]{3,2,1,0:T(8,128)(2,1)S(1)} %copy-done, f32[8,128]{1,0:T(8,128)S(1)} %get-tuple-element.27.after.trail), custom_call_target="tpu_custom_call" | custom-call | tf_op jit(solution)/shard_map/forecast_first/pallas_call | solution.py:28
  2.7 0.5 %collective-permute-start = (bf16[32,4096]{1,0:T(8,128)(2,1)S(1)}, bf16[32,4096]{1,0:T(8,128)(2,1)S(1)}, u32[]{:S(2)}, u32[]{:S(2)}) collective-permute-start(bf16[32,4096]{1,0:T(8,128)(2,1)S(1)} %forecast_first.1.own), channel_id=1, source_target_pairs={{0,4},{4,0},{8,12},{12,8},{16,20},{20,16},{24,28},{28,24},{1,5},{5... | collective-permute-start | bytes 786440 | tf_op jit(solution)/shard_map/ppermute | solution.py:444
  3.2 2.6 %collective-permute-start.1 = (f32[1,128]{1,0:T(1,128)S(1)}, f32[1,128]{1,0:T(1,128)S(1)}, u32[]{:S(2)}, u32[]{:S(2)}) collective-permute-start(f32[1,128]{1,0:T(1,128)S(1)} %get-tuple-element.29), channel_id=1, source_target_pairs={{0,8},{4,12},{8,0},{12,4},{16,24},{20,28},{24,16},{28,20},{1,9},{5... | collective-permute-start | bytes 1544 | tf_op jit(solution)/shard_map/ppermute | solution.py:444
  5.7 1.5 %collective-permute-start.2 = (f32[1,128]{1,0:T(1,128)S(1)}, f32[1,128]{1,0:T(1,128)S(1)}, u32[]{:S(2)}, u32[]{:S(2)}) collective-permute-start(f32[1,128]{1,0:T(1,128)S(1)} %get-tuple-element.30), channel_id=1, source_target_pairs={{0,16},{4,20},{8,24},{12,28},{16,0},{20,4},{24,8},{28,12},{1,17},{... | collective-permute-start | bytes 1544 | tf_op jit(solution)/shard_map/ppermute | solution.py:444
  7.3 0.0 collective-permute-start.3
  7.3 0.0 collective-permute-done.1.refs_1_
  7.3 2.0 %collective-permute-done.2.refs_2_ = f32[1,128]{1,0:T(1,128)S(1)} collective-permute-done((f32[1,128]{1,0:T(1,128)S(1)}, f32[1,128]{1,0:T(1,128)S(1)}, u32[]{:S(2)}, u32[]{:S(2)}) %collective-permute-start.2) | collective-permute-done | bytes 544 | tf_op jit(solution)/shard_map/ppermute | solution.py:444
  9.3 2.4 %collective-permute-done.3.refs_3_ = f32[1,128]{1,0:T(1,128)S(1)} collective-permute-done((f32[1,128]{1,0:T(1,128)S(1)}, f32[1,128]{1,0:T(1,128)S(1)}, u32[]{:S(2)}, u32[]{:S(2)}) %collective-permute-start.3) | collective-permute-done | bytes 544 | tf_op jit(solution)/shard_map/ppermute | solution.py:444
  11.7 0.0 collective-permute-done.other
  11.7 0.4 send_first.1
  12.1 0.0 copy-start.6
  12.1 0.0 copy-start.7
  12.1 0.1 collective-permute-start.4
  12.2 0.6 %collective-permute-start.7 = (bf16[16,4096]{1,0:T(8,128)(2,1)S(1)}, bf16[16,4096]{1,0:T(8,128)(2,1)S(1)}, u32[]{:S(2)}, u32[]{:S(2)}) collective-permute-start(bf16[16,4096]{1,0:T(8,128)(2,1)S(1)} %get-tuple-element.39), channel_id=1, source_target_pairs={{0,8},{4,12},{8,0},{12,4},{16,24},{20,28},{24,16},{28,20},{1,9},{5... | collective-permute-start | bytes 393224 | tf_op jit(solution)/shard_map/ppermute | solution.py:444
  12.8 0.1 collective-permute-start.8
  12.8 2.9 %collective-permute-start.9 = (bf16[16,4096]{1,0:T(8,128)(2,1)S(1)}, bf16[16,4096]{1,0:T(8,128)(2,1)S(1)}, u32[]{:S(2)}, u32[]{:S(2)}) collective-permute-start(bf16[16,4096]{1,0:T(8,128)(2,1)S(1)} %get-tuple-element.41), channel_id=1, source_target_pairs={{0,24},{4,28},{8,16},{12,20},{16,8},{20,12},{24,0},{28,4},{1,25},{... | collective-permute-start | bytes 393224 | tf_op jit(solution)/shard_map/ppermute | solution.py:444
  15.7 0.0 collective-permute-done.4
  15.8 0.0 copy-start.4
  15.8 1.4 %collective-permute-start.6 = (f32[24,128]{1,0:T(8,128)S(1)}, f32[24,128]{1,0:T(8,128)S(1)}, u32[]{:S(2)}, u32[]{:S(2)}) collective-permute-start(f32[24,128]{1,0:T(8,128)S(1)} %pad_maximum_fusion.message), channel_id=1, source_target_pairs={{1,0},{2,1},{3,2},{5,4},{6,5},{7,6},{9,8},{10,9},{11,10},{13,12},{... | collective-permute-start | bytes 36872 | tf_op jit(solution)/shard_map/ppermute | solution.py:476
  17.2 4.5 %collective-permute-start.5 = (f32[24,128]{1,0:T(8,128)S(1)}, f32[24,128]{1,0:T(8,128)S(1)}, u32[]{:S(2)}, u32[]{:S(2)}) collective-permute-start(f32[24,128]{1,0:T(8,128)S(1)} %pad_maximum_fusion.message), channel_id=1, source_target_pairs={{0,1},{1,2},{2,3},{4,5},{5,6},{6,7},{8,9},{9,10},{10,11},{12,13},{... | collective-permute-start | bytes 36872 | tf_op jit(solution)/shard_map/ppermute | solution.py:475
  21.8 0.0 copy-start.8
  21.8 0.0 copy-done.6
  21.8 0.6 %copy-done.8 = s32[32]{0:T(128)S(1)} copy-done((s32[32]{0:T(128)S(1)}, s32[32]{0:T(128)}, u32[]{:S(2)}) %copy-start.8) | copy-done | bytes 152
  22.4 0.2 observe.1
  22.6 0.0 collective-permute-done.6.above
  22.6 0.5 %collective-permute-done.5.below = f32[24,128]{1,0:T(8,128)S(1)} collective-permute-done((f32[24,128]{1,0:T(8,128)S(1)}, f32[24,128]{1,0:T(8,128)S(1)}, u32[]{:S(2)}, u32[]{:S(2)}) %collective-permute-start.5) | collective-permute-done | bytes 12320 | tf_op jit(solution)/shard_map/ppermute | solution.py:475
  23.1 1.0 %assess_first.1 = (bf16[16,640]{1,0:T(8,128)(2,1)S(1)}, bf16[16,640]{1,0:T(8,128)(2,1)S(1)}, bf16[16,640]{1,0:T(8,128)(2,1)S(1)}, bf16[16,640]{1,0:T(8,128)(2,1)...) custom-call(bf16[32,4096]{1,0:T(8,128)(2,1)S(1)} %forecast_first.1.own, ...), custom_call_target="tpu_custom_call" | custom-call | tf_op jit(solution)/shard_map/assess_first/pallas_call | solution.py:28
  24.2 0.0 collective-permute-done.7.refs_1_
  24.2 0.0 collective-permute-done.8.refs_2_
  24.2 0.0 collective-permute-done.9.refs_3_
  24.2 0.8 %forecast_second.1.own = bf16[32,4096]{1,0:T(8,128)(2,1)S(1)} custom-call(s32[2,32,128]{2,1,0:T(8,128)S(1)} %get-tuple-element.26.keys, f32[16,4096]{1,0:T(8,128)S(1)} %copy-done.1, bf16[2,2,16,4096]{3,2,1,0:T(8,128)(2,1)S(1)} %copy-done, f32[24,128]{1,0:T(8,128)S(1)} %pad_maximum_fusion.message, f32[24,128]{1,0:T(8,128)S(1)} %collective-permute-done.5.below, ...), custom_call_target="tpu_custom_call" | custom-call | tf_op jit(solution)/shard_map/forecast_second/pallas_call | solution.py:28
  25.1 0.1 collective-permute-start.10
  25.1 1.5 %collective-permute-done.10.other = bf16[32,4096]{1,0:T(8,128)(2,1)S(1)} collective-permute-done((bf16[32,4096]{1,0:T(8,128)(2,1)S(1)}, bf16[32,4096]{1,0:T(8,128)(2,1)S(1)}, u32[]{:S(2)}, u32[]{:S(2)}) %collective-permute-start.10) | collective-permute-done | bytes 262176 | tf_op jit(solution)/shard_map/ppermute | solution.py:444
  26.7 0.9 %send_second.1 = (bf16[16,5376]{1,0:T(8,128)(2,1)S(1)}, bf16[16,5376]{1,0:T(8,128)(2,1)S(1)}, bf16[16,5376]{1,0:T(8,128)(2,1)S(1)}, bf16[16,5376]{1,0:T(8,128)(2,1)S(1)}) custom-call(bf16[32,4096]{1,0:T(8,128)(2,1)S(1)} %forecast_second.1.own, bf16[32,4096]{1,0:T(8,128)(2,1)S(1)} %collective-permute-done.10.other, s32[2,512]{1,0:T(2,128)S(1)} %get-tuple-element.33.where, ...), custom_call_target="tpu_custom_call" | custom-call | tf_op jit(solution)/shard_map/send_second/pallas_call | solution.py:28
  27.6 0.6 %collective-permute-start.11 = (bf16[16,5376]{1,0:T(8,128)(2,1)S(1)}, bf16[16,5376]{1,0:T(8,128)(2,1)S(1)}, u32[]{:S(2)}, u32[]{:S(2)}) collective-permute-start(bf16[16,5376]{1,0:T(8,128)(2,1)S(1)} %get-tuple-element.47), channel_id=1, source_target_pairs={{0,8},{4,12},{8,0},{12,4},{16,24},{20,28},{24,16},{28,20},{1,9},{5... | collective-permute-start | bytes 516104 | tf_op jit(solution)/shard_map/ppermute | solution.py:444
  28.2 0.1 collective-permute-start.12
  28.2 2.9 %collective-permute-start.13 = (bf16[16,5376]{1,0:T(8,128)(2,1)S(1)}, bf16[16,5376]{1,0:T(8,128)(2,1)S(1)}, u32[]{:S(2)}, u32[]{:S(2)}) collective-permute-start(bf16[16,5376]{1,0:T(8,128)(2,1)S(1)} %get-tuple-element.49), channel_id=1, source_target_pairs={{0,24},{4,28},{8,16},{12,20},{16,8},{20,12},{24,0},{28,4},{1,25},{... | collective-permute-start | bytes 516104 | tf_op jit(solution)/shard_map/ppermute | solution.py:444
  31.1 3.7 %collective-permute-done.11.refs_1_ = bf16[16,5376]{1,0:T(8,128)(2,1)S(1)} collective-permute-done((bf16[16,5376]{1,0:T(8,128)(2,1)S(1)}, bf16[16,5376]{1,0:T(8,128)(2,1)S(1)}, u32[]{:S(2)}, u32[]{:S(2)}) %collective-permute-start.11) | collective-permute-done | bytes 172064 | tf_op jit(solution)/shard_map/ppermute | solution.py:444
  34.9 3.1 %collective-permute-done.12.refs_2_ = bf16[16,5376]{1,0:T(8,128)(2,1)S(1)} collective-permute-done((bf16[16,5376]{1,0:T(8,128)(2,1)S(1)}, bf16[16,5376]{1,0:T(8,128)(2,1)S(1)}, u32[]{:S(2)}, u32[]{:S(2)}) %collective-permute-start.12) | collective-permute-done | bytes 172064 | tf_op jit(solution)/shard_map/ppermute | solution.py:444
  38.0 0.0 collective-permute-done.13.refs_3_
  38.0 0.9 %finish.1 = (bf16[2,16,4096]{2,1,0:T(8,128)(2,1)}, f32[2,16,512]{2,1,0:T(8,128)}) custom-call(s32[2,32,128]{2,1,0:T(8,128)S(1)} %get-tuple-element.26.keys, bf16[16,5376]{1,0:T(8,128)(2,1)S(1)} %get-tuple-element.46.refs_0_, bf16[16,5376]{1,0:T(8,128)(2,1)S(1)} %collective-permute-done.11.refs_1_, bf16[16,5376]{1,0:T(8,128)(2,1)S(1)} %collective-permute-done.12.refs_2_, ...), custom_call_target="tpu_custom_call" | custom-call | tf_op jit(solution)/shard_map/finish/pallas_call | solution.py:28
  (8 shorter events, 0.0 us)
Async XLA Ops:
  0.6 1.3 %copy-start = (bf16[2,2,16,4096]{3,2,1,0:T(8,128)(2,1)S(1)}, bf16[2,2,16,4096]{3,2,1,0:T(8,128)(2,1)}, u32[]{:S(2)}) copy-start(bf16[2,2,16,4096]{3,2,1,0:T(8,128)(2,1)} %pert.3) | copy-start | bytes 1572868
  0.6 1.4 %copy-start.1 = (f32[16,4096]{1,0:T(8,128)S(1)}, f32[16,4096]{1,0:T(8,128)}, u32[]{:S(2)}) copy-start(f32[16,4096]{1,0:T(8,128)} %diff.3) | copy-start | bytes 786436
  0.7 1.4 %copy-start.2 = (bf16[2,16,4096]{2,1,0:T(8,128)(2,1)S(1)}, bf16[2,16,4096]{2,1,0:T(8,128)(2,1)}, u32[]{:S(2)}) copy-start(bf16[2,16,4096]{2,1,0:T(8,128)(2,1)} %state.1) | copy-start | bytes 786436
  2.7 9.0 %collective-permute-start = (bf16[32,4096]{1,0:T(8,128)(2,1)S(1)}, bf16[32,4096]{1,0:T(8,128)(2,1)S(1)}, u32[]{:S(2)}, u32[]{:S(2)}) collective-permute-start(bf16[32,4096]{1,0:T(8,128)(2,1)S(1)} %forecast_first.1.own), channel_id=1, source_target_pairs={{0,4},{4,0},{8,12},{12,8},{16,20},{20,16},{24,28},{28,24},{1,5},{5... | collective-permute-start | bytes 786440 | tf_op jit(solution)/shard_map/ppermute | solution.py:444
  3.2 4.1 %collective-permute-start.1 = (f32[1,128]{1,0:T(1,128)S(1)}, f32[1,128]{1,0:T(1,128)S(1)}, u32[]{:S(2)}, u32[]{:S(2)}) collective-permute-start(f32[1,128]{1,0:T(1,128)S(1)} %get-tuple-element.29), channel_id=1, source_target_pairs={{0,8},{4,12},{8,0},{12,4},{16,24},{20,28},{24,16},{28,20},{1,9},{5... | collective-permute-start | bytes 1544 | tf_op jit(solution)/shard_map/ppermute | solution.py:444
  5.7 3.5 %collective-permute-start.2 = (f32[1,128]{1,0:T(1,128)S(1)}, f32[1,128]{1,0:T(1,128)S(1)}, u32[]{:S(2)}, u32[]{:S(2)}) collective-permute-start(f32[1,128]{1,0:T(1,128)S(1)} %get-tuple-element.30), channel_id=1, source_target_pairs={{0,16},{4,20},{8,24},{12,28},{16,0},{20,4},{24,8},{28,12},{1,17},{... | collective-permute-start | bytes 1544 | tf_op jit(solution)/shard_map/ppermute | solution.py:444
  7.3 4.4 %collective-permute-start.3 = (f32[1,128]{1,0:T(1,128)S(1)}, f32[1,128]{1,0:T(1,128)S(1)}, u32[]{:S(2)}, u32[]{:S(2)}) collective-permute-start(f32[1,128]{1,0:T(1,128)S(1)} %get-tuple-element.31), channel_id=1, source_target_pairs={{0,24},{4,28},{8,16},{12,20},{16,8},{20,12},{24,0},{28,4},{1,25},{... | collective-permute-start | bytes 1544 | tf_op jit(solution)/shard_map/ppermute | solution.py:444
  12.1 9.7 %copy-start.6 = (s32[16,6]{0,1:T(8,128)S(1)}, s32[16,6]{0,1:T(8,128)}, u32[]{:S(2)}) copy-start(s32[16,6]{0,1:T(8,128)} %param.18) | copy-start | bytes 1156
  12.1 9.7 %copy-start.7 = (f32[16,6]{0,1:T(8,128)S(1)}, f32[16,6]{0,1:T(8,128)}, u32[]{:S(2)}) copy-start(f32[16,6]{0,1:T(8,128)} %param.19) | copy-start | bytes 1156
  12.1 3.6 %collective-permute-start.4 = (f32[16,128]{1,0:T(8,128)S(1)}, f32[16,128]{1,0:T(8,128)S(1)}, u32[]{:S(2)}, u32[]{:S(2)}) collective-permute-start(f32[16,128]{1,0:T(8,128)S(1)} %get-tuple-element.32), channel_id=1, source_target_pairs={{0,4},{4,0},{8,12},{12,8},{16,20},{20,16},{24,28},{28,24},{1,5},{5... | collective-permute-start | bytes 24584 | tf_op jit(solution)/shard_map/ppermute | solution.py:444
  12.2 12.0 %collective-permute-start.7 = (bf16[16,4096]{1,0:T(8,128)(2,1)S(1)}, bf16[16,4096]{1,0:T(8,128)(2,1)S(1)}, u32[]{:S(2)}, u32[]{:S(2)}) collective-permute-start(bf16[16,4096]{1,0:T(8,128)(2,1)S(1)} %get-tuple-element.39), channel_id=1, source_target_pairs={{0,8},{4,12},{8,0},{12,4},{16,24},{20,28},{24,16},{28,20},{1,9},{5... | collective-permute-start | bytes 393224 | tf_op jit(solution)/shard_map/ppermute | solution.py:444
  12.8 11.4 %collective-permute-start.8 = (bf16[16,4096]{1,0:T(8,128)(2,1)S(1)}, bf16[16,4096]{1,0:T(8,128)(2,1)S(1)}, u32[]{:S(2)}, u32[]{:S(2)}) collective-permute-start(bf16[16,4096]{1,0:T(8,128)(2,1)S(1)} %get-tuple-element.40), channel_id=1, source_target_pairs={{0,16},{4,20},{8,24},{12,28},{16,0},{20,4},{24,8},{28,12},{1,17},{... | collective-permute-start | bytes 393224 | tf_op jit(solution)/shard_map/ppermute | solution.py:444
  12.8 11.4 %collective-permute-start.9 = (bf16[16,4096]{1,0:T(8,128)(2,1)S(1)}, bf16[16,4096]{1,0:T(8,128)(2,1)S(1)}, u32[]{:S(2)}, u32[]{:S(2)}) collective-permute-start(bf16[16,4096]{1,0:T(8,128)(2,1)S(1)} %get-tuple-element.41), channel_id=1, source_target_pairs={{0,24},{4,28},{8,16},{12,20},{16,8},{20,12},{24,0},{28,4},{1,25},{... | collective-permute-start | bytes 393224 | tf_op jit(solution)/shard_map/ppermute | solution.py:444
  15.7 6.1 %copy-start.3 = (f32[2,32,16]{1,2,0:T(8,128)S(1)}, f32[2,32,16]{1,2,0:T(8,128)}, u32[]{:S(2)}) copy-start(f32[2,32,16]{1,2,0:T(8,128)} %param.14) | copy-start | bytes 12292
  15.7 6.1 %copy-start.5 = (f32[32,16]{0,1:T(8,128)S(1)}, f32[32,16]{0,1:T(8,128)}, u32[]{:S(2)}) copy-start(f32[32,16]{0,1:T(8,128)} %param.15) | copy-start | bytes 6148
  15.8 6.1 %copy-start.4 = (s32[32,16]{0,1:T(8,128)S(1)}, s32[32,16]{0,1:T(8,128)}, u32[]{:S(2)}) copy-start(s32[32,16]{0,1:T(8,128)} %param.17) | copy-start | bytes 6148
  15.8 6.8 %collective-permute-start.6 = (f32[24,128]{1,0:T(8,128)S(1)}, f32[24,128]{1,0:T(8,128)S(1)}, u32[]{:S(2)}, u32[]{:S(2)}) collective-permute-start(f32[24,128]{1,0:T(8,128)S(1)} %pad_maximum_fusion.message), channel_id=1, source_target_pairs={{1,0},{2,1},{3,2},{5,4},{6,5},{7,6},{9,8},{10,9},{11,10},{13,12},{... | collective-permute-start | bytes 36872 | tf_op jit(solution)/shard_map/ppermute | solution.py:476
  17.2 5.9 %collective-permute-start.5 = (f32[24,128]{1,0:T(8,128)S(1)}, f32[24,128]{1,0:T(8,128)S(1)}, u32[]{:S(2)}, u32[]{:S(2)}) collective-permute-start(f32[24,128]{1,0:T(8,128)S(1)} %pad_maximum_fusion.message), channel_id=1, source_target_pairs={{0,1},{1,2},{2,3},{4,5},{5,6},{6,7},{8,9},{9,10},{10,11},{12,13},{... | collective-permute-start | bytes 36872 | tf_op jit(solution)/shard_map/ppermute | solution.py:475
  21.8 0.7 %copy-start.8 = (s32[32]{0:T(128)S(1)}, s32[32]{0:T(128)}, u32[]{:S(2)}) copy-start(s32[32]{0:T(128)} %param.16) | copy-start | bytes 388
  25.1 1.6 %collective-permute-start.10 = (bf16[32,4096]{1,0:T(8,128)(2,1)S(1)}, bf16[32,4096]{1,0:T(8,128)(2,1)S(1)}, u32[]{:S(2)}, u32[]{:S(2)}) collective-permute-start(bf16[32,4096]{1,0:T(8,128)(2,1)S(1)} %forecast_second.1.own), channel_id=1, source_target_pairs={{0,4},{4,0},{8,12},{12,8},{16,20},{20,16},{24,28},{28,24},{1,5},{5... | collective-permute-start | bytes 786440 | tf_op jit(solution)/shard_map/ppermute | solution.py:444
  27.6 7.3 %collective-permute-start.11 = (bf16[16,5376]{1,0:T(8,128)(2,1)S(1)}, bf16[16,5376]{1,0:T(8,128)(2,1)S(1)}, u32[]{:S(2)}, u32[]{:S(2)}) collective-permute-start(bf16[16,5376]{1,0:T(8,128)(2,1)S(1)} %get-tuple-element.47), channel_id=1, source_target_pairs={{0,8},{4,12},{8,0},{12,4},{16,24},{20,28},{24,16},{28,20},{1,9},{5... | collective-permute-start | bytes 516104 | tf_op jit(solution)/shard_map/ppermute | solution.py:444
  28.2 9.8 %collective-permute-start.12 = (bf16[16,5376]{1,0:T(8,128)(2,1)S(1)}, bf16[16,5376]{1,0:T(8,128)(2,1)S(1)}, u32[]{:S(2)}, u32[]{:S(2)}) collective-permute-start(bf16[16,5376]{1,0:T(8,128)(2,1)S(1)} %get-tuple-element.48), channel_id=1, source_target_pairs={{0,16},{4,20},{8,24},{12,28},{16,0},{20,4},{24,8},{28,12},{1,17},{... | collective-permute-start | bytes 516104 | tf_op jit(solution)/shard_map/ppermute | solution.py:444
  28.2 9.8 %collective-permute-start.13 = (bf16[16,5376]{1,0:T(8,128)(2,1)S(1)}, bf16[16,5376]{1,0:T(8,128)(2,1)S(1)}, u32[]{:S(2)}, u32[]{:S(2)}) collective-permute-start(bf16[16,5376]{1,0:T(8,128)(2,1)S(1)} %get-tuple-element.49), channel_id=1, source_target_pairs={{0,24},{4,28},{8,16},{12,20},{16,8},{20,12},{24,0},{28,4},{1,25},{... | collective-permute-start | bytes 516104 | tf_op jit(solution)/shard_map/ppermute | solution.py:444

commit v5 on v4

--- a/solution.py
+++ b/solution.py
@@ -104,13 +104,20 @@
     return kernel
 
 
+def halves(mine, theirs):
+    half = theirs.shape[0] // 2
+    theirs = jnp.concatenate([theirs[half:, :], theirs[:half, :]], axis=0)
+    first = jnp.broadcast_to(here() % 2, mine.shape) == 0
+    return jnp.where(first, mine, theirs), jnp.where(first, theirs, mine)
+
+
 def edge_windows(own, below, above, size, parts):
     width = 2 * STEPS
 
     def field(note, p, i):
         at = EDGE_AT + STRIDE * (4 * p + i)
         start = 0 if i % 2 else LANES - width
-        both = jnp.concatenate([note[:size, :], note[size + 8:, :]], axis=0)
+        both = jnp.concatenate([note[:size, :], note[size + 8:2 * size + 8, :]], axis=0)
         return pltpu.roll(both, (start - at) % LANES, 1)
 
     low, high = [], []
@@ -310,9 +317,9 @@
 def make_assess(pairs, parts, tiles, cells, share):
     size = padded(pairs)
 
-    def kernel(own, other, message, below, above, where, terms, local, *refs):
+    def kernel(own, other, message, mine, theirs, where, terms, local, *refs):
         outs, low_out, high_out, sums = refs[:pairs], refs[pairs], refs[pairs + 1], refs[pairs + 2]
-        low, high = edge_windows(message[...], below[...], above[...], size, parts)
+        low, high = edge_windows(message[...], *halves(mine[...], theirs[...]), size, parts)
         low_out[...] = low.astype(BF16)
         high_out[...] = high.astype(BF16)
         fixed = []
@@ -334,17 +341,17 @@
 def make_second(pairs, parts, tiles, cells):
     size = padded(pairs)
 
-    def kernel(keys, diff, pert, message, below, above, low, high, *refs):
+    def kernel(keys, diff, pert, message, mine, theirs, low, high, *refs):
         got, prior = refs[:pairs], refs[pairs]
+        below, above = [x[size:size + 8, :] for x in halves(mine[...], theirs[...])]
         arrived = jnp.concatenate([x[...] for x in got], axis=0)
         moved = pick_rows(keys[0], arrived)
-        at = size + 2
-        mine = message[at:at + 2 * parts, :].astype(I32)
-        codes = jnp.concatenate([mine[parts:], below[at:at + parts, :].astype(I32)], axis=0)
+        here_codes = message[size + 2:size + 2 + 2 * parts, :].astype(I32)
+        codes = jnp.concatenate([here_codes[parts:], below[2:2 + parts, :].astype(I32)], axis=0)
         start = pick_rows(codes, low[...])
-        codes = jnp.concatenate([mine[:parts], above[at + parts:at + 2 * parts, :].astype(I32)], axis=0)
+        codes = jnp.concatenate([here_codes[:parts], above[2 + parts:2 + 2 * parts, :].astype(I32)], axis=0)
         end = pick_rows(codes, high[...])
-        d = widen(diff[...], below[size:size + 1, :], above[size + 1:size + 2, :])
+        d = widen(diff[...], below[0:1, :], above[1:2, :])
         for p in range(parts):
             x = patch(moved[p * tiles:(p + 1) * tiles, :], start[p:p + 1, LANES:], end[p:p + 1, :LANES])
             q = parts + p
@@ -443,7 +450,11 @@
     def trade(x, k):
         return lax.ppermute(x, "member", [(i, i ^ k) for i in range(members)])
 
-    notes = notes[:1] + [trade(notes[k], 2 * k) for k in range(1, pairs)]
+    def exchange(sends):
+        got = {k: trade(sends[k], 2 * k) for k in range(pairs - 1, 0, -1)}
+        return [sends[0]] + [got[k] for k in range(1, pairs)]
+
+    notes = exchange(notes)
 
     where, terms, local = call(
         make_observe(blocks, per_block, tiles, near),
@@ -469,21 +480,24 @@
         [prior, other, trail, *notes],
         name="send_first",
     )
-    got = [sends[0]] + [trade(sends[k], 2 * k) for k in range(1, pairs)]
-    message = jnp.concatenate([half, trade(half, 1)[:size]], axis=0)
-    forward = [(i, i + 1) for i in range(regions - 1)]
-    below = lax.ppermute(message, "region", forward)
-    above = lax.ppermute(message, "region", [(j, i) for i, j in forward])
+    got = exchange(sends)
+    message = jnp.concatenate([half, trade(half, 1)], axis=0)
+    steps = []
+    for i in range(members):
+        first, last = (0, regions - 1) if i % 2 == 0 else (1, regions)
+        steps += [(i * regions + r, i * regions + r + 1 - 2 * (i % 2)) for r in range(first, last)]
+    mine = lax.ppermute(message, ("member", "region"), steps)
+    theirs = trade(mine, 1)
     window = ((parts * 2 * size, 2 * LANES), BF16)
     sums = [((tiles, cells), F32)]
     *kept, low, high = call(
         make_assess(pairs, parts, tiles, cells, share),
         [((rows, extra), BF16)] * pairs + [window, window],
-        [prior, other, message, below, above, where, terms, local],
+        [prior, other, message, mine, theirs, where, terms, local],
         scratch=sums,
         name="assess_first",
     )
-    args = [keys, diffusivity, model_perturbation, message, below, above, low, high, *got]
+    args = [keys, diffusivity, model_perturbation, message, mine, theirs, low, high, *got]
     specs = [whole_spec(a.shape) for a in args]
     specs[2] = noise_spec(1)
     (prior,) = call(
@@ -500,7 +514,7 @@
         scratch=sums,
         name="send_second",
     )
-    got = [sends[0]] + [trade(sends[k], 2 * k) for k in range(1, pairs)]
+    got = exchange(sends)
     return tuple(
         call(
             make_last(pairs, rows, parts, tiles, cells),

time: 39.2 us -> 38 us (0.969)
  starting transfers between devices: 17.8 us -> 15.7 us
  waiting for transfers between devices: 13.3 us -> 14.4 us
    ppermute x2 -> x1, starting transfers between devices: 5.97 us -> 3.6 us  [body(): mine = lax.ppermute(message, ('member', 'region'), steps)]
    ppermute x2 -> x1, waiting for transfers between devices: 0.53 us -> 1.43 us  [body(): mine = lax.ppermute(message, ('member', 'region'), steps)]
    ppermute x12 -> x13, waiting for transfers between devices: 12.8 us -> 13 us  [trade(): return lax.ppermute(x, 'member', [(i, i ^ k) for i in range(members)])]
    ppermute x12 -> x13, starting transfers between devices: 11.9 us -> 12.1 us  [trade(): return lax.ppermute(x, 'member', [(i, i ^ k) for i in range(members)])]
  transfers between devices with their start and end apart: 14 -> 14, of which waited for: 6 -> 7; matrix products, arithmetic and copies ran while one was open for 0% -> 0% of each run, Pallas kernels for 3% -> 3%
where the time goes in v5:
time: 38 us; the launch traced here: 37.8 us
  starting transfers between devices  15.7 us (41%)
  waiting for transfers between devices  14.4 us (38%)
  Pallas kernels  6.17 us (16%)
  between operations  0.85 us (2%)
  local copies, waits for them, and re-layouts  0.67 us (2%)
    ppermute x13, waiting for transfers between devices, trade(): return lax.ppermute(x, 'member', [(i, i ^ k) for i in range(members)])  13 us
    ppermute x13, starting transfers between devices, trade(): return lax.ppermute(x, 'member', [(i, i ^ k) for i in range(members)])  12.1 us
    pallas_call x8, Pallas kernels, call(): pl.pallas_call(kernel, out_shape=[jax.ShapeDtypeStruct(s, d) for s, d in...  6.17 us
    ppermute x1, starting transfers between devices, body(): mine = lax.ppermute(message, ('member', 'region'), steps)  3.6 us
    ppermute x1, waiting for transfers between devices, body(): mine = lax.ppermute(message, ('member', 'region'), steps)  1.43 us
  transfers between devices with their start and end apart: 14, of which 7 were waited for; matrix products, arithmetic and copies ran while one was open for 0% of the time, Pallas kernels for 3%

profile of v5, /device:TPU:0, one launch (start us, length us, event | category | flops | bytes accessed | tf_op | source)
XLA Modules:
  0.0 37.8 jit_solution(11433531071215127634)
XLA Ops:
  0.6 0.0 copy-start
  0.6 0.0 copy-start.1
  0.7 0.0 copy-start.2
  0.7 1.3 %prepare.1 = (f32[1,128]{1,0:T(1,128)S(1)}, f32[1,128]{1,0:T(1,128)S(1)}, f32[1,128]{1,0:T(1,128)S(1)}, f32[1,128]{1,0:T(1,128)S(1)}, f32[8,128]{1,0:T(8,128)S(1)}, /*index=5*/s32[2,32,128]{2,1,0:T(8,128)S(1)}) custom-call(bf16[2,16,4096]{2,1,0:T(8,128)(2,1)} %state.1, bf16[2,16,4096]{2,1,0:T(8,128)(2,1)} %state.1, f32[16,4096]{1,0:T(8,128)} %diff.3, ...), custom_call_target="tpu_custom_call" | custom-call | tf_op jit(solution)/shard_map/prepare/pallas_call | solution.py:28
  2.0 0.0 copy-done
  2.0 0.0 copy-done.1
  2.0 0.0 copy-done.2
  2.0 0.6 %forecast_first.1.own = bf16[32,4096]{1,0:T(8,128)(2,1)S(1)} custom-call(bf16[2,16,4096]{2,1,0:T(8,128)(2,1)S(1)} %copy-done.2, f32[16,4096]{1,0:T(8,128)S(1)} %copy-done.1, bf16[2,2,16,4096]{3,2,1,0:T(8,128)(2,1)S(1)} %copy-done, f32[8,128]{1,0:T(8,128)S(1)} %get-tuple-element.27.after.trail), custom_call_target="tpu_custom_call" | custom-call | tf_op jit(solution)/shard_map/forecast_first/pallas_call | solution.py:28
  2.6 0.5 %collective-permute-start = (bf16[32,4096]{1,0:T(8,128)(2,1)S(1)}, bf16[32,4096]{1,0:T(8,128)(2,1)S(1)}, u32[]{:S(2)}, u32[]{:S(2)}) collective-permute-start(bf16[32,4096]{1,0:T(8,128)(2,1)S(1)} %forecast_first.1.own), channel_id=1, source_target_pairs={{0,4},{4,0},{8,12},{12,8},{16,20},{20,16},{24,28},{28,24},{1,5},{5... | collective-permute-start | bytes 786440 | tf_op jit(solution)/shard_map/ppermute | solution.py:451
  3.1 2.6 %collective-permute-start.1 = (f32[1,128]{1,0:T(1,128)S(1)}, f32[1,128]{1,0:T(1,128)S(1)}, u32[]{:S(2)}, u32[]{:S(2)}) collective-permute-start(f32[1,128]{1,0:T(1,128)S(1)} %get-tuple-element.29), channel_id=1, source_target_pairs={{0,8},{4,12},{8,0},{12,4},{16,24},{20,28},{24,16},{28,20},{1,9},{5... | collective-permute-start | bytes 1544 | tf_op jit(solution)/shard_map/ppermute | solution.py:451
  5.7 1.5 %collective-permute-start.2 = (f32[1,128]{1,0:T(1,128)S(1)}, f32[1,128]{1,0:T(1,128)S(1)}, u32[]{:S(2)}, u32[]{:S(2)}) collective-permute-start(f32[1,128]{1,0:T(1,128)S(1)} %get-tuple-element.30), channel_id=1, source_target_pairs={{0,16},{4,20},{8,24},{12,28},{16,0},{20,4},{24,8},{28,12},{1,17},{... | collective-permute-start | bytes 1544 | tf_op jit(solution)/shard_map/ppermute | solution.py:451
  7.2 0.0 collective-permute-start.3
  7.3 0.0 collective-permute-done.1.refs_1_
  7.3 2.0 %collective-permute-done.2.refs_2_ = f32[1,128]{1,0:T(1,128)S(1)} collective-permute-done((f32[1,128]{1,0:T(1,128)S(1)}, f32[1,128]{1,0:T(1,128)S(1)}, u32[]{:S(2)}, u32[]{:S(2)}) %collective-permute-start.2) | collective-permute-done | bytes 544 | tf_op jit(solution)/shard_map/ppermute | solution.py:451
  9.3 2.4 %collective-permute-done.3.refs_3_ = f32[1,128]{1,0:T(1,128)S(1)} collective-permute-done((f32[1,128]{1,0:T(1,128)S(1)}, f32[1,128]{1,0:T(1,128)S(1)}, u32[]{:S(2)}, u32[]{:S(2)}) %collective-permute-start.3) | collective-permute-done | bytes 544 | tf_op jit(solution)/shard_map/ppermute | solution.py:451
  11.7 0.0 collective-permute-done.other
  11.7 0.4 send_first.1
  12.0 0.0 copy-start.6
  12.1 0.0 copy-start.7
  12.1 0.1 collective-permute-start.4
  12.2 0.0 copy-start.3
  12.2 0.6 %collective-permute-start.7 = (bf16[16,4096]{1,0:T(8,128)(2,1)S(1)}, bf16[16,4096]{1,0:T(8,128)(2,1)S(1)}, u32[]{:S(2)}, u32[]{:S(2)}) collective-permute-start(bf16[16,4096]{1,0:T(8,128)(2,1)S(1)} %get-tuple-element.39), channel_id=1, source_target_pairs={{0,8},{4,12},{8,0},{12,4},{16,24},{20,28},{24,16},{28,20},{1,9},{5... | collective-permute-start | bytes 393224 | tf_op jit(solution)/shard_map/ppermute | solution.py:451
  12.8 0.1 collective-permute-start.8
  12.8 2.9 %collective-permute-start.9 = (bf16[16,4096]{1,0:T(8,128)(2,1)S(1)}, bf16[16,4096]{1,0:T(8,128)(2,1)S(1)}, u32[]{:S(2)}, u32[]{:S(2)}) collective-permute-start(bf16[16,4096]{1,0:T(8,128)(2,1)S(1)} %get-tuple-element.41), channel_id=1, source_target_pairs={{0,24},{4,28},{8,16},{12,20},{16,8},{20,12},{24,0},{28,4},{1,25},{... | collective-permute-start | bytes 393224 | tf_op jit(solution)/shard_map/ppermute | solution.py:451
  15.7 0.0 collective-permute-done.4
  15.7 3.6 %collective-permute-start.5 = (f32[32,128]{1,0:T(8,128)S(1)}, f32[32,128]{1,0:T(8,128)S(1)}, u32[]{:S(2)}, u32[]{:S(2)}) collective-permute-start(f32[32,128]{1,0:T(8,128)S(1)} %constant_dynamic-update-slice_fusion.message), channel_id=1, source_target_pairs={{0,1},{1,2},{2,3},{5,4},{6,5},{7,6},{8,9},{9,10},{10,11},{13,12},{... | collective-permute-start | bytes 49160 | tf_op jit(solution)/shard_map/ppermute | solution.py:489
  19.3 1.4 %collective-permute-done.5.mine = f32[32,128]{1,0:T(8,128)S(1)} collective-permute-done((f32[32,128]{1,0:T(8,128)S(1)}, f32[32,128]{1,0:T(8,128)S(1)}, u32[]{:S(2)}, u32[]{:S(2)}) %collective-permute-start.5) | collective-permute-done | bytes 16416 | tf_op jit(solution)/shard_map/ppermute | solution.py:489
  20.8 0.0 collective-permute-start.6
  20.8 0.0 copy-done.5
  20.8 0.0 copy-done.6
  20.8 0.6 %copy-done.8 = s32[32]{0:T(128)S(1)} copy-done((s32[32]{0:T(128)S(1)}, s32[32]{0:T(128)}, u32[]{:S(2)}) %copy-start.8) | copy-done | bytes 152
  21.4 0.2 observe.1
  21.6 0.3 collective-permute-done.6.theirs
  22.0 1.0 %assess_first.1 = (bf16[16,640]{1,0:T(8,128)(2,1)S(1)}, bf16[16,640]{1,0:T(8,128)(2,1)S(1)}, bf16[16,640]{1,0:T(8,128)(2,1)S(1)}, bf16[16,640]{1,0:T(8,128)(2,1)...) custom-call(bf16[32,4096]{1,0:T(8,128)(2,1)S(1)} %forecast_first.1.own, ...), custom_call_target="tpu_custom_call" | custom-call | tf_op jit(solution)/shard_map/assess_first/pallas_call | solution.py:28
  23.0 0.0 collective-permute-done.7.refs_1_
  23.0 0.0 collective-permute-done.8.refs_2_
  23.0 0.0 collective-permute-done.9.refs_3_
  23.0 0.8 %forecast_second.1.own = bf16[32,4096]{1,0:T(8,128)(2,1)S(1)} custom-call(s32[2,32,128]{2,1,0:T(8,128)S(1)} %get-tuple-element.26.keys, f32[16,4096]{1,0:T(8,128)S(1)} %copy-done.1, bf16[2,2,16,4096]{3,2,1,0:T(8,128)(2,1)S(1)} %copy-done, f32[32,128]{1,0:T(8,128)S(1)} %constant_dynamic-update-slice_fusion.message, ...), custom_call_target="tpu_custom_call" | custom-call | tf_op jit(solution)/shard_map/forecast_second/pallas_call | solution.py:28
  23.8 0.3 collective-permute-start.10
  24.1 1.3 %collective-permute-done.10.other = bf16[32,4096]{1,0:T(8,128)(2,1)S(1)} collective-permute-done((bf16[32,4096]{1,0:T(8,128)(2,1)S(1)}, bf16[32,4096]{1,0:T(8,128)(2,1)S(1)}, u32[]{:S(2)}, u32[]{:S(2)}) %collective-permute-start.10) | collective-permute-done | bytes 262176 | tf_op jit(solution)/shard_map/ppermute | solution.py:451
  25.5 0.9 %send_second.1 = (bf16[16,5376]{1,0:T(8,128)(2,1)S(1)}, bf16[16,5376]{1,0:T(8,128)(2,1)S(1)}, bf16[16,5376]{1,0:T(8,128)(2,1)S(1)}, bf16[16,5376]{1,0:T(8,128)(2,1)S(1)}) custom-call(bf16[32,4096]{1,0:T(8,128)(2,1)S(1)} %forecast_second.1.own, bf16[32,4096]{1,0:T(8,128)(2,1)S(1)} %collective-permute-done.10.other, s32[2,512]{1,0:T(2,128)S(1)} %get-tuple-element.33.where, ...), custom_call_target="tpu_custom_call" | custom-call | tf_op jit(solution)/shard_map/send_second/pallas_call | solution.py:28
  26.4 0.6 %collective-permute-start.11 = (bf16[16,5376]{1,0:T(8,128)(2,1)S(1)}, bf16[16,5376]{1,0:T(8,128)(2,1)S(1)}, u32[]{:S(2)}, u32[]{:S(2)}) collective-permute-start(bf16[16,5376]{1,0:T(8,128)(2,1)S(1)} %get-tuple-element.47), channel_id=1, source_target_pairs={{0,8},{4,12},{8,0},{12,4},{16,24},{20,28},{24,16},{28,20},{1,9},{5... | collective-permute-start | bytes 516104 | tf_op jit(solution)/shard_map/ppermute | solution.py:451
  27.0 0.5 %collective-permute-start.12 = (bf16[16,5376]{1,0:T(8,128)(2,1)S(1)}, bf16[16,5376]{1,0:T(8,128)(2,1)S(1)}, u32[]{:S(2)}, u32[]{:S(2)}) collective-permute-start(bf16[16,5376]{1,0:T(8,128)(2,1)S(1)} %get-tuple-element.48), channel_id=1, source_target_pairs={{0,16},{4,20},{8,24},{12,28},{16,0},{20,4},{24,8},{28,12},{1,17},{... | collective-permute-start | bytes 516104 | tf_op jit(solution)/shard_map/ppermute | solution.py:451
  27.5 2.5 %collective-permute-start.13 = (bf16[16,5376]{1,0:T(8,128)(2,1)S(1)}, bf16[16,5376]{1,0:T(8,128)(2,1)S(1)}, u32[]{:S(2)}, u32[]{:S(2)}) collective-permute-start(bf16[16,5376]{1,0:T(8,128)(2,1)S(1)} %get-tuple-element.49), channel_id=1, source_target_pairs={{0,24},{4,28},{8,16},{12,20},{16,8},{20,12},{24,0},{28,4},{1,25},{... | collective-permute-start | bytes 516104 | tf_op jit(solution)/shard_map/ppermute | solution.py:451
  29.9 3.7 %collective-permute-done.11.refs_1_ = bf16[16,5376]{1,0:T(8,128)(2,1)S(1)} collective-permute-done((bf16[16,5376]{1,0:T(8,128)(2,1)S(1)}, bf16[16,5376]{1,0:T(8,128)(2,1)S(1)}, u32[]{:S(2)}, u32[]{:S(2)}) %collective-permute-start.11) | collective-permute-done | bytes 172064 | tf_op jit(solution)/shard_map/ppermute | solution.py:451
  33.7 3.2 %collective-permute-done.12.refs_2_ = bf16[16,5376]{1,0:T(8,128)(2,1)S(1)} collective-permute-done((bf16[16,5376]{1,0:T(8,128)(2,1)S(1)}, bf16[16,5376]{1,0:T(8,128)(2,1)S(1)}, u32[]{:S(2)}, u32[]{:S(2)}) %collective-permute-start.12) | collective-permute-done | bytes 172064 | tf_op jit(solution)/shard_map/ppermute | solution.py:451
  36.8 0.0 collective-permute-done.13.refs_3_
  36.8 0.9 %finish.1 = (bf16[2,16,4096]{2,1,0:T(8,128)(2,1)}, f32[2,16,512]{2,1,0:T(8,128)}) custom-call(s32[2,32,128]{2,1,0:T(8,128)S(1)} %get-tuple-element.26.keys, bf16[16,5376]{1,0:T(8,128)(2,1)S(1)} %get-tuple-element.46.refs_0_, bf16[16,5376]{1,0:T(8,128)(2,1)S(1)} %collective-permute-done.11.refs_1_, bf16[16,5376]{1,0:T(8,128)(2,1)S(1)} %collective-permute-done.12.refs_2_, ...), custom_call_target="tpu_custom_call" | custom-call | tf_op jit(solution)/shard_map/finish/pallas_call | solution.py:28
  (8 shorter events, 0.0 us)
Async XLA Ops:
  0.6 1.3 %copy-start = (bf16[2,2,16,4096]{3,2,1,0:T(8,128)(2,1)S(1)}, bf16[2,2,16,4096]{3,2,1,0:T(8,128)(2,1)}, u32[]{:S(2)}) copy-start(bf16[2,2,16,4096]{3,2,1,0:T(8,128)(2,1)} %pert.3) | copy-start | bytes 1572868
  0.6 1.4 %copy-start.1 = (f32[16,4096]{1,0:T(8,128)S(1)}, f32[16,4096]{1,0:T(8,128)}, u32[]{:S(2)}) copy-start(f32[16,4096]{1,0:T(8,128)} %diff.3) | copy-start | bytes 786436
  0.7 1.4 %copy-start.2 = (bf16[2,16,4096]{2,1,0:T(8,128)(2,1)S(1)}, bf16[2,16,4096]{2,1,0:T(8,128)(2,1)}, u32[]{:S(2)}) copy-start(bf16[2,16,4096]{2,1,0:T(8,128)(2,1)} %state.1) | copy-start | bytes 786436
  2.6 9.0 %collective-permute-start = (bf16[32,4096]{1,0:T(8,128)(2,1)S(1)}, bf16[32,4096]{1,0:T(8,128)(2,1)S(1)}, u32[]{:S(2)}, u32[]{:S(2)}) collective-permute-start(bf16[32,4096]{1,0:T(8,128)(2,1)S(1)} %forecast_first.1.own), channel_id=1, source_target_pairs={{0,4},{4,0},{8,12},{12,8},{16,20},{20,16},{24,28},{28,24},{1,5},{5... | collective-permute-start | bytes 786440 | tf_op jit(solution)/shard_map/ppermute | solution.py:451
  3.1 4.1 %collective-permute-start.1 = (f32[1,128]{1,0:T(1,128)S(1)}, f32[1,128]{1,0:T(1,128)S(1)}, u32[]{:S(2)}, u32[]{:S(2)}) collective-permute-start(f32[1,128]{1,0:T(1,128)S(1)} %get-tuple-element.29), channel_id=1, source_target_pairs={{0,8},{4,12},{8,0},{12,4},{16,24},{20,28},{24,16},{28,20},{1,9},{5... | collective-permute-start | bytes 1544 | tf_op jit(solution)/shard_map/ppermute | solution.py:451
  5.7 3.5 %collective-permute-start.2 = (f32[1,128]{1,0:T(1,128)S(1)}, f32[1,128]{1,0:T(1,128)S(1)}, u32[]{:S(2)}, u32[]{:S(2)}) collective-permute-start(f32[1,128]{1,0:T(1,128)S(1)} %get-tuple-element.30), channel_id=1, source_target_pairs={{0,16},{4,20},{8,24},{12,28},{16,0},{20,4},{24,8},{28,12},{1,17},{... | collective-permute-start | bytes 1544 | tf_op jit(solution)/shard_map/ppermute | solution.py:451
  7.2 4.4 %collective-permute-start.3 = (f32[1,128]{1,0:T(1,128)S(1)}, f32[1,128]{1,0:T(1,128)S(1)}, u32[]{:S(2)}, u32[]{:S(2)}) collective-permute-start(f32[1,128]{1,0:T(1,128)S(1)} %get-tuple-element.31), channel_id=1, source_target_pairs={{0,24},{4,28},{8,16},{12,20},{16,8},{20,12},{24,0},{28,4},{1,25},{... | collective-permute-start | bytes 1544 | tf_op jit(solution)/shard_map/ppermute | solution.py:451
  11.7 9.1 %copy-start.5 = (f32[32,16]{0,1:T(8,128)S(1)}, f32[32,16]{0,1:T(8,128)}, u32[]{:S(2)}) copy-start(f32[32,16]{0,1:T(8,128)} %param.15) | copy-start | bytes 6148
  12.0 8.7 %copy-start.6 = (s32[16,6]{0,1:T(8,128)S(1)}, s32[16,6]{0,1:T(8,128)}, u32[]{:S(2)}) copy-start(s32[16,6]{0,1:T(8,128)} %param.18) | copy-start | bytes 1156
  12.1 8.7 %copy-start.7 = (f32[16,6]{0,1:T(8,128)S(1)}, f32[16,6]{0,1:T(8,128)}, u32[]{:S(2)}) copy-start(f32[16,6]{0,1:T(8,128)} %param.19) | copy-start | bytes 1156
  12.1 3.7 %collective-permute-start.4 = (f32[16,128]{1,0:T(8,128)S(1)}, f32[16,128]{1,0:T(8,128)S(1)}, u32[]{:S(2)}, u32[]{:S(2)}) collective-permute-start(f32[16,128]{1,0:T(8,128)S(1)} %get-tuple-element.32), channel_id=1, source_target_pairs={{0,4},{4,0},{8,12},{12,8},{16,20},{20,16},{24,28},{28,24},{1,5},{5... | collective-permute-start | bytes 24584 | tf_op jit(solution)/shard_map/ppermute | solution.py:451
  12.2 8.6 %copy-start.3 = (f32[2,32,16]{1,2,0:T(8,128)S(1)}, f32[2,32,16]{1,2,0:T(8,128)}, u32[]{:S(2)}) copy-start(f32[2,32,16]{1,2,0:T(8,128)} %param.14) | copy-start | bytes 12292
  12.2 10.8 %collective-permute-start.7 = (bf16[16,4096]{1,0:T(8,128)(2,1)S(1)}, bf16[16,4096]{1,0:T(8,128)(2,1)S(1)}, u32[]{:S(2)}, u32[]{:S(2)}) collective-permute-start(bf16[16,4096]{1,0:T(8,128)(2,1)S(1)} %get-tuple-element.39), channel_id=1, source_target_pairs={{0,8},{4,12},{8,0},{12,4},{16,24},{20,28},{24,16},{28,20},{1,9},{5... | collective-permute-start | bytes 393224 | tf_op jit(solution)/shard_map/ppermute | solution.py:451
  12.8 10.2 %collective-permute-start.8 = (bf16[16,4096]{1,0:T(8,128)(2,1)S(1)}, bf16[16,4096]{1,0:T(8,128)(2,1)S(1)}, u32[]{:S(2)}, u32[]{:S(2)}) collective-permute-start(bf16[16,4096]{1,0:T(8,128)(2,1)S(1)} %get-tuple-element.40), channel_id=1, source_target_pairs={{0,16},{4,20},{8,24},{12,28},{16,0},{20,4},{24,8},{28,12},{1,17},{... | collective-permute-start | bytes 393224 | tf_op jit(solution)/shard_map/ppermute | solution.py:451
  12.8 10.2 %collective-permute-start.9 = (bf16[16,4096]{1,0:T(8,128)(2,1)S(1)}, bf16[16,4096]{1,0:T(8,128)(2,1)S(1)}, u32[]{:S(2)}, u32[]{:S(2)}) collective-permute-start(bf16[16,4096]{1,0:T(8,128)(2,1)S(1)} %get-tuple-element.41), channel_id=1, source_target_pairs={{0,24},{4,28},{8,16},{12,20},{16,8},{20,12},{24,0},{28,4},{1,25},{... | collective-permute-start | bytes 393224 | tf_op jit(solution)/shard_map/ppermute | solution.py:451
  15.7 5.1 %copy-start.4 = (s32[32,16]{0,1:T(8,128)S(1)}, s32[32,16]{0,1:T(8,128)}, u32[]{:S(2)}) copy-start(s32[32,16]{0,1:T(8,128)} %param.17) | copy-start | bytes 6148
  15.7 5.0 %collective-permute-start.5 = (f32[32,128]{1,0:T(8,128)S(1)}, f32[32,128]{1,0:T(8,128)S(1)}, u32[]{:S(2)}, u32[]{:S(2)}) collective-permute-start(f32[32,128]{1,0:T(8,128)S(1)} %constant_dynamic-update-slice_fusion.message), channel_id=1, source_target_pairs={{0,1},{1,2},{2,3},{5,4},{6,5},{7,6},{8,9},{9,10},{10,11},{13,12},{... | collective-permute-start | bytes 49160 | tf_op jit(solution)/shard_map/ppermute | solution.py:489
  20.8 1.2 %collective-permute-start.6 = (f32[32,128]{1,0:T(8,128)S(1)}, f32[32,128]{1,0:T(8,128)S(1)}, u32[]{:S(2)}, u32[]{:S(2)}) collective-permute-start(f32[32,128]{1,0:T(8,128)S(1)} %collective-permute-done.5.mine), channel_id=1, source_target_pairs={{0,4},{4,0},{8,12},{12,8},{16,20},{20,16},{24,28},{28,24},{1,5},{5... | collective-permute-start | bytes 49160 | tf_op jit(solution)/shard_map/ppermute | solution.py:451
  20.8 0.7 %copy-start.8 = (s32[32]{0:T(128)S(1)}, s32[32]{0:T(128)}, u32[]{:S(2)}) copy-start(s32[32]{0:T(128)} %param.16) | copy-start | bytes 388
  23.8 1.6 %collective-permute-start.10 = (bf16[32,4096]{1,0:T(8,128)(2,1)S(1)}, bf16[32,4096]{1,0:T(8,128)(2,1)S(1)}, u32[]{:S(2)}, u32[]{:S(2)}) collective-permute-start(bf16[32,4096]{1,0:T(8,128)(2,1)S(1)} %forecast_second.1.own), channel_id=1, source_target_pairs={{0,4},{4,0},{8,12},{12,8},{16,20},{20,16},{24,28},{28,24},{1,5},{5... | collective-permute-start | bytes 786440 | tf_op jit(solution)/shard_map/ppermute | solution.py:451
  26.4 7.3 %collective-permute-start.11 = (bf16[16,5376]{1,0:T(8,128)(2,1)S(1)}, bf16[16,5376]{1,0:T(8,128)(2,1)S(1)}, u32[]{:S(2)}, u32[]{:S(2)}) collective-permute-start(bf16[16,5376]{1,0:T(8,128)(2,1)S(1)} %get-tuple-element.47), channel_id=1, source_target_pairs={{0,8},{4,12},{8,0},{12,4},{16,24},{20,28},{24,16},{28,20},{1,9},{5... | collective-permute-start | bytes 516104 | tf_op jit(solution)/shard_map/ppermute | solution.py:451
  27.0 9.9 %collective-permute-start.12 = (bf16[16,5376]{1,0:T(8,128)(2,1)S(1)}, bf16[16,5376]{1,0:T(8,128)(2,1)S(1)}, u32[]{:S(2)}, u32[]{:S(2)}) collective-permute-start(bf16[16,5376]{1,0:T(8,128)(2,1)S(1)} %get-tuple-element.48), channel_id=1, source_target_pairs={{0,16},{4,20},{8,24},{12,28},{16,0},{20,4},{24,8},{28,12},{1,17},{... | collective-permute-start | bytes 516104 | tf_op jit(solution)/shard_map/ppermute | solution.py:451
  27.5 9.4 %collective-permute-start.13 = (bf16[16,5376]{1,0:T(8,128)(2,1)S(1)}, bf16[16,5376]{1,0:T(8,128)(2,1)S(1)}, u32[]{:S(2)}, u32[]{:S(2)}) collective-permute-start(bf16[16,5376]{1,0:T(8,128)(2,1)S(1)} %get-tuple-element.49), channel_id=1, source_target_pairs={{0,24},{4,28},{8,16},{12,20},{16,8},{20,12},{24,0},{28,4},{1,25},{... | collective-permute-start | bytes 516104 | tf_op jit(solution)/shard_map/ppermute | solution.py:451

commit v6 on v5

--- a/solution.py
+++ b/solution.py
@@ -51,6 +51,10 @@
 STRIDE = 8
 
 
+def apart(i, pairs):
+    return (pairs - i) % pairs
+
+
 def padded(pairs):
     return max(8, pairs)
 
@@ -72,7 +76,7 @@
         for p in range(parts):
             for i, t in enumerate((last, 0)):
                 source = am[0, p:p + 1, t:t + 1] ^ m
-                code = (slot[0, p:p + 1, t:t + 1] * 2 + source % 2) * padded(pairs) + source // 2
+                code = (slot[0, p:p + 1, t:t + 1] * 2 + source % 2) * padded(pairs) + apart(source // 2, pairs)
                 row = 2 + i * parts + p
                 trail[row:row + 1, :] = jnp.broadcast_to(code.astype(F32), (1, LANES))
             fields = (st1[p, last:last + 1, :], st0[p, 0:1, :], pb1[0, p, last:last + 1, :], pb0[0, p, 0:1, :])
@@ -94,9 +98,9 @@
                 half = source % 2
                 code = half * rows + slot[c, p:p + 1, :] * tiles + iota((1, tiles), 1)
                 spot = (iota((LANES, tiles), 0) == (2 * c + half) * capacity + rank).astype(F32)
-                pair = jnp.where(iota((pairs, tiles), 0) == source // 2, (code + 1).astype(F32), 0.0)
+                pair = jnp.where(iota((pairs, tiles), 0) == apart(source // 2, pairs), (code + 1).astype(F32), 0.0)
                 asked = asked + lax.dot_general(pair, spot, (((1,), (1,)), ((), ())), preferred_element_type=F32)
-                column = column_of(source * capacity + rank)
+                column = column_of((2 * apart(source // 2, pairs) + half) * capacity + rank)
                 keys[c, p * tiles:(p + 1) * tiles, :] = jnp.broadcast_to(column, (tiles, LANES))
         for k in range(pairs):
             notes[k][...] = jnp.where(lane < EDGE_AT, asked[k:k + 1, :] - 1.0, edge)
@@ -253,7 +257,7 @@
                 spot += 1
     end = at + groups * share
     for k, out in enumerate(outs):
-        block = share_of(sums, m ^ (2 * k), share)
+        block = share_of(sums, m ^ (2 * apart(k, len(outs))), share)
         for g in range(groups):
             out[:, at + g * share:at + (g + 1) * share] = block[g * rows:(g + 1) * rows, :].astype(BF16)
         out[:, end:end + LANES] = misc.astype(BF16)
@@ -317,11 +321,8 @@
 def make_assess(pairs, parts, tiles, cells, share):
     size = padded(pairs)
 
-    def kernel(own, other, message, mine, theirs, where, terms, local, *refs):
-        outs, low_out, high_out, sums = refs[:pairs], refs[pairs], refs[pairs + 1], refs[pairs + 2]
-        low, high = edge_windows(message[...], *halves(mine[...], theirs[...]), size, parts)
-        low_out[...] = low.astype(BF16)
-        high_out[...] = high.astype(BF16)
+    def kernel(own, other, low, high, where, terms, local, *refs):
+        outs, sums = refs[:pairs], refs[pairs]
         fixed = []
         for h, prior in enumerate((own, other)):
             for p in range(parts):
@@ -341,16 +342,20 @@
 def make_second(pairs, parts, tiles, cells):
     size = padded(pairs)
 
-    def kernel(keys, diff, pert, message, mine, theirs, low, high, *refs):
-        got, prior = refs[:pairs], refs[pairs]
-        below, above = [x[size:size + 8, :] for x in halves(mine[...], theirs[...])]
+    def kernel(keys, diff, pert, message, mine, theirs, *refs):
+        got, prior, low_out, high_out = refs[:pairs], refs[pairs], refs[pairs + 1], refs[pairs + 2]
+        below, above = halves(mine[...], theirs[...])
+        low, high = edge_windows(message[...], below, above, size, parts)
+        low_out[...] = low
+        high_out[...] = high
+        below, above = below[size:size + 8, :], above[size:size + 8, :]
         arrived = jnp.concatenate([x[...] for x in got], axis=0)
         moved = pick_rows(keys[0], arrived)
         here_codes = message[size + 2:size + 2 + 2 * parts, :].astype(I32)
         codes = jnp.concatenate([here_codes[parts:], below[2:2 + parts, :].astype(I32)], axis=0)
-        start = pick_rows(codes, low[...])
+        start = pick_rows(codes, low.astype(BF16))
         codes = jnp.concatenate([here_codes[:parts], above[2 + parts:2 + 2 * parts, :].astype(I32)], axis=0)
-        end = pick_rows(codes, high[...])
+        end = pick_rows(codes, high.astype(BF16))
         d = widen(diff[...], below[0:1, :], above[1:2, :])
         for p in range(parts):
             x = patch(moved[p * tiles:(p + 1) * tiles, :], start[p:p + 1, LANES:], end[p:p + 1, :LANES])
@@ -451,8 +456,7 @@
         return lax.ppermute(x, "member", [(i, i ^ k) for i in range(members)])
 
     def exchange(sends):
-        got = {k: trade(sends[k], 2 * k) for k in range(pairs - 1, 0, -1)}
-        return [sends[0]] + [got[k] for k in range(1, pairs)]
+        return [sends[0]] + [trade(sends[k], 2 * apart(k, pairs)) for k in range(1, pairs)]
 
     notes = exchange(notes)
 
@@ -488,29 +492,29 @@
         steps += [(i * regions + r, i * regions + r + 1 - 2 * (i % 2)) for r in range(first, last)]
     mine = lax.ppermute(message, ("member", "region"), steps)
     theirs = trade(mine, 1)
-    window = ((parts * 2 * size, 2 * LANES), BF16)
+    window = ((parts * 2 * size, 2 * LANES), F32)
     sums = [((tiles, cells), F32)]
-    *kept, low, high = call(
-        make_assess(pairs, parts, tiles, cells, share),
-        [((rows, extra), BF16)] * pairs + [window, window],
-        [prior, other, message, mine, theirs, where, terms, local],
-        scratch=sums,
-        name="assess_first",
-    )
-    args = [keys, diffusivity, model_perturbation, message, mine, theirs, low, high, *got]
+    args = [keys, diffusivity, model_perturbation, message, mine, theirs, *got]
     specs = [whole_spec(a.shape) for a in args]
     specs[2] = noise_spec(1)
-    (prior,) = call(
+    second, low, high = call(
         make_second(pairs, parts, tiles, cells),
-        [((parts * tiles, cells), BF16)],
+        [((parts * tiles, cells), BF16), window, window],
         args,
         specs,
         name="forecast_second",
     )
+    kept = call(
+        make_assess(pairs, parts, tiles, cells, share),
+        [((rows, extra), BF16)] * pairs,
+        [prior, other, low, high, where, terms, local],
+        scratch=sums,
+        name="assess_first",
+    )
     sends = call(
         make_send_second(pairs, rows, parts, tiles, cells, share),
         [((rows, cells + CYCLES * extra), BF16)] * pairs,
-        [prior, trade(prior, 1), where, terms, local, *notes, *kept],
+        [second, trade(second, 1), where, terms, local, *notes, *kept],
         scratch=sums,
         name="send_second",
     )

time: 38 us -> 37 us (0.974)
  waiting for transfers between devices: 14.4 us -> 13.9 us
    ppermute x13, waiting for transfers between devices: 13 us -> 12.5 us  [trade(): return lax.ppermute(x, 'member', [(i, i ^ k) for i in range(members)])]
  transfers between devices with their start and end apart: 14 -> 14, of which waited for: 7 -> 8; matrix products, arithmetic and copies ran while one was open for 0% -> 0% of each run, Pallas kernels for 3% -> 2%
where the time goes in v6:
time: 37 us; the launch traced here: 36.8 us
  starting transfers between devices  15.6 us (42%)
  waiting for transfers between devices  13.9 us (38%)
  Pallas kernels  5.83 us (16%)
  between operations  0.8 us (2%)
  local copies, waits for them, and re-layouts  0.71 us (2%)
    ppermute x13, waiting for transfers between devices, trade(): return lax.ppermute(x, 'member', [(i, i ^ k) for i in range(members)])  12.5 us
    ppermute x13, starting transfers between devices, trade(): return lax.ppermute(x, 'member', [(i, i ^ k) for i in range(members)])  12.1 us
    pallas_call x8, Pallas kernels, call(): pl.pallas_call(kernel, out_shape=[jax.ShapeDtypeStruct(s, d) for s, d in...  5.83 us
    ppermute x1, starting transfers between devices, body(): mine = lax.ppermute(message, ('member', 'region'), steps)  3.48 us
    ppermute x1, waiting for transfers between devices, body(): mine = lax.ppermute(message, ('member', 'region'), steps)  1.43 us
  transfers between devices with their start and end apart: 14, of which 8 were waited for; matrix products, arithmetic and copies ran while one was open for 0% of the time, Pallas kernels for 2%

profile of v6, /device:TPU:0, one launch (start us, length us, event | category | flops | bytes accessed | tf_op | source)
XLA Modules:
  0.0 36.8 jit_solution(10545664951422825107)
XLA Ops:
  0.6 0.0 copy-start
  0.6 0.0 copy-start.1
  0.7 0.0 copy-start.2
  0.7 1.3 %prepare.1 = (f32[1,128]{1,0:T(1,128)S(1)}, f32[1,128]{1,0:T(1,128)S(1)}, f32[1,128]{1,0:T(1,128)S(1)}, f32[1,128]{1,0:T(1,128)S(1)}, f32[8,128]{1,0:T(8,128)S(1)}, /*index=5*/s32[2,32,128]{2,1,0:T(8,128)S(1)}) custom-call(bf16[2,16,4096]{2,1,0:T(8,128)(2,1)} %state.1, bf16[2,16,4096]{2,1,0:T(8,128)(2,1)} %state.1, f32[16,4096]{1,0:T(8,128)} %diff.3, ...), custom_call_target="tpu_custom_call" | custom-call | tf_op jit(solution)/shard_map/prepare/pallas_call | solution.py:28
  2.0 0.0 copy-done
  2.0 0.0 copy-done.1
  2.0 0.0 copy-done.2
  2.0 0.6 %forecast_first.1.own = bf16[32,4096]{1,0:T(8,128)(2,1)S(1)} custom-call(bf16[2,16,4096]{2,1,0:T(8,128)(2,1)S(1)} %copy-done.2, f32[16,4096]{1,0:T(8,128)S(1)} %copy-done.1, bf16[2,2,16,4096]{3,2,1,0:T(8,128)(2,1)S(1)} %copy-done, f32[8,128]{1,0:T(8,128)S(1)} %get-tuple-element.28.after.trail), custom_call_target="tpu_custom_call" | custom-call | tf_op jit(solution)/shard_map/forecast_first/pallas_call | solution.py:28
  2.6 0.5 %collective-permute-start = (bf16[32,4096]{1,0:T(8,128)(2,1)S(1)}, bf16[32,4096]{1,0:T(8,128)(2,1)S(1)}, u32[]{:S(2)}, u32[]{:S(2)}) collective-permute-start(bf16[32,4096]{1,0:T(8,128)(2,1)S(1)} %forecast_first.1.own), channel_id=1, source_target_pairs={{0,4},{4,0},{8,12},{12,8},{16,20},{20,16},{24,28},{28,24},{1,5},{5... | collective-permute-start | bytes 786440 | tf_op jit(solution)/shard_map/ppermute | solution.py:456
  3.1 3.5 %collective-permute-start.1 = (f32[1,128]{1,0:T(1,128)S(1)}, f32[1,128]{1,0:T(1,128)S(1)}, u32[]{:S(2)}, u32[]{:S(2)}) collective-permute-start(f32[1,128]{1,0:T(1,128)S(1)} %get-tuple-element.30), channel_id=1, source_target_pairs={{0,24},{4,28},{8,16},{12,20},{16,8},{20,12},{24,0},{28,4},{1,25},{... | collective-permute-start | bytes 1544 | tf_op jit(solution)/shard_map/ppermute | solution.py:456
  6.7 0.5 %collective-permute-start.2 = (f32[1,128]{1,0:T(1,128)S(1)}, f32[1,128]{1,0:T(1,128)S(1)}, u32[]{:S(2)}, u32[]{:S(2)}) collective-permute-start(f32[1,128]{1,0:T(1,128)S(1)} %get-tuple-element.31), channel_id=1, source_target_pairs={{0,16},{4,20},{8,24},{12,28},{16,0},{20,4},{24,8},{28,12},{1,17},{... | collective-permute-start | bytes 1544 | tf_op jit(solution)/shard_map/ppermute | solution.py:456
  7.2 0.1 collective-permute-start.3
  7.3 0.9 %collective-permute-done.1.refs_1_ = f32[1,128]{1,0:T(1,128)S(1)} collective-permute-done((f32[1,128]{1,0:T(1,128)S(1)}, f32[1,128]{1,0:T(1,128)S(1)}, u32[]{:S(2)}, u32[]{:S(2)}) %collective-permute-start.1) | collective-permute-done | bytes 544 | tf_op jit(solution)/shard_map/ppermute | solution.py:456
  8.2 2.0 %collective-permute-done.2.refs_2_ = f32[1,128]{1,0:T(1,128)S(1)} collective-permute-done((f32[1,128]{1,0:T(1,128)S(1)}, f32[1,128]{1,0:T(1,128)S(1)}, u32[]{:S(2)}, u32[]{:S(2)}) %collective-permute-start.2) | collective-permute-done | bytes 544 | tf_op jit(solution)/shard_map/ppermute | solution.py:456
  10.2 0.5 %collective-permute-done.3.refs_3_ = f32[1,128]{1,0:T(1,128)S(1)} collective-permute-done((f32[1,128]{1,0:T(1,128)S(1)}, f32[1,128]{1,0:T(1,128)S(1)}, u32[]{:S(2)}, u32[]{:S(2)}) %collective-permute-start.3) | collective-permute-done | bytes 544 | tf_op jit(solution)/shard_map/ppermute | solution.py:456
  10.7 0.0 collective-permute-done.other
  10.7 0.3 send_first.1
  11.1 0.1 collective-permute-start.4
  11.2 1.6 %collective-permute-start.7 = (bf16[16,4096]{1,0:T(8,128)(2,1)S(1)}, bf16[16,4096]{1,0:T(8,128)(2,1)S(1)}, u32[]{:S(2)}, u32[]{:S(2)}) collective-permute-start(bf16[16,4096]{1,0:T(8,128)(2,1)S(1)} %get-tuple-element.35), channel_id=1, source_target_pairs={{0,24},{4,28},{8,16},{12,20},{16,8},{20,12},{24,0},{28,4},{1,25},{... | collective-permute-start | bytes 393224 | tf_op jit(solution)/shard_map/ppermute | solution.py:456
  12.7 0.1 collective-permute-start.8
  12.8 1.9 %collective-permute-start.9 = (bf16[16,4096]{1,0:T(8,128)(2,1)S(1)}, bf16[16,4096]{1,0:T(8,128)(2,1)S(1)}, u32[]{:S(2)}, u32[]{:S(2)}) collective-permute-start(bf16[16,4096]{1,0:T(8,128)(2,1)S(1)} %get-tuple-element.37), channel_id=1, source_target_pairs={{0,8},{4,12},{8,0},{12,4},{16,24},{20,28},{24,16},{28,20},{1,9},{5... | collective-permute-start | bytes 393224 | tf_op jit(solution)/shard_map/ppermute | solution.py:456
  14.7 0.0 collective-permute-done.4
  14.7 3.5 %collective-permute-start.5 = (f32[32,128]{1,0:T(8,128)S(1)}, f32[32,128]{1,0:T(8,128)S(1)}, u32[]{:S(2)}, u32[]{:S(2)}) collective-permute-start(f32[32,128]{1,0:T(8,128)S(1)} %constant_dynamic-update-slice_fusion.message), channel_id=1, source_target_pairs={{0,1},{1,2},{2,3},{5,4},{6,5},{7,6},{8,9},{9,10},{10,11},{13,12},{... | collective-permute-start | bytes 49160 | tf_op jit(solution)/shard_map/ppermute | solution.py:493
  18.2 1.4 %collective-permute-done.5.mine = f32[32,128]{1,0:T(8,128)S(1)} collective-permute-done((f32[32,128]{1,0:T(8,128)S(1)}, f32[32,128]{1,0:T(8,128)S(1)}, u32[]{:S(2)}, u32[]{:S(2)}) %collective-permute-start.5) | collective-permute-done | bytes 16416 | tf_op jit(solution)/shard_map/ppermute | solution.py:493
  19.6 0.0 collective-permute-start.6
  19.6 1.2 %collective-permute-done.6.theirs = f32[32,128]{1,0:T(8,128)S(1)} collective-permute-done((f32[32,128]{1,0:T(8,128)S(1)}, f32[32,128]{1,0:T(8,128)S(1)}, u32[]{:S(2)}, u32[]{:S(2)}) %collective-permute-start.6) | collective-permute-done | bytes 16416 | tf_op jit(solution)/shard_map/ppermute | solution.py:456
  20.8 0.0 collective-permute-done.7.refs_1_
  20.8 0.0 collective-permute-done.8.refs_2_
  20.8 0.0 collective-permute-done.9.refs_3_
  20.9 0.8 %forecast_second.1 = (bf16[32,4096]{1,0:T(8,128)(2,1)S(1)}, f32[32,256]{1,0:T(8,128)S(1)}, f32[32,256]{1,0:T(8,128)S(1)}) custom-call(s32[2,32,128]{2,1,0:T(8,128)S(1)} %get-tuple-element.27.keys, f32[16,4096]{1,0:T(8,128)S(1)} %copy-done.1, bf16[2,2,16,4096]{3,2,1,0:T(8,128)(2,1)S(1)} %copy-done, f32[32,128]{1,0:T(8,128)S(1)} %constant_dynamic-update-slice_fusion.message, ...), custom_call_target="tpu_custom_call" | custom-call | tf_op jit(solution)/shard_map/forecast_second/pallas_call | solution.py:28
  21.7 0.0 copy-start.4
  21.8 0.2 collective-permute-start.10
  22.0 0.0 copy-done.3
  22.0 0.0 copy-done.5
  22.0 0.0 copy-done.7
  22.0 0.4 %copy-done.4 = s32[32,16]{0,1:T(8,128)S(1)} copy-done((s32[32,16]{0,1:T(8,128)S(1)}, s32[32,16]{0,1:T(8,128)}, u32[]{:S(2)}) %copy-start.4) | copy-done | bytes 2072
  22.4 0.2 copy-done.6
  22.7 0.2 observe.1
  22.9 0.7 %assess_first.1 = (bf16[16,640]{1,0:T(8,128)(2,1)S(1)}, bf16[16,640]{1,0:T(8,128)(2,1)S(1)}, bf16[16,640]{1,0:T(8,128)(2,1)S(1)}, bf16[16,640]{1,0:T(8,128)(2,1)S(1)}) custom-call(bf16[32,4096]{1,0:T(8,128)(2,1)S(1)} %forecast_first.1.own, bf16[32,4096]{1,0:T(8,128)(2,1)S(1)} %collective-permute-done.other, f32[32,256]{1,0:T(8,128)S(1)} %get-tuple-element.42.low, ...), custom_call_target="tpu_custom_call" | custom-call | tf_op jit(solution)/shard_map/assess_first/pallas_call | solution.py:28
  23.6 0.0 collective-permute-done.10.other
  23.6 0.9 %send_second.1 = (bf16[16,5376]{1,0:T(8,128)(2,1)S(1)}, bf16[16,5376]{1,0:T(8,128)(2,1)S(1)}, bf16[16,5376]{1,0:T(8,128)(2,1)S(1)}, bf16[16,5376]{1,0:T(8,128)(2,1)S(1)}) custom-call(bf16[32,4096]{1,0:T(8,128)(2,1)S(1)} %get-tuple-element.38.own, bf16[32,4096]{1,0:T(8,128)(2,1)S(1)} %collective-permute-done.10.other, s32[2,512]{1,0:T(2,128)S(1)} %get-tuple-element.39.where, ...), custom_call_target="tpu_custom_call" | custom-call | tf_op jit(solution)/shard_map/send_second/pallas_call | solution.py:28
  24.5 1.6 %collective-permute-start.11 = (bf16[16,5376]{1,0:T(8,128)(2,1)S(1)}, bf16[16,5376]{1,0:T(8,128)(2,1)S(1)}, u32[]{:S(2)}, u32[]{:S(2)}) collective-permute-start(bf16[16,5376]{1,0:T(8,128)(2,1)S(1)} %get-tuple-element.49), channel_id=1, source_target_pairs={{0,24},{4,28},{8,16},{12,20},{16,8},{20,12},{24,0},{28,4},{1,25},{... | collective-permute-start | bytes 516104 | tf_op jit(solution)/shard_map/ppermute | solution.py:456
  26.1 0.5 %collective-permute-start.12 = (bf16[16,5376]{1,0:T(8,128)(2,1)S(1)}, bf16[16,5376]{1,0:T(8,128)(2,1)S(1)}, u32[]{:S(2)}, u32[]{:S(2)}) collective-permute-start(bf16[16,5376]{1,0:T(8,128)(2,1)S(1)} %get-tuple-element.50), channel_id=1, source_target_pairs={{0,16},{4,20},{8,24},{12,28},{16,0},{20,4},{24,8},{28,12},{1,17},{... | collective-permute-start | bytes 516104 | tf_op jit(solution)/shard_map/ppermute | solution.py:456
  26.6 1.5 %collective-permute-start.13 = (bf16[16,5376]{1,0:T(8,128)(2,1)S(1)}, bf16[16,5376]{1,0:T(8,128)(2,1)S(1)}, u32[]{:S(2)}, u32[]{:S(2)}) collective-permute-start(bf16[16,5376]{1,0:T(8,128)(2,1)S(1)} %get-tuple-element.51), channel_id=1, source_target_pairs={{0,8},{4,12},{8,0},{12,4},{16,24},{20,28},{24,16},{28,20},{1,9},{5... | collective-permute-start | bytes 516104 | tf_op jit(solution)/shard_map/ppermute | solution.py:456
  28.0 4.6 %collective-permute-done.11.refs_1_ = bf16[16,5376]{1,0:T(8,128)(2,1)S(1)} collective-permute-done((bf16[16,5376]{1,0:T(8,128)(2,1)S(1)}, bf16[16,5376]{1,0:T(8,128)(2,1)S(1)}, u32[]{:S(2)}, u32[]{:S(2)}) %collective-permute-start.11) | collective-permute-done | bytes 172064 | tf_op jit(solution)/shard_map/ppermute | solution.py:456
  32.7 3.1 %collective-permute-done.12.refs_2_ = bf16[16,5376]{1,0:T(8,128)(2,1)S(1)} collective-permute-done((bf16[16,5376]{1,0:T(8,128)(2,1)S(1)}, bf16[16,5376]{1,0:T(8,128)(2,1)S(1)}, u32[]{:S(2)}, u32[]{:S(2)}) %collective-permute-start.12) | collective-permute-done | bytes 172064 | tf_op jit(solution)/shard_map/ppermute | solution.py:456
  35.8 0.1 collective-permute-done.13.refs_3_
  35.9 0.9 %finish.1 = (bf16[2,16,4096]{2,1,0:T(8,128)(2,1)}, f32[2,16,512]{2,1,0:T(8,128)}) custom-call(s32[2,32,128]{2,1,0:T(8,128)S(1)} %get-tuple-element.27.keys, bf16[16,5376]{1,0:T(8,128)(2,1)S(1)} %get-tuple-element.48.refs_0_, bf16[16,5376]{1,0:T(8,128)(2,1)S(1)} %collective-permute-done.11.refs_1_, bf16[16,5376]{1,0:T(8,128)(2,1)S(1)} %collective-permute-done.12.refs_2_, ...), custom_call_target="tpu_custom_call" | custom-call | tf_op jit(solution)/shard_map/finish/pallas_call | solution.py:28
  (8 shorter events, 0.0 us)
Async XLA Ops:
  0.6 1.3 %copy-start = (bf16[2,2,16,4096]{3,2,1,0:T(8,128)(2,1)S(1)}, bf16[2,2,16,4096]{3,2,1,0:T(8,128)(2,1)}, u32[]{:S(2)}) copy-start(bf16[2,2,16,4096]{3,2,1,0:T(8,128)(2,1)} %pert.3) | copy-start | bytes 1572868
  0.6 1.3 %copy-start.1 = (f32[16,4096]{1,0:T(8,128)S(1)}, f32[16,4096]{1,0:T(8,128)}, u32[]{:S(2)}) copy-start(f32[16,4096]{1,0:T(8,128)} %diff.3) | copy-start | bytes 786436
  0.7 1.3 %copy-start.2 = (bf16[2,16,4096]{2,1,0:T(8,128)(2,1)S(1)}, bf16[2,16,4096]{2,1,0:T(8,128)(2,1)}, u32[]{:S(2)}) copy-start(bf16[2,16,4096]{2,1,0:T(8,128)(2,1)} %state.1) | copy-start | bytes 786436
  2.6 8.1 %collective-permute-start = (bf16[32,4096]{1,0:T(8,128)(2,1)S(1)}, bf16[32,4096]{1,0:T(8,128)(2,1)S(1)}, u32[]{:S(2)}, u32[]{:S(2)}) collective-permute-start(bf16[32,4096]{1,0:T(8,128)(2,1)S(1)} %forecast_first.1.own), channel_id=1, source_target_pairs={{0,4},{4,0},{8,12},{12,8},{16,20},{20,16},{24,28},{28,24},{1,5},{5... | collective-permute-start | bytes 786440 | tf_op jit(solution)/shard_map/ppermute | solution.py:456
  3.1 5.0 %collective-permute-start.1 = (f32[1,128]{1,0:T(1,128)S(1)}, f32[1,128]{1,0:T(1,128)S(1)}, u32[]{:S(2)}, u32[]{:S(2)}) collective-permute-start(f32[1,128]{1,0:T(1,128)S(1)} %get-tuple-element.30), channel_id=1, source_target_pairs={{0,24},{4,28},{8,16},{12,20},{16,8},{20,12},{24,0},{28,4},{1,25},{... | collective-permute-start | bytes 1544 | tf_op jit(solution)/shard_map/ppermute | solution.py:456
  6.7 3.5 %collective-permute-start.2 = (f32[1,128]{1,0:T(1,128)S(1)}, f32[1,128]{1,0:T(1,128)S(1)}, u32[]{:S(2)}, u32[]{:S(2)}) collective-permute-start(f32[1,128]{1,0:T(1,128)S(1)} %get-tuple-element.31), channel_id=1, source_target_pairs={{0,16},{4,20},{8,24},{12,28},{16,0},{20,4},{24,8},{28,12},{1,17},{... | collective-permute-start | bytes 1544 | tf_op jit(solution)/shard_map/ppermute | solution.py:456
  7.2 3.5 %collective-permute-start.3 = (f32[1,128]{1,0:T(1,128)S(1)}, f32[1,128]{1,0:T(1,128)S(1)}, u32[]{:S(2)}, u32[]{:S(2)}) collective-permute-start(f32[1,128]{1,0:T(1,128)S(1)} %get-tuple-element.32), channel_id=1, source_target_pairs={{0,8},{4,12},{8,0},{12,4},{16,24},{20,28},{24,16},{28,20},{1,9},{5... | collective-permute-start | bytes 1544 | tf_op jit(solution)/shard_map/ppermute | solution.py:456
  11.1 3.6 %collective-permute-start.4 = (f32[16,128]{1,0:T(8,128)S(1)}, f32[16,128]{1,0:T(8,128)S(1)}, u32[]{:S(2)}, u32[]{:S(2)}) collective-permute-start(f32[16,128]{1,0:T(8,128)S(1)} %get-tuple-element.33), channel_id=1, source_target_pairs={{0,4},{4,0},{8,12},{12,8},{16,20},{20,16},{24,28},{28,24},{1,5},{5... | collective-permute-start | bytes 24584 | tf_op jit(solution)/shard_map/ppermute | solution.py:456
  11.2 9.7 %collective-permute-start.7 = (bf16[16,4096]{1,0:T(8,128)(2,1)S(1)}, bf16[16,4096]{1,0:T(8,128)(2,1)S(1)}, u32[]{:S(2)}, u32[]{:S(2)}) collective-permute-start(bf16[16,4096]{1,0:T(8,128)(2,1)S(1)} %get-tuple-element.35), channel_id=1, source_target_pairs={{0,24},{4,28},{8,16},{12,20},{16,8},{20,12},{24,0},{28,4},{1,25},{... | collective-permute-start | bytes 393224 | tf_op jit(solution)/shard_map/ppermute | solution.py:456
  12.7 8.1 %collective-permute-start.8 = (bf16[16,4096]{1,0:T(8,128)(2,1)S(1)}, bf16[16,4096]{1,0:T(8,128)(2,1)S(1)}, u32[]{:S(2)}, u32[]{:S(2)}) collective-permute-start(bf16[16,4096]{1,0:T(8,128)(2,1)S(1)} %get-tuple-element.36), channel_id=1, source_target_pairs={{0,16},{4,20},{8,24},{12,28},{16,0},{20,4},{24,8},{28,12},{1,17},{... | collective-permute-start | bytes 393224 | tf_op jit(solution)/shard_map/ppermute | solution.py:456
  12.8 8.0 %collective-permute-start.9 = (bf16[16,4096]{1,0:T(8,128)(2,1)S(1)}, bf16[16,4096]{1,0:T(8,128)(2,1)S(1)}, u32[]{:S(2)}, u32[]{:S(2)}) collective-permute-start(bf16[16,4096]{1,0:T(8,128)(2,1)S(1)} %get-tuple-element.37), channel_id=1, source_target_pairs={{0,8},{4,12},{8,0},{12,4},{16,24},{20,28},{24,16},{28,20},{1,9},{5... | collective-permute-start | bytes 393224 | tf_op jit(solution)/shard_map/ppermute | solution.py:456
  14.7 4.9 %collective-permute-start.5 = (f32[32,128]{1,0:T(8,128)S(1)}, f32[32,128]{1,0:T(8,128)S(1)}, u32[]{:S(2)}, u32[]{:S(2)}) collective-permute-start(f32[32,128]{1,0:T(8,128)S(1)} %constant_dynamic-update-slice_fusion.message), channel_id=1, source_target_pairs={{0,1},{1,2},{2,3},{5,4},{6,5},{7,6},{8,9},{9,10},{10,11},{13,12},{... | collective-permute-start | bytes 49160 | tf_op jit(solution)/shard_map/ppermute | solution.py:493
  19.6 1.2 %collective-permute-start.6 = (f32[32,128]{1,0:T(8,128)S(1)}, f32[32,128]{1,0:T(8,128)S(1)}, u32[]{:S(2)}, u32[]{:S(2)}) collective-permute-start(f32[32,128]{1,0:T(8,128)S(1)} %collective-permute-done.5.mine), channel_id=1, source_target_pairs={{0,4},{4,0},{8,12},{12,8},{16,20},{20,16},{24,28},{28,24},{1,5},{5... | collective-permute-start | bytes 49160 | tf_op jit(solution)/shard_map/ppermute | solution.py:456
  20.9 1.1 %copy-start.3 = (f32[2,32,16]{1,2,0:T(8,128)S(1)}, f32[2,32,16]{1,2,0:T(8,128)}, u32[]{:S(2)}) copy-start(f32[2,32,16]{1,2,0:T(8,128)} %param.14) | copy-start | bytes 12292
  20.9 1.1 %copy-start.5 = (f32[32,16]{0,1:T(8,128)S(1)}, f32[32,16]{0,1:T(8,128)}, u32[]{:S(2)}) copy-start(f32[32,16]{0,1:T(8,128)} %param.15) | copy-start | bytes 6148
  20.9 1.1 %copy-start.7 = (f32[16,6]{0,1:T(8,128)S(1)}, f32[16,6]{0,1:T(8,128)}, u32[]{:S(2)}) copy-start(f32[16,6]{0,1:T(8,128)} %param.19) | copy-start | bytes 1156
  21.7 0.7 %copy-start.4 = (s32[32,16]{0,1:T(8,128)S(1)}, s32[32,16]{0,1:T(8,128)}, u32[]{:S(2)}) copy-start(s32[32,16]{0,1:T(8,128)} %param.17) | copy-start | bytes 6148
  21.8 1.8 %collective-permute-start.10 = (bf16[32,4096]{1,0:T(8,128)(2,1)S(1)}, bf16[32,4096]{1,0:T(8,128)(2,1)S(1)}, u32[]{:S(2)}, u32[]{:S(2)}) collective-permute-start(bf16[32,4096]{1,0:T(8,128)(2,1)S(1)} %get-tuple-element.38.own), channel_id=1, source_target_pairs={{0,4},{4,0},{8,12},{12,8},{16,20},{20,16},{24,28},{28,24},{1,5},{5... | collective-permute-start | bytes 786440 | tf_op jit(solution)/shard_map/ppermute | solution.py:456
  22.0 0.7 %copy-start.6 = (s32[16,6]{0,1:T(8,128)S(1)}, s32[16,6]{0,1:T(8,128)}, u32[]{:S(2)}) copy-start(s32[16,6]{0,1:T(8,128)} %param.18) | copy-start | bytes 1156
  22.0 0.7 %copy-start.8 = (s32[32]{0:T(128)S(1)}, s32[32]{0:T(128)}, u32[]{:S(2)}) copy-start(s32[32]{0:T(128)} %param.16) | copy-start | bytes 388
  24.5 8.2 %collective-permute-start.11 = (bf16[16,5376]{1,0:T(8,128)(2,1)S(1)}, bf16[16,5376]{1,0:T(8,128)(2,1)S(1)}, u32[]{:S(2)}, u32[]{:S(2)}) collective-permute-start(bf16[16,5376]{1,0:T(8,128)(2,1)S(1)} %get-tuple-element.49), channel_id=1, source_target_pairs={{0,24},{4,28},{8,16},{12,20},{16,8},{20,12},{24,0},{28,4},{1,25},{... | collective-permute-start | bytes 516104 | tf_op jit(solution)/shard_map/ppermute | solution.py:456
  26.1 9.7 %collective-permute-start.12 = (bf16[16,5376]{1,0:T(8,128)(2,1)S(1)}, bf16[16,5376]{1,0:T(8,128)(2,1)S(1)}, u32[]{:S(2)}, u32[]{:S(2)}) collective-permute-start(bf16[16,5376]{1,0:T(8,128)(2,1)S(1)} %get-tuple-element.50), channel_id=1, source_target_pairs={{0,16},{4,20},{8,24},{12,28},{16,0},{20,4},{24,8},{28,12},{1,17},{... | collective-permute-start | bytes 516104 | tf_op jit(solution)/shard_map/ppermute | solution.py:456
  26.6 9.3 %collective-permute-start.13 = (bf16[16,5376]{1,0:T(8,128)(2,1)S(1)}, bf16[16,5376]{1,0:T(8,128)(2,1)S(1)}, u32[]{:S(2)}, u32[]{:S(2)}) collective-permute-start(bf16[16,5376]{1,0:T(8,128)(2,1)S(1)} %get-tuple-element.51), channel_id=1, source_target_pairs={{0,8},{4,12},{8,0},{12,4},{16,24},{20,28},{24,16},{28,20},{1,9},{5... | collective-permute-start | bytes 516104 | tf_op jit(solution)/shard_map/ppermute | solution.py:456

commit v7 on v6

--- a/solution.py
+++ b/solution.py
@@ -134,11 +134,11 @@
     return jnp.concatenate(low, axis=0), jnp.concatenate(high, axis=0)
 
 
-def patch(x, first, last):
+def patch(x, first, last, width):
     tiles = x.shape[0]
     row, lane = iota((tiles, LANES), 0), iota((tiles, LANES), 1)
-    head = jnp.where((row == 0) & (lane < STEPS), first, x[:, :LANES])
-    tail = jnp.where((row == tiles - 1) & (lane >= LANES - STEPS), last, x[:, -LANES:])
+    head = jnp.where((row == 0) & (lane < width), first, x[:, :LANES])
+    tail = jnp.where((row == tiles - 1) & (lane >= LANES - width), last, x[:, -LANES:])
     return jnp.concatenate([head, x[:, LANES:-LANES], tail], axis=1)
 
 
@@ -321,14 +321,17 @@
 def make_assess(pairs, parts, tiles, cells, share):
     size = padded(pairs)
 
-    def kernel(own, other, low, high, where, terms, local, *refs):
-        outs, sums = refs[:pairs], refs[pairs]
+    def kernel(own, other, message, mine, theirs, where, terms, local, *refs):
+        outs, low_out, high_out, sums = refs[:pairs], refs[pairs], refs[pairs + 1], refs[pairs + 2]
+        low, high = edge_windows(message[...], *halves(mine[...], theirs[...]), size, parts)
+        low_out[...] = low
+        high_out[...] = high
         fixed = []
         for h, prior in enumerate((own, other)):
             for p in range(parts):
                 row = (2 * p + h) * size
                 x = prior[p * tiles:(p + 1) * tiles, :].astype(F32)
-                x = patch(x, low[row:row + 1, LANES:], high[row:row + 1, :LANES])
+                x = patch(x, low[row:row + 1, LANES:], high[row:row + 1, :LANES], STEPS)
                 fixed.append(x.astype(BF16))
         least, total, weighted = assess(
             fixed, where[...], terms[0:1, :], terms[1:2, :], local[...], 2 * parts, tiles, cells
@@ -340,45 +343,73 @@
 
 
 def make_second(pairs, parts, tiles, cells):
-    size = padded(pairs)
-
-    def kernel(keys, diff, pert, message, mine, theirs, *refs):
-        got, prior, low_out, high_out = refs[:pairs], refs[pairs], refs[pairs + 1], refs[pairs + 2]
-        below, above = halves(mine[...], theirs[...])
-        low, high = edge_windows(message[...], below, above, size, parts)
-        low_out[...] = low
-        high_out[...] = high
-        below, above = below[size:size + 8, :], above[size:size + 8, :]
+    def kernel(keys, diff, pert, after, also, *refs):
+        got, prior, rim = refs[:pairs], refs[pairs], refs[pairs + 1]
         arrived = jnp.concatenate([x[...] for x in got], axis=0)
         moved = pick_rows(keys[0], arrived)
-        here_codes = message[size + 2:size + 2 + 2 * parts, :].astype(I32)
-        codes = jnp.concatenate([here_codes[parts:], below[2:2 + parts, :].astype(I32)], axis=0)
-        start = pick_rows(codes, low.astype(BF16))
-        codes = jnp.concatenate([here_codes[:parts], above[2 + parts:2 + 2 * parts, :].astype(I32)], axis=0)
-        end = pick_rows(codes, high.astype(BF16))
-        d = widen(diff[...], below[0:1, :], above[1:2, :])
+        nothing = jnp.zeros((1, LANES), F32)
+        d = widen(diff[...], nothing, nothing)
+        last = tiles - 1
         for p in range(parts):
-            x = patch(moved[p * tiles:(p + 1) * tiles, :], start[p:p + 1, LANES:], end[p:p + 1, :LANES])
-            q = parts + p
-            x = widen(x, start[q:q + 1, :LANES], end[q:q + 1, LANES:])
-            x = diffuse(x, d)[:, LANES:LANES + cells]
-            prior[p * tiles:(p + 1) * tiles, :] = (x + pert[0, p].astype(F32)).astype(BF16)
-
-    return kernel
+            x = moved[p * tiles:(p + 1) * tiles, :]
+            noise = pert[0, p].astype(F32)
+            ends = (x[0:1, :LANES], x[last:, -LANES:], noise[0:1, :LANES], noise[last:, -LANES:])
+            for i, row in enumerate(ends):
+                rim[i * parts + p:i * parts + p + 1, :] = row
+            x = diffuse(widen(x, nothing, nothing), d)[:, LANES:LANES + cells]
+            prior[p * tiles:(p + 1) * tiles, :] = (x + noise).astype(BF16)
+
+    return kernel
+
+
+def rims(own, other, message, below, above, low, high, size, parts):
+    n = 2 * parts
+    lane = iota((n, LANES), 1)
+
+    def both(i):
+        return jnp.concatenate([own[i * parts:(i + 1) * parts, :], other[i * parts:(i + 1) * parts, :]], axis=0)
+
+    def codes(note, i):
+        at = size + 2 + i * parts
+        first = note[at:at + parts, :].astype(I32)
+        at += size + 8
+        return jnp.concatenate([first, note[at:at + parts, :].astype(I32) ^ size], axis=0)
+
+    def picked(here_codes, there_codes, windows):
+        x = pick_rows(jnp.concatenate([here_codes, there_codes], axis=0), windows.astype(BF16))
+        return x[:n, :], x[n:, :]
+
+    fix, halo = picked(codes(message, 1), codes(below, 0), low)
+    x = jnp.concatenate([halo[:, :LANES], jnp.where(lane < STEPS, fix[:, LANES:], both(0))], axis=1)
+    d = jnp.concatenate([below[size:size + 1, :], message[size + 1:size + 2, :]], axis=1)
+    first = diffuse(x, d)[:, LANES:] + both(2)
+    fix, halo = picked(codes(message, 0), codes(above, 1), high)
+    x = jnp.concatenate([jnp.where(lane >= LANES - STEPS, fix[:, :LANES], both(1)), halo[:, LANES:]], axis=1)
+    d = jnp.concatenate([message[size:size + 1, :], above[size + 1:size + 2, :]], axis=1)
+    return first, diffuse(x, d)[:, :LANES] + both(3)
 
 
 def make_send_second(pairs, rows, parts, tiles, cells, share):
-    def kernel(own, other, where, terms, local, *refs):
+    size = padded(pairs)
+
+    def kernel(own, other, rim, other_rim, message, mine, theirs, low, high, where, terms, local, *refs):
         notes, kept, outs, sums = refs[:pairs], refs[pairs:2 * pairs], refs[2 * pairs:3 * pairs], refs[3 * pairs]
-        prior = jnp.concatenate([own[...], other[...]], axis=0)
-        sent = requested([x[...] for x in notes], prior, 1, rows)
+        below, above = halves(mine[...], theirs[...])
+        first, last = rims(rim[...], other_rim[...], message[...], below, above, low[...], high[...], size, parts)
+        prior = []
+        for h, x in enumerate((own, other)):
+            for p in range(parts):
+                q = h * parts + p
+                now = x[p * tiles:(p + 1) * tiles, :].astype(F32)
+                now = patch(now, first[q:q + 1, :], last[q:q + 1, :], 2 * STEPS)
+                prior.append(now.astype(BF16))
+        sent = requested([x[...] for x in notes], jnp.concatenate(prior, axis=0), 1, rows)
         extra = kept[0].shape[1]
         for k in range(pairs):
             outs[k][:, :cells] = sent[k * rows:(k + 1) * rows, :].astype(BF16)
             outs[k][:, cells:cells + extra] = kept[k][...]
         least, total, weighted = assess(
-            [x[p * tiles:(p + 1) * tiles, :] for x in (own, other) for p in range(parts)],
-            where[...], terms[0:1, :], terms[2:3, :], local[...], 2 * parts, tiles, cells,
+            prior, where[...], terms[0:1, :], terms[2:3, :], local[...], 2 * parts, tiles, cells
         )
         sums[...] = weighted
         pack_mean(outs, cells + extra, least, total, sums, share)
@@ -494,27 +525,28 @@
     theirs = trade(mine, 1)
     window = ((parts * 2 * size, 2 * LANES), F32)
     sums = [((tiles, cells), F32)]
-    args = [keys, diffusivity, model_perturbation, message, mine, theirs, *got]
+    args = [keys, diffusivity, model_perturbation, where, mine, *got]
     specs = [whole_spec(a.shape) for a in args]
     specs[2] = noise_spec(1)
-    second, low, high = call(
+    second, rim = call(
         make_second(pairs, parts, tiles, cells),
-        [((parts * tiles, cells), BF16), window, window],
+        [((parts * tiles, cells), BF16), ((4 * parts, LANES), F32)],
         args,
         specs,
         name="forecast_second",
     )
-    kept = call(
+    *kept, low, high = call(
         make_assess(pairs, parts, tiles, cells, share),
-        [((rows, extra), BF16)] * pairs,
-        [prior, other, low, high, where, terms, local],
+        [((rows, extra), BF16)] * pairs + [window, window],
+        [prior, other, message, mine, theirs, where, terms, local],
         scratch=sums,
         name="assess_first",
     )
+    args = [second, trade(second, 1), rim, trade(rim, 1), message, mine, theirs, low, high, where, terms, local]
     sends = call(
         make_send_second(pairs, rows, parts, tiles, cells, share),
         [((rows, cells + CYCLES * extra), BF16)] * pairs,
-        [second, trade(second, 1), where, terms, local, *notes, *kept],
+        [*args, *notes, *kept],
         scratch=sums,
         name="send_second",
     )

time: 37 us -> 37.9 us (1.024)
  Pallas kernels: 5.83 us -> 6.46 us
  starting transfers between devices: 15.6 us -> 16 us
    ppermute x1, waiting for transfers between devices: 1.43 us -> 0.58 us  [body(): mine = lax.ppermute(message, ('member', 'region'), steps)]
    ppermute x13 -> x14, waiting for transfers between devices: 12.5 us -> 13.1 us  [trade(): return lax.ppermute(x, 'member', [(i, i ^ k) for i in range(members)])]
    pallas_call x8, Pallas kernels: 5.83 us -> 6.46 us  [call(): pl.pallas_call(kernel, out_shape=[jax.ShapeDtypeStruct(s, d) for s, d in...]
    ppermute x13 -> x14, starting transfers between devices: 12.1 us -> 12.5 us  [trade(): return lax.ppermute(x, 'member', [(i, i ^ k) for i in range(members)])]
  transfers between devices with their start and end apart: 14 -> 15, of which waited for: 8 -> 9; matrix products, arithmetic and copies ran while one was open for 0% -> 0% of each run, Pallas kernels for 2% -> 3%
where the time goes in v7:
time: 37.9 us; the launch traced here: 37.7 us
  starting transfers between devices  16 us (42%)
  waiting for transfers between devices  13.7 us (36%)
  Pallas kernels  6.46 us (17%)
  between operations  0.87 us (2%)
  local copies, waits for them, and re-layouts  0.65 us (2%)
    ppermute x14, waiting for transfers between devices, trade(): return lax.ppermute(x, 'member', [(i, i ^ k) for i in range(members)])  13.1 us
    ppermute x14, starting transfers between devices, trade(): return lax.ppermute(x, 'member', [(i, i ^ k) for i in range(members)])  12.5 us
    pallas_call x8, Pallas kernels, call(): pl.pallas_call(kernel, out_shape=[jax.ShapeDtypeStruct(s, d) for s, d in...  6.46 us
    ppermute x1, starting transfers between devices, body(): mine = lax.ppermute(message, ('member', 'region'), steps)  3.48 us
  transfers between devices with their start and end apart: 15, of which 9 were waited for; matrix products, arithmetic and copies ran while one was open for 0% of the time, Pallas kernels for 3%

profile of v7, /device:TPU:0, one launch (start us, length us, event | category | flops | bytes accessed | tf_op | source)
XLA Modules:
  0.0 37.7 jit_solution(17650054851433351732)
XLA Ops:
  0.6 0.0 copy-start
  0.6 0.0 copy-start.1
  0.7 0.0 copy-start.2
  0.7 1.3 %prepare.1 = (f32[1,128]{1,0:T(1,128)S(1)}, f32[1,128]{1,0:T(1,128)S(1)}, f32[1,128]{1,0:T(1,128)S(1)}, f32[1,128]{1,0:T(1,128)S(1)}, f32[8,128]{1,0:T(8,128)S(1)}, /*index=5*/s32[2,32,128]{2,1,0:T(8,128)S(1)}) custom-call(bf16[2,16,4096]{2,1,0:T(8,128)(2,1)} %state.1, bf16[2,16,4096]{2,1,0:T(8,128)(2,1)} %state.1, f32[16,4096]{1,0:T(8,128)} %diff.3, ...), custom_call_target="tpu_custom_call" | custom-call | tf_op jit(solution)/shard_map/prepare/pallas_call | solution.py:28
  2.0 0.0 copy-done
  2.0 0.0 copy-done.1
  2.0 0.6 %forecast_first.1.own = bf16[32,4096]{1,0:T(8,128)(2,1)S(1)} custom-call(bf16[2,16,4096]{2,1,0:T(8,128)(2,1)S(1)} %copy-done.2, f32[16,4096]{1,0:T(8,128)S(1)} %copy-done.1, bf16[2,2,16,4096]{3,2,1,0:T(8,128)(2,1)S(1)} %copy-done, f32[8,128]{1,0:T(8,128)S(1)} %get-tuple-element.30.after.trail), custom_call_target="tpu_custom_call" | custom-call | tf_op jit(solution)/shard_map/forecast_first/pallas_call | solution.py:28
  2.7 0.5 %collective-permute-start = (bf16[32,4096]{1,0:T(8,128)(2,1)S(1)}, bf16[32,4096]{1,0:T(8,128)(2,1)S(1)}, u32[]{:S(2)}, u32[]{:S(2)}) collective-permute-start(bf16[32,4096]{1,0:T(8,128)(2,1)S(1)} %forecast_first.1.own), channel_id=1, source_target_pairs={{0,4},{4,0},{8,12},{12,8},{16,20},{20,16},{24,28},{28,24},{1,5},{5... | collective-permute-start | bytes 786440 | tf_op jit(solution)/shard_map/ppermute | solution.py:487
  3.2 3.5 %collective-permute-start.1 = (f32[1,128]{1,0:T(1,128)S(1)}, f32[1,128]{1,0:T(1,128)S(1)}, u32[]{:S(2)}, u32[]{:S(2)}) collective-permute-start(f32[1,128]{1,0:T(1,128)S(1)} %get-tuple-element.32), channel_id=1, source_target_pairs={{0,24},{4,28},{8,16},{12,20},{16,8},{20,12},{24,0},{28,4},{1,25},{... | collective-permute-start | bytes 1544 | tf_op jit(solution)/shard_map/ppermute | solution.py:487
  6.7 0.5 %collective-permute-start.2 = (f32[1,128]{1,0:T(1,128)S(1)}, f32[1,128]{1,0:T(1,128)S(1)}, u32[]{:S(2)}, u32[]{:S(2)}) collective-permute-start(f32[1,128]{1,0:T(1,128)S(1)} %get-tuple-element.33), channel_id=1, source_target_pairs={{0,16},{4,20},{8,24},{12,28},{16,0},{20,4},{24,8},{28,12},{1,17},{... | collective-permute-start | bytes 1544 | tf_op jit(solution)/shard_map/ppermute | solution.py:487
  7.2 0.1 collective-permute-start.3
  7.3 0.9 %collective-permute-done.1.refs_1_ = f32[1,128]{1,0:T(1,128)S(1)} collective-permute-done((f32[1,128]{1,0:T(1,128)S(1)}, f32[1,128]{1,0:T(1,128)S(1)}, u32[]{:S(2)}, u32[]{:S(2)}) %collective-permute-start.1) | collective-permute-done | bytes 544 | tf_op jit(solution)/shard_map/ppermute | solution.py:487
  8.2 2.0 %collective-permute-done.2.refs_2_ = f32[1,128]{1,0:T(1,128)S(1)} collective-permute-done((f32[1,128]{1,0:T(1,128)S(1)}, f32[1,128]{1,0:T(1,128)S(1)}, u32[]{:S(2)}, u32[]{:S(2)}) %collective-permute-start.2) | collective-permute-done | bytes 544 | tf_op jit(solution)/shard_map/ppermute | solution.py:487
  10.2 0.5 %collective-permute-done.3.refs_3_ = f32[1,128]{1,0:T(1,128)S(1)} collective-permute-done((f32[1,128]{1,0:T(1,128)S(1)}, f32[1,128]{1,0:T(1,128)S(1)}, u32[]{:S(2)}, u32[]{:S(2)}) %collective-permute-start.3) | collective-permute-done | bytes 544 | tf_op jit(solution)/shard_map/ppermute | solution.py:487
  10.7 0.0 collective-permute-done.other
  10.7 0.4 send_first.1
  11.1 0.0 copy-start.6
  11.1 0.0 copy-start.7
  11.1 0.1 collective-permute-start.4
  11.2 1.6 %collective-permute-start.6 = (bf16[16,4096]{1,0:T(8,128)(2,1)S(1)}, bf16[16,4096]{1,0:T(8,128)(2,1)S(1)}, u32[]{:S(2)}, u32[]{:S(2)}) collective-permute-start(bf16[16,4096]{1,0:T(8,128)(2,1)S(1)} %get-tuple-element.37), channel_id=1, source_target_pairs={{0,24},{4,28},{8,16},{12,20},{16,8},{20,12},{24,0},{28,4},{1,25},{... | collective-permute-start | bytes 393224 | tf_op jit(solution)/shard_map/ppermute | solution.py:487
  12.8 0.1 collective-permute-start.7
  12.9 1.9 %collective-permute-start.8 = (bf16[16,4096]{1,0:T(8,128)(2,1)S(1)}, bf16[16,4096]{1,0:T(8,128)(2,1)S(1)}, u32[]{:S(2)}, u32[]{:S(2)}) collective-permute-start(bf16[16,4096]{1,0:T(8,128)(2,1)S(1)} %get-tuple-element.39), channel_id=1, source_target_pairs={{0,8},{4,12},{8,0},{12,4},{16,24},{20,28},{24,16},{28,20},{1,9},{5... | collective-permute-start | bytes 393224 | tf_op jit(solution)/shard_map/ppermute | solution.py:487
  14.8 0.0 collective-permute-done.4
  14.8 0.0 copy-start.4
  14.8 3.5 %collective-permute-start.5 = (f32[32,128]{1,0:T(8,128)S(1)}, f32[32,128]{1,0:T(8,128)S(1)}, u32[]{:S(2)}, u32[]{:S(2)}) collective-permute-start(f32[32,128]{1,0:T(8,128)S(1)} %constant_dynamic-update-slice_fusion.message), channel_id=1, source_target_pairs={{0,1},{1,2},{2,3},{5,4},{6,5},{7,6},{8,9},{9,10},{10,11},{13,12},{... | collective-permute-start | bytes 49160 | tf_op jit(solution)/shard_map/ppermute | solution.py:524
  18.3 0.0 copy-start.8
  18.4 0.6 %copy-done.8 = s32[32]{0:T(128)S(1)} copy-done((s32[32]{0:T(128)S(1)}, s32[32]{0:T(128)}, u32[]{:S(2)}) %copy-start.8) | copy-done | bytes 152
  19.0 0.2 observe.1
  19.1 0.6 %collective-permute-done.5.also.mine = f32[32,128]{1,0:T(8,128)S(1)} collective-permute-done((f32[32,128]{1,0:T(8,128)S(1)}, f32[32,128]{1,0:T(8,128)S(1)}, u32[]{:S(2)}, u32[]{:S(2)}) %collective-permute-start.5) | collective-permute-done | bytes 16416 | tf_op jit(solution)/shard_map/ppermute | solution.py:524
  19.7 0.0 collective-permute-done.6.refs_1_
  19.7 1.1 %collective-permute-done.7.refs_2_ = bf16[16,4096]{1,0:T(8,128)(2,1)S(1)} collective-permute-done((bf16[16,4096]{1,0:T(8,128)(2,1)S(1)}, bf16[16,4096]{1,0:T(8,128)(2,1)S(1)}, u32[]{:S(2)}, u32[]{:S(2)}) %collective-permute-start.7) | collective-permute-done | bytes 131104 | tf_op jit(solution)/shard_map/ppermute | solution.py:487
  20.8 0.1 collective-permute-done.8.refs_3_
  20.9 0.8 %forecast_second.1 = (bf16[32,4096]{1,0:T(8,128)(2,1)S(1)}, f32[8,128]{1,0:T(8,128)S(1)}) custom-call(s32[2,32,128]{2,1,0:T(8,128)S(1)} %get-tuple-element.28.keys, f32[16,4096]{1,0:T(8,128)S(1)} %copy-done.1, bf16[2,2,16,4096]{3,2,1,0:T(8,128)(2,1)S(1)} %copy-done, s32[2,512]{1,0:T(2,128)S(1)} %get-tuple-element.29.after.where, ...), custom_call_target="tpu_custom_call" | custom-call | tf_op jit(solution)/shard_map/forecast_second/pallas_call | solution.py:28
  21.8 0.1 collective-permute-start.9
  21.9 0.5 %collective-permute-start.11 = (f32[32,128]{1,0:T(8,128)S(1)}, f32[32,128]{1,0:T(8,128)S(1)}, u32[]{:S(2)}, u32[]{:S(2)}) collective-permute-start(f32[32,128]{1,0:T(8,128)S(1)} %collective-permute-done.5.also.mine), channel_id=1, source_target_pairs={{0,4},{4,0},{8,12},{12,8},{16,20},{20,16},{24,28},{28,24},{1,5},{5... | collective-permute-start | bytes 49160 | tf_op jit(solution)/shard_map/ppermute | solution.py:487
  22.4 0.1 collective-permute-start.10
  22.4 1.0 %collective-permute-done.11.theirs = f32[32,128]{1,0:T(8,128)S(1)} collective-permute-done((f32[32,128]{1,0:T(8,128)S(1)}, f32[32,128]{1,0:T(8,128)S(1)}, u32[]{:S(2)}, u32[]{:S(2)}) %collective-permute-start.11) | collective-permute-done | bytes 16416 | tf_op jit(solution)/shard_map/ppermute | solution.py:487
  23.4 1.0 %assess_first.1 = (bf16[16,640]{1,0:T(8,128)(2,1)S(1)}, bf16[16,640]{1,0:T(8,128)(2,1)S(1)}, bf16[16,640]{1,0:T(8,128)(2,1)S(1)}, bf16[16,640]{1,0:T(8,128)(2,1)...) custom-call(bf16[32,4096]{1,0:T(8,128)(2,1)S(1)} %forecast_first.1.own, ...), custom_call_target="tpu_custom_call" | custom-call | tf_op jit(solution)/shard_map/assess_first/pallas_call | solution.py:28
  24.5 0.0 collective-permute-done.10.other_rim
  24.5 0.0 collective-permute-done.9.other
  24.5 1.2 %send_second.1 = (bf16[16,5376]{1,0:T(8,128)(2,1)S(1)}, bf16[16,5376]{1,0:T(8,128)(2,1)S(1)}, bf16[16,5376]{1,0:T(8,128)(2,1)S(1)}, bf16[16,5376]{1,0:T(8,128)(2,1)S(1)}) custom-call(bf16[32,4096]{1,0:T(8,128)(2,1)S(1)} %get-tuple-element.40.own, bf16[32,4096]{1,0:T(8,128)(2,1)S(1)} %collective-permute-done.9.other, f32[8,128]{1,0:T(8,128)S(1)} %get-tuple-element.41.rim, ...), custom_call_target="tpu_custom_call" | custom-call | tf_op jit(solution)/shard_map/send_second/pallas_call | solution.py:28
  25.6 1.5 %collective-permute-start.12 = (bf16[16,5376]{1,0:T(8,128)(2,1)S(1)}, bf16[16,5376]{1,0:T(8,128)(2,1)S(1)}, u32[]{:S(2)}, u32[]{:S(2)}) collective-permute-start(bf16[16,5376]{1,0:T(8,128)(2,1)S(1)} %get-tuple-element.51), channel_id=1, source_target_pairs={{0,24},{4,28},{8,16},{12,20},{16,8},{20,12},{24,0},{28,4},{1,25},{... | collective-permute-start | bytes 516104 | tf_op jit(solution)/shard_map/ppermute | solution.py:487
  27.1 0.6 %collective-permute-start.13 = (bf16[16,5376]{1,0:T(8,128)(2,1)S(1)}, bf16[16,5376]{1,0:T(8,128)(2,1)S(1)}, u32[]{:S(2)}, u32[]{:S(2)}) collective-permute-start(bf16[16,5376]{1,0:T(8,128)(2,1)S(1)} %get-tuple-element.52), channel_id=1, source_target_pairs={{0,16},{4,20},{8,24},{12,28},{16,0},{20,4},{24,8},{28,12},{1,17},{... | collective-permute-start | bytes 516104 | tf_op jit(solution)/shard_map/ppermute | solution.py:487
  27.7 1.5 %collective-permute-start.14 = (bf16[16,5376]{1,0:T(8,128)(2,1)S(1)}, bf16[16,5376]{1,0:T(8,128)(2,1)S(1)}, u32[]{:S(2)}, u32[]{:S(2)}) collective-permute-start(bf16[16,5376]{1,0:T(8,128)(2,1)S(1)} %get-tuple-element.53), channel_id=1, source_target_pairs={{0,8},{4,12},{8,0},{12,4},{16,24},{20,28},{24,16},{28,20},{1,9},{5... | collective-permute-start | bytes 516104 | tf_op jit(solution)/shard_map/ppermute | solution.py:487
  29.2 4.7 %collective-permute-done.12.refs_1_ = bf16[16,5376]{1,0:T(8,128)(2,1)S(1)} collective-permute-done((bf16[16,5376]{1,0:T(8,128)(2,1)S(1)}, bf16[16,5376]{1,0:T(8,128)(2,1)S(1)}, u32[]{:S(2)}, u32[]{:S(2)}) %collective-permute-start.12) | collective-permute-done | bytes 172064 | tf_op jit(solution)/shard_map/ppermute | solution.py:487
  33.9 2.8 %collective-permute-done.13.refs_2_ = bf16[16,5376]{1,0:T(8,128)(2,1)S(1)} collective-permute-done((bf16[16,5376]{1,0:T(8,128)(2,1)S(1)}, bf16[16,5376]{1,0:T(8,128)(2,1)S(1)}, u32[]{:S(2)}, u32[]{:S(2)}) %collective-permute-start.13) | collective-permute-done | bytes 172064 | tf_op jit(solution)/shard_map/ppermute | solution.py:487
  36.7 0.0 collective-permute-done.14.refs_3_
  36.7 0.9 %finish.1 = (bf16[2,16,4096]{2,1,0:T(8,128)(2,1)}, f32[2,16,512]{2,1,0:T(8,128)}) custom-call(s32[2,32,128]{2,1,0:T(8,128)S(1)} %get-tuple-element.28.keys, bf16[16,5376]{1,0:T(8,128)(2,1)S(1)} %get-tuple-element.50.refs_0_, bf16[16,5376]{1,0:T(8,128)(2,1)S(1)} %collective-permute-done.12.refs_1_, bf16[16,5376]{1,0:T(8,128)(2,1)S(1)} %collective-permute-done.13.refs_2_, ...), custom_call_target="tpu_custom_call" | custom-call | tf_op jit(solution)/shard_map/finish/pallas_call | solution.py:28
  (10 shorter events, 0.0 us)
Async XLA Ops:
  0.6 1.3 %copy-start = (bf16[2,2,16,4096]{3,2,1,0:T(8,128)(2,1)S(1)}, bf16[2,2,16,4096]{3,2,1,0:T(8,128)(2,1)}, u32[]{:S(2)}) copy-start(bf16[2,2,16,4096]{3,2,1,0:T(8,128)(2,1)} %pert.3) | copy-start | bytes 1572868
  0.6 1.3 %copy-start.1 = (f32[16,4096]{1,0:T(8,128)S(1)}, f32[16,4096]{1,0:T(8,128)}, u32[]{:S(2)}) copy-start(f32[16,4096]{1,0:T(8,128)} %diff.3) | copy-start | bytes 786436
  0.7 1.3 %copy-start.2 = (bf16[2,16,4096]{2,1,0:T(8,128)(2,1)S(1)}, bf16[2,16,4096]{2,1,0:T(8,128)(2,1)}, u32[]{:S(2)}) copy-start(bf16[2,16,4096]{2,1,0:T(8,128)(2,1)} %state.1) | copy-start | bytes 786436
  2.7 8.1 %collective-permute-start = (bf16[32,4096]{1,0:T(8,128)(2,1)S(1)}, bf16[32,4096]{1,0:T(8,128)(2,1)S(1)}, u32[]{:S(2)}, u32[]{:S(2)}) collective-permute-start(bf16[32,4096]{1,0:T(8,128)(2,1)S(1)} %forecast_first.1.own), channel_id=1, source_target_pairs={{0,4},{4,0},{8,12},{12,8},{16,20},{20,16},{24,28},{28,24},{1,5},{5... | collective-permute-start | bytes 786440 | tf_op jit(solution)/shard_map/ppermute | solution.py:487
  3.2 5.0 %collective-permute-start.1 = (f32[1,128]{1,0:T(1,128)S(1)}, f32[1,128]{1,0:T(1,128)S(1)}, u32[]{:S(2)}, u32[]{:S(2)}) collective-permute-start(f32[1,128]{1,0:T(1,128)S(1)} %get-tuple-element.32), channel_id=1, source_target_pairs={{0,24},{4,28},{8,16},{12,20},{16,8},{20,12},{24,0},{28,4},{1,25},{... | collective-permute-start | bytes 1544 | tf_op jit(solution)/shard_map/ppermute | solution.py:487
  6.7 3.5 %collective-permute-start.2 = (f32[1,128]{1,0:T(1,128)S(1)}, f32[1,128]{1,0:T(1,128)S(1)}, u32[]{:S(2)}, u32[]{:S(2)}) collective-permute-start(f32[1,128]{1,0:T(1,128)S(1)} %get-tuple-element.33), channel_id=1, source_target_pairs={{0,16},{4,20},{8,24},{12,28},{16,0},{20,4},{24,8},{28,12},{1,17},{... | collective-permute-start | bytes 1544 | tf_op jit(solution)/shard_map/ppermute | solution.py:487
  7.2 3.5 %collective-permute-start.3 = (f32[1,128]{1,0:T(1,128)S(1)}, f32[1,128]{1,0:T(1,128)S(1)}, u32[]{:S(2)}, u32[]{:S(2)}) collective-permute-start(f32[1,128]{1,0:T(1,128)S(1)} %get-tuple-element.34), channel_id=1, source_target_pairs={{0,8},{4,12},{8,0},{12,4},{16,24},{20,28},{24,16},{28,20},{1,9},{5... | collective-permute-start | bytes 1544 | tf_op jit(solution)/shard_map/ppermute | solution.py:487
  11.1 7.2 %copy-start.6 = (s32[16,6]{0,1:T(8,128)S(1)}, s32[16,6]{0,1:T(8,128)}, u32[]{:S(2)}) copy-start(s32[16,6]{0,1:T(8,128)} %param.18) | copy-start | bytes 1156
  11.1 7.2 %copy-start.7 = (f32[16,6]{0,1:T(8,128)S(1)}, f32[16,6]{0,1:T(8,128)}, u32[]{:S(2)}) copy-start(f32[16,6]{0,1:T(8,128)} %param.19) | copy-start | bytes 1156
  11.1 3.6 %collective-permute-start.4 = (f32[16,128]{1,0:T(8,128)S(1)}, f32[16,128]{1,0:T(8,128)S(1)}, u32[]{:S(2)}, u32[]{:S(2)}) collective-permute-start(f32[16,128]{1,0:T(8,128)S(1)} %get-tuple-element.35), channel_id=1, source_target_pairs={{0,4},{4,0},{8,12},{12,8},{16,20},{20,16},{24,28},{28,24},{1,5},{5... | collective-permute-start | bytes 24584 | tf_op jit(solution)/shard_map/ppermute | solution.py:487
  11.2 8.5 %collective-permute-start.6 = (bf16[16,4096]{1,0:T(8,128)(2,1)S(1)}, bf16[16,4096]{1,0:T(8,128)(2,1)S(1)}, u32[]{:S(2)}, u32[]{:S(2)}) collective-permute-start(bf16[16,4096]{1,0:T(8,128)(2,1)S(1)} %get-tuple-element.37), channel_id=1, source_target_pairs={{0,24},{4,28},{8,16},{12,20},{16,8},{20,12},{24,0},{28,4},{1,25},{... | collective-permute-start | bytes 393224 | tf_op jit(solution)/shard_map/ppermute | solution.py:487
  12.8 8.1 %collective-permute-start.7 = (bf16[16,4096]{1,0:T(8,128)(2,1)S(1)}, bf16[16,4096]{1,0:T(8,128)(2,1)S(1)}, u32[]{:S(2)}, u32[]{:S(2)}) collective-permute-start(bf16[16,4096]{1,0:T(8,128)(2,1)S(1)} %get-tuple-element.38), channel_id=1, source_target_pairs={{0,16},{4,20},{8,24},{12,28},{16,0},{20,4},{24,8},{28,12},{1,17},{... | collective-permute-start | bytes 393224 | tf_op jit(solution)/shard_map/ppermute | solution.py:487
  12.9 8.1 %collective-permute-start.8 = (bf16[16,4096]{1,0:T(8,128)(2,1)S(1)}, bf16[16,4096]{1,0:T(8,128)(2,1)S(1)}, u32[]{:S(2)}, u32[]{:S(2)}) collective-permute-start(bf16[16,4096]{1,0:T(8,128)(2,1)S(1)} %get-tuple-element.39), channel_id=1, source_target_pairs={{0,8},{4,12},{8,0},{12,4},{16,24},{20,28},{24,16},{28,20},{1,9},{5... | collective-permute-start | bytes 393224 | tf_op jit(solution)/shard_map/ppermute | solution.py:487
  14.8 3.6 %copy-start.5 = (f32[32,16]{0,1:T(8,128)S(1)}, f32[32,16]{0,1:T(8,128)}, u32[]{:S(2)}) copy-start(f32[32,16]{0,1:T(8,128)} %param.15) | copy-start | bytes 6148
  14.8 3.6 %copy-start.3 = (f32[2,32,16]{1,2,0:T(8,128)S(1)}, f32[2,32,16]{1,2,0:T(8,128)}, u32[]{:S(2)}) copy-start(f32[2,32,16]{1,2,0:T(8,128)} %param.14) | copy-start | bytes 12292
  14.8 3.6 %copy-start.4 = (s32[32,16]{0,1:T(8,128)S(1)}, s32[32,16]{0,1:T(8,128)}, u32[]{:S(2)}) copy-start(s32[32,16]{0,1:T(8,128)} %param.17) | copy-start | bytes 6148
  14.8 4.9 %collective-permute-start.5 = (f32[32,128]{1,0:T(8,128)S(1)}, f32[32,128]{1,0:T(8,128)S(1)}, u32[]{:S(2)}, u32[]{:S(2)}) collective-permute-start(f32[32,128]{1,0:T(8,128)S(1)} %constant_dynamic-update-slice_fusion.message), channel_id=1, source_target_pairs={{0,1},{1,2},{2,3},{5,4},{6,5},{7,6},{8,9},{9,10},{10,11},{13,12},{... | collective-permute-start | bytes 49160 | tf_op jit(solution)/shard_map/ppermute | solution.py:524
  18.3 0.7 %copy-start.8 = (s32[32]{0:T(128)S(1)}, s32[32]{0:T(128)}, u32[]{:S(2)}) copy-start(s32[32]{0:T(128)} %param.16) | copy-start | bytes 388
  21.8 2.7 %collective-permute-start.9 = (bf16[32,4096]{1,0:T(8,128)(2,1)S(1)}, bf16[32,4096]{1,0:T(8,128)(2,1)S(1)}, u32[]{:S(2)}, u32[]{:S(2)}) collective-permute-start(bf16[32,4096]{1,0:T(8,128)(2,1)S(1)} %get-tuple-element.40.own), channel_id=1, source_target_pairs={{0,4},{4,0},{8,12},{12,8},{16,20},{20,16},{24,28},{28,24},{1,5},{5... | collective-permute-start | bytes 786440 | tf_op jit(solution)/shard_map/ppermute | solution.py:487
  21.9 1.5 %collective-permute-start.11 = (f32[32,128]{1,0:T(8,128)S(1)}, f32[32,128]{1,0:T(8,128)S(1)}, u32[]{:S(2)}, u32[]{:S(2)}) collective-permute-start(f32[32,128]{1,0:T(8,128)S(1)} %collective-permute-done.5.also.mine), channel_id=1, source_target_pairs={{0,4},{4,0},{8,12},{12,8},{16,20},{20,16},{24,28},{28,24},{1,5},{5... | collective-permute-start | bytes 49160 | tf_op jit(solution)/shard_map/ppermute | solution.py:487
  22.4 2.1 %collective-permute-start.10 = (f32[8,128]{1,0:T(8,128)S(1)}, f32[8,128]{1,0:T(8,128)S(1)}, u32[]{:S(2)}, u32[]{:S(2)}) collective-permute-start(f32[8,128]{1,0:T(8,128)S(1)} %get-tuple-element.41.rim), channel_id=1, source_target_pairs={{0,4},{4,0},{8,12},{12,8},{16,20},{20,16},{24,28},{28,24},{1,5},{5... | collective-permute-start | bytes 12296 | tf_op jit(solution)/shard_map/ppermute | solution.py:487
  25.6 8.2 %collective-permute-start.12 = (bf16[16,5376]{1,0:T(8,128)(2,1)S(1)}, bf16[16,5376]{1,0:T(8,128)(2,1)S(1)}, u32[]{:S(2)}, u32[]{:S(2)}) collective-permute-start(bf16[16,5376]{1,0:T(8,128)(2,1)S(1)} %get-tuple-element.51), channel_id=1, source_target_pairs={{0,24},{4,28},{8,16},{12,20},{16,8},{20,12},{24,0},{28,4},{1,25},{... | collective-permute-start | bytes 516104 | tf_op jit(solution)/shard_map/ppermute | solution.py:487
  27.1 9.6 %collective-permute-start.13 = (bf16[16,5376]{1,0:T(8,128)(2,1)S(1)}, bf16[16,5376]{1,0:T(8,128)(2,1)S(1)}, u32[]{:S(2)}, u32[]{:S(2)}) collective-permute-start(bf16[16,5376]{1,0:T(8,128)(2,1)S(1)} %get-tuple-element.52), channel_id=1, source_target_pairs={{0,16},{4,20},{8,24},{12,28},{16,0},{20,4},{24,8},{28,12},{1,17},{... | collective-permute-start | bytes 516104 | tf_op jit(solution)/shard_map/ppermute | solution.py:487
  27.7 9.0 %collective-permute-start.14 = (bf16[16,5376]{1,0:T(8,128)(2,1)S(1)}, bf16[16,5376]{1,0:T(8,128)(2,1)S(1)}, u32[]{:S(2)}, u32[]{:S(2)}) collective-permute-start(bf16[16,5376]{1,0:T(8,128)(2,1)S(1)} %get-tuple-element.53), channel_id=1, source_target_pairs={{0,8},{4,12},{8,0},{12,4},{16,24},{20,28},{24,16},{28,20},{1,9},{5... | collective-permute-start | bytes 516104 | tf_op jit(solution)/shard_map/ppermute | solution.py:487

commit v8 on v6

--- a/solution.py
+++ b/solution.py
@@ -51,8 +51,12 @@
 STRIDE = 8
 
 
-def apart(i, pairs):
-    return (pairs - i) % pairs
+def apart(i, half, pairs):
+    if pairs < 4:
+        return i
+    if isinstance(i, int) and isinstance(half, int):
+        return 3 - i if half == 1 and i in (1, 2) else i
+    return jnp.where((half == 1) & ((i == 1) | (i == 2)), 3 - i, i)
 
 
 def padded(pairs):
@@ -76,7 +80,9 @@
         for p in range(parts):
             for i, t in enumerate((last, 0)):
                 source = am[0, p:p + 1, t:t + 1] ^ m
-                code = (slot[0, p:p + 1, t:t + 1] * 2 + source % 2) * padded(pairs) + apart(source // 2, pairs)
+                half = source % 2
+                index = apart(source // 2, (m % 2) ^ half, pairs)
+                code = (slot[0, p:p + 1, t:t + 1] * 2 + half) * padded(pairs) + index
                 row = 2 + i * parts + p
                 trail[row:row + 1, :] = jnp.broadcast_to(code.astype(F32), (1, LANES))
             fields = (st1[p, last:last + 1, :], st0[p, 0:1, :], pb1[0, p, last:last + 1, :], pb0[0, p, 0:1, :])
@@ -98,9 +104,10 @@
                 half = source % 2
                 code = half * rows + slot[c, p:p + 1, :] * tiles + iota((1, tiles), 1)
                 spot = (iota((LANES, tiles), 0) == (2 * c + half) * capacity + rank).astype(F32)
-                pair = jnp.where(iota((pairs, tiles), 0) == apart(source // 2, pairs), (code + 1).astype(F32), 0.0)
+                index = apart(source // 2, m % 2, pairs)
+                pair = jnp.where(iota((pairs, tiles), 0) == index, (code + 1).astype(F32), 0.0)
                 asked = asked + lax.dot_general(pair, spot, (((1,), (1,)), ((), ())), preferred_element_type=F32)
-                column = column_of((2 * apart(source // 2, pairs) + half) * capacity + rank)
+                column = column_of((2 * index + half) * capacity + rank)
                 keys[c, p * tiles:(p + 1) * tiles, :] = jnp.broadcast_to(column, (tiles, LANES))
         for k in range(pairs):
             notes[k][...] = jnp.where(lane < EDGE_AT, asked[k:k + 1, :] - 1.0, edge)
@@ -257,7 +264,7 @@
                 spot += 1
     end = at + groups * share
     for k, out in enumerate(outs):
-        block = share_of(sums, m ^ (2 * apart(k, len(outs))), share)
+        block = share_of(sums, m ^ (2 * apart(k, m % 2, len(outs))), share)
         for g in range(groups):
             out[:, at + g * share:at + (g + 1) * share] = block[g * rows:(g + 1) * rows, :].astype(BF16)
         out[:, end:end + LANES] = misc.astype(BF16)
@@ -342,7 +349,7 @@
 def make_second(pairs, parts, tiles, cells):
     size = padded(pairs)
 
-    def kernel(keys, diff, pert, message, mine, theirs, *refs):
+    def kernel(keys, diff, pert, message, mine, theirs, after, *refs):
         got, prior, low_out, high_out = refs[:pairs], refs[pairs], refs[pairs + 1], refs[pairs + 2]
         below, above = halves(mine[...], theirs[...])
         low, high = edge_windows(message[...], below, above, size, parts)
@@ -452,11 +459,15 @@
         name="prepare",
     )
 
-    def trade(x, k):
-        return lax.ppermute(x, "member", [(i, i ^ k) for i in range(members)])
+    def trade(x):
+        return lax.ppermute(x, "member", [(i, i ^ 1) for i in range(members)])
 
     def exchange(sends):
-        return [sends[0]] + [trade(sends[k], 2 * apart(k, pairs)) for k in range(1, pairs)]
+        got = [sends[0]]
+        for k in range(1, pairs):
+            steps = [(i, i ^ (2 * apart(k, i % 2, pairs))) for i in range(members)]
+            got.append(lax.ppermute(sends[k], "member", steps))
+        return got
 
     notes = exchange(notes)
 
@@ -476,7 +487,7 @@
     (prior,) = call(
         make_first(parts, tiles, cells), [((parts * tiles, cells), BF16)], args, specs, name="forecast_first"
     )
-    other = trade(prior, 1)
+    other = trade(prior)
     size = padded(pairs)
     *sends, half = call(
         make_send(pairs, rows),
@@ -485,16 +496,16 @@
         name="send_first",
     )
     got = exchange(sends)
-    message = jnp.concatenate([half, trade(half, 1)], axis=0)
+    message = jnp.concatenate([half, trade(half)], axis=0)
     steps = []
     for i in range(members):
         first, last = (0, regions - 1) if i % 2 == 0 else (1, regions)
         steps += [(i * regions + r, i * regions + r + 1 - 2 * (i % 2)) for r in range(first, last)]
     mine = lax.ppermute(message, ("member", "region"), steps)
-    theirs = trade(mine, 1)
+    theirs = trade(mine)
     window = ((parts * 2 * size, 2 * LANES), F32)
     sums = [((tiles, cells), F32)]
-    args = [keys, diffusivity, model_perturbation, message, mine, theirs, *got]
+    args = [keys, diffusivity, model_perturbation, message, mine, theirs, where, *got]
     specs = [whole_spec(a.shape) for a in args]
     specs[2] = noise_spec(1)
     second, low, high = call(
@@ -514,7 +525,7 @@
     sends = call(
         make_send_second(pairs, rows, parts, tiles, cells, share),
         [((rows, cells + CYCLES * extra), BF16)] * pairs,
-        [second, trade(second, 1), where, terms, local, *notes, *kept],
+        [second, trade(second), where, terms, local, *notes, *kept],
         scratch=sums,
         name="send_second",
     )

time: 37 us -> 37.3 us (level)
  transfers between devices with their start and end apart: 14 -> 14, of which waited for: 8 -> 7; matrix products, arithmetic and copies ran while one was open for 0% -> 0% of each run, Pallas kernels for 2% -> 2%
where the time goes in v8:
time: 37.3 us; the launch traced here: 37.1 us
  starting transfers between devices  15.7 us (42%)
  waiting for transfers between devices  14 us (38%)
  Pallas kernels  5.91 us (16%)
  between operations  0.82 us (2%)
  local copies, waits for them, and re-layouts  0.67 us (2%)
    ppermute x9, waiting for transfers between devices, exchange(): got.append(lax.ppermute(sends[k], 'member', steps))  11.6 us
    ppermute x9, starting transfers between devices, exchange(): got.append(lax.ppermute(sends[k], 'member', steps))  11.2 us
    pallas_call x8, Pallas kernels, call(): pl.pallas_call(kernel, out_shape=[jax.ShapeDtypeStruct(s, d) for s, d in...  5.91 us
    ppermute x1, starting transfers between devices, body(): mine = lax.ppermute(message, ('member', 'region'), steps)  3.6 us
    ppermute x1, waiting for transfers between devices, body(): mine = lax.ppermute(message, ('member', 'region'), steps)  1.43 us
    ppermute x4, waiting for transfers between devices, trade(): return lax.ppermute(x, 'member', [(i, i ^ 1) for i in range(members)])  0.98 us
    ppermute x4, starting transfers between devices, trade(): return lax.ppermute(x, 'member', [(i, i ^ 1) for i in range(members)])  0.86 us
  transfers between devices with their start and end apart: 14, of which 7 were waited for; matrix products, arithmetic and copies ran while one was open for 0% of the time, Pallas kernels for 2%

profile of v8, /device:TPU:0, one launch (start us, length us, event | category | flops | bytes accessed | tf_op | source)
XLA Modules:
  0.0 37.1 jit_solution(5946774600091845720)
XLA Ops:
  0.6 0.0 copy-start
  0.6 0.0 copy-start.1
  0.7 1.3 %prepare.1 = (f32[1,128]{1,0:T(1,128)S(1)}, f32[1,128]{1,0:T(1,128)S(1)}, f32[1,128]{1,0:T(1,128)S(1)}, f32[1,128]{1,0:T(1,128)S(1)}, f32[8,128]{1,0:T(8,128)S(1)}, /*index=5*/s32[2,32,128]{2,1,0:T(8,128)S(1)}) custom-call(bf16[2,16,4096]{2,1,0:T(8,128)(2,1)} %state.1, bf16[2,16,4096]{2,1,0:T(8,128)(2,1)} %state.1, f32[16,4096]{1,0:T(8,128)} %diff.3, ...), custom_call_target="tpu_custom_call" | custom-call | tf_op jit(solution)/shard_map/prepare/pallas_call | solution.py:28
  2.0 0.0 copy-done
  2.0 0.0 copy-done.1
  2.0 0.0 copy-done.2
  2.0 0.6 %forecast_first.1.own = bf16[32,4096]{1,0:T(8,128)(2,1)S(1)} custom-call(bf16[2,16,4096]{2,1,0:T(8,128)(2,1)S(1)} %copy-done.2, f32[16,4096]{1,0:T(8,128)S(1)} %copy-done.1, bf16[2,2,16,4096]{3,2,1,0:T(8,128)(2,1)S(1)} %copy-done, f32[8,128]{1,0:T(8,128)S(1)} %get-tuple-element.28.after.trail), custom_call_target="tpu_custom_call" | custom-call | tf_op jit(solution)/shard_map/forecast_first/pallas_call | solution.py:28
  2.7 0.5 %collective-permute-start = (bf16[32,4096]{1,0:T(8,128)(2,1)S(1)}, bf16[32,4096]{1,0:T(8,128)(2,1)S(1)}, u32[]{:S(2)}, u32[]{:S(2)}) collective-permute-start(bf16[32,4096]{1,0:T(8,128)(2,1)S(1)} %forecast_first.1.own), channel_id=1, source_target_pairs={{0,4},{4,0},{8,12},{12,8},{16,20},{20,16},{24,28},{28,24},{1,5},{5... | collective-permute-start | bytes 786440 | tf_op jit(solution)/shard_map/ppermute | solution.py:463
  3.2 2.6 %collective-permute-start.1 = (f32[1,128]{1,0:T(1,128)S(1)}, f32[1,128]{1,0:T(1,128)S(1)}, u32[]{:S(2)}, u32[]{:S(2)}) collective-permute-start(f32[1,128]{1,0:T(1,128)S(1)} %get-tuple-element.30), channel_id=1, source_target_pairs={{0,8},{4,20},{8,0},{12,28},{16,24},{20,4},{24,16},{28,12},{1,9},{5... | collective-permute-start | bytes 1544 | tf_op jit(solution)/shard_map/ppermute | solution.py:469
  5.7 1.5 %collective-permute-start.2 = (f32[1,128]{1,0:T(1,128)S(1)}, f32[1,128]{1,0:T(1,128)S(1)}, u32[]{:S(2)}, u32[]{:S(2)}) collective-permute-start(f32[1,128]{1,0:T(1,128)S(1)} %get-tuple-element.31), channel_id=1, source_target_pairs={{0,16},{4,12},{8,24},{12,4},{16,0},{20,28},{24,8},{28,20},{1,17},{... | collective-permute-start | bytes 1544 | tf_op jit(solution)/shard_map/ppermute | solution.py:469
  7.3 0.0 collective-permute-start.3
  7.3 0.0 collective-permute-done.1.refs_1_
  7.3 2.0 %collective-permute-done.2.refs_2_ = f32[1,128]{1,0:T(1,128)S(1)} collective-permute-done((f32[1,128]{1,0:T(1,128)S(1)}, f32[1,128]{1,0:T(1,128)S(1)}, u32[]{:S(2)}, u32[]{:S(2)}) %collective-permute-start.2) | collective-permute-done | bytes 544 | tf_op jit(solution)/shard_map/ppermute | solution.py:469
  9.3 2.4 %collective-permute-done.3.refs_3_ = f32[1,128]{1,0:T(1,128)S(1)} collective-permute-done((f32[1,128]{1,0:T(1,128)S(1)}, f32[1,128]{1,0:T(1,128)S(1)}, u32[]{:S(2)}, u32[]{:S(2)}) %collective-permute-start.3) | collective-permute-done | bytes 544 | tf_op jit(solution)/shard_map/ppermute | solution.py:469
  11.7 0.0 collective-permute-done.other
  11.7 0.4 send_first.1
  12.1 0.0 copy-start.6
  12.1 0.0 copy-start.7
  12.1 0.1 collective-permute-start.4
  12.2 0.0 copy-start.3
  12.2 0.6 %collective-permute-start.7 = (bf16[16,4096]{1,0:T(8,128)(2,1)S(1)}, bf16[16,4096]{1,0:T(8,128)(2,1)S(1)}, u32[]{:S(2)}, u32[]{:S(2)}) collective-permute-start(bf16[16,4096]{1,0:T(8,128)(2,1)S(1)} %get-tuple-element.36), channel_id=1, source_target_pairs={{0,8},{4,20},{8,0},{12,28},{16,24},{20,4},{24,16},{28,12},{1,9},{5... | collective-permute-start | bytes 393224 | tf_op jit(solution)/shard_map/ppermute | solution.py:469
  12.8 0.1 collective-permute-start.8
  12.8 2.9 %collective-permute-start.9 = (bf16[16,4096]{1,0:T(8,128)(2,1)S(1)}, bf16[16,4096]{1,0:T(8,128)(2,1)S(1)}, u32[]{:S(2)}, u32[]{:S(2)}) collective-permute-start(bf16[16,4096]{1,0:T(8,128)(2,1)S(1)} %get-tuple-element.38), channel_id=1, source_target_pairs={{0,24},{4,28},{8,16},{12,20},{16,8},{20,12},{24,0},{28,4},{1,25},{... | collective-permute-start | bytes 393224 | tf_op jit(solution)/shard_map/ppermute | solution.py:469
  15.8 0.0 collective-permute-done.4
  15.8 3.6 %collective-permute-start.5 = (f32[32,128]{1,0:T(8,128)S(1)}, f32[32,128]{1,0:T(8,128)S(1)}, u32[]{:S(2)}, u32[]{:S(2)}) collective-permute-start(f32[32,128]{1,0:T(8,128)S(1)} %constant_dynamic-update-slice_fusion.message), channel_id=1, source_target_pairs={{0,1},{1,2},{2,3},{5,4},{6,5},{7,6},{8,9},{9,10},{10,11},{13,12},{... | collective-permute-start | bytes 49160 | tf_op jit(solution)/shard_map/ppermute | solution.py:504
  19.4 1.4 %collective-permute-done.5.mine = f32[32,128]{1,0:T(8,128)S(1)} collective-permute-done((f32[32,128]{1,0:T(8,128)S(1)}, f32[32,128]{1,0:T(8,128)S(1)}, u32[]{:S(2)}, u32[]{:S(2)}) %collective-permute-start.5) | collective-permute-done | bytes 16416 | tf_op jit(solution)/shard_map/ppermute | solution.py:504
  20.8 0.0 collective-permute-start.6
  20.8 0.0 copy-done.7
  20.8 0.0 copy-done.3
  20.8 0.0 copy-done.4
  20.8 0.6 %copy-done.8 = s32[32]{0:T(128)S(1)} copy-done((s32[32]{0:T(128)S(1)}, s32[32]{0:T(128)}, u32[]{:S(2)}) %copy-start.8) | copy-done | bytes 152
  21.5 0.2 observe.1
  21.6 0.3 collective-permute-done.6.theirs
  22.0 0.0 collective-permute-done.7.refs_1_
  22.0 0.0 collective-permute-done.8.refs_2_
  22.0 0.0 collective-permute-done.9.refs_3_
  22.0 0.9 %forecast_second.1 = (bf16[32,4096]{1,0:T(8,128)(2,1)S(1)}, f32[32,256]{1,0:T(8,128)S(1)}, f32[32,256]{1,0:T(8,128)S(1)}) custom-call(s32[2,32,128]{2,1,0:T(8,128)S(1)} %get-tuple-element.27.keys, f32[16,4096]{1,0:T(8,128)S(1)} %copy-done.1, bf16[2,2,16,4096]{3,2,1,0:T(8,128)(2,1)S(1)} %copy-done, f32[32,128]{1,0:T(8,128)S(1)} %constant_dynamic-update-slice_fusion.message, ...), custom_call_target="tpu_custom_call" | custom-call | tf_op jit(solution)/shard_map/forecast_second/pallas_call | solution.py:28
  22.9 0.3 collective-permute-start.10
  23.1 0.7 %assess_first.1 = (bf16[16,640]{1,0:T(8,128)(2,1)S(1)}, bf16[16,640]{1,0:T(8,128)(2,1)S(1)}, bf16[16,640]{1,0:T(8,128)(2,1)S(1)}, bf16[16,640]{1,0:T(8,128)(2,1)S(1)}) custom-call(bf16[32,4096]{1,0:T(8,128)(2,1)S(1)} %forecast_first.1.own, bf16[32,4096]{1,0:T(8,128)(2,1)S(1)} %collective-permute-done.other, f32[32,256]{1,0:T(8,128)S(1)} %get-tuple-element.42.low, ...), custom_call_target="tpu_custom_call" | custom-call | tf_op jit(solution)/shard_map/assess_first/pallas_call | solution.py:28
  23.8 0.6 %collective-permute-done.10.other = bf16[32,4096]{1,0:T(8,128)(2,1)S(1)} collective-permute-done((bf16[32,4096]{1,0:T(8,128)(2,1)S(1)}, bf16[32,4096]{1,0:T(8,128)(2,1)S(1)}, u32[]{:S(2)}, u32[]{:S(2)}) %collective-permute-start.10) | collective-permute-done | bytes 262176 | tf_op jit(solution)/shard_map/ppermute | solution.py:463
  24.5 0.9 %send_second.1 = (bf16[16,5376]{1,0:T(8,128)(2,1)S(1)}, bf16[16,5376]{1,0:T(8,128)(2,1)S(1)}, bf16[16,5376]{1,0:T(8,128)(2,1)S(1)}, bf16[16,5376]{1,0:T(8,128)(2,1)S(1)}) custom-call(bf16[32,4096]{1,0:T(8,128)(2,1)S(1)} %get-tuple-element.39.own, bf16[32,4096]{1,0:T(8,128)(2,1)S(1)} %collective-permute-done.10.other, ...), custom_call_target="tpu_custom_call" | custom-call | tf_op jit(solution)/shard_map/send_second/pallas_call | solution.py:28
  25.4 0.6 %collective-permute-start.11 = (bf16[16,5376]{1,0:T(8,128)(2,1)S(1)}, bf16[16,5376]{1,0:T(8,128)(2,1)S(1)}, u32[]{:S(2)}, u32[]{:S(2)}) collective-permute-start(bf16[16,5376]{1,0:T(8,128)(2,1)S(1)} %get-tuple-element.49), channel_id=1, source_target_pairs={{0,8},{4,20},{8,0},{12,28},{16,24},{20,4},{24,16},{28,12},{1,9},{5... | collective-permute-start | bytes 516104 | tf_op jit(solution)/shard_map/ppermute | solution.py:469
  26.0 0.5 %collective-permute-start.12 = (bf16[16,5376]{1,0:T(8,128)(2,1)S(1)}, bf16[16,5376]{1,0:T(8,128)(2,1)S(1)}, u32[]{:S(2)}, u32[]{:S(2)}) collective-permute-start(bf16[16,5376]{1,0:T(8,128)(2,1)S(1)} %get-tuple-element.50), channel_id=1, source_target_pairs={{0,16},{4,12},{8,24},{12,4},{16,0},{20,28},{24,8},{28,20},{1,17},{... | collective-permute-start | bytes 516104 | tf_op jit(solution)/shard_map/ppermute | solution.py:469
  26.5 2.5 %collective-permute-start.13 = (bf16[16,5376]{1,0:T(8,128)(2,1)S(1)}, bf16[16,5376]{1,0:T(8,128)(2,1)S(1)}, u32[]{:S(2)}, u32[]{:S(2)}) collective-permute-start(bf16[16,5376]{1,0:T(8,128)(2,1)S(1)} %get-tuple-element.51), channel_id=1, source_target_pairs={{0,24},{4,28},{8,16},{12,20},{16,8},{20,12},{24,0},{28,4},{1,25},{... | collective-permute-start | bytes 516104 | tf_op jit(solution)/shard_map/ppermute | solution.py:469
  29.0 3.7 %collective-permute-done.11.refs_1_ = bf16[16,5376]{1,0:T(8,128)(2,1)S(1)} collective-permute-done((bf16[16,5376]{1,0:T(8,128)(2,1)S(1)}, bf16[16,5376]{1,0:T(8,128)(2,1)S(1)}, u32[]{:S(2)}, u32[]{:S(2)}) %collective-permute-start.11) | collective-permute-done | bytes 172064 | tf_op jit(solution)/shard_map/ppermute | solution.py:469
  32.6 0.0 collective-permute-done.12.refs_2_
  32.6 3.5 %collective-permute-done.13.refs_3_ = bf16[16,5376]{1,0:T(8,128)(2,1)S(1)} collective-permute-done((bf16[16,5376]{1,0:T(8,128)(2,1)S(1)}, bf16[16,5376]{1,0:T(8,128)(2,1)S(1)}, u32[]{:S(2)}, u32[]{:S(2)}) %collective-permute-start.13) | collective-permute-done | bytes 172064 | tf_op jit(solution)/shard_map/ppermute | solution.py:469
  36.1 0.9 %finish.1 = (bf16[2,16,4096]{2,1,0:T(8,128)(2,1)}, f32[2,16,512]{2,1,0:T(8,128)}) custom-call(s32[2,32,128]{2,1,0:T(8,128)S(1)} %get-tuple-element.27.keys, bf16[16,5376]{1,0:T(8,128)(2,1)S(1)} %get-tuple-element.48.refs_0_, bf16[16,5376]{1,0:T(8,128)(2,1)S(1)} %collective-permute-done.11.refs_1_, bf16[16,5376]{1,0:T(8,128)(2,1)S(1)} %collective-permute-done.12.refs_2_, ...), custom_call_target="tpu_custom_call" | custom-call | tf_op jit(solution)/shard_map/finish/pallas_call | solution.py:28
  (8 shorter events, 0.0 us)
Async XLA Ops:
  0.6 1.3 %copy-start = (bf16[2,2,16,4096]{3,2,1,0:T(8,128)(2,1)S(1)}, bf16[2,2,16,4096]{3,2,1,0:T(8,128)(2,1)}, u32[]{:S(2)}) copy-start(bf16[2,2,16,4096]{3,2,1,0:T(8,128)(2,1)} %pert.3) | copy-start | bytes 1572868
  0.6 1.4 %copy-start.1 = (f32[16,4096]{1,0:T(8,128)S(1)}, f32[16,4096]{1,0:T(8,128)}, u32[]{:S(2)}) copy-start(f32[16,4096]{1,0:T(8,128)} %diff.3) | copy-start | bytes 786436
  0.7 1.4 %copy-start.2 = (bf16[2,16,4096]{2,1,0:T(8,128)(2,1)S(1)}, bf16[2,16,4096]{2,1,0:T(8,128)(2,1)}, u32[]{:S(2)}) copy-start(bf16[2,16,4096]{2,1,0:T(8,128)(2,1)} %state.1) | copy-start | bytes 786436
  2.7 9.0 %collective-permute-start = (bf16[32,4096]{1,0:T(8,128)(2,1)S(1)}, bf16[32,4096]{1,0:T(8,128)(2,1)S(1)}, u32[]{:S(2)}, u32[]{:S(2)}) collective-permute-start(bf16[32,4096]{1,0:T(8,128)(2,1)S(1)} %forecast_first.1.own), channel_id=1, source_target_pairs={{0,4},{4,0},{8,12},{12,8},{16,20},{20,16},{24,28},{28,24},{1,5},{5... | collective-permute-start | bytes 786440 | tf_op jit(solution)/shard_map/ppermute | solution.py:463
  3.2 4.1 %collective-permute-start.1 = (f32[1,128]{1,0:T(1,128)S(1)}, f32[1,128]{1,0:T(1,128)S(1)}, u32[]{:S(2)}, u32[]{:S(2)}) collective-permute-start(f32[1,128]{1,0:T(1,128)S(1)} %get-tuple-element.30), channel_id=1, source_target_pairs={{0,8},{4,20},{8,0},{12,28},{16,24},{20,4},{24,16},{28,12},{1,9},{5... | collective-permute-start | bytes 1544 | tf_op jit(solution)/shard_map/ppermute | solution.py:469
  5.7 3.5 %collective-permute-start.2 = (f32[1,128]{1,0:T(1,128)S(1)}, f32[1,128]{1,0:T(1,128)S(1)}, u32[]{:S(2)}, u32[]{:S(2)}) collective-permute-start(f32[1,128]{1,0:T(1,128)S(1)} %get-tuple-element.31), channel_id=1, source_target_pairs={{0,16},{4,12},{8,24},{12,4},{16,0},{20,28},{24,8},{28,20},{1,17},{... | collective-permute-start | bytes 1544 | tf_op jit(solution)/shard_map/ppermute | solution.py:469
  7.3 4.4 %collective-permute-start.3 = (f32[1,128]{1,0:T(1,128)S(1)}, f32[1,128]{1,0:T(1,128)S(1)}, u32[]{:S(2)}, u32[]{:S(2)}) collective-permute-start(f32[1,128]{1,0:T(1,128)S(1)} %get-tuple-element.32), channel_id=1, source_target_pairs={{0,24},{4,28},{8,16},{12,20},{16,8},{20,12},{24,0},{28,4},{1,25},{... | collective-permute-start | bytes 1544 | tf_op jit(solution)/shard_map/ppermute | solution.py:469
  11.7 9.1 %copy-start.5 = (f32[32,16]{0,1:T(8,128)S(1)}, f32[32,16]{0,1:T(8,128)}, u32[]{:S(2)}) copy-start(f32[32,16]{0,1:T(8,128)} %param.15) | copy-start | bytes 6148
  12.1 8.7 %copy-start.6 = (s32[16,6]{0,1:T(8,128)S(1)}, s32[16,6]{0,1:T(8,128)}, u32[]{:S(2)}) copy-start(s32[16,6]{0,1:T(8,128)} %param.18) | copy-start | bytes 1156
  12.1 8.7 %copy-start.7 = (f32[16,6]{0,1:T(8,128)S(1)}, f32[16,6]{0,1:T(8,128)}, u32[]{:S(2)}) copy-start(f32[16,6]{0,1:T(8,128)} %param.19) | copy-start | bytes 1156
  12.1 3.7 %collective-permute-start.4 = (f32[16,128]{1,0:T(8,128)S(1)}, f32[16,128]{1,0:T(8,128)S(1)}, u32[]{:S(2)}, u32[]{:S(2)}) collective-permute-start(f32[16,128]{1,0:T(8,128)S(1)} %get-tuple-element.33), channel_id=1, source_target_pairs={{0,4},{4,0},{8,12},{12,8},{16,20},{20,16},{24,28},{28,24},{1,5},{5... | collective-permute-start | bytes 24584 | tf_op jit(solution)/shard_map/ppermute | solution.py:463
  12.2 8.6 %copy-start.3 = (f32[2,32,16]{1,2,0:T(8,128)S(1)}, f32[2,32,16]{1,2,0:T(8,128)}, u32[]{:S(2)}) copy-start(f32[2,32,16]{1,2,0:T(8,128)} %param.14) | copy-start | bytes 12292
  12.2 9.8 %collective-permute-start.7 = (bf16[16,4096]{1,0:T(8,128)(2,1)S(1)}, bf16[16,4096]{1,0:T(8,128)(2,1)S(1)}, u32[]{:S(2)}, u32[]{:S(2)}) collective-permute-start(bf16[16,4096]{1,0:T(8,128)(2,1)S(1)} %get-tuple-element.36), channel_id=1, source_target_pairs={{0,8},{4,20},{8,0},{12,28},{16,24},{20,4},{24,16},{28,12},{1,9},{5... | collective-permute-start | bytes 393224 | tf_op jit(solution)/shard_map/ppermute | solution.py:469
  12.8 9.2 %collective-permute-start.8 = (bf16[16,4096]{1,0:T(8,128)(2,1)S(1)}, bf16[16,4096]{1,0:T(8,128)(2,1)S(1)}, u32[]{:S(2)}, u32[]{:S(2)}) collective-permute-start(bf16[16,4096]{1,0:T(8,128)(2,1)S(1)} %get-tuple-element.37), channel_id=1, source_target_pairs={{0,16},{4,12},{8,24},{12,4},{16,0},{20,28},{24,8},{28,20},{1,17},{... | collective-permute-start | bytes 393224 | tf_op jit(solution)/shard_map/ppermute | solution.py:469
  12.8 9.1 %collective-permute-start.9 = (bf16[16,4096]{1,0:T(8,128)(2,1)S(1)}, bf16[16,4096]{1,0:T(8,128)(2,1)S(1)}, u32[]{:S(2)}, u32[]{:S(2)}) collective-permute-start(bf16[16,4096]{1,0:T(8,128)(2,1)S(1)} %get-tuple-element.38), channel_id=1, source_target_pairs={{0,24},{4,28},{8,16},{12,20},{16,8},{20,12},{24,0},{28,4},{1,25},{... | collective-permute-start | bytes 393224 | tf_op jit(solution)/shard_map/ppermute | solution.py:469
  15.8 5.1 %copy-start.4 = (s32[32,16]{0,1:T(8,128)S(1)}, s32[32,16]{0,1:T(8,128)}, u32[]{:S(2)}) copy-start(s32[32,16]{0,1:T(8,128)} %param.17) | copy-start | bytes 6148
  15.8 5.0 %collective-permute-start.5 = (f32[32,128]{1,0:T(8,128)S(1)}, f32[32,128]{1,0:T(8,128)S(1)}, u32[]{:S(2)}, u32[]{:S(2)}) collective-permute-start(f32[32,128]{1,0:T(8,128)S(1)} %constant_dynamic-update-slice_fusion.message), channel_id=1, source_target_pairs={{0,1},{1,2},{2,3},{5,4},{6,5},{7,6},{8,9},{9,10},{10,11},{13,12},{... | collective-permute-start | bytes 49160 | tf_op jit(solution)/shard_map/ppermute | solution.py:504
  20.8 1.2 %collective-permute-start.6 = (f32[32,128]{1,0:T(8,128)S(1)}, f32[32,128]{1,0:T(8,128)S(1)}, u32[]{:S(2)}, u32[]{:S(2)}) collective-permute-start(f32[32,128]{1,0:T(8,128)S(1)} %collective-permute-done.5.mine), channel_id=1, source_target_pairs={{0,4},{4,0},{8,12},{12,8},{16,20},{20,16},{24,28},{28,24},{1,5},{5... | collective-permute-start | bytes 49160 | tf_op jit(solution)/shard_map/ppermute | solution.py:463
  20.8 0.7 %copy-start.8 = (s32[32]{0:T(128)S(1)}, s32[32]{0:T(128)}, u32[]{:S(2)}) copy-start(s32[32]{0:T(128)} %param.16) | copy-start | bytes 388
  22.9 1.6 %collective-permute-start.10 = (bf16[32,4096]{1,0:T(8,128)(2,1)S(1)}, bf16[32,4096]{1,0:T(8,128)(2,1)S(1)}, u32[]{:S(2)}, u32[]{:S(2)}) collective-permute-start(bf16[32,4096]{1,0:T(8,128)(2,1)S(1)} %get-tuple-element.39.own), channel_id=1, source_target_pairs={{0,4},{4,0},{8,12},{12,8},{16,20},{20,16},{24,28},{28,24},{1,5},{5... | collective-permute-start | bytes 786440 | tf_op jit(solution)/shard_map/ppermute | solution.py:463
  25.4 7.2 %collective-permute-start.11 = (bf16[16,5376]{1,0:T(8,128)(2,1)S(1)}, bf16[16,5376]{1,0:T(8,128)(2,1)S(1)}, u32[]{:S(2)}, u32[]{:S(2)}) collective-permute-start(bf16[16,5376]{1,0:T(8,128)(2,1)S(1)} %get-tuple-element.49), channel_id=1, source_target_pairs={{0,8},{4,20},{8,0},{12,28},{16,24},{20,4},{24,16},{28,12},{1,9},{5... | collective-permute-start | bytes 516104 | tf_op jit(solution)/shard_map/ppermute | solution.py:469
  26.0 6.7 %collective-permute-start.12 = (bf16[16,5376]{1,0:T(8,128)(2,1)S(1)}, bf16[16,5376]{1,0:T(8,128)(2,1)S(1)}, u32[]{:S(2)}, u32[]{:S(2)}) collective-permute-start(bf16[16,5376]{1,0:T(8,128)(2,1)S(1)} %get-tuple-element.50), channel_id=1, source_target_pairs={{0,16},{4,12},{8,24},{12,4},{16,0},{20,28},{24,8},{28,20},{1,17},{... | collective-permute-start | bytes 516104 | tf_op jit(solution)/shard_map/ppermute | solution.py:469
  26.5 9.6 %collective-permute-start.13 = (bf16[16,5376]{1,0:T(8,128)(2,1)S(1)}, bf16[16,5376]{1,0:T(8,128)(2,1)S(1)}, u32[]{:S(2)}, u32[]{:S(2)}) collective-permute-start(bf16[16,5376]{1,0:T(8,128)(2,1)S(1)} %get-tuple-element.51), channel_id=1, source_target_pairs={{0,24},{4,28},{8,16},{12,20},{16,8},{20,12},{24,0},{28,4},{1,25},{... | collective-permute-start | bytes 516104 | tf_op jit(solution)/shard_map/ppermute | solution.py:469

commit v9 on v8

--- a/solution.py
+++ b/solution.py
@@ -51,14 +51,6 @@
 STRIDE = 8
 
 
-def apart(i, half, pairs):
-    if pairs < 4:
-        return i
-    if isinstance(i, int) and isinstance(half, int):
-        return 3 - i if half == 1 and i in (1, 2) else i
-    return jnp.where((half == 1) & ((i == 1) | (i == 2)), 3 - i, i)
-
-
 def padded(pairs):
     return max(8, pairs)
 
@@ -80,9 +72,7 @@
         for p in range(parts):
             for i, t in enumerate((last, 0)):
                 source = am[0, p:p + 1, t:t + 1] ^ m
-                half = source % 2
-                index = apart(source // 2, (m % 2) ^ half, pairs)
-                code = (slot[0, p:p + 1, t:t + 1] * 2 + half) * padded(pairs) + index
+                code = (slot[0, p:p + 1, t:t + 1] * 2 + source % 2) * padded(pairs) + source // 2
                 row = 2 + i * parts + p
                 trail[row:row + 1, :] = jnp.broadcast_to(code.astype(F32), (1, LANES))
             fields = (st1[p, last:last + 1, :], st0[p, 0:1, :], pb1[0, p, last:last + 1, :], pb0[0, p, 0:1, :])
@@ -104,10 +94,9 @@
                 half = source % 2
                 code = half * rows + slot[c, p:p + 1, :] * tiles + iota((1, tiles), 1)
                 spot = (iota((LANES, tiles), 0) == (2 * c + half) * capacity + rank).astype(F32)
-                index = apart(source // 2, m % 2, pairs)
-                pair = jnp.where(iota((pairs, tiles), 0) == index, (code + 1).astype(F32), 0.0)
+                pair = jnp.where(iota((pairs, tiles), 0) == source // 2, (code + 1).astype(F32), 0.0)
                 asked = asked + lax.dot_general(pair, spot, (((1,), (1,)), ((), ())), preferred_element_type=F32)
-                column = column_of((2 * index + half) * capacity + rank)
+                column = column_of(source * capacity + rank)
                 keys[c, p * tiles:(p + 1) * tiles, :] = jnp.broadcast_to(column, (tiles, LANES))
         for k in range(pairs):
             notes[k][...] = jnp.where(lane < EDGE_AT, asked[k:k + 1, :] - 1.0, edge)
@@ -264,7 +253,7 @@
                 spot += 1
     end = at + groups * share
     for k, out in enumerate(outs):
-        block = share_of(sums, m ^ (2 * apart(k, m % 2, len(outs))), share)
+        block = share_of(sums, m ^ (2 * k), share)
         for g in range(groups):
             out[:, at + g * share:at + (g + 1) * share] = block[g * rows:(g + 1) * rows, :].astype(BF16)
         out[:, end:end + LANES] = misc.astype(BF16)
@@ -465,8 +454,7 @@
     def exchange(sends):
         got = [sends[0]]
         for k in range(1, pairs):
-            steps = [(i, i ^ (2 * apart(k, i % 2, pairs))) for i in range(members)]
-            got.append(lax.ppermute(sends[k], "member", steps))
+            got.append(lax.ppermute(sends[k], "member", [(i, i ^ (2 * k)) for i in range(members)]))
         return got
 
     notes = exchange(notes)

time: 37.3 us -> 37.1 us (level)
  no operation moved by 1% of the time
where the time goes in v9:
time: 37.1 us; the launch traced here: 36.9 us
  starting transfers between devices  15.7 us (42%)
  waiting for transfers between devices  13.8 us (37%)
  Pallas kernels  5.91 us (16%)
  between operations  0.82 us (2%)
  local copies, waits for them, and re-layouts  0.67 us (2%)
    ppermute x9, waiting for transfers between devices, exchange(): lax.ppermute(sends[k], 'member', [(i, i ^ 2 * k) for i in range(members)])  11.4 us
    ppermute x9, starting transfers between devices, exchange(): lax.ppermute(sends[k], 'member', [(i, i ^ 2 * k) for i in range(members)])  11.2 us
    pallas_call x8, Pallas kernels, call(): pl.pallas_call(kernel, out_shape=[jax.ShapeDtypeStruct(s, d) for s, d in...  5.91 us
    ppermute x1, starting transfers between devices, body(): mine = lax.ppermute(message, ('member', 'region'), steps)  3.6 us
    ppermute x1, waiting for transfers between devices, body(): mine = lax.ppermute(message, ('member', 'region'), steps)  1.43 us
    ppermute x4, waiting for transfers between devices, trade(): return lax.ppermute(x, 'member', [(i, i ^ 1) for i in range(members)])  0.98 us
    ppermute x4, starting transfers between devices, trade(): return lax.ppermute(x, 'member', [(i, i ^ 1) for i in range(members)])  0.86 us
  transfers between devices with their start and end apart: 14, of which 7 were waited for; matrix products, arithmetic and copies ran while one was open for 0% of the time, Pallas kernels for 2%

profile of v9, /device:TPU:0, one launch (start us, length us, event | category | flops | bytes accessed | tf_op | source)
XLA Modules:
  0.0 36.9 jit_solution(5737195643979414687)
XLA Ops:
  0.6 0.0 copy-start
  0.6 0.0 copy-start.1
  0.7 1.3 %prepare.1 = (f32[1,128]{1,0:T(1,128)S(1)}, f32[1,128]{1,0:T(1,128)S(1)}, f32[1,128]{1,0:T(1,128)S(1)}, f32[1,128]{1,0:T(1,128)S(1)}, f32[8,128]{1,0:T(8,128)S(1)}, /*index=5*/s32[2,32,128]{2,1,0:T(8,128)S(1)}) custom-call(bf16[2,16,4096]{2,1,0:T(8,128)(2,1)} %state.1, bf16[2,16,4096]{2,1,0:T(8,128)(2,1)} %state.1, f32[16,4096]{1,0:T(8,128)} %diff.3, ...), custom_call_target="tpu_custom_call" | custom-call | tf_op jit(solution)/shard_map/prepare/pallas_call | solution.py:28
  2.0 0.0 copy-done.1
  2.0 0.0 copy-done.2
  2.0 0.6 %forecast_first.1.own = bf16[32,4096]{1,0:T(8,128)(2,1)S(1)} custom-call(bf16[2,16,4096]{2,1,0:T(8,128)(2,1)S(1)} %copy-done.2, f32[16,4096]{1,0:T(8,128)S(1)} %copy-done.1, bf16[2,2,16,4096]{3,2,1,0:T(8,128)(2,1)S(1)} %copy-done, f32[8,128]{1,0:T(8,128)S(1)} %get-tuple-element.28.after.trail), custom_call_target="tpu_custom_call" | custom-call | tf_op jit(solution)/shard_map/forecast_first/pallas_call | solution.py:28
  2.7 0.5 %collective-permute-start = (bf16[32,4096]{1,0:T(8,128)(2,1)S(1)}, bf16[32,4096]{1,0:T(8,128)(2,1)S(1)}, u32[]{:S(2)}, u32[]{:S(2)}) collective-permute-start(bf16[32,4096]{1,0:T(8,128)(2,1)S(1)} %forecast_first.1.own), channel_id=1, source_target_pairs={{0,4},{4,0},{8,12},{12,8},{16,20},{20,16},{24,28},{28,24},{1,5},{5... | collective-permute-start | bytes 786440 | tf_op jit(solution)/shard_map/ppermute | solution.py:452
  3.2 2.6 %collective-permute-start.1 = (f32[1,128]{1,0:T(1,128)S(1)}, f32[1,128]{1,0:T(1,128)S(1)}, u32[]{:S(2)}, u32[]{:S(2)}) collective-permute-start(f32[1,128]{1,0:T(1,128)S(1)} %get-tuple-element.30), channel_id=1, source_target_pairs={{0,8},{4,12},{8,0},{12,4},{16,24},{20,28},{24,16},{28,20},{1,9},{5... | collective-permute-start | bytes 1544 | tf_op jit(solution)/shard_map/ppermute | solution.py:457
  5.7 1.5 %collective-permute-start.2 = (f32[1,128]{1,0:T(1,128)S(1)}, f32[1,128]{1,0:T(1,128)S(1)}, u32[]{:S(2)}, u32[]{:S(2)}) collective-permute-start(f32[1,128]{1,0:T(1,128)S(1)} %get-tuple-element.31), channel_id=1, source_target_pairs={{0,16},{4,20},{8,24},{12,28},{16,0},{20,4},{24,8},{28,12},{1,17},{... | collective-permute-start | bytes 1544 | tf_op jit(solution)/shard_map/ppermute | solution.py:457
  7.3 0.0 collective-permute-start.3
  7.3 0.0 collective-permute-done.1.refs_1_
  7.3 2.0 %collective-permute-done.2.refs_2_ = f32[1,128]{1,0:T(1,128)S(1)} collective-permute-done((f32[1,128]{1,0:T(1,128)S(1)}, f32[1,128]{1,0:T(1,128)S(1)}, u32[]{:S(2)}, u32[]{:S(2)}) %collective-permute-start.2) | collective-permute-done | bytes 544 | tf_op jit(solution)/shard_map/ppermute | solution.py:457
  9.3 2.4 %collective-permute-done.3.refs_3_ = f32[1,128]{1,0:T(1,128)S(1)} collective-permute-done((f32[1,128]{1,0:T(1,128)S(1)}, f32[1,128]{1,0:T(1,128)S(1)}, u32[]{:S(2)}, u32[]{:S(2)}) %collective-permute-start.3) | collective-permute-done | bytes 544 | tf_op jit(solution)/shard_map/ppermute | solution.py:457
  11.7 0.0 collective-permute-done.other
  11.7 0.4 send_first.1
  12.1 0.0 copy-start.6
  12.1 0.0 copy-start.7
  12.1 0.1 collective-permute-start.4
  12.2 0.0 copy-start.3
  12.2 0.6 %collective-permute-start.7 = (bf16[16,4096]{1,0:T(8,128)(2,1)S(1)}, bf16[16,4096]{1,0:T(8,128)(2,1)S(1)}, u32[]{:S(2)}, u32[]{:S(2)}) collective-permute-start(bf16[16,4096]{1,0:T(8,128)(2,1)S(1)} %get-tuple-element.36), channel_id=1, source_target_pairs={{0,8},{4,12},{8,0},{12,4},{16,24},{20,28},{24,16},{28,20},{1,9},{5... | collective-permute-start | bytes 393224 | tf_op jit(solution)/shard_map/ppermute | solution.py:457
  12.8 0.1 collective-permute-start.8
  12.8 2.9 %collective-permute-start.9 = (bf16[16,4096]{1,0:T(8,128)(2,1)S(1)}, bf16[16,4096]{1,0:T(8,128)(2,1)S(1)}, u32[]{:S(2)}, u32[]{:S(2)}) collective-permute-start(bf16[16,4096]{1,0:T(8,128)(2,1)S(1)} %get-tuple-element.38), channel_id=1, source_target_pairs={{0,24},{4,28},{8,16},{12,20},{16,8},{20,12},{24,0},{28,4},{1,25},{... | collective-permute-start | bytes 393224 | tf_op jit(solution)/shard_map/ppermute | solution.py:457
  15.8 0.0 collective-permute-done.4
  15.8 3.6 %collective-permute-start.5 = (f32[32,128]{1,0:T(8,128)S(1)}, f32[32,128]{1,0:T(8,128)S(1)}, u32[]{:S(2)}, u32[]{:S(2)}) collective-permute-start(f32[32,128]{1,0:T(8,128)S(1)} %constant_dynamic-update-slice_fusion.message), channel_id=1, source_target_pairs={{0,1},{1,2},{2,3},{5,4},{6,5},{7,6},{8,9},{9,10},{10,11},{13,12},{... | collective-permute-start | bytes 49160 | tf_op jit(solution)/shard_map/ppermute | solution.py:492
  19.4 1.4 %collective-permute-done.5.mine = f32[32,128]{1,0:T(8,128)S(1)} collective-permute-done((f32[32,128]{1,0:T(8,128)S(1)}, f32[32,128]{1,0:T(8,128)S(1)}, u32[]{:S(2)}, u32[]{:S(2)}) %collective-permute-start.5) | collective-permute-done | bytes 16416 | tf_op jit(solution)/shard_map/ppermute | solution.py:492
  20.8 0.0 collective-permute-start.6
  20.8 0.0 copy-done.6
  20.8 0.0 copy-done.7
  20.8 0.0 copy-done.3
  20.8 0.0 copy-done.4
  20.8 0.6 %copy-done.8 = s32[32]{0:T(128)S(1)} copy-done((s32[32]{0:T(128)S(1)}, s32[32]{0:T(128)}, u32[]{:S(2)}) %copy-start.8) | copy-done | bytes 152
  21.5 0.2 observe.1
  21.6 0.3 collective-permute-done.6.theirs
  22.0 0.0 collective-permute-done.7.refs_1_
  22.0 0.0 collective-permute-done.8.refs_2_
  22.0 0.0 collective-permute-done.9.refs_3_
  22.0 0.9 %forecast_second.1 = (bf16[32,4096]{1,0:T(8,128)(2,1)S(1)}, f32[32,256]{1,0:T(8,128)S(1)}, f32[32,256]{1,0:T(8,128)S(1)}) custom-call(s32[2,32,128]{2,1,0:T(8,128)S(1)} %get-tuple-element.27.keys, f32[16,4096]{1,0:T(8,128)S(1)} %copy-done.1, bf16[2,2,16,4096]{3,2,1,0:T(8,128)(2,1)S(1)} %copy-done, f32[32,128]{1,0:T(8,128)S(1)} %constant_dynamic-update-slice_fusion.message, ...), custom_call_target="tpu_custom_call" | custom-call | tf_op jit(solution)/shard_map/forecast_second/pallas_call | solution.py:28
  22.9 0.3 collective-permute-start.10
  23.1 0.7 %assess_first.1 = (bf16[16,640]{1,0:T(8,128)(2,1)S(1)}, bf16[16,640]{1,0:T(8,128)(2,1)S(1)}, bf16[16,640]{1,0:T(8,128)(2,1)S(1)}, bf16[16,640]{1,0:T(8,128)(2,1)S(1)}) custom-call(bf16[32,4096]{1,0:T(8,128)(2,1)S(1)} %forecast_first.1.own, bf16[32,4096]{1,0:T(8,128)(2,1)S(1)} %collective-permute-done.other, f32[32,256]{1,0:T(8,128)S(1)} %get-tuple-element.42.low, ...), custom_call_target="tpu_custom_call" | custom-call | tf_op jit(solution)/shard_map/assess_first/pallas_call | solution.py:28
  23.8 0.6 %collective-permute-done.10.other = bf16[32,4096]{1,0:T(8,128)(2,1)S(1)} collective-permute-done((bf16[32,4096]{1,0:T(8,128)(2,1)S(1)}, bf16[32,4096]{1,0:T(8,128)(2,1)S(1)}, u32[]{:S(2)}, u32[]{:S(2)}) %collective-permute-start.10) | collective-permute-done | bytes 262176 | tf_op jit(solution)/shard_map/ppermute | solution.py:452
  24.5 0.9 %send_second.1 = (bf16[16,5376]{1,0:T(8,128)(2,1)S(1)}, bf16[16,5376]{1,0:T(8,128)(2,1)S(1)}, bf16[16,5376]{1,0:T(8,128)(2,1)S(1)}, bf16[16,5376]{1,0:T(8,128)(2,1)S(1)}) custom-call(bf16[32,4096]{1,0:T(8,128)(2,1)S(1)} %get-tuple-element.39.own, bf16[32,4096]{1,0:T(8,128)(2,1)S(1)} %collective-permute-done.10.other, ...), custom_call_target="tpu_custom_call" | custom-call | tf_op jit(solution)/shard_map/send_second/pallas_call | solution.py:28
  25.4 0.7 %collective-permute-start.11 = (bf16[16,5376]{1,0:T(8,128)(2,1)S(1)}, bf16[16,5376]{1,0:T(8,128)(2,1)S(1)}, u32[]{:S(2)}, u32[]{:S(2)}) collective-permute-start(bf16[16,5376]{1,0:T(8,128)(2,1)S(1)} %get-tuple-element.49), channel_id=1, source_target_pairs={{0,8},{4,12},{8,0},{12,4},{16,24},{20,28},{24,16},{28,20},{1,9},{5... | collective-permute-start | bytes 516104 | tf_op jit(solution)/shard_map/ppermute | solution.py:457
  26.1 0.5 %collective-permute-start.12 = (bf16[16,5376]{1,0:T(8,128)(2,1)S(1)}, bf16[16,5376]{1,0:T(8,128)(2,1)S(1)}, u32[]{:S(2)}, u32[]{:S(2)}) collective-permute-start(bf16[16,5376]{1,0:T(8,128)(2,1)S(1)} %get-tuple-element.50), channel_id=1, source_target_pairs={{0,16},{4,20},{8,24},{12,28},{16,0},{20,4},{24,8},{28,12},{1,17},{... | collective-permute-start | bytes 516104 | tf_op jit(solution)/shard_map/ppermute | solution.py:457
  26.6 2.3 %collective-permute-start.13 = (bf16[16,5376]{1,0:T(8,128)(2,1)S(1)}, bf16[16,5376]{1,0:T(8,128)(2,1)S(1)}, u32[]{:S(2)}, u32[]{:S(2)}) collective-permute-start(bf16[16,5376]{1,0:T(8,128)(2,1)S(1)} %get-tuple-element.51), channel_id=1, source_target_pairs={{0,24},{4,28},{8,16},{12,20},{16,8},{20,12},{24,0},{28,4},{1,25},{... | collective-permute-start | bytes 516104 | tf_op jit(solution)/shard_map/ppermute | solution.py:457
  29.0 3.7 %collective-permute-done.11.refs_1_ = bf16[16,5376]{1,0:T(8,128)(2,1)S(1)} collective-permute-done((bf16[16,5376]{1,0:T(8,128)(2,1)S(1)}, bf16[16,5376]{1,0:T(8,128)(2,1)S(1)}, u32[]{:S(2)}, u32[]{:S(2)}) %collective-permute-start.11) | collective-permute-done | bytes 172064 | tf_op jit(solution)/shard_map/ppermute | solution.py:457
  32.7 3.3 %collective-permute-done.12.refs_2_ = bf16[16,5376]{1,0:T(8,128)(2,1)S(1)} collective-permute-done((bf16[16,5376]{1,0:T(8,128)(2,1)S(1)}, bf16[16,5376]{1,0:T(8,128)(2,1)S(1)}, u32[]{:S(2)}, u32[]{:S(2)}) %collective-permute-start.12) | collective-permute-done | bytes 172064 | tf_op jit(solution)/shard_map/ppermute | solution.py:457
  36.0 0.0 collective-permute-done.13.refs_3_
  36.0 0.9 %finish.1 = (bf16[2,16,4096]{2,1,0:T(8,128)(2,1)}, f32[2,16,512]{2,1,0:T(8,128)}) custom-call(s32[2,32,128]{2,1,0:T(8,128)S(1)} %get-tuple-element.27.keys, bf16[16,5376]{1,0:T(8,128)(2,1)S(1)} %get-tuple-element.48.refs_0_, bf16[16,5376]{1,0:T(8,128)(2,1)S(1)} %collective-permute-done.11.refs_1_, bf16[16,5376]{1,0:T(8,128)(2,1)S(1)} %collective-permute-done.12.refs_2_, ...), custom_call_target="tpu_custom_call" | custom-call | tf_op jit(solution)/shard_map/finish/pallas_call | solution.py:28
  (8 shorter events, 0.0 us)
Async XLA Ops:
  0.6 1.3 %copy-start = (bf16[2,2,16,4096]{3,2,1,0:T(8,128)(2,1)S(1)}, bf16[2,2,16,4096]{3,2,1,0:T(8,128)(2,1)}, u32[]{:S(2)}) copy-start(bf16[2,2,16,4096]{3,2,1,0:T(8,128)(2,1)} %pert.3) | copy-start | bytes 1572868
  0.6 1.4 %copy-start.1 = (f32[16,4096]{1,0:T(8,128)S(1)}, f32[16,4096]{1,0:T(8,128)}, u32[]{:S(2)}) copy-start(f32[16,4096]{1,0:T(8,128)} %diff.3) | copy-start | bytes 786436
  0.7 1.4 %copy-start.2 = (bf16[2,16,4096]{2,1,0:T(8,128)(2,1)S(1)}, bf16[2,16,4096]{2,1,0:T(8,128)(2,1)}, u32[]{:S(2)}) copy-start(bf16[2,16,4096]{2,1,0:T(8,128)(2,1)} %state.1) | copy-start | bytes 786436
  2.7 9.0 %collective-permute-start = (bf16[32,4096]{1,0:T(8,128)(2,1)S(1)}, bf16[32,4096]{1,0:T(8,128)(2,1)S(1)}, u32[]{:S(2)}, u32[]{:S(2)}) collective-permute-start(bf16[32,4096]{1,0:T(8,128)(2,1)S(1)} %forecast_first.1.own), channel_id=1, source_target_pairs={{0,4},{4,0},{8,12},{12,8},{16,20},{20,16},{24,28},{28,24},{1,5},{5... | collective-permute-start | bytes 786440 | tf_op jit(solution)/shard_map/ppermute | solution.py:452
  3.2 4.1 %collective-permute-start.1 = (f32[1,128]{1,0:T(1,128)S(1)}, f32[1,128]{1,0:T(1,128)S(1)}, u32[]{:S(2)}, u32[]{:S(2)}) collective-permute-start(f32[1,128]{1,0:T(1,128)S(1)} %get-tuple-element.30), channel_id=1, source_target_pairs={{0,8},{4,12},{8,0},{12,4},{16,24},{20,28},{24,16},{28,20},{1,9},{5... | collective-permute-start | bytes 1544 | tf_op jit(solution)/shard_map/ppermute | solution.py:457
  5.7 3.5 %collective-permute-start.2 = (f32[1,128]{1,0:T(1,128)S(1)}, f32[1,128]{1,0:T(1,128)S(1)}, u32[]{:S(2)}, u32[]{:S(2)}) collective-permute-start(f32[1,128]{1,0:T(1,128)S(1)} %get-tuple-element.31), channel_id=1, source_target_pairs={{0,16},{4,20},{8,24},{12,28},{16,0},{20,4},{24,8},{28,12},{1,17},{... | collective-permute-start | bytes 1544 | tf_op jit(solution)/shard_map/ppermute | solution.py:457
  7.3 4.4 %collective-permute-start.3 = (f32[1,128]{1,0:T(1,128)S(1)}, f32[1,128]{1,0:T(1,128)S(1)}, u32[]{:S(2)}, u32[]{:S(2)}) collective-permute-start(f32[1,128]{1,0:T(1,128)S(1)} %get-tuple-element.32), channel_id=1, source_target_pairs={{0,24},{4,28},{8,16},{12,20},{16,8},{20,12},{24,0},{28,4},{1,25},{... | collective-permute-start | bytes 1544 | tf_op jit(solution)/shard_map/ppermute | solution.py:457
  11.7 9.1 %copy-start.5 = (f32[32,16]{0,1:T(8,128)S(1)}, f32[32,16]{0,1:T(8,128)}, u32[]{:S(2)}) copy-start(f32[32,16]{0,1:T(8,128)} %param.15) | copy-start | bytes 6148
  12.1 8.7 %copy-start.6 = (s32[16,6]{0,1:T(8,128)S(1)}, s32[16,6]{0,1:T(8,128)}, u32[]{:S(2)}) copy-start(s32[16,6]{0,1:T(8,128)} %param.18) | copy-start | bytes 1156
  12.1 8.7 %copy-start.7 = (f32[16,6]{0,1:T(8,128)S(1)}, f32[16,6]{0,1:T(8,128)}, u32[]{:S(2)}) copy-start(f32[16,6]{0,1:T(8,128)} %param.19) | copy-start | bytes 1156
  12.1 3.7 %collective-permute-start.4 = (f32[16,128]{1,0:T(8,128)S(1)}, f32[16,128]{1,0:T(8,128)S(1)}, u32[]{:S(2)}, u32[]{:S(2)}) collective-permute-start(f32[16,128]{1,0:T(8,128)S(1)} %get-tuple-element.33), channel_id=1, source_target_pairs={{0,4},{4,0},{8,12},{12,8},{16,20},{20,16},{24,28},{28,24},{1,5},{5... | collective-permute-start | bytes 24584 | tf_op jit(solution)/shard_map/ppermute | solution.py:452
  12.2 8.6 %copy-start.3 = (f32[2,32,16]{1,2,0:T(8,128)S(1)}, f32[2,32,16]{1,2,0:T(8,128)}, u32[]{:S(2)}) copy-start(f32[2,32,16]{1,2,0:T(8,128)} %param.14) | copy-start | bytes 12292
  12.2 9.8 %collective-permute-start.7 = (bf16[16,4096]{1,0:T(8,128)(2,1)S(1)}, bf16[16,4096]{1,0:T(8,128)(2,1)S(1)}, u32[]{:S(2)}, u32[]{:S(2)}) collective-permute-start(bf16[16,4096]{1,0:T(8,128)(2,1)S(1)} %get-tuple-element.36), channel_id=1, source_target_pairs={{0,8},{4,12},{8,0},{12,4},{16,24},{20,28},{24,16},{28,20},{1,9},{5... | collective-permute-start | bytes 393224 | tf_op jit(solution)/shard_map/ppermute | solution.py:457
  12.8 9.2 %collective-permute-start.8 = (bf16[16,4096]{1,0:T(8,128)(2,1)S(1)}, bf16[16,4096]{1,0:T(8,128)(2,1)S(1)}, u32[]{:S(2)}, u32[]{:S(2)}) collective-permute-start(bf16[16,4096]{1,0:T(8,128)(2,1)S(1)} %get-tuple-element.37), channel_id=1, source_target_pairs={{0,16},{4,20},{8,24},{12,28},{16,0},{20,4},{24,8},{28,12},{1,17},{... | collective-permute-start | bytes 393224 | tf_op jit(solution)/shard_map/ppermute | solution.py:457
  12.8 9.1 %collective-permute-start.9 = (bf16[16,4096]{1,0:T(8,128)(2,1)S(1)}, bf16[16,4096]{1,0:T(8,128)(2,1)S(1)}, u32[]{:S(2)}, u32[]{:S(2)}) collective-permute-start(bf16[16,4096]{1,0:T(8,128)(2,1)S(1)} %get-tuple-element.38), channel_id=1, source_target_pairs={{0,24},{4,28},{8,16},{12,20},{16,8},{20,12},{24,0},{28,4},{1,25},{... | collective-permute-start | bytes 393224 | tf_op jit(solution)/shard_map/ppermute | solution.py:457
  15.8 5.1 %copy-start.4 = (s32[32,16]{0,1:T(8,128)S(1)}, s32[32,16]{0,1:T(8,128)}, u32[]{:S(2)}) copy-start(s32[32,16]{0,1:T(8,128)} %param.17) | copy-start | bytes 6148
  15.8 5.0 %collective-permute-start.5 = (f32[32,128]{1,0:T(8,128)S(1)}, f32[32,128]{1,0:T(8,128)S(1)}, u32[]{:S(2)}, u32[]{:S(2)}) collective-permute-start(f32[32,128]{1,0:T(8,128)S(1)} %constant_dynamic-update-slice_fusion.message), channel_id=1, source_target_pairs={{0,1},{1,2},{2,3},{5,4},{6,5},{7,6},{8,9},{9,10},{10,11},{13,12},{... | collective-permute-start | bytes 49160 | tf_op jit(solution)/shard_map/ppermute | solution.py:492
  20.8 1.2 %collective-permute-start.6 = (f32[32,128]{1,0:T(8,128)S(1)}, f32[32,128]{1,0:T(8,128)S(1)}, u32[]{:S(2)}, u32[]{:S(2)}) collective-permute-start(f32[32,128]{1,0:T(8,128)S(1)} %collective-permute-done.5.mine), channel_id=1, source_target_pairs={{0,4},{4,0},{8,12},{12,8},{16,20},{20,16},{24,28},{28,24},{1,5},{5... | collective-permute-start | bytes 49160 | tf_op jit(solution)/shard_map/ppermute | solution.py:452
  20.8 0.7 %copy-start.8 = (s32[32]{0:T(128)S(1)}, s32[32]{0:T(128)}, u32[]{:S(2)}) copy-start(s32[32]{0:T(128)} %param.16) | copy-start | bytes 388
  22.9 1.6 %collective-permute-start.10 = (bf16[32,4096]{1,0:T(8,128)(2,1)S(1)}, bf16[32,4096]{1,0:T(8,128)(2,1)S(1)}, u32[]{:S(2)}, u32[]{:S(2)}) collective-permute-start(bf16[32,4096]{1,0:T(8,128)(2,1)S(1)} %get-tuple-element.39.own), channel_id=1, source_target_pairs={{0,4},{4,0},{8,12},{12,8},{16,20},{20,16},{24,28},{28,24},{1,5},{5... | collective-permute-start | bytes 786440 | tf_op jit(solution)/shard_map/ppermute | solution.py:452
  25.4 7.3 %collective-permute-start.11 = (bf16[16,5376]{1,0:T(8,128)(2,1)S(1)}, bf16[16,5376]{1,0:T(8,128)(2,1)S(1)}, u32[]{:S(2)}, u32[]{:S(2)}) collective-permute-start(bf16[16,5376]{1,0:T(8,128)(2,1)S(1)} %get-tuple-element.49), channel_id=1, source_target_pairs={{0,8},{4,12},{8,0},{12,4},{16,24},{20,28},{24,16},{28,20},{1,9},{5... | collective-permute-start | bytes 516104 | tf_op jit(solution)/shard_map/ppermute | solution.py:457
  26.1 9.8 %collective-permute-start.12 = (bf16[16,5376]{1,0:T(8,128)(2,1)S(1)}, bf16[16,5376]{1,0:T(8,128)(2,1)S(1)}, u32[]{:S(2)}, u32[]{:S(2)}) collective-permute-start(bf16[16,5376]{1,0:T(8,128)(2,1)S(1)} %get-tuple-element.50), channel_id=1, source_target_pairs={{0,16},{4,20},{8,24},{12,28},{16,0},{20,4},{24,8},{28,12},{1,17},{... | collective-permute-start | bytes 516104 | tf_op jit(solution)/shard_map/ppermute | solution.py:457
  26.6 9.3 %collective-permute-start.13 = (bf16[16,5376]{1,0:T(8,128)(2,1)S(1)}, bf16[16,5376]{1,0:T(8,128)(2,1)S(1)}, u32[]{:S(2)}, u32[]{:S(2)}) collective-permute-start(bf16[16,5376]{1,0:T(8,128)(2,1)S(1)} %get-tuple-element.51), channel_id=1, source_target_pairs={{0,24},{4,28},{8,16},{12,20},{16,8},{20,12},{24,0},{28,4},{1,25},{... | collective-permute-start | bytes 516104 | tf_op jit(solution)/shard_map/ppermute | solution.py:457

commit v10 on v9

--- a/solution.py
+++ b/solution.py
@@ -96,7 +96,7 @@
                 spot = (iota((LANES, tiles), 0) == (2 * c + half) * capacity + rank).astype(F32)
                 pair = jnp.where(iota((pairs, tiles), 0) == source // 2, (code + 1).astype(F32), 0.0)
                 asked = asked + lax.dot_general(pair, spot, (((1,), (1,)), ((), ())), preferred_element_type=F32)
-                column = column_of(source * capacity + rank)
+                column = column_of((source ^ (m // 2 * 2)) * capacity + rank)
                 keys[c, p * tiles:(p + 1) * tiles, :] = jnp.broadcast_to(column, (tiles, LANES))
         for k in range(pairs):
             notes[k][...] = jnp.where(lane < EDGE_AT, asked[k:k + 1, :] - 1.0, edge)
@@ -300,11 +300,12 @@
 
 def make_send(pairs, rows):
     def kernel(own, other, trail, *refs):
-        notes, sends, half = refs[:pairs], refs[pairs:2 * pairs], refs[2 * pairs]
+        notes, send, half = refs[:pairs], refs[pairs], refs[pairs + 1]
         prior = jnp.concatenate([own[...], other[...]], axis=0)
         sent = requested([x[...] for x in notes], prior, 0, rows)
+        g = here() // 2
         for k in range(pairs):
-            sends[k][...] = sent[k * rows:(k + 1) * rows, :].astype(BF16)
+            send[g ^ k] = sent[k * rows:(k + 1) * rows, :].astype(BF16)
         size = padded(pairs)
         half[...] = jnp.zeros(half.shape, F32)
         for k in range(pairs):
@@ -339,14 +340,13 @@
     size = padded(pairs)
 
     def kernel(keys, diff, pert, message, mine, theirs, after, *refs):
-        got, prior, low_out, high_out = refs[:pairs], refs[pairs], refs[pairs + 1], refs[pairs + 2]
+        got, prior, low_out, high_out = refs
         below, above = halves(mine[...], theirs[...])
         low, high = edge_windows(message[...], below, above, size, parts)
         low_out[...] = low
         high_out[...] = high
         below, above = below[size:size + 8, :], above[size:size + 8, :]
-        arrived = jnp.concatenate([x[...] for x in got], axis=0)
-        moved = pick_rows(keys[0], arrived)
+        moved = pick_rows(keys[0], got[...].reshape(-1, cells))
         here_codes = message[size + 2:size + 2 + 2 * parts, :].astype(I32)
         codes = jnp.concatenate([here_codes[parts:], below[2:2 + parts, :].astype(I32)], axis=0)
         start = pick_rows(codes, low.astype(BF16))
@@ -365,7 +365,9 @@
 
 def make_send_second(pairs, rows, parts, tiles, cells, share):
     def kernel(own, other, where, terms, local, *refs):
-        notes, kept, outs, sums = refs[:pairs], refs[pairs:2 * pairs], refs[2 * pairs:3 * pairs], refs[3 * pairs]
+        notes, kept, send, sums = refs[:pairs], refs[pairs:2 * pairs], refs[2 * pairs], refs[2 * pairs + 1]
+        g = here() // 2
+        outs = [send.at[g ^ k] for k in range(pairs)]
         prior = jnp.concatenate([own[...], other[...]], axis=0)
         sent = requested([x[...] for x in notes], prior, 1, rows)
         extra = kept[0].shape[1]
@@ -383,10 +385,9 @@
 
 
 def make_last(pairs, rows, parts, tiles, cells):
-    def kernel(keys, *refs):
-        got, analysis, mean = refs[:pairs], refs[pairs], refs[pairs + 1]
-        arrived = jnp.concatenate([x[:, :cells] for x in got], axis=0)
-        picked = pick_rows(keys[1], arrived)
+    def kernel(keys, arrived, analysis, mean):
+        got = [arrived.at[k] for k in range(pairs)]
+        picked = pick_rows(keys[1], arrived[:, :, :cells].reshape(pairs * rows, cells))
         for p in range(parts):
             analysis[p] = picked[p * tiles:(p + 1) * tiles, :].astype(BF16)
         share = mean.shape[2]
@@ -451,13 +452,12 @@
     def trade(x):
         return lax.ppermute(x, "member", [(i, i ^ 1) for i in range(members)])
 
-    def exchange(sends):
-        got = [sends[0]]
-        for k in range(1, pairs):
-            got.append(lax.ppermute(sends[k], "member", [(i, i ^ (2 * k)) for i in range(members)]))
-        return got
-
-    notes = exchange(notes)
+    def exchange(send):
+        groups = [[2 * k + h for k in range(pairs)] for h in range(2)]
+        return lax.all_to_all(send, "member", 0, 0, axis_index_groups=groups, tiled=True)
+
+    for k in range(1, pairs):
+        notes[k] = lax.ppermute(notes[k], "member", [(i, i ^ (2 * k)) for i in range(members)])
 
     where, terms, local = call(
         make_observe(blocks, per_block, tiles, near),
@@ -477,13 +477,13 @@
     )
     other = trade(prior)
     size = padded(pairs)
-    *sends, half = call(
+    send, half = call(
         make_send(pairs, rows),
-        [((rows, cells), BF16)] * pairs + [((size + trail.shape[0], LANES), F32)],
+        [((pairs, rows, cells), BF16), ((size + trail.shape[0], LANES), F32)],
         [prior, other, trail, *notes],
         name="send_first",
     )
-    got = exchange(sends)
+    got = exchange(send)
     message = jnp.concatenate([half, trade(half)], axis=0)
     steps = []
     for i in range(members):
@@ -493,7 +493,7 @@
     theirs = trade(mine)
     window = ((parts * 2 * size, 2 * LANES), F32)
     sums = [((tiles, cells), F32)]
-    args = [keys, diffusivity, model_perturbation, message, mine, theirs, where, *got]
+    args = [keys, diffusivity, model_perturbation, message, mine, theirs, where, got]
     specs = [whole_spec(a.shape) for a in args]
     specs[2] = noise_spec(1)
     second, low, high = call(
@@ -510,19 +510,19 @@
         scratch=sums,
         name="assess_first",
     )
-    sends = call(
+    (send,) = call(
         make_send_second(pairs, rows, parts, tiles, cells, share),
-        [((rows, cells + CYCLES * extra), BF16)] * pairs,
+        [((pairs, rows, cells + CYCLES * extra), BF16)],
         [second, trade(second), where, terms, local, *notes, *kept],
         scratch=sums,
         name="send_second",
     )
-    got = exchange(sends)
+    got = exchange(send)
     return tuple(
         call(
             make_last(pairs, rows, parts, tiles, cells),
             [(state.shape, BF16), ((CYCLES, tiles, share), F32)],
-            [keys, *got],
+            [keys, got],
             name="finish",
         )
     )

time: 37.1 us -> 43.4 us (1.17)
  blocking collectives: 0 us -> 14.8 us
  waiting for transfers between devices: 13.8 us -> 7.94 us
  starting transfers between devices: 15.7 us -> 12.2 us
  Pallas kernels: 5.91 us -> 6.7 us
    all_to_all x0 -> x1, blocking collectives: none -> 14.8 us  [exchange(): lax.all_to_all(send, 'member', 0, 0, axis_index_groups=groups, tiled=True)]
    ppermute x9 -> x3, starting transfers between devices: 11.2 us -> 4.1 us  [body(): lax.ppermute(notes[k], 'member', [(i, i ^ 2 * k) for i in range(members)])]
    ppermute x9 -> x3, waiting for transfers between devices: 11.4 us -> 4.42 us  [body(): lax.ppermute(notes[k], 'member', [(i, i ^ 2 * k) for i in range(members)])]
    all_to_all x0 -> x1, starting transfers between devices: none -> 3.6 us  [exchange(): lax.all_to_all(send, 'member', 0, 0, axis_index_groups=groups, tiled=True)]
    ppermute x4, waiting for transfers between devices: 0.98 us -> 2.09 us  [trade(): return lax.ppermute(x, 'member', [(i, i ^ 1) for i in range(members)])]
    pallas_call x8, Pallas kernels: 5.91 us -> 6.7 us  [call(): pl.pallas_call(kernel, out_shape=[jax.ShapeDtypeStruct(s, d) for s, d in...]
  transfers between devices with their start and end apart: 14 -> 9, of which waited for: 7 -> 6; matrix products, arithmetic and copies ran while one was open for 0% -> 0% of each run, Pallas kernels for 2% -> 2%
where the time goes in v10:
time: 43.4 us; the launch traced here: 43.1 us
  blocking collectives  14.8 us (34%)
  starting transfers between devices  12.2 us (28%)
  waiting for transfers between devices  7.94 us (18%)
  Pallas kernels  6.7 us (15%)
  between operations  0.8 us (2%)
  local copies, waits for them, and re-layouts  0.67 us (2%)
    all_to_all x1, blocking collectives, exchange(): lax.all_to_all(send, 'member', 0, 0, axis_index_groups=groups, tiled=True)  14.8 us
    pallas_call x8, Pallas kernels, call(): pl.pallas_call(kernel, out_shape=[jax.ShapeDtypeStruct(s, d) for s, d in...  6.7 us
    ppermute x3, waiting for transfers between devices, body(): lax.ppermute(notes[k], 'member', [(i, i ^ 2 * k) for i in range(members)])  4.42 us
    ppermute x3, starting transfers between devices, body(): lax.ppermute(notes[k], 'member', [(i, i ^ 2 * k) for i in range(members)])  4.1 us
    ppermute x1, starting transfers between devices, body(): mine = lax.ppermute(message, ('member', 'region'), steps)  3.6 us
    all_to_all x1, starting transfers between devices, exchange(): lax.all_to_all(send, 'member', 0, 0, axis_index_groups=groups, tiled=True)  3.6 us
    ppermute x4, waiting for transfers between devices, trade(): return lax.ppermute(x, 'member', [(i, i ^ 1) for i in range(members)])  2.09 us
    ppermute x1, waiting for transfers between devices, body(): mine = lax.ppermute(message, ('member', 'region'), steps)  1.43 us
  transfers between devices with their start and end apart: 9, of which 6 were waited for; matrix products, arithmetic and copies ran while one was open for 0% of the time, Pallas kernels for 2%

profile of v10, /device:TPU:0, one launch (start us, length us, event | category | flops | bytes accessed | tf_op | source)
XLA Modules:
  0.0 43.1 jit_solution(5990804488025292592)
XLA Ops:
  0.6 0.0 copy-start
  0.6 0.0 copy-start.1
  0.7 0.0 copy-start.2
  0.7 1.3 %prepare.1 = (f32[1,128]{1,0:T(1,128)S(1)}, f32[1,128]{1,0:T(1,128)S(1)}, f32[1,128]{1,0:T(1,128)S(1)}, f32[1,128]{1,0:T(1,128)S(1)}, f32[8,128]{1,0:T(8,128)S(1)}, /*index=5*/s32[2,32,128]{2,1,0:T(8,128)S(1)}) custom-call(bf16[2,16,4096]{2,1,0:T(8,128)(2,1)} %state.1, bf16[2,16,4096]{2,1,0:T(8,128)(2,1)} %state.1, f32[16,4096]{1,0:T(8,128)} %diff.3, ...), custom_call_target="tpu_custom_call" | custom-call | tf_op jit(solution)/shard_map/prepare/pallas_call | solution.py:28
  2.0 0.0 copy-done
  2.0 0.0 copy-done.1
  2.0 0.0 copy-done.2
  2.0 0.6 %forecast_first.1.own = bf16[32,4096]{1,0:T(8,128)(2,1)S(1)} custom-call(bf16[2,16,4096]{2,1,0:T(8,128)(2,1)S(1)} %copy-done.2, f32[16,4096]{1,0:T(8,128)S(1)} %copy-done.1, bf16[2,2,16,4096]{3,2,1,0:T(8,128)(2,1)S(1)} %copy-done, f32[8,128]{1,0:T(8,128)S(1)} %get-tuple-element.21.after.trail), custom_call_target="tpu_custom_call" | custom-call | tf_op jit(solution)/shard_map/forecast_first/pallas_call | solution.py:28
  2.6 0.5 %collective-permute-start = (bf16[32,4096]{1,0:T(8,128)(2,1)S(1)}, bf16[32,4096]{1,0:T(8,128)(2,1)S(1)}, u32[]{:S(2)}, u32[]{:S(2)}) collective-permute-start(bf16[32,4096]{1,0:T(8,128)(2,1)S(1)} %forecast_first.1.own), channel_id=1, source_target_pairs={{0,4},{4,0},{8,12},{12,8},{16,20},{20,16},{24,28},{28,24},{1,5},{5... | collective-permute-start | bytes 786440 | tf_op jit(solution)/shard_map/ppermute | solution.py:453
  3.1 2.6 %collective-permute-start.1 = (f32[1,128]{1,0:T(1,128)S(1)}, f32[1,128]{1,0:T(1,128)S(1)}, u32[]{:S(2)}, u32[]{:S(2)}) collective-permute-start(f32[1,128]{1,0:T(1,128)S(1)} %get-tuple-element.23), channel_id=1, source_target_pairs={{0,8},{4,12},{8,0},{12,4},{16,24},{20,28},{24,16},{28,20},{1,9},{5... | collective-permute-start | bytes 1544 | tf_op jit(solution)/shard_map/ppermute | solution.py:460
  5.7 1.5 %collective-permute-start.2 = (f32[1,128]{1,0:T(1,128)S(1)}, f32[1,128]{1,0:T(1,128)S(1)}, u32[]{:S(2)}, u32[]{:S(2)}) collective-permute-start(f32[1,128]{1,0:T(1,128)S(1)} %get-tuple-element.24), channel_id=1, source_target_pairs={{0,16},{4,20},{8,24},{12,28},{16,0},{20,4},{24,8},{28,12},{1,17},{... | collective-permute-start | bytes 1544 | tf_op jit(solution)/shard_map/ppermute | solution.py:460
  7.2 0.0 collective-permute-start.3
  7.3 0.0 collective-permute-done.1.refs_1_
  7.3 2.0 %collective-permute-done.2.refs_2_ = f32[1,128]{1,0:T(1,128)S(1)} collective-permute-done((f32[1,128]{1,0:T(1,128)S(1)}, f32[1,128]{1,0:T(1,128)S(1)}, u32[]{:S(2)}, u32[]{:S(2)}) %collective-permute-start.2) | collective-permute-done | bytes 544 | tf_op jit(solution)/shard_map/ppermute | solution.py:460
  9.3 2.4 %collective-permute-done.3.refs_3_ = f32[1,128]{1,0:T(1,128)S(1)} collective-permute-done((f32[1,128]{1,0:T(1,128)S(1)}, f32[1,128]{1,0:T(1,128)S(1)}, u32[]{:S(2)}, u32[]{:S(2)}) %collective-permute-start.3) | collective-permute-done | bytes 544 | tf_op jit(solution)/shard_map/ppermute | solution.py:460
  11.7 0.0 collective-permute-done.other
  11.7 1.2 %send_first.1 = (bf16[4,16,4096]{2,1,0:T(8,128)(2,1)}, f32[16,128]{1,0:T(8,128)S(1)}) custom-call(bf16[32,4096]{1,0:T(8,128)(2,1)S(1)} %forecast_first.1.own, bf16[32,4096]{1,0:T(8,128)(2,1)S(1)} %collective-permute-done.other, f32[8,128]{1,0:T(8,128)S(1)} %get-tuple-element.21.after.trail, f32[1,128]{1,0:T(1,128)S(1)} %get-tuple-element.22.refs_0_, ...), custom_call_target="tpu_custom_call" | custom-call | tf_op jit(solution)/shard_map/send_first/pallas_call | solution.py:28
  12.9 0.0 copy-start.6
  12.9 0.0 copy-start.7
  12.9 3.6 %all-to-all-start = ((bf16[4,16,4096]{2,1,0:T(8,128)(2,1)}), bf16[4,16,4096]{2,1,0:T(8,128)(2,1)S(1)}, u32[]{:S(2)}, u32[]{:S(2)}) async-start(bf16[4,16,4096]{2,1,0:T(8,128)(2,1)} %get-tuple-element.28), calls=%async_computation | async-start | bytes 1048576 | tf_op jit(solution)/shard_map/all_to_all | solution.py:457
  16.5 0.1 collective-permute-start.4
  16.6 0.0 copy-start.5
  16.6 0.0 copy-start.3
  16.6 1.1 %collective-permute-done.4 = f32[16,128]{1,0:T(8,128)S(1)} collective-permute-done((f32[16,128]{1,0:T(8,128)S(1)}, f32[16,128]{1,0:T(8,128)S(1)}, u32[]{:S(2)}, u32[]{:S(2)}) %collective-permute-start.4) | collective-permute-done | bytes 8224 | tf_op jit(solution)/shard_map/ppermute | solution.py:453
  17.7 0.0 copy-start.4
  17.7 3.6 %collective-permute-start.5 = (f32[32,128]{1,0:T(8,128)S(1)}, f32[32,128]{1,0:T(8,128)S(1)}, u32[]{:S(2)}, u32[]{:S(2)}) collective-permute-start(f32[32,128]{1,0:T(8,128)S(1)} %constant_dynamic-update-slice_fusion.message), channel_id=1, source_target_pairs={{0,1},{1,2},{2,3},{5,4},{6,5},{7,6},{8,9},{9,10},{10,11},{13,12},{... | collective-permute-start | bytes 49160 | tf_op jit(solution)/shard_map/ppermute | solution.py:492
  21.3 1.4 %collective-permute-done.5.mine = f32[32,128]{1,0:T(8,128)S(1)} collective-permute-done((f32[32,128]{1,0:T(8,128)S(1)}, f32[32,128]{1,0:T(8,128)S(1)}, u32[]{:S(2)}, u32[]{:S(2)}) %collective-permute-start.5) | collective-permute-done | bytes 16416 | tf_op jit(solution)/shard_map/ppermute | solution.py:492
  22.8 0.0 collective-permute-start.6
  22.8 0.0 copy-start.8
  22.8 0.0 copy-done.6
  22.8 0.0 copy-done.7
  22.8 0.0 copy-done.5
  22.8 0.0 copy-done.3
  22.8 0.0 copy-done.4
  22.8 0.6 %copy-done.8 = s32[32]{0:T(128)S(1)} copy-done((s32[32]{0:T(128)S(1)}, s32[32]{0:T(128)}, u32[]{:S(2)}) %copy-start.8) | copy-done | bytes 152
  23.4 0.2 observe.1
  23.6 0.3 collective-permute-done.6.theirs
  23.9 0.0 all-to-all-done.refs_0_
  23.9 0.9 %forecast_second.1 = (bf16[32,4096]{1,0:T(8,128)(2,1)S(1)}, f32[32,256]{1,0:T(8,128)S(1)}, f32[32,256]{1,0:T(8,128)S(1)}) custom-call(s32[2,32,128]{2,1,0:T(8,128)S(1)} %get-tuple-element.20.keys, f32[16,4096]{1,0:T(8,128)S(1)} %copy-done.1, bf16[2,2,16,4096]{3,2,1,0:T(8,128)(2,1)S(1)} %copy-done, f32[32,128]{1,0:T(8,128)S(1)} %constant_dynamic-update-slice_fusion.message, ...), custom_call_target="tpu_custom_call" | custom-call | tf_op jit(solution)/shard_map/forecast_second/pallas_call | solution.py:28
  24.8 0.3 collective-permute-start.7
  25.1 0.7 %assess_first.1 = (bf16[16,640]{1,0:T(8,128)(2,1)S(1)}, bf16[16,640]{1,0:T(8,128)(2,1)S(1)}, bf16[16,640]{1,0:T(8,128)(2,1)S(1)}, bf16[16,640]{1,0:T(8,128)(2,1)S(1)}) custom-call(bf16[32,4096]{1,0:T(8,128)(2,1)S(1)} %forecast_first.1.own, bf16[32,4096]{1,0:T(8,128)(2,1)S(1)} %collective-permute-done.other, f32[32,256]{1,0:T(8,128)S(1)} %get-tuple-element.32.low, ...), custom_call_target="tpu_custom_call" | custom-call | tf_op jit(solution)/shard_map/assess_first/pallas_call | solution.py:28
  25.7 0.7 %collective-permute-done.7.other = bf16[32,4096]{1,0:T(8,128)(2,1)S(1)} collective-permute-done((bf16[32,4096]{1,0:T(8,128)(2,1)S(1)}, bf16[32,4096]{1,0:T(8,128)(2,1)S(1)}, u32[]{:S(2)}, u32[]{:S(2)}) %collective-permute-start.7) | collective-permute-done | bytes 262176 | tf_op jit(solution)/shard_map/ppermute | solution.py:453
  26.4 0.9 %send_second.1 = bf16[4,16,5376]{2,1,0:T(8,128)(2,1)S(1)} custom-call(bf16[32,4096]{1,0:T(8,128)(2,1)S(1)} %get-tuple-element.29.own, bf16[32,4096]{1,0:T(8,128)(2,1)S(1)} %collective-permute-done.7.other, s32[2,512]{1,0:T(2,128)S(1)} %get-tuple-element.27.after.where, f32[3,512]{1,0:T(4,128)S(1)} %get-tuple-element.30.terms, ...), custom_call_target="tpu_custom_call" | custom-call | tf_op jit(solution)/shard_map/send_second/pallas_call | solution.py:28
  27.4 14.8 %all_to_all.10.arrived = bf16[4,16,5376]{2,1,0:T(8,128)(2,1)S(1)} all-to-all(bf16[4,16,5376]{2,1,0:T(8,128)(2,1)S(1)} %send_second.1), channel_id=1, replica_groups={{0,8,16,24},{4,12,20,28},{1,9,17,25},{5,13,21,29},{2,10,18,26},{6,14,22..., dimensions={0} | all-to-all | bytes 1376256 | tf_op jit(solution)/shard_map/all_to_all | solution.py:457
  42.1 0.9 %finish.1 = (bf16[2,16,4096]{2,1,0:T(8,128)(2,1)}, f32[2,16,512]{2,1,0:T(8,128)}) custom-call(s32[2,32,128]{2,1,0:T(8,128)S(1)} %get-tuple-element.20.keys, bf16[4,16,5376]{2,1,0:T(8,128)(2,1)S(1)} %all_to_all.10.arrived), custom_call_target="tpu_custom_call" | custom-call | tf_op jit(solution)/shard_map/finish/pallas_call | solution.py:28
  (2 shorter events, 0.0 us)
Async XLA Ops:
  0.6 1.3 %copy-start = (bf16[2,2,16,4096]{3,2,1,0:T(8,128)(2,1)S(1)}, bf16[2,2,16,4096]{3,2,1,0:T(8,128)(2,1)}, u32[]{:S(2)}) copy-start(bf16[2,2,16,4096]{3,2,1,0:T(8,128)(2,1)} %pert.3) | copy-start | bytes 1572868
  0.6 1.4 %copy-start.1 = (f32[16,4096]{1,0:T(8,128)S(1)}, f32[16,4096]{1,0:T(8,128)}, u32[]{:S(2)}) copy-start(f32[16,4096]{1,0:T(8,128)} %diff.3) | copy-start | bytes 786436
  0.7 1.4 %copy-start.2 = (bf16[2,16,4096]{2,1,0:T(8,128)(2,1)S(1)}, bf16[2,16,4096]{2,1,0:T(8,128)(2,1)}, u32[]{:S(2)}) copy-start(bf16[2,16,4096]{2,1,0:T(8,128)(2,1)} %state.1) | copy-start | bytes 786436
  2.6 9.0 %collective-permute-start = (bf16[32,4096]{1,0:T(8,128)(2,1)S(1)}, bf16[32,4096]{1,0:T(8,128)(2,1)S(1)}, u32[]{:S(2)}, u32[]{:S(2)}) collective-permute-start(bf16[32,4096]{1,0:T(8,128)(2,1)S(1)} %forecast_first.1.own), channel_id=1, source_target_pairs={{0,4},{4,0},{8,12},{12,8},{16,20},{20,16},{24,28},{28,24},{1,5},{5... | collective-permute-start | bytes 786440 | tf_op jit(solution)/shard_map/ppermute | solution.py:453
  3.1 4.1 %collective-permute-start.1 = (f32[1,128]{1,0:T(1,128)S(1)}, f32[1,128]{1,0:T(1,128)S(1)}, u32[]{:S(2)}, u32[]{:S(2)}) collective-permute-start(f32[1,128]{1,0:T(1,128)S(1)} %get-tuple-element.23), channel_id=1, source_target_pairs={{0,8},{4,12},{8,0},{12,4},{16,24},{20,28},{24,16},{28,20},{1,9},{5... | collective-permute-start | bytes 1544 | tf_op jit(solution)/shard_map/ppermute | solution.py:460
  5.7 3.5 %collective-permute-start.2 = (f32[1,128]{1,0:T(1,128)S(1)}, f32[1,128]{1,0:T(1,128)S(1)}, u32[]{:S(2)}, u32[]{:S(2)}) collective-permute-start(f32[1,128]{1,0:T(1,128)S(1)} %get-tuple-element.24), channel_id=1, source_target_pairs={{0,16},{4,20},{8,24},{12,28},{16,0},{20,4},{24,8},{28,12},{1,17},{... | collective-permute-start | bytes 1544 | tf_op jit(solution)/shard_map/ppermute | solution.py:460
  7.2 4.4 %collective-permute-start.3 = (f32[1,128]{1,0:T(1,128)S(1)}, f32[1,128]{1,0:T(1,128)S(1)}, u32[]{:S(2)}, u32[]{:S(2)}) collective-permute-start(f32[1,128]{1,0:T(1,128)S(1)} %get-tuple-element.25), channel_id=1, source_target_pairs={{0,24},{4,28},{8,16},{12,20},{16,8},{20,12},{24,0},{28,4},{1,25},{... | collective-permute-start | bytes 1544 | tf_op jit(solution)/shard_map/ppermute | solution.py:460
  12.9 9.9 %copy-start.6 = (s32[16,6]{0,1:T(8,128)S(1)}, s32[16,6]{0,1:T(8,128)}, u32[]{:S(2)}) copy-start(s32[16,6]{0,1:T(8,128)} %param.18) | copy-start | bytes 1156
  12.9 9.9 %copy-start.7 = (f32[16,6]{0,1:T(8,128)S(1)}, f32[16,6]{0,1:T(8,128)}, u32[]{:S(2)}) copy-start(f32[16,6]{0,1:T(8,128)} %param.19) | copy-start | bytes 1156
  12.9 11.1 %all-to-all-start = ((bf16[4,16,4096]{2,1,0:T(8,128)(2,1)}), bf16[4,16,4096]{2,1,0:T(8,128)(2,1)S(1)}, u32[]{:S(2)}, u32[]{:S(2)}) async-start(bf16[4,16,4096]{2,1,0:T(8,128)(2,1)} %get-tuple-element.28), calls=%async_computation | async-start | bytes 1048576 | tf_op jit(solution)/shard_map/all_to_all | solution.py:457
  16.5 1.2 %collective-permute-start.4 = (f32[16,128]{1,0:T(8,128)S(1)}, f32[16,128]{1,0:T(8,128)S(1)}, u32[]{:S(2)}, u32[]{:S(2)}) collective-permute-start(f32[16,128]{1,0:T(8,128)S(1)} %get-tuple-element.26), channel_id=1, source_target_pairs={{0,4},{4,0},{8,12},{12,8},{16,20},{20,16},{24,28},{28,24},{1,5},{5... | collective-permute-start | bytes 24584 | tf_op jit(solution)/shard_map/ppermute | solution.py:453
  16.6 6.2 %copy-start.5 = (f32[32,16]{0,1:T(8,128)S(1)}, f32[32,16]{0,1:T(8,128)}, u32[]{:S(2)}) copy-start(f32[32,16]{0,1:T(8,128)} %param.15) | copy-start | bytes 6148
  16.6 6.2 %copy-start.3 = (f32[2,32,16]{1,2,0:T(8,128)S(1)}, f32[2,32,16]{1,2,0:T(8,128)}, u32[]{:S(2)}) copy-start(f32[2,32,16]{1,2,0:T(8,128)} %param.14) | copy-start | bytes 12292
  17.7 5.1 %copy-start.4 = (s32[32,16]{0,1:T(8,128)S(1)}, s32[32,16]{0,1:T(8,128)}, u32[]{:S(2)}) copy-start(s32[32,16]{0,1:T(8,128)} %param.17) | copy-start | bytes 6148
  17.7 5.0 %collective-permute-start.5 = (f32[32,128]{1,0:T(8,128)S(1)}, f32[32,128]{1,0:T(8,128)S(1)}, u32[]{:S(2)}, u32[]{:S(2)}) collective-permute-start(f32[32,128]{1,0:T(8,128)S(1)} %constant_dynamic-update-slice_fusion.message), channel_id=1, source_target_pairs={{0,1},{1,2},{2,3},{5,4},{6,5},{7,6},{8,9},{9,10},{10,11},{13,12},{... | collective-permute-start | bytes 49160 | tf_op jit(solution)/shard_map/ppermute | solution.py:492
  22.8 1.2 %collective-permute-start.6 = (f32[32,128]{1,0:T(8,128)S(1)}, f32[32,128]{1,0:T(8,128)S(1)}, u32[]{:S(2)}, u32[]{:S(2)}) collective-permute-start(f32[32,128]{1,0:T(8,128)S(1)} %collective-permute-done.5.mine), channel_id=1, source_target_pairs={{0,4},{4,0},{8,12},{12,8},{16,20},{20,16},{24,28},{28,24},{1,5},{5... | collective-permute-start | bytes 49160 | tf_op jit(solution)/shard_map/ppermute | solution.py:453
  22.8 0.7 %copy-start.8 = (s32[32]{0:T(128)S(1)}, s32[32]{0:T(128)}, u32[]{:S(2)}) copy-start(s32[32]{0:T(128)} %param.16) | copy-start | bytes 388
  24.8 1.6 %collective-permute-start.7 = (bf16[32,4096]{1,0:T(8,128)(2,1)S(1)}, bf16[32,4096]{1,0:T(8,128)(2,1)S(1)}, u32[]{:S(2)}, u32[]{:S(2)}) collective-permute-start(bf16[32,4096]{1,0:T(8,128)(2,1)S(1)} %get-tuple-element.29.own), channel_id=1, source_target_pairs={{0,4},{4,0},{8,12},{12,8},{16,20},{20,16},{24,28},{28,24},{1,5},{5... | collective-permute-start | bytes 786440 | tf_op jit(solution)/shard_map/ppermute | solution.py:453

commit v11 on v9

--- a/solution.py
+++ b/solution.py
@@ -61,7 +61,7 @@
     rows = parts * tiles
 
     def kernel(st0, st1, df0, df1, pb0, pb1, am, slot, *outs):
-        notes, trail, keys = outs[:pairs], outs[pairs], outs[pairs + 1]
+        *notes, trail, keys = outs
         m = here()
         lane = iota((1, LANES), 1)
         last = tiles - 1
@@ -98,8 +98,10 @@
                 asked = asked + lax.dot_general(pair, spot, (((1,), (1,)), ((), ())), preferred_element_type=F32)
                 column = column_of(source * capacity + rank)
                 keys[c, p * tiles:(p + 1) * tiles, :] = jnp.broadcast_to(column, (tiles, LANES))
-        for k in range(pairs):
-            notes[k][...] = jnp.where(lane < EDGE_AT, asked[k:k + 1, :] - 1.0, edge)
+        evens = [[k] for k in range(0, pairs, 2)]
+        for ref, rows_of in zip(notes, evens + [list(range(1, pairs, 2))]):
+            for i, k in enumerate(rows_of):
+                ref[i:i + 1, :] = jnp.where(lane < EDGE_AT, asked[k:k + 1, :] - 1.0, edge)
 
     return kernel
 
@@ -298,17 +300,24 @@
     return kernel
 
 
-def make_send(pairs, rows):
+def read_notes(refs, spots):
+    return [refs[i][row:row + 1, :] for i, row in spots]
+
+
+def make_send(pairs, rows, spots):
+    count = 1 + max(i for i, _ in spots)
+
     def kernel(own, other, trail, *refs):
-        notes, sends, half = refs[:pairs], refs[pairs:2 * pairs], refs[2 * pairs]
+        notes = read_notes(refs, spots)
+        sends, half = refs[count:count + pairs], refs[count + pairs]
         prior = jnp.concatenate([own[...], other[...]], axis=0)
-        sent = requested([x[...] for x in notes], prior, 0, rows)
+        sent = requested(notes, prior, 0, rows)
         for k in range(pairs):
             sends[k][...] = sent[k * rows:(k + 1) * rows, :].astype(BF16)
         size = padded(pairs)
         half[...] = jnp.zeros(half.shape, F32)
         for k in range(pairs):
-            half[k:k + 1, :] = notes[k][...]
+            half[k:k + 1, :] = notes[k]
         half[size:, :] = trail[...]
 
     return kernel
@@ -363,11 +372,14 @@
     return kernel
 
 
-def make_send_second(pairs, rows, parts, tiles, cells, share):
+def make_send_second(pairs, rows, parts, tiles, cells, share, spots):
+    count = 1 + max(i for i, _ in spots)
+
     def kernel(own, other, where, terms, local, *refs):
-        notes, kept, outs, sums = refs[:pairs], refs[pairs:2 * pairs], refs[2 * pairs:3 * pairs], refs[3 * pairs]
+        notes, refs = read_notes(refs, spots), refs[count:]
+        kept, outs, sums = refs[:pairs], refs[pairs:2 * pairs], refs[2 * pairs]
         prior = jnp.concatenate([own[...], other[...]], axis=0)
-        sent = requested([x[...] for x in notes], prior, 1, rows)
+        sent = requested(notes, prior, 1, rows)
         extra = kept[0].shape[1]
         for k in range(pairs):
             outs[k][:, :cells] = sent[k * rows:(k + 1) * rows, :].astype(BF16)
@@ -433,7 +445,7 @@
     edges = [state, state, diffusivity, diffusivity, model_perturbation, model_perturbation, member_of, slot_of]
     *notes, trail, keys = call(
         make_prepare(members, capacity, parts, tiles),
-        [((1, LANES), F32)] * pairs + [((8, LANES), F32), ((CYCLES, parts * tiles, LANES), I32)],
+        [((1, LANES), F32)] * (pairs // 2) + [((pairs // 2, LANES), F32), ((8, LANES), F32), ((CYCLES, parts * tiles, LANES), I32)],
         [pltpu.with_memory_space_constraint(x, pltpu.HBM) for x in edges],
         [
             block((parts, tiles, LANES), 0),
@@ -457,7 +469,22 @@
             got.append(lax.ppermute(sends[k], "member", [(i, i ^ (2 * k)) for i in range(members)]))
         return got
 
-    notes = exchange(notes)
+    held = {k: (notes[k // 2], 0) for k in range(0, pairs, 2)}
+    held.update({k: (notes[-1], k // 2) for k in range(1, pairs, 2)})
+    bit = 1
+    while bit < pairs:
+        moving = [k for k in range(pairs) if k & bit]
+        message = notes[-1]
+        if bit > 1:
+            message = jnp.concatenate([held[k][0][held[k][1]:held[k][1] + 1] for k in moving], axis=0)
+        arrived = lax.ppermute(message, "member", [(i, i ^ (2 * bit)) for i in range(members)])
+        held.update({k: (arrived, i) for i, k in enumerate(moving)})
+        bit *= 2
+    notes = []
+    for x, _ in held.values():
+        if not any(x is y for y in notes):
+            notes.append(x)
+    spots = [([x is held[k][0] for x in notes].index(True), held[k][1]) for k in range(pairs)]
 
     where, terms, local = call(
         make_observe(blocks, per_block, tiles, near),
@@ -478,7 +505,7 @@
     other = trade(prior)
     size = padded(pairs)
     *sends, half = call(
-        make_send(pairs, rows),
+        make_send(pairs, rows, spots),
         [((rows, cells), BF16)] * pairs + [((size + trail.shape[0], LANES), F32)],
         [prior, other, trail, *notes],
         name="send_first",
@@ -511,7 +538,7 @@
         name="assess_first",
     )
     sends = call(
-        make_send_second(pairs, rows, parts, tiles, cells, share),
+        make_send_second(pairs, rows, parts, tiles, cells, share, spots),
         [((rows, cells + CYCLES * extra), BF16)] * pairs,
         [second, trade(second), where, terms, local, *notes, *kept],
         scratch=sums,

time: 37.1 us -> 37.8 us (1.019)
  starting transfers between devices: 15.7 us -> 16.6 us
    ppermute x0 -> x2, starting transfers between devices: none -> 4.68 us  [body(): lax.ppermute(message, 'member', [(i, i ^ 2 * bit) for i in range(members)])]
    ppermute x9 -> x6, starting transfers between devices: 11.2 us -> 7.16 us  [exchange(): lax.ppermute(sends[k], 'member', [(i, i ^ 2 * k) for i in range(members)])]
    ppermute x9 -> x6, waiting for transfers between devices: 11.4 us -> 7.91 us  [exchange(): lax.ppermute(sends[k], 'member', [(i, i ^ 2 * k) for i in range(members)])]
    ppermute x0 -> x2, waiting for transfers between devices: none -> 3.1 us  [body(): lax.ppermute(message, 'member', [(i, i ^ 2 * bit) for i in range(members)])]
    ppermute x1, starting transfers between devices: 3.6 us -> 4.06 us  [body(): mine = lax.ppermute(message, ('member', 'region'), steps)]
  transfers between devices with their start and end apart: 14 -> 13, of which waited for: 7 -> 8; matrix products, arithmetic and copies ran while one was open for 0% -> 0% of each run, Pallas kernels for 2% -> 2%
where the time goes in v11:
time: 37.8 us; the launch traced here: 37.5 us
  starting transfers between devices  16.6 us (44%)
  waiting for transfers between devices  13.5 us (36%)
  Pallas kernels  5.88 us (16%)
  between operations  0.82 us (2%)
  local copies, waits for them, and re-layouts  0.67 us (2%)
    ppermute x6, waiting for transfers between devices, exchange(): lax.ppermute(sends[k], 'member', [(i, i ^ 2 * k) for i in range(members)])  7.91 us
    ppermute x6, starting transfers between devices, exchange(): lax.ppermute(sends[k], 'member', [(i, i ^ 2 * k) for i in range(members)])  7.16 us
    pallas_call x8, Pallas kernels, call(): pl.pallas_call(kernel, out_shape=[jax.ShapeDtypeStruct(s, d) for s, d in...  5.88 us
    ppermute x2, starting transfers between devices, body(): lax.ppermute(message, 'member', [(i, i ^ 2 * bit) for i in range(members)])  4.68 us
    ppermute x1, starting transfers between devices, body(): mine = lax.ppermute(message, ('member', 'region'), steps)  4.06 us
    ppermute x2, waiting for transfers between devices, body(): lax.ppermute(message, 'member', [(i, i ^ 2 * bit) for i in range(members)])  3.1 us
    ppermute x1, waiting for transfers between devices, body(): mine = lax.ppermute(message, ('member', 'region'), steps)  1.43 us
    ppermute x4, waiting for transfers between devices, trade(): return lax.ppermute(x, 'member', [(i, i ^ 1) for i in range(members)])  1.11 us
  transfers between devices with their start and end apart: 13, of which 8 were waited for; matrix products, arithmetic and copies ran while one was open for 0% of the time, Pallas kernels for 2%

profile of v11, /device:TPU:0, one launch (start us, length us, event | category | flops | bytes accessed | tf_op | source)
XLA Modules:
  0.0 37.5 jit_solution(2260088548614837048)
XLA Ops:
  0.6 0.0 copy-start
  0.6 0.0 copy-start.1
  0.7 0.0 copy-start.2
  0.7 1.3 %prepare.1 = (f32[1,128]{1,0:T(1,128)S(1)}, f32[1,128]{1,0:T(1,128)S(1)}, f32[2,128]{1,0:T(2,128)S(1)}, f32[8,128]{1,0:T(8,128)S(1)}, s32[2,32,128]{2,1,0:T(8,128)S(1)}) custom-call(bf16[2,16,4096]{2,1,0:T(8,128)(2,1)} %state.1, bf16[2,16,4096]{2,1,0:T(8,128)(2,1)} %state.1, f32[16,4096]{1,0:T(8,128)} %diff.3, f32[16,4096]{1,0:T(8,128)} %diff.3, ...), custom_call_target="tpu_custom_call" | custom-call | tf_op jit(solution)/shard_map/prepare/pallas_call | solution.py:28
  2.0 0.0 copy-done
  2.0 0.0 copy-done.1
  2.0 0.0 copy-done.2
  2.0 0.6 %forecast_first.1.own = bf16[32,4096]{1,0:T(8,128)(2,1)S(1)} custom-call(bf16[2,16,4096]{2,1,0:T(8,128)(2,1)S(1)} %copy-done.2, f32[16,4096]{1,0:T(8,128)S(1)} %copy-done.1, bf16[2,2,16,4096]{3,2,1,0:T(8,128)(2,1)S(1)} %copy-done, f32[8,128]{1,0:T(8,128)S(1)} %get-tuple-element.27.after.trail), custom_call_target="tpu_custom_call" | custom-call | tf_op jit(solution)/shard_map/forecast_first/pallas_call | solution.py:28
  2.7 0.5 %collective-permute-start = (bf16[32,4096]{1,0:T(8,128)(2,1)S(1)}, bf16[32,4096]{1,0:T(8,128)(2,1)S(1)}, u32[]{:S(2)}, u32[]{:S(2)}) collective-permute-start(bf16[32,4096]{1,0:T(8,128)(2,1)S(1)} %forecast_first.1.own), channel_id=1, source_target_pairs={{0,4},{4,0},{8,12},{12,8},{16,20},{20,16},{24,28},{28,24},{1,5},{5... | collective-permute-start | bytes 786440 | tf_op jit(solution)/shard_map/ppermute | solution.py:464
  3.2 2.6 %collective-permute-start.1 = (f32[2,128]{1,0:T(2,128)S(1)}, f32[2,128]{1,0:T(2,128)S(1)}, u32[]{:S(2)}, u32[]{:S(2)}) collective-permute-start(f32[2,128]{1,0:T(2,128)S(1)} %get-tuple-element.30), channel_id=1, source_target_pairs={{0,8},{4,12},{8,0},{12,4},{16,24},{20,28},{24,16},{28,20},{1,9},{5... | collective-permute-start | bytes 3080 | tf_op jit(solution)/shard_map/ppermute | solution.py:480
  5.7 1.5 %collective-permute-done.1.refs_2_ = f32[2,128]{1,0:T(2,128)S(1)} collective-permute-done((f32[2,128]{1,0:T(2,128)S(1)}, f32[2,128]{1,0:T(2,128)S(1)}, u32[]{:S(2)}, u32[]{:S(2)}) %collective-permute-start.1) | collective-permute-done | bytes 1056 | tf_op jit(solution)/shard_map/ppermute | solution.py:480
  7.3 2.1 %collective-permute-start.2 = (f32[2,128]{1,0:T(2,128)S(1)}, f32[2,128]{1,0:T(2,128)S(1)}, u32[]{:S(2)}, u32[]{:S(2)}) collective-permute-start(f32[2,128]{1,0:T(2,128)S(1)} %pad_maximum_fusion), channel_id=1, source_target_pairs={{0,16},{4,20},{8,24},{12,28},{16,0},{20,4},{24,8},{28,12},{1,17},{... | collective-permute-start | bytes 3080 | tf_op jit(solution)/shard_map/ppermute | solution.py:480
  9.4 1.5 %collective-permute-done.2.refs_1_ = f32[2,128]{1,0:T(2,128)S(1)} collective-permute-done((f32[2,128]{1,0:T(2,128)S(1)}, f32[2,128]{1,0:T(2,128)S(1)}, u32[]{:S(2)}, u32[]{:S(2)}) %collective-permute-start.2) | collective-permute-done | bytes 1056 | tf_op jit(solution)/shard_map/ppermute | solution.py:480
  11.0 0.0 collective-permute-done.other
  11.0 0.3 send_first.1
  11.3 0.0 copy-start.6
  11.3 0.0 copy-start.7
  11.3 0.1 collective-permute-start.3
  11.4 0.0 copy-start.3
  11.4 2.1 %collective-permute-start.6 = (bf16[16,4096]{1,0:T(8,128)(2,1)S(1)}, bf16[16,4096]{1,0:T(8,128)(2,1)S(1)}, u32[]{:S(2)}, u32[]{:S(2)}) collective-permute-start(bf16[16,4096]{1,0:T(8,128)(2,1)S(1)} %get-tuple-element.34), channel_id=1, source_target_pairs={{0,8},{4,12},{8,0},{12,4},{16,24},{20,28},{24,16},{28,20},{1,9},{5... | collective-permute-start | bytes 393224 | tf_op jit(solution)/shard_map/ppermute | solution.py:469
  13.5 1.5 %collective-permute-start.7 = (bf16[16,4096]{1,0:T(8,128)(2,1)S(1)}, bf16[16,4096]{1,0:T(8,128)(2,1)S(1)}, u32[]{:S(2)}, u32[]{:S(2)}) collective-permute-start(bf16[16,4096]{1,0:T(8,128)(2,1)S(1)} %get-tuple-element.35), channel_id=1, source_target_pairs={{0,16},{4,20},{8,24},{12,28},{16,0},{20,4},{24,8},{28,12},{1,17},{... | collective-permute-start | bytes 393224 | tf_op jit(solution)/shard_map/ppermute | solution.py:469
  15.0 0.0 collective-permute-start.8
  15.1 0.0 collective-permute-done.3
  15.1 4.1 %collective-permute-start.4 = (f32[32,128]{1,0:T(8,128)S(1)}, f32[32,128]{1,0:T(8,128)S(1)}, u32[]{:S(2)}, u32[]{:S(2)}) collective-permute-start(f32[32,128]{1,0:T(8,128)S(1)} %constant_dynamic-update-slice_fusion.message), channel_id=1, source_target_pairs={{0,1},{1,2},{2,3},{5,4},{6,5},{7,6},{8,9},{9,10},{10,11},{13,12},{... | collective-permute-start | bytes 49160 | tf_op jit(solution)/shard_map/ppermute | solution.py:519
  19.1 1.4 %collective-permute-done.4.mine = f32[32,128]{1,0:T(8,128)S(1)} collective-permute-done((f32[32,128]{1,0:T(8,128)S(1)}, f32[32,128]{1,0:T(8,128)S(1)}, u32[]{:S(2)}, u32[]{:S(2)}) %collective-permute-start.4) | collective-permute-done | bytes 16416 | tf_op jit(solution)/shard_map/ppermute | solution.py:519
  20.6 0.0 collective-permute-start.5
  20.6 0.0 copy-done.5
  20.6 0.0 copy-done.6
  20.6 0.0 copy-done.7
  20.6 0.0 copy-done.3
  20.6 0.6 %copy-done.8 = s32[32]{0:T(128)S(1)} copy-done((s32[32]{0:T(128)S(1)}, s32[32]{0:T(128)}, u32[]{:S(2)}) %copy-start.8) | copy-done | bytes 152
  21.2 0.2 observe.1
  21.4 0.3 collective-permute-done.5.theirs
  21.7 0.0 collective-permute-done.6.refs_1_
  21.7 0.1 collective-permute-done.7.refs_2_
  21.9 0.0 collective-permute-done.8.refs_3_
  21.9 0.9 %forecast_second.1 = (bf16[32,4096]{1,0:T(8,128)(2,1)S(1)}, f32[32,256]{1,0:T(8,128)S(1)}, f32[32,256]{1,0:T(8,128)S(1)}) custom-call(s32[2,32,128]{2,1,0:T(8,128)S(1)} %get-tuple-element.26.keys, f32[16,4096]{1,0:T(8,128)S(1)} %copy-done.1, bf16[2,2,16,4096]{3,2,1,0:T(8,128)(2,1)S(1)} %copy-done, f32[32,128]{1,0:T(8,128)S(1)} %constant_dynamic-update-slice_fusion.message, ...), custom_call_target="tpu_custom_call" | custom-call | tf_op jit(solution)/shard_map/forecast_second/pallas_call | solution.py:28
  22.8 0.1 collective-permute-start.9
  22.9 0.7 %assess_first.1 = (bf16[16,640]{1,0:T(8,128)(2,1)S(1)}, bf16[16,640]{1,0:T(8,128)(2,1)S(1)}, bf16[16,640]{1,0:T(8,128)(2,1)S(1)}, bf16[16,640]{1,0:T(8,128)(2,1)S(1)}) custom-call(bf16[32,4096]{1,0:T(8,128)(2,1)S(1)} %forecast_first.1.own, bf16[32,4096]{1,0:T(8,128)(2,1)S(1)} %collective-permute-done.other, f32[32,256]{1,0:T(8,128)S(1)} %get-tuple-element.40.low, ...), custom_call_target="tpu_custom_call" | custom-call | tf_op jit(solution)/shard_map/assess_first/pallas_call | solution.py:28
  23.6 0.8 %collective-permute-done.9.other = bf16[32,4096]{1,0:T(8,128)(2,1)S(1)} collective-permute-done((bf16[32,4096]{1,0:T(8,128)(2,1)S(1)}, bf16[32,4096]{1,0:T(8,128)(2,1)S(1)}, u32[]{:S(2)}, u32[]{:S(2)}) %collective-permute-start.9) | collective-permute-done | bytes 262176 | tf_op jit(solution)/shard_map/ppermute | solution.py:464
  24.4 0.9 %send_second.1 = (bf16[16,5376]{1,0:T(8,128)(2,1)S(1)}, bf16[16,5376]{1,0:T(8,128)(2,1)S(1)}, bf16[16,5376]{1,0:T(8,128)(2,1)S(1)}, bf16[16,5376]{1,0:T(8,128)(2,1)S(1)}) custom-call(bf16[32,4096]{1,0:T(8,128)(2,1)S(1)} %get-tuple-element.37.own, bf16[32,4096]{1,0:T(8,128)(2,1)S(1)} %collective-permute-done.9.other, ...), custom_call_target="tpu_custom_call" | custom-call | tf_op jit(solution)/shard_map/send_second/pallas_call | solution.py:28
  25.3 1.4 %collective-permute-start.10 = (bf16[16,5376]{1,0:T(8,128)(2,1)S(1)}, bf16[16,5376]{1,0:T(8,128)(2,1)S(1)}, u32[]{:S(2)}, u32[]{:S(2)}) collective-permute-start(bf16[16,5376]{1,0:T(8,128)(2,1)S(1)} %get-tuple-element.47), channel_id=1, source_target_pairs={{0,8},{4,12},{8,0},{12,4},{16,24},{20,28},{24,16},{28,20},{1,9},{5... | collective-permute-start | bytes 516104 | tf_op jit(solution)/shard_map/ppermute | solution.py:469
  26.7 1.5 %collective-permute-start.11 = (bf16[16,5376]{1,0:T(8,128)(2,1)S(1)}, bf16[16,5376]{1,0:T(8,128)(2,1)S(1)}, u32[]{:S(2)}, u32[]{:S(2)}) collective-permute-start(bf16[16,5376]{1,0:T(8,128)(2,1)S(1)} %get-tuple-element.48), channel_id=1, source_target_pairs={{0,16},{4,20},{8,24},{12,28},{16,0},{20,4},{24,8},{28,12},{1,17},{... | collective-permute-start | bytes 516104 | tf_op jit(solution)/shard_map/ppermute | solution.py:469
  28.2 0.6 %collective-permute-start.12 = (bf16[16,5376]{1,0:T(8,128)(2,1)S(1)}, bf16[16,5376]{1,0:T(8,128)(2,1)S(1)}, u32[]{:S(2)}, u32[]{:S(2)}) collective-permute-start(bf16[16,5376]{1,0:T(8,128)(2,1)S(1)} %get-tuple-element.49), channel_id=1, source_target_pairs={{0,24},{4,28},{8,16},{12,20},{16,8},{20,12},{24,0},{28,4},{1,25},{... | collective-permute-start | bytes 516104 | tf_op jit(solution)/shard_map/ppermute | solution.py:469
  28.8 3.7 %collective-permute-done.10.refs_1_ = bf16[16,5376]{1,0:T(8,128)(2,1)S(1)} collective-permute-done((bf16[16,5376]{1,0:T(8,128)(2,1)S(1)}, bf16[16,5376]{1,0:T(8,128)(2,1)S(1)}, u32[]{:S(2)}, u32[]{:S(2)}) %collective-permute-start.10) | collective-permute-done | bytes 172064 | tf_op jit(solution)/shard_map/ppermute | solution.py:469
  32.6 4.0 %collective-permute-done.11.refs_2_ = bf16[16,5376]{1,0:T(8,128)(2,1)S(1)} collective-permute-done((bf16[16,5376]{1,0:T(8,128)(2,1)S(1)}, bf16[16,5376]{1,0:T(8,128)(2,1)S(1)}, u32[]{:S(2)}, u32[]{:S(2)}) %collective-permute-start.11) | collective-permute-done | bytes 172064 | tf_op jit(solution)/shard_map/ppermute | solution.py:469
  36.6 0.0 collective-permute-done.12.refs_3_
  36.6 0.9 %finish.1 = (bf16[2,16,4096]{2,1,0:T(8,128)(2,1)}, f32[2,16,512]{2,1,0:T(8,128)}) custom-call(s32[2,32,128]{2,1,0:T(8,128)S(1)} %get-tuple-element.26.keys, bf16[16,5376]{1,0:T(8,128)(2,1)S(1)} %get-tuple-element.46.refs_0_, bf16[16,5376]{1,0:T(8,128)(2,1)S(1)} %collective-permute-done.10.refs_1_, bf16[16,5376]{1,0:T(8,128)(2,1)S(1)} %collective-permute-done.11.refs_2_, ...), custom_call_target="tpu_custom_call" | custom-call | tf_op jit(solution)/shard_map/finish/pallas_call | solution.py:28
  (8 shorter events, 0.0 us)
Async XLA Ops:
  0.6 1.3 %copy-start = (bf16[2,2,16,4096]{3,2,1,0:T(8,128)(2,1)S(1)}, bf16[2,2,16,4096]{3,2,1,0:T(8,128)(2,1)}, u32[]{:S(2)}) copy-start(bf16[2,2,16,4096]{3,2,1,0:T(8,128)(2,1)} %pert.3) | copy-start | bytes 1572868
  0.6 1.3 %copy-start.1 = (f32[16,4096]{1,0:T(8,128)S(1)}, f32[16,4096]{1,0:T(8,128)}, u32[]{:S(2)}) copy-start(f32[16,4096]{1,0:T(8,128)} %diff.3) | copy-start | bytes 786436
  0.7 1.3 %copy-start.2 = (bf16[2,16,4096]{2,1,0:T(8,128)(2,1)S(1)}, bf16[2,16,4096]{2,1,0:T(8,128)(2,1)}, u32[]{:S(2)}) copy-start(bf16[2,16,4096]{2,1,0:T(8,128)(2,1)} %state.1) | copy-start | bytes 786436
  2.7 8.3 %collective-permute-start = (bf16[32,4096]{1,0:T(8,128)(2,1)S(1)}, bf16[32,4096]{1,0:T(8,128)(2,1)S(1)}, u32[]{:S(2)}, u32[]{:S(2)}) collective-permute-start(bf16[32,4096]{1,0:T(8,128)(2,1)S(1)} %forecast_first.1.own), channel_id=1, source_target_pairs={{0,4},{4,0},{8,12},{12,8},{16,20},{20,16},{24,28},{28,24},{1,5},{5... | collective-permute-start | bytes 786440 | tf_op jit(solution)/shard_map/ppermute | solution.py:464
  3.2 4.1 %collective-permute-start.1 = (f32[2,128]{1,0:T(2,128)S(1)}, f32[2,128]{1,0:T(2,128)S(1)}, u32[]{:S(2)}, u32[]{:S(2)}) collective-permute-start(f32[2,128]{1,0:T(2,128)S(1)} %get-tuple-element.30), channel_id=1, source_target_pairs={{0,8},{4,12},{8,0},{12,4},{16,24},{20,28},{24,16},{28,20},{1,9},{5... | collective-permute-start | bytes 3080 | tf_op jit(solution)/shard_map/ppermute | solution.py:480
  7.3 3.7 %collective-permute-start.2 = (f32[2,128]{1,0:T(2,128)S(1)}, f32[2,128]{1,0:T(2,128)S(1)}, u32[]{:S(2)}, u32[]{:S(2)}) collective-permute-start(f32[2,128]{1,0:T(2,128)S(1)} %pad_maximum_fusion), channel_id=1, source_target_pairs={{0,16},{4,20},{8,24},{12,28},{16,0},{20,4},{24,8},{28,12},{1,17},{... | collective-permute-start | bytes 3080 | tf_op jit(solution)/shard_map/ppermute | solution.py:480
  11.0 9.6 %copy-start.5 = (f32[32,16]{0,1:T(8,128)S(1)}, f32[32,16]{0,1:T(8,128)}, u32[]{:S(2)}) copy-start(f32[32,16]{0,1:T(8,128)} %param.15) | copy-start | bytes 6148
  11.3 9.2 %copy-start.6 = (s32[16,6]{0,1:T(8,128)S(1)}, s32[16,6]{0,1:T(8,128)}, u32[]{:S(2)}) copy-start(s32[16,6]{0,1:T(8,128)} %param.18) | copy-start | bytes 1156
  11.3 9.2 %copy-start.7 = (f32[16,6]{0,1:T(8,128)S(1)}, f32[16,6]{0,1:T(8,128)}, u32[]{:S(2)}) copy-start(f32[16,6]{0,1:T(8,128)} %param.19) | copy-start | bytes 1156
  11.3 3.7 %collective-permute-start.3 = (f32[16,128]{1,0:T(8,128)S(1)}, f32[16,128]{1,0:T(8,128)S(1)}, u32[]{:S(2)}, u32[]{:S(2)}) collective-permute-start(f32[16,128]{1,0:T(8,128)S(1)} %get-tuple-element.31), channel_id=1, source_target_pairs={{0,4},{4,0},{8,12},{12,8},{16,20},{20,16},{24,28},{28,24},{1,5},{5... | collective-permute-start | bytes 24584 | tf_op jit(solution)/shard_map/ppermute | solution.py:464
  11.4 9.1 %copy-start.3 = (f32[2,32,16]{1,2,0:T(8,128)S(1)}, f32[2,32,16]{1,2,0:T(8,128)}, u32[]{:S(2)}) copy-start(f32[2,32,16]{1,2,0:T(8,128)} %param.14) | copy-start | bytes 12292
  11.4 10.3 %collective-permute-start.6 = (bf16[16,4096]{1,0:T(8,128)(2,1)S(1)}, bf16[16,4096]{1,0:T(8,128)(2,1)S(1)}, u32[]{:S(2)}, u32[]{:S(2)}) collective-permute-start(bf16[16,4096]{1,0:T(8,128)(2,1)S(1)} %get-tuple-element.34), channel_id=1, source_target_pairs={{0,8},{4,12},{8,0},{12,4},{16,24},{20,28},{24,16},{28,20},{1,9},{5... | collective-permute-start | bytes 393224 | tf_op jit(solution)/shard_map/ppermute | solution.py:469
  13.5 8.4 %collective-permute-start.7 = (bf16[16,4096]{1,0:T(8,128)(2,1)S(1)}, bf16[16,4096]{1,0:T(8,128)(2,1)S(1)}, u32[]{:S(2)}, u32[]{:S(2)}) collective-permute-start(bf16[16,4096]{1,0:T(8,128)(2,1)S(1)} %get-tuple-element.35), channel_id=1, source_target_pairs={{0,16},{4,20},{8,24},{12,28},{16,0},{20,4},{24,8},{28,12},{1,17},{... | collective-permute-start | bytes 393224 | tf_op jit(solution)/shard_map/ppermute | solution.py:469
  15.0 6.9 %collective-permute-start.8 = (bf16[16,4096]{1,0:T(8,128)(2,1)S(1)}, bf16[16,4096]{1,0:T(8,128)(2,1)S(1)}, u32[]{:S(2)}, u32[]{:S(2)}) collective-permute-start(bf16[16,4096]{1,0:T(8,128)(2,1)S(1)} %get-tuple-element.36), channel_id=1, source_target_pairs={{0,24},{4,28},{8,16},{12,20},{16,8},{20,12},{24,0},{28,4},{1,25},{... | collective-permute-start | bytes 393224 | tf_op jit(solution)/shard_map/ppermute | solution.py:469
  15.1 5.5 %copy-start.4 = (s32[32,16]{0,1:T(8,128)S(1)}, s32[32,16]{0,1:T(8,128)}, u32[]{:S(2)}) copy-start(s32[32,16]{0,1:T(8,128)} %param.17) | copy-start | bytes 6148
  15.1 5.5 %collective-permute-start.4 = (f32[32,128]{1,0:T(8,128)S(1)}, f32[32,128]{1,0:T(8,128)S(1)}, u32[]{:S(2)}, u32[]{:S(2)}) collective-permute-start(f32[32,128]{1,0:T(8,128)S(1)} %constant_dynamic-update-slice_fusion.message), channel_id=1, source_target_pairs={{0,1},{1,2},{2,3},{5,4},{6,5},{7,6},{8,9},{9,10},{10,11},{13,12},{... | collective-permute-start | bytes 49160 | tf_op jit(solution)/shard_map/ppermute | solution.py:519
  20.6 1.2 %collective-permute-start.5 = (f32[32,128]{1,0:T(8,128)S(1)}, f32[32,128]{1,0:T(8,128)S(1)}, u32[]{:S(2)}, u32[]{:S(2)}) collective-permute-start(f32[32,128]{1,0:T(8,128)S(1)} %collective-permute-done.4.mine), channel_id=1, source_target_pairs={{0,4},{4,0},{8,12},{12,8},{16,20},{20,16},{24,28},{28,24},{1,5},{5... | collective-permute-start | bytes 49160 | tf_op jit(solution)/shard_map/ppermute | solution.py:464
  20.6 0.7 %copy-start.8 = (s32[32]{0:T(128)S(1)}, s32[32]{0:T(128)}, u32[]{:S(2)}) copy-start(s32[32]{0:T(128)} %param.16) | copy-start | bytes 388
  22.8 1.6 %collective-permute-start.9 = (bf16[32,4096]{1,0:T(8,128)(2,1)S(1)}, bf16[32,4096]{1,0:T(8,128)(2,1)S(1)}, u32[]{:S(2)}, u32[]{:S(2)}) collective-permute-start(bf16[32,4096]{1,0:T(8,128)(2,1)S(1)} %get-tuple-element.37.own), channel_id=1, source_target_pairs={{0,4},{4,0},{8,12},{12,8},{16,20},{20,16},{24,28},{28,24},{1,5},{5... | collective-permute-start | bytes 786440 | tf_op jit(solution)/shard_map/ppermute | solution.py:464
  25.3 7.3 %collective-permute-start.10 = (bf16[16,5376]{1,0:T(8,128)(2,1)S(1)}, bf16[16,5376]{1,0:T(8,128)(2,1)S(1)}, u32[]{:S(2)}, u32[]{:S(2)}) collective-permute-start(bf16[16,5376]{1,0:T(8,128)(2,1)S(1)} %get-tuple-element.47), channel_id=1, source_target_pairs={{0,8},{4,12},{8,0},{12,4},{16,24},{20,28},{24,16},{28,20},{1,9},{5... | collective-permute-start | bytes 516104 | tf_op jit(solution)/shard_map/ppermute | solution.py:469
  26.7 9.9 %collective-permute-start.11 = (bf16[16,5376]{1,0:T(8,128)(2,1)S(1)}, bf16[16,5376]{1,0:T(8,128)(2,1)S(1)}, u32[]{:S(2)}, u32[]{:S(2)}) collective-permute-start(bf16[16,5376]{1,0:T(8,128)(2,1)S(1)} %get-tuple-element.48), channel_id=1, source_target_pairs={{0,16},{4,20},{8,24},{12,28},{16,0},{20,4},{24,8},{28,12},{1,17},{... | collective-permute-start | bytes 516104 | tf_op jit(solution)/shard_map/ppermute | solution.py:469
  28.2 8.4 %collective-permute-start.12 = (bf16[16,5376]{1,0:T(8,128)(2,1)S(1)}, bf16[16,5376]{1,0:T(8,128)(2,1)S(1)}, u32[]{:S(2)}, u32[]{:S(2)}) collective-permute-start(bf16[16,5376]{1,0:T(8,128)(2,1)S(1)} %get-tuple-element.49), channel_id=1, source_target_pairs={{0,24},{4,28},{8,16},{12,20},{16,8},{20,12},{24,0},{28,4},{1,25},{... | collective-permute-start | bytes 516104 | tf_op jit(solution)/shard_map/ppermute | solution.py:469

commit v12 on v9

--- a/solution.py
+++ b/solution.py
@@ -49,6 +49,10 @@
 
 EDGE_AT = 32
 STRIDE = 8
+
+
+def falling(pairs):
+    return [0, *range(pairs - 1, 0, -1)]
 
 
 def padded(pairs):
@@ -317,8 +321,8 @@
 def make_assess(pairs, parts, tiles, cells, share):
     size = padded(pairs)
 
-    def kernel(own, other, low, high, where, terms, local, *refs):
-        outs, sums = refs[:pairs], refs[pairs]
+    def kernel(own, other, low, high, where, terms, local, second, *refs):
+        outs, stats, weighted_out, sums = refs[:pairs], refs[pairs], refs[pairs + 1], refs[pairs + 2]
         fixed = []
         for h, prior in enumerate((own, other)):
             for p in range(parts):
@@ -331,6 +335,12 @@
         )
         sums[...] = weighted
         pack_mean(outs, 0, least, total, sums, share)
+        least, total, weighted = assess(
+            [second[p * tiles:(p + 1) * tiles, :] for p in range(parts)],
+            where[...], terms[0:1, :], terms[2:3, :], local[...], parts, tiles, cells,
+        )
+        stats[...] = jnp.where(iota((tiles, LANES), 1) == 0, least, total)
+        weighted_out[...] = weighted
 
     return kernel
 
@@ -364,8 +374,9 @@
 
 
 def make_send_second(pairs, rows, parts, tiles, cells, share):
-    def kernel(own, other, where, terms, local, *refs):
+    def kernel(own, other, where, terms, local, stats, own_sums, *refs):
         notes, kept, outs, sums = refs[:pairs], refs[pairs:2 * pairs], refs[2 * pairs:3 * pairs], refs[3 * pairs]
+        outs = [outs[falling(pairs).index(k)] for k in range(pairs)]
         prior = jnp.concatenate([own[...], other[...]], axis=0)
         sent = requested([x[...] for x in notes], prior, 1, rows)
         extra = kept[0].shape[1]
@@ -373,10 +384,15 @@
             outs[k][:, :cells] = sent[k * rows:(k + 1) * rows, :].astype(BF16)
             outs[k][:, cells:cells + extra] = kept[k][...]
         least, total, weighted = assess(
-            [x[p * tiles:(p + 1) * tiles, :] for x in (own, other) for p in range(parts)],
-            where[...], terms[0:1, :], terms[2:3, :], local[...], 2 * parts, tiles, cells,
+            [other[p * tiles:(p + 1) * tiles, :] for p in range(parts)],
+            where[...], terms[0:1, :], terms[2:3, :], local[...], parts, tiles, cells,
         )
-        sums[...] = weighted
+        mine = stats[:, 0:1]
+        lower = jnp.minimum(least, mine)
+        scale, own_scale = jnp.exp(lower - least), jnp.exp(lower - mine)
+        total = scale * total + own_scale * stats[:, 1:2]
+        sums[...] = scale * weighted + own_scale * own_sums[...]
+        least = lower
         pack_mean(outs, cells + extra, least, total, sums, share)
 
     return kernel
@@ -385,6 +401,7 @@
 def make_last(pairs, rows, parts, tiles, cells):
     def kernel(keys, *refs):
         got, analysis, mean = refs[:pairs], refs[pairs], refs[pairs + 1]
+        got = [got[falling(pairs).index(k)] for k in range(pairs)]
         arrived = jnp.concatenate([x[:, :cells] for x in got], axis=0)
         picked = pick_rows(keys[1], arrived)
         for p in range(parts):
@@ -451,13 +468,13 @@
     def trade(x):
         return lax.ppermute(x, "member", [(i, i ^ 1) for i in range(members)])
 
-    def exchange(sends):
+    def exchange(sends, order):
         got = [sends[0]]
-        for k in range(1, pairs):
-            got.append(lax.ppermute(sends[k], "member", [(i, i ^ (2 * k)) for i in range(members)]))
+        for x, k in list(zip(sends, order))[1:]:
+            got.append(lax.ppermute(x, "member", [(i, i ^ (2 * k)) for i in range(members)]))
         return got
 
-    notes = exchange(notes)
+    notes = exchange(notes, range(pairs))
 
     where, terms, local = call(
         make_observe(blocks, per_block, tiles, near),
@@ -483,7 +500,7 @@
         [prior, other, trail, *notes],
         name="send_first",
     )
-    got = exchange(sends)
+    got = exchange(sends, range(pairs))
     message = jnp.concatenate([half, trade(half)], axis=0)
     steps = []
     for i in range(members):
@@ -503,21 +520,21 @@
         specs,
         name="forecast_second",
     )
-    kept = call(
+    *kept, stats, own_sums = call(
         make_assess(pairs, parts, tiles, cells, share),
-        [((rows, extra), BF16)] * pairs,
-        [prior, other, low, high, where, terms, local],
+        [((rows, extra), BF16)] * pairs + [((tiles, LANES), F32), ((tiles, cells), F32)],
+        [prior, other, low, high, where, terms, local, second],
         scratch=sums,
         name="assess_first",
     )
     sends = call(
         make_send_second(pairs, rows, parts, tiles, cells, share),
         [((rows, cells + CYCLES * extra), BF16)] * pairs,
-        [second, trade(second), where, terms, local, *notes, *kept],
+        [second, trade(second), where, terms, local, stats, own_sums, *notes, *kept],
         scratch=sums,
         name="send_second",
     )
-    got = exchange(sends)
+    got = exchange(sends, falling(pairs))
     return tuple(
         call(
             make_last(pairs, rows, parts, tiles, cells),

time: 37.1 us -> 36.9 us (level)
  transfers between devices with their start and end apart: 14 -> 14, of which waited for: 7 -> 7; matrix products, arithmetic and copies ran while one was open for 0% -> 0% of each run, Pallas kernels for 2% -> 3%
where the time goes in v12:
time: 36.9 us; the launch traced here: 36.7 us
  starting transfers between devices  15.7 us (43%)
  waiting for transfers between devices  13.5 us (37%)
  Pallas kernels  6.08 us (16%)
  between operations  0.83 us (2%)
  local copies, waits for them, and re-layouts  0.67 us (2%)
    ppermute x9, waiting for transfers between devices, exchange(): lax.ppermute(x, 'member', [(i, i ^ 2 * k) for i in range(members)])  11.3 us
    ppermute x9, starting transfers between devices, exchange(): lax.ppermute(x, 'member', [(i, i ^ 2 * k) for i in range(members)])  11.2 us
    pallas_call x8, Pallas kernels, call(): pl.pallas_call(kernel, out_shape=[jax.ShapeDtypeStruct(s, d) for s, d in...  6.08 us
    ppermute x1, starting transfers between devices, body(): mine = lax.ppermute(message, ('member', 'region'), steps)  3.6 us
    ppermute x1, waiting for transfers between devices, body(): mine = lax.ppermute(message, ('member', 'region'), steps)  1.43 us
    ppermute x4, starting transfers between devices, trade(): return lax.ppermute(x, 'member', [(i, i ^ 1) for i in range(members)])  0.86 us
  transfers between devices with their start and end apart: 14, of which 7 were waited for; matrix products, arithmetic and copies ran while one was open for 0% of the time, Pallas kernels for 3%

profile of v12, /device:TPU:0, one launch (start us, length us, event | category | flops | bytes accessed | tf_op | source)
XLA Modules:
  0.0 36.7 jit_solution(270327810942572324)
XLA Ops:
  0.6 0.0 copy-start
  0.6 0.0 copy-start.1
  0.7 0.0 copy-start.2
  0.7 1.3 %prepare.1 = (f32[1,128]{1,0:T(1,128)S(1)}, f32[1,128]{1,0:T(1,128)S(1)}, f32[1,128]{1,0:T(1,128)S(1)}, f32[1,128]{1,0:T(1,128)S(1)}, f32[8,128]{1,0:T(8,128)S(1)}, /*index=5*/s32[2,32,128]{2,1,0:T(8,128)S(1)}) custom-call(bf16[2,16,4096]{2,1,0:T(8,128)(2,1)} %state.1, bf16[2,16,4096]{2,1,0:T(8,128)(2,1)} %state.1, f32[16,4096]{1,0:T(8,128)} %diff.3, ...), custom_call_target="tpu_custom_call" | custom-call | tf_op jit(solution)/shard_map/prepare/pallas_call | solution.py:28
  2.0 0.0 copy-done
  2.0 0.0 copy-done.1
  2.0 0.0 copy-done.2
  2.0 0.6 %forecast_first.1.own = bf16[32,4096]{1,0:T(8,128)(2,1)S(1)} custom-call(bf16[2,16,4096]{2,1,0:T(8,128)(2,1)S(1)} %copy-done.2, f32[16,4096]{1,0:T(8,128)S(1)} %copy-done.1, bf16[2,2,16,4096]{3,2,1,0:T(8,128)(2,1)S(1)} %copy-done, f32[8,128]{1,0:T(8,128)S(1)} %get-tuple-element.30.after.trail), custom_call_target="tpu_custom_call" | custom-call | tf_op jit(solution)/shard_map/forecast_first/pallas_call | solution.py:28
  2.7 0.5 %collective-permute-start = (bf16[32,4096]{1,0:T(8,128)(2,1)S(1)}, bf16[32,4096]{1,0:T(8,128)(2,1)S(1)}, u32[]{:S(2)}, u32[]{:S(2)}) collective-permute-start(bf16[32,4096]{1,0:T(8,128)(2,1)S(1)} %forecast_first.1.own), channel_id=1, source_target_pairs={{0,4},{4,0},{8,12},{12,8},{16,20},{20,16},{24,28},{28,24},{1,5},{5... | collective-permute-start | bytes 786440 | tf_op jit(solution)/shard_map/ppermute | solution.py:469
  3.2 2.6 %collective-permute-start.1 = (f32[1,128]{1,0:T(1,128)S(1)}, f32[1,128]{1,0:T(1,128)S(1)}, u32[]{:S(2)}, u32[]{:S(2)}) collective-permute-start(f32[1,128]{1,0:T(1,128)S(1)} %get-tuple-element.32), channel_id=1, source_target_pairs={{0,8},{4,12},{8,0},{12,4},{16,24},{20,28},{24,16},{28,20},{1,9},{5... | collective-permute-start | bytes 1544 | tf_op jit(solution)/shard_map/ppermute | solution.py:474
  5.7 1.5 %collective-permute-start.2 = (f32[1,128]{1,0:T(1,128)S(1)}, f32[1,128]{1,0:T(1,128)S(1)}, u32[]{:S(2)}, u32[]{:S(2)}) collective-permute-start(f32[1,128]{1,0:T(1,128)S(1)} %get-tuple-element.33), channel_id=1, source_target_pairs={{0,16},{4,20},{8,24},{12,28},{16,0},{20,4},{24,8},{28,12},{1,17},{... | collective-permute-start | bytes 1544 | tf_op jit(solution)/shard_map/ppermute | solution.py:474
  7.3 0.0 collective-permute-start.3
  7.3 0.0 collective-permute-done.1.refs_1_
  7.3 2.0 %collective-permute-done.2.refs_2_ = f32[1,128]{1,0:T(1,128)S(1)} collective-permute-done((f32[1,128]{1,0:T(1,128)S(1)}, f32[1,128]{1,0:T(1,128)S(1)}, u32[]{:S(2)}, u32[]{:S(2)}) %collective-permute-start.2) | collective-permute-done | bytes 544 | tf_op jit(solution)/shard_map/ppermute | solution.py:474
  9.3 2.4 %collective-permute-done.3.refs_3_ = f32[1,128]{1,0:T(1,128)S(1)} collective-permute-done((f32[1,128]{1,0:T(1,128)S(1)}, f32[1,128]{1,0:T(1,128)S(1)}, u32[]{:S(2)}, u32[]{:S(2)}) %collective-permute-start.3) | collective-permute-done | bytes 544 | tf_op jit(solution)/shard_map/ppermute | solution.py:474
  11.7 0.0 collective-permute-done.other
  11.7 0.4 send_first.1
  12.1 0.0 copy-start.6
  12.1 0.0 copy-start.7
  12.1 0.1 collective-permute-start.4
  12.2 0.0 copy-start.3
  12.2 0.6 %collective-permute-start.7 = (bf16[16,4096]{1,0:T(8,128)(2,1)S(1)}, bf16[16,4096]{1,0:T(8,128)(2,1)S(1)}, u32[]{:S(2)}, u32[]{:S(2)}) collective-permute-start(bf16[16,4096]{1,0:T(8,128)(2,1)S(1)} %get-tuple-element.38), channel_id=1, source_target_pairs={{0,8},{4,12},{8,0},{12,4},{16,24},{20,28},{24,16},{28,20},{1,9},{5... | collective-permute-start | bytes 393224 | tf_op jit(solution)/shard_map/ppermute | solution.py:474
  12.8 0.1 collective-permute-start.8
  12.8 2.9 %collective-permute-start.9 = (bf16[16,4096]{1,0:T(8,128)(2,1)S(1)}, bf16[16,4096]{1,0:T(8,128)(2,1)S(1)}, u32[]{:S(2)}, u32[]{:S(2)}) collective-permute-start(bf16[16,4096]{1,0:T(8,128)(2,1)S(1)} %get-tuple-element.40), channel_id=1, source_target_pairs={{0,24},{4,28},{8,16},{12,20},{16,8},{20,12},{24,0},{28,4},{1,25},{... | collective-permute-start | bytes 393224 | tf_op jit(solution)/shard_map/ppermute | solution.py:474
  15.8 0.0 collective-permute-done.4
  15.8 3.6 %collective-permute-start.5 = (f32[32,128]{1,0:T(8,128)S(1)}, f32[32,128]{1,0:T(8,128)S(1)}, u32[]{:S(2)}, u32[]{:S(2)}) collective-permute-start(f32[32,128]{1,0:T(8,128)S(1)} %constant_dynamic-update-slice_fusion.message), channel_id=1, source_target_pairs={{0,1},{1,2},{2,3},{5,4},{6,5},{7,6},{8,9},{9,10},{10,11},{13,12},{... | collective-permute-start | bytes 49160 | tf_op jit(solution)/shard_map/ppermute | solution.py:509
  19.4 1.4 %collective-permute-done.5.mine = f32[32,128]{1,0:T(8,128)S(1)} collective-permute-done((f32[32,128]{1,0:T(8,128)S(1)}, f32[32,128]{1,0:T(8,128)S(1)}, u32[]{:S(2)}, u32[]{:S(2)}) %collective-permute-start.5) | collective-permute-done | bytes 16416 | tf_op jit(solution)/shard_map/ppermute | solution.py:509
  20.8 0.0 collective-permute-start.6
  20.8 0.0 copy-done.5
  20.8 0.0 copy-done.6
  20.8 0.6 %copy-done.8 = s32[32]{0:T(128)S(1)} copy-done((s32[32]{0:T(128)S(1)}, s32[32]{0:T(128)}, u32[]{:S(2)}) %copy-start.8) | copy-done | bytes 152
  21.5 0.2 observe.1
  21.6 0.3 collective-permute-done.6.theirs
  22.0 0.0 collective-permute-done.7.refs_1_
  22.0 0.0 collective-permute-done.8.refs_2_
  22.0 0.0 collective-permute-done.9.refs_3_
  22.0 0.9 %forecast_second.1 = (bf16[32,4096]{1,0:T(8,128)(2,1)S(1)}, f32[32,256]{1,0:T(8,128)S(1)}, f32[32,256]{1,0:T(8,128)S(1)}) custom-call(s32[2,32,128]{2,1,0:T(8,128)S(1)} %get-tuple-element.29.keys, f32[16,4096]{1,0:T(8,128)S(1)} %copy-done.1, bf16[2,2,16,4096]{3,2,1,0:T(8,128)(2,1)S(1)} %copy-done, f32[32,128]{1,0:T(8,128)S(1)} %constant_dynamic-update-slice_fusion.message, ...), custom_call_target="tpu_custom_call" | custom-call | tf_op jit(solution)/shard_map/forecast_second/pallas_call | solution.py:28
  22.9 0.3 collective-permute-start.10
  23.1 1.0 %assess_first.1 = (bf16[16,640]{1,0:T(8,128)(2,1)S(1)}, bf16[16,640]{1,0:T(8,128)(2,1)S(1)}, bf16[16,640]{1,0:T(8,128)(2,1)S(1)}, bf16[16,640]{1,0:T(8,128)(2,1)...) custom-call(bf16[32,4096]{1,0:T(8,128)(2,1)S(1)} %forecast_first.1.own, ...), custom_call_target="tpu_custom_call" | custom-call | tf_op jit(solution)/shard_map/assess_first/pallas_call | solution.py:28
  24.1 0.4 collective-permute-done.10.other
  24.5 0.8 %send_second.1 = (bf16[16,5376]{1,0:T(8,128)(2,1)S(1)}, bf16[16,5376]{1,0:T(8,128)(2,1)S(1)}, bf16[16,5376]{1,0:T(8,128)(2,1)S(1)}, bf16[16,5376]{1,0:T(8,128)(2,1)S(1)}) custom-call(bf16[32,4096]{1,0:T(8,128)(2,1)S(1)} %get-tuple-element.41.second.own, bf16[32,4096]{1,0:T(8,128)(2,1)S(1)} %collective-permute-done.10.other, ...), custom_call_target="tpu_custom_call" | custom-call | tf_op jit(solution)/shard_map/send_second/pallas_call | solution.py:28
  25.3 0.7 %collective-permute-start.11 = (bf16[16,5376]{1,0:T(8,128)(2,1)S(1)}, bf16[16,5376]{1,0:T(8,128)(2,1)S(1)}, u32[]{:S(2)}, u32[]{:S(2)}) collective-permute-start(bf16[16,5376]{1,0:T(8,128)(2,1)S(1)} %get-tuple-element.53), channel_id=1, source_target_pairs={{0,24},{4,28},{8,16},{12,20},{16,8},{20,12},{24,0},{28,4},{1,25},{... | collective-permute-start | bytes 516104 | tf_op jit(solution)/shard_map/ppermute | solution.py:474
  26.0 1.5 %collective-permute-start.12 = (bf16[16,5376]{1,0:T(8,128)(2,1)S(1)}, bf16[16,5376]{1,0:T(8,128)(2,1)S(1)}, u32[]{:S(2)}, u32[]{:S(2)}) collective-permute-start(bf16[16,5376]{1,0:T(8,128)(2,1)S(1)} %get-tuple-element.54), channel_id=1, source_target_pairs={{0,16},{4,20},{8,24},{12,28},{16,0},{20,4},{24,8},{28,12},{1,17},{... | collective-permute-start | bytes 516104 | tf_op jit(solution)/shard_map/ppermute | solution.py:474
  27.5 1.4 %collective-permute-start.13 = (bf16[16,5376]{1,0:T(8,128)(2,1)S(1)}, bf16[16,5376]{1,0:T(8,128)(2,1)S(1)}, u32[]{:S(2)}, u32[]{:S(2)}) collective-permute-start(bf16[16,5376]{1,0:T(8,128)(2,1)S(1)} %get-tuple-element.55), channel_id=1, source_target_pairs={{0,8},{4,12},{8,0},{12,4},{16,24},{20,28},{24,16},{28,20},{1,9},{5... | collective-permute-start | bytes 516104 | tf_op jit(solution)/shard_map/ppermute | solution.py:474
  28.8 4.7 %collective-permute-done.11.refs_1_ = bf16[16,5376]{1,0:T(8,128)(2,1)S(1)} collective-permute-done((bf16[16,5376]{1,0:T(8,128)(2,1)S(1)}, bf16[16,5376]{1,0:T(8,128)(2,1)S(1)}, u32[]{:S(2)}, u32[]{:S(2)}) %collective-permute-start.11) | collective-permute-done | bytes 172064 | tf_op jit(solution)/shard_map/ppermute | solution.py:474
  33.5 2.2 %collective-permute-done.12.refs_2_ = bf16[16,5376]{1,0:T(8,128)(2,1)S(1)} collective-permute-done((bf16[16,5376]{1,0:T(8,128)(2,1)S(1)}, bf16[16,5376]{1,0:T(8,128)(2,1)S(1)}, u32[]{:S(2)}, u32[]{:S(2)}) %collective-permute-start.12) | collective-permute-done | bytes 172064 | tf_op jit(solution)/shard_map/ppermute | solution.py:474
  35.8 0.0 collective-permute-done.13.refs_3_
  35.8 0.9 %finish.1 = (bf16[2,16,4096]{2,1,0:T(8,128)(2,1)}, f32[2,16,512]{2,1,0:T(8,128)}) custom-call(s32[2,32,128]{2,1,0:T(8,128)S(1)} %get-tuple-element.29.keys, bf16[16,5376]{1,0:T(8,128)(2,1)S(1)} %get-tuple-element.52.refs_0_, bf16[16,5376]{1,0:T(8,128)(2,1)S(1)} %collective-permute-done.11.refs_1_, bf16[16,5376]{1,0:T(8,128)(2,1)S(1)} %collective-permute-done.12.refs_2_, ...), custom_call_target="tpu_custom_call" | custom-call | tf_op jit(solution)/shard_map/finish/pallas_call | solution.py:28
  (8 shorter events, 0.0 us)
Async XLA Ops:
  0.6 1.3 %copy-start = (bf16[2,2,16,4096]{3,2,1,0:T(8,128)(2,1)S(1)}, bf16[2,2,16,4096]{3,2,1,0:T(8,128)(2,1)}, u32[]{:S(2)}) copy-start(bf16[2,2,16,4096]{3,2,1,0:T(8,128)(2,1)} %pert.3) | copy-start | bytes 1572868
  0.6 1.4 %copy-start.1 = (f32[16,4096]{1,0:T(8,128)S(1)}, f32[16,4096]{1,0:T(8,128)}, u32[]{:S(2)}) copy-start(f32[16,4096]{1,0:T(8,128)} %diff.3) | copy-start | bytes 786436
  0.7 1.4 %copy-start.2 = (bf16[2,16,4096]{2,1,0:T(8,128)(2,1)S(1)}, bf16[2,16,4096]{2,1,0:T(8,128)(2,1)}, u32[]{:S(2)}) copy-start(bf16[2,16,4096]{2,1,0:T(8,128)(2,1)} %state.1) | copy-start | bytes 786436
  2.7 9.0 %collective-permute-start = (bf16[32,4096]{1,0:T(8,128)(2,1)S(1)}, bf16[32,4096]{1,0:T(8,128)(2,1)S(1)}, u32[]{:S(2)}, u32[]{:S(2)}) collective-permute-start(bf16[32,4096]{1,0:T(8,128)(2,1)S(1)} %forecast_first.1.own), channel_id=1, source_target_pairs={{0,4},{4,0},{8,12},{12,8},{16,20},{20,16},{24,28},{28,24},{1,5},{5... | collective-permute-start | bytes 786440 | tf_op jit(solution)/shard_map/ppermute | solution.py:469
  3.2 4.1 %collective-permute-start.1 = (f32[1,128]{1,0:T(1,128)S(1)}, f32[1,128]{1,0:T(1,128)S(1)}, u32[]{:S(2)}, u32[]{:S(2)}) collective-permute-start(f32[1,128]{1,0:T(1,128)S(1)} %get-tuple-element.32), channel_id=1, source_target_pairs={{0,8},{4,12},{8,0},{12,4},{16,24},{20,28},{24,16},{28,20},{1,9},{5... | collective-permute-start | bytes 1544 | tf_op jit(solution)/shard_map/ppermute | solution.py:474
  5.7 3.5 %collective-permute-start.2 = (f32[1,128]{1,0:T(1,128)S(1)}, f32[1,128]{1,0:T(1,128)S(1)}, u32[]{:S(2)}, u32[]{:S(2)}) collective-permute-start(f32[1,128]{1,0:T(1,128)S(1)} %get-tuple-element.33), channel_id=1, source_target_pairs={{0,16},{4,20},{8,24},{12,28},{16,0},{20,4},{24,8},{28,12},{1,17},{... | collective-permute-start | bytes 1544 | tf_op jit(solution)/shard_map/ppermute | solution.py:474
  7.3 4.4 %collective-permute-start.3 = (f32[1,128]{1,0:T(1,128)S(1)}, f32[1,128]{1,0:T(1,128)S(1)}, u32[]{:S(2)}, u32[]{:S(2)}) collective-permute-start(f32[1,128]{1,0:T(1,128)S(1)} %get-tuple-element.34), channel_id=1, source_target_pairs={{0,24},{4,28},{8,16},{12,20},{16,8},{20,12},{24,0},{28,4},{1,25},{... | collective-permute-start | bytes 1544 | tf_op jit(solution)/shard_map/ppermute | solution.py:474
  11.7 9.1 %copy-start.5 = (f32[32,16]{0,1:T(8,128)S(1)}, f32[32,16]{0,1:T(8,128)}, u32[]{:S(2)}) copy-start(f32[32,16]{0,1:T(8,128)} %param.15) | copy-start | bytes 6148
  12.1 8.7 %copy-start.6 = (s32[16,6]{0,1:T(8,128)S(1)}, s32[16,6]{0,1:T(8,128)}, u32[]{:S(2)}) copy-start(s32[16,6]{0,1:T(8,128)} %param.18) | copy-start | bytes 1156
  12.1 8.7 %copy-start.7 = (f32[16,6]{0,1:T(8,128)S(1)}, f32[16,6]{0,1:T(8,128)}, u32[]{:S(2)}) copy-start(f32[16,6]{0,1:T(8,128)} %param.19) | copy-start | bytes 1156
  12.1 3.7 %collective-permute-start.4 = (f32[16,128]{1,0:T(8,128)S(1)}, f32[16,128]{1,0:T(8,128)S(1)}, u32[]{:S(2)}, u32[]{:S(2)}) collective-permute-start(f32[16,128]{1,0:T(8,128)S(1)} %get-tuple-element.35), channel_id=1, source_target_pairs={{0,4},{4,0},{8,12},{12,8},{16,20},{20,16},{24,28},{28,24},{1,5},{5... | collective-permute-start | bytes 24584 | tf_op jit(solution)/shard_map/ppermute | solution.py:469
  12.2 8.6 %copy-start.3 = (f32[2,32,16]{1,2,0:T(8,128)S(1)}, f32[2,32,16]{1,2,0:T(8,128)}, u32[]{:S(2)}) copy-start(f32[2,32,16]{1,2,0:T(8,128)} %param.14) | copy-start | bytes 12292
  12.2 9.8 %collective-permute-start.7 = (bf16[16,4096]{1,0:T(8,128)(2,1)S(1)}, bf16[16,4096]{1,0:T(8,128)(2,1)S(1)}, u32[]{:S(2)}, u32[]{:S(2)}) collective-permute-start(bf16[16,4096]{1,0:T(8,128)(2,1)S(1)} %get-tuple-element.38), channel_id=1, source_target_pairs={{0,8},{4,12},{8,0},{12,4},{16,24},{20,28},{24,16},{28,20},{1,9},{5... | collective-permute-start | bytes 393224 | tf_op jit(solution)/shard_map/ppermute | solution.py:474
  12.8 9.2 %collective-permute-start.8 = (bf16[16,4096]{1,0:T(8,128)(2,1)S(1)}, bf16[16,4096]{1,0:T(8,128)(2,1)S(1)}, u32[]{:S(2)}, u32[]{:S(2)}) collective-permute-start(bf16[16,4096]{1,0:T(8,128)(2,1)S(1)} %get-tuple-element.39), channel_id=1, source_target_pairs={{0,16},{4,20},{8,24},{12,28},{16,0},{20,4},{24,8},{28,12},{1,17},{... | collective-permute-start | bytes 393224 | tf_op jit(solution)/shard_map/ppermute | solution.py:474
  12.8 9.1 %collective-permute-start.9 = (bf16[16,4096]{1,0:T(8,128)(2,1)S(1)}, bf16[16,4096]{1,0:T(8,128)(2,1)S(1)}, u32[]{:S(2)}, u32[]{:S(2)}) collective-permute-start(bf16[16,4096]{1,0:T(8,128)(2,1)S(1)} %get-tuple-element.40), channel_id=1, source_target_pairs={{0,24},{4,28},{8,16},{12,20},{16,8},{20,12},{24,0},{28,4},{1,25},{... | collective-permute-start | bytes 393224 | tf_op jit(solution)/shard_map/ppermute | solution.py:474
  15.8 5.1 %copy-start.4 = (s32[32,16]{0,1:T(8,128)S(1)}, s32[32,16]{0,1:T(8,128)}, u32[]{:S(2)}) copy-start(s32[32,16]{0,1:T(8,128)} %param.17) | copy-start | bytes 6148
  15.8 5.0 %collective-permute-start.5 = (f32[32,128]{1,0:T(8,128)S(1)}, f32[32,128]{1,0:T(8,128)S(1)}, u32[]{:S(2)}, u32[]{:S(2)}) collective-permute-start(f32[32,128]{1,0:T(8,128)S(1)} %constant_dynamic-update-slice_fusion.message), channel_id=1, source_target_pairs={{0,1},{1,2},{2,3},{5,4},{6,5},{7,6},{8,9},{9,10},{10,11},{13,12},{... | collective-permute-start | bytes 49160 | tf_op jit(solution)/shard_map/ppermute | solution.py:509
  20.8 1.2 %collective-permute-start.6 = (f32[32,128]{1,0:T(8,128)S(1)}, f32[32,128]{1,0:T(8,128)S(1)}, u32[]{:S(2)}, u32[]{:S(2)}) collective-permute-start(f32[32,128]{1,0:T(8,128)S(1)} %collective-permute-done.5.mine), channel_id=1, source_target_pairs={{0,4},{4,0},{8,12},{12,8},{16,20},{20,16},{24,28},{28,24},{1,5},{5... | collective-permute-start | bytes 49160 | tf_op jit(solution)/shard_map/ppermute | solution.py:469
  20.8 0.7 %copy-start.8 = (s32[32]{0:T(128)S(1)}, s32[32]{0:T(128)}, u32[]{:S(2)}) copy-start(s32[32]{0:T(128)} %param.16) | copy-start | bytes 388
  22.9 1.6 %collective-permute-start.10 = (bf16[32,4096]{1,0:T(8,128)(2,1)S(1)}, bf16[32,4096]{1,0:T(8,128)(2,1)S(1)}, u32[]{:S(2)}, u32[]{:S(2)}) collective-permute-start(bf16[32,4096]{1,0:T(8,128)(2,1)S(1)} %get-tuple-element.41.second.own), channel_id=1, source_target_pairs={{0,4},{4,0},{8,12},{12,8},{16,20},{20,16},{24,28},{28,24},{1,5},{5... | collective-permute-start | bytes 786440 | tf_op jit(solution)/shard_map/ppermute | solution.py:469
  25.3 8.2 %collective-permute-start.11 = (bf16[16,5376]{1,0:T(8,128)(2,1)S(1)}, bf16[16,5376]{1,0:T(8,128)(2,1)S(1)}, u32[]{:S(2)}, u32[]{:S(2)}) collective-permute-start(bf16[16,5376]{1,0:T(8,128)(2,1)S(1)} %get-tuple-element.53), channel_id=1, source_target_pairs={{0,24},{4,28},{8,16},{12,20},{16,8},{20,12},{24,0},{28,4},{1,25},{... | collective-permute-start | bytes 516104 | tf_op jit(solution)/shard_map/ppermute | solution.py:474
  26.0 9.8 %collective-permute-start.12 = (bf16[16,5376]{1,0:T(8,128)(2,1)S(1)}, bf16[16,5376]{1,0:T(8,128)(2,1)S(1)}, u32[]{:S(2)}, u32[]{:S(2)}) collective-permute-start(bf16[16,5376]{1,0:T(8,128)(2,1)S(1)} %get-tuple-element.54), channel_id=1, source_target_pairs={{0,16},{4,20},{8,24},{12,28},{16,0},{20,4},{24,8},{28,12},{1,17},{... | collective-permute-start | bytes 516104 | tf_op jit(solution)/shard_map/ppermute | solution.py:474
  27.5 8.3 %collective-permute-start.13 = (bf16[16,5376]{1,0:T(8,128)(2,1)S(1)}, bf16[16,5376]{1,0:T(8,128)(2,1)S(1)}, u32[]{:S(2)}, u32[]{:S(2)}) collective-permute-start(bf16[16,5376]{1,0:T(8,128)(2,1)S(1)} %get-tuple-element.55), channel_id=1, source_target_pairs={{0,8},{4,12},{8,0},{12,4},{16,24},{20,28},{24,16},{28,20},{1,9},{5... | collective-permute-start | bytes 516104 | tf_op jit(solution)/shard_map/ppermute | solution.py:474

commit v13 on v12

--- a/solution.py
+++ b/solution.py
@@ -52,7 +52,7 @@
 
 
 def falling(pairs):
-    return [0, *range(pairs - 1, 0, -1)]
+    return [0, 1, *range(pairs - 1, 1, -1)]
 
 
 def padded(pairs):
@@ -399,18 +399,27 @@
 
 
 def make_last(pairs, rows, parts, tiles, cells):
+    pieces_of = 4
+    piece = cells // pieces_of
+
     def kernel(keys, *refs):
-        got, analysis, mean = refs[:pairs], refs[pairs], refs[pairs + 1]
+        got, (analysis, mean, buffer, sems) = refs[:pairs], refs[pairs:]
         got = [got[falling(pairs).index(k)] for k in range(pairs)]
-        arrived = jnp.concatenate([x[:, :cells] for x in got], axis=0)
-        picked = pick_rows(keys[1], arrived)
-        for p in range(parts):
-            analysis[p] = picked[p * tiles:(p + 1) * tiles, :].astype(BF16)
+        copies = []
+        for i in range(pieces_of):
+            cut = slice(i * piece, (i + 1) * piece)
+            picked = pick_rows(keys[1], jnp.concatenate([x[:, cut] for x in got], axis=0))
+            for p in range(parts):
+                buffer[p, :, cut] = picked[p * tiles:(p + 1) * tiles, :].astype(BF16)
+            copies.append(pltpu.make_async_copy(buffer.at[:, :, cut], analysis.at[:, :, cut], sems.at[i]))
+            copies[-1].start()
         share = mean.shape[2]
         extra = tiles // rows * share + LANES
         for c in range(CYCLES):
             for g, x in enumerate(unpack_mean(got, cells + c * extra, tiles, share)):
                 mean[c, g * rows:(g + 1) * rows, :] = x
+        for copy in copies:
+            copy.wait()
 
     return kernel
 
@@ -535,13 +544,19 @@
         name="send_second",
     )
     got = exchange(sends, falling(pairs))
+    mean_shape = (CYCLES, tiles, share)
+    args = [keys, *got]
     return tuple(
-        call(
+        pl.pallas_call(
             make_last(pairs, rows, parts, tiles, cells),
-            [(state.shape, BF16), ((CYCLES, tiles, share), F32)],
-            [keys, *got],
+            out_shape=[jax.ShapeDtypeStruct(state.shape, BF16), jax.ShapeDtypeStruct(mean_shape, F32)],
+            grid=(1,),
+            in_specs=[whole_spec(a.shape) for a in args],
+            out_specs=[pl.BlockSpec(memory_space=pl.ANY), whole_spec(mean_shape)],
+            scratch_shapes=[pltpu.VMEM(state.shape, BF16), pltpu.SemaphoreType.DMA((4,))],
+            compiler_params=PARAMS,
             name="finish",
-        )
+        )(*args)
     )
 
 

time: 36.9 us -> 38.6 us (1.046)
  waiting for transfers between devices: 13.5 us -> 14.6 us
  Pallas kernels: 6.08 us -> 6.66 us
    pallas_call x0 -> x1, Pallas kernels: none -> 1.52 us  [body(): pl.pallas_call(make_last(pairs, rows, parts, tiles, cells), out_shape=[ja...]
    ppermute x9, waiting for transfers between devices: 11.3 us -> 12.5 us  [exchange(): lax.ppermute(x, 'member', [(i, i ^ 2 * k) for i in range(members)])]
    pallas_call x8 -> x7, Pallas kernels: 6.08 us -> 5.14 us  [call(): pl.pallas_call(kernel, out_shape=[jax.ShapeDtypeStruct(s, d) for s, d in...]
  transfers between devices with their start and end apart: 14 -> 14, of which waited for: 7 -> 8; matrix products, arithmetic and copies ran while one was open for 0% -> 0% of each run, Pallas kernels for 3% -> 3%
where the time goes in v13:
time: 38.6 us; the launch traced here: 38.5 us
  starting transfers between devices  15.7 us (41%)
  waiting for transfers between devices  14.6 us (38%)
  Pallas kernels  6.66 us (17%)
  between operations  0.83 us (2%)
  local copies, waits for them, and re-layouts  0.67 us (2%)
    ppermute x9, waiting for transfers between devices, exchange(): lax.ppermute(x, 'member', [(i, i ^ 2 * k) for i in range(members)])  12.5 us
    ppermute x9, starting transfers between devices, exchange(): lax.ppermute(x, 'member', [(i, i ^ 2 * k) for i in range(members)])  11.2 us
    pallas_call x7, Pallas kernels, call(): pl.pallas_call(kernel, out_shape=[jax.ShapeDtypeStruct(s, d) for s, d in...  5.14 us
    ppermute x1, starting transfers between devices, body(): mine = lax.ppermute(message, ('member', 'region'), steps)  3.6 us
    pallas_call x1, Pallas kernels, body(): pl.pallas_call(make_last(pairs, rows, parts, tiles, cells), out_shape=[ja...  1.52 us
    ppermute x1, waiting for transfers between devices, body(): mine = lax.ppermute(message, ('member', 'region'), steps)  1.43 us
    ppermute x4, starting transfers between devices, trade(): return lax.ppermute(x, 'member', [(i, i ^ 1) for i in range(members)])  0.86 us
  transfers between devices with their start and end apart: 14, of which 8 were waited for; matrix products, arithmetic and copies ran while one was open for 0% of the time, Pallas kernels for 3%

profile of v13, /device:TPU:0, one launch (start us, length us, event | category | flops | bytes accessed | tf_op | source)
XLA Modules:
  0.0 38.5 jit_solution(16597554522544720768)
XLA Ops:
  0.6 0.0 copy-start
  0.6 0.0 copy-start.1
  0.7 0.0 copy-start.2
  0.7 1.3 %prepare.1 = (f32[1,128]{1,0:T(1,128)S(1)}, f32[1,128]{1,0:T(1,128)S(1)}, f32[1,128]{1,0:T(1,128)S(1)}, f32[1,128]{1,0:T(1,128)S(1)}, f32[8,128]{1,0:T(8,128)S(1)}, /*index=5*/s32[2,32,128]{2,1,0:T(8,128)S(1)}) custom-call(bf16[2,16,4096]{2,1,0:T(8,128)(2,1)} %state.1, bf16[2,16,4096]{2,1,0:T(8,128)(2,1)} %state.1, f32[16,4096]{1,0:T(8,128)} %diff.3, ...), custom_call_target="tpu_custom_call" | custom-call | tf_op jit(solution)/shard_map/prepare/pallas_call | solution.py:28
  2.0 0.0 copy-done
  2.0 0.0 copy-done.1
  2.0 0.0 copy-done.2
  2.0 0.6 %forecast_first.1.own = bf16[32,4096]{1,0:T(8,128)(2,1)S(1)} custom-call(bf16[2,16,4096]{2,1,0:T(8,128)(2,1)S(1)} %copy-done.2, f32[16,4096]{1,0:T(8,128)S(1)} %copy-done.1, bf16[2,2,16,4096]{3,2,1,0:T(8,128)(2,1)S(1)} %copy-done, f32[8,128]{1,0:T(8,128)S(1)} %get-tuple-element.30.after.trail), custom_call_target="tpu_custom_call" | custom-call | tf_op jit(solution)/shard_map/forecast_first/pallas_call | solution.py:28
  2.7 0.5 %collective-permute-start = (bf16[32,4096]{1,0:T(8,128)(2,1)S(1)}, bf16[32,4096]{1,0:T(8,128)(2,1)S(1)}, u32[]{:S(2)}, u32[]{:S(2)}) collective-permute-start(bf16[32,4096]{1,0:T(8,128)(2,1)S(1)} %forecast_first.1.own), channel_id=1, source_target_pairs={{0,4},{4,0},{8,12},{12,8},{16,20},{20,16},{24,28},{28,24},{1,5},{5... | collective-permute-start | bytes 786440 | tf_op jit(solution)/shard_map/ppermute | solution.py:478
  3.2 2.6 %collective-permute-start.1 = (f32[1,128]{1,0:T(1,128)S(1)}, f32[1,128]{1,0:T(1,128)S(1)}, u32[]{:S(2)}, u32[]{:S(2)}) collective-permute-start(f32[1,128]{1,0:T(1,128)S(1)} %get-tuple-element.32), channel_id=1, source_target_pairs={{0,8},{4,12},{8,0},{12,4},{16,24},{20,28},{24,16},{28,20},{1,9},{5... | collective-permute-start | bytes 1544 | tf_op jit(solution)/shard_map/ppermute | solution.py:483
  5.7 1.5 %collective-permute-start.2 = (f32[1,128]{1,0:T(1,128)S(1)}, f32[1,128]{1,0:T(1,128)S(1)}, u32[]{:S(2)}, u32[]{:S(2)}) collective-permute-start(f32[1,128]{1,0:T(1,128)S(1)} %get-tuple-element.33), channel_id=1, source_target_pairs={{0,16},{4,20},{8,24},{12,28},{16,0},{20,4},{24,8},{28,12},{1,17},{... | collective-permute-start | bytes 1544 | tf_op jit(solution)/shard_map/ppermute | solution.py:483
  7.3 0.0 collective-permute-start.3
  7.3 0.0 collective-permute-done.1.refs_1_
  7.3 2.0 %collective-permute-done.2.refs_2_ = f32[1,128]{1,0:T(1,128)S(1)} collective-permute-done((f32[1,128]{1,0:T(1,128)S(1)}, f32[1,128]{1,0:T(1,128)S(1)}, u32[]{:S(2)}, u32[]{:S(2)}) %collective-permute-start.2) | collective-permute-done | bytes 544 | tf_op jit(solution)/shard_map/ppermute | solution.py:483
  9.3 2.4 %collective-permute-done.3.refs_3_ = f32[1,128]{1,0:T(1,128)S(1)} collective-permute-done((f32[1,128]{1,0:T(1,128)S(1)}, f32[1,128]{1,0:T(1,128)S(1)}, u32[]{:S(2)}, u32[]{:S(2)}) %collective-permute-start.3) | collective-permute-done | bytes 544 | tf_op jit(solution)/shard_map/ppermute | solution.py:483
  11.7 0.0 collective-permute-done.other
  11.7 0.4 send_first.1
  12.1 0.0 copy-start.6
  12.1 0.0 copy-start.7
  12.1 0.1 collective-permute-start.4
  12.2 0.0 copy-start.3
  12.2 0.6 %collective-permute-start.7 = (bf16[16,4096]{1,0:T(8,128)(2,1)S(1)}, bf16[16,4096]{1,0:T(8,128)(2,1)S(1)}, u32[]{:S(2)}, u32[]{:S(2)}) collective-permute-start(bf16[16,4096]{1,0:T(8,128)(2,1)S(1)} %get-tuple-element.38), channel_id=1, source_target_pairs={{0,8},{4,12},{8,0},{12,4},{16,24},{20,28},{24,16},{28,20},{1,9},{5... | collective-permute-start | bytes 393224 | tf_op jit(solution)/shard_map/ppermute | solution.py:483
  12.8 0.1 collective-permute-start.8
  12.8 2.9 %collective-permute-start.9 = (bf16[16,4096]{1,0:T(8,128)(2,1)S(1)}, bf16[16,4096]{1,0:T(8,128)(2,1)S(1)}, u32[]{:S(2)}, u32[]{:S(2)}) collective-permute-start(bf16[16,4096]{1,0:T(8,128)(2,1)S(1)} %get-tuple-element.40), channel_id=1, source_target_pairs={{0,24},{4,28},{8,16},{12,20},{16,8},{20,12},{24,0},{28,4},{1,25},{... | collective-permute-start | bytes 393224 | tf_op jit(solution)/shard_map/ppermute | solution.py:483
  15.8 0.0 collective-permute-done.4
  15.8 3.6 %collective-permute-start.5 = (f32[32,128]{1,0:T(8,128)S(1)}, f32[32,128]{1,0:T(8,128)S(1)}, u32[]{:S(2)}, u32[]{:S(2)}) collective-permute-start(f32[32,128]{1,0:T(8,128)S(1)} %constant_dynamic-update-slice_fusion.message), channel_id=1, source_target_pairs={{0,1},{1,2},{2,3},{5,4},{6,5},{7,6},{8,9},{9,10},{10,11},{13,12},{... | collective-permute-start | bytes 49160 | tf_op jit(solution)/shard_map/ppermute | solution.py:518
  19.4 1.4 %collective-permute-done.5.mine = f32[32,128]{1,0:T(8,128)S(1)} collective-permute-done((f32[32,128]{1,0:T(8,128)S(1)}, f32[32,128]{1,0:T(8,128)S(1)}, u32[]{:S(2)}, u32[]{:S(2)}) %collective-permute-start.5) | collective-permute-done | bytes 16416 | tf_op jit(solution)/shard_map/ppermute | solution.py:518
  20.8 0.0 collective-permute-start.6
  20.8 0.0 copy-done.5
  20.8 0.0 copy-done.6
  20.8 0.6 %copy-done.8 = s32[32]{0:T(128)S(1)} copy-done((s32[32]{0:T(128)S(1)}, s32[32]{0:T(128)}, u32[]{:S(2)}) %copy-start.8) | copy-done | bytes 152
  21.5 0.2 observe.1
  21.6 0.3 collective-permute-done.6.theirs
  22.0 0.0 collective-permute-done.7.refs_1_
  22.0 0.0 collective-permute-done.8.refs_2_
  22.0 0.0 collective-permute-done.9.refs_3_
  22.0 0.9 %forecast_second.1 = (bf16[32,4096]{1,0:T(8,128)(2,1)S(1)}, f32[32,256]{1,0:T(8,128)S(1)}, f32[32,256]{1,0:T(8,128)S(1)}) custom-call(s32[2,32,128]{2,1,0:T(8,128)S(1)} %get-tuple-element.29.keys, f32[16,4096]{1,0:T(8,128)S(1)} %copy-done.1, bf16[2,2,16,4096]{3,2,1,0:T(8,128)(2,1)S(1)} %copy-done, f32[32,128]{1,0:T(8,128)S(1)} %constant_dynamic-update-slice_fusion.message, ...), custom_call_target="tpu_custom_call" | custom-call | tf_op jit(solution)/shard_map/forecast_second/pallas_call | solution.py:28
  22.9 0.3 collective-permute-start.10
  23.1 1.0 %assess_first.1 = (bf16[16,640]{1,0:T(8,128)(2,1)S(1)}, bf16[16,640]{1,0:T(8,128)(2,1)S(1)}, bf16[16,640]{1,0:T(8,128)(2,1)S(1)}, bf16[16,640]{1,0:T(8,128)(2,1)...) custom-call(bf16[32,4096]{1,0:T(8,128)(2,1)S(1)} %forecast_first.1.own, ...), custom_call_target="tpu_custom_call" | custom-call | tf_op jit(solution)/shard_map/assess_first/pallas_call | solution.py:28
  24.1 0.4 collective-permute-done.10.other
  24.5 0.8 %send_second.1 = (bf16[16,5376]{1,0:T(8,128)(2,1)S(1)}, bf16[16,5376]{1,0:T(8,128)(2,1)S(1)}, bf16[16,5376]{1,0:T(8,128)(2,1)S(1)}, bf16[16,5376]{1,0:T(8,128)(2,1)S(1)}) custom-call(bf16[32,4096]{1,0:T(8,128)(2,1)S(1)} %get-tuple-element.41.second.own, bf16[32,4096]{1,0:T(8,128)(2,1)S(1)} %collective-permute-done.10.other, ...), custom_call_target="tpu_custom_call" | custom-call | tf_op jit(solution)/shard_map/send_second/pallas_call | solution.py:28
  25.3 0.7 %collective-permute-start.11 = (bf16[16,5376]{1,0:T(8,128)(2,1)S(1)}, bf16[16,5376]{1,0:T(8,128)(2,1)S(1)}, u32[]{:S(2)}, u32[]{:S(2)}) collective-permute-start(bf16[16,5376]{1,0:T(8,128)(2,1)S(1)} %get-tuple-element.53), channel_id=1, source_target_pairs={{0,8},{4,12},{8,0},{12,4},{16,24},{20,28},{24,16},{28,20},{1,9},{5... | collective-permute-start | bytes 516104 | tf_op jit(solution)/shard_map/ppermute | solution.py:483
  26.0 1.3 %collective-permute-start.12 = (bf16[16,5376]{1,0:T(8,128)(2,1)S(1)}, bf16[16,5376]{1,0:T(8,128)(2,1)S(1)}, u32[]{:S(2)}, u32[]{:S(2)}) collective-permute-start(bf16[16,5376]{1,0:T(8,128)(2,1)S(1)} %get-tuple-element.54), channel_id=1, source_target_pairs={{0,24},{4,28},{8,16},{12,20},{16,8},{20,12},{24,0},{28,4},{1,25},{... | collective-permute-start | bytes 516104 | tf_op jit(solution)/shard_map/ppermute | solution.py:483
  27.3 1.5 %collective-permute-start.13 = (bf16[16,5376]{1,0:T(8,128)(2,1)S(1)}, bf16[16,5376]{1,0:T(8,128)(2,1)S(1)}, u32[]{:S(2)}, u32[]{:S(2)}) collective-permute-start(bf16[16,5376]{1,0:T(8,128)(2,1)S(1)} %get-tuple-element.55), channel_id=1, source_target_pairs={{0,16},{4,20},{8,24},{12,28},{16,0},{20,4},{24,8},{28,12},{1,17},{... | collective-permute-start | bytes 516104 | tf_op jit(solution)/shard_map/ppermute | solution.py:483
  28.8 3.7 %collective-permute-done.11.refs_1_ = bf16[16,5376]{1,0:T(8,128)(2,1)S(1)} collective-permute-done((bf16[16,5376]{1,0:T(8,128)(2,1)S(1)}, bf16[16,5376]{1,0:T(8,128)(2,1)S(1)}, u32[]{:S(2)}, u32[]{:S(2)}) %collective-permute-start.11) | collective-permute-done | bytes 172064 | tf_op jit(solution)/shard_map/ppermute | solution.py:483
  32.6 3.0 %collective-permute-done.12.refs_2_ = bf16[16,5376]{1,0:T(8,128)(2,1)S(1)} collective-permute-done((bf16[16,5376]{1,0:T(8,128)(2,1)S(1)}, bf16[16,5376]{1,0:T(8,128)(2,1)S(1)}, u32[]{:S(2)}, u32[]{:S(2)}) %collective-permute-start.12) | collective-permute-done | bytes 172064 | tf_op jit(solution)/shard_map/ppermute | solution.py:483
  35.6 1.4 %collective-permute-done.13.refs_3_ = bf16[16,5376]{1,0:T(8,128)(2,1)S(1)} collective-permute-done((bf16[16,5376]{1,0:T(8,128)(2,1)S(1)}, bf16[16,5376]{1,0:T(8,128)(2,1)S(1)}, u32[]{:S(2)}, u32[]{:S(2)}) %collective-permute-start.13) | collective-permute-done | bytes 172064 | tf_op jit(solution)/shard_map/ppermute | solution.py:483
  36.9 1.5 %finish.1 = (bf16[2,16,4096]{2,1,0:T(8,128)(2,1)}, f32[2,16,512]{2,1,0:T(8,128)}) custom-call(s32[2,32,128]{2,1,0:T(8,128)S(1)} %get-tuple-element.29.keys, bf16[16,5376]{1,0:T(8,128)(2,1)S(1)} %get-tuple-element.52.refs_0_, bf16[16,5376]{1,0:T(8,128)(2,1)S(1)} %collective-permute-done.11.refs_1_, bf16[16,5376]{1,0:T(8,128)(2,1)S(1)} %collective-permute-done.12.refs_2_, ...), custom_call_target="tpu_custom_call" | custom-call | tf_op jit(solution)/shard_map/finish/pallas_call | solution.py:550
  (8 shorter events, 0.0 us)
Async XLA Ops:
  0.6 1.3 %copy-start = (bf16[2,2,16,4096]{3,2,1,0:T(8,128)(2,1)S(1)}, bf16[2,2,16,4096]{3,2,1,0:T(8,128)(2,1)}, u32[]{:S(2)}) copy-start(bf16[2,2,16,4096]{3,2,1,0:T(8,128)(2,1)} %pert.3) | copy-start | bytes 1572868
  0.6 1.4 %copy-start.1 = (f32[16,4096]{1,0:T(8,128)S(1)}, f32[16,4096]{1,0:T(8,128)}, u32[]{:S(2)}) copy-start(f32[16,4096]{1,0:T(8,128)} %diff.3) | copy-start | bytes 786436
  0.7 1.4 %copy-start.2 = (bf16[2,16,4096]{2,1,0:T(8,128)(2,1)S(1)}, bf16[2,16,4096]{2,1,0:T(8,128)(2,1)}, u32[]{:S(2)}) copy-start(bf16[2,16,4096]{2,1,0:T(8,128)(2,1)} %state.1) | copy-start | bytes 786436
  2.7 9.0 %collective-permute-start = (bf16[32,4096]{1,0:T(8,128)(2,1)S(1)}, bf16[32,4096]{1,0:T(8,128)(2,1)S(1)}, u32[]{:S(2)}, u32[]{:S(2)}) collective-permute-start(bf16[32,4096]{1,0:T(8,128)(2,1)S(1)} %forecast_first.1.own), channel_id=1, source_target_pairs={{0,4},{4,0},{8,12},{12,8},{16,20},{20,16},{24,28},{28,24},{1,5},{5... | collective-permute-start | bytes 786440 | tf_op jit(solution)/shard_map/ppermute | solution.py:478
  3.2 4.1 %collective-permute-start.1 = (f32[1,128]{1,0:T(1,128)S(1)}, f32[1,128]{1,0:T(1,128)S(1)}, u32[]{:S(2)}, u32[]{:S(2)}) collective-permute-start(f32[1,128]{1,0:T(1,128)S(1)} %get-tuple-element.32), channel_id=1, source_target_pairs={{0,8},{4,12},{8,0},{12,4},{16,24},{20,28},{24,16},{28,20},{1,9},{5... | collective-permute-start | bytes 1544 | tf_op jit(solution)/shard_map/ppermute | solution.py:483
  5.7 3.5 %collective-permute-start.2 = (f32[1,128]{1,0:T(1,128)S(1)}, f32[1,128]{1,0:T(1,128)S(1)}, u32[]{:S(2)}, u32[]{:S(2)}) collective-permute-start(f32[1,128]{1,0:T(1,128)S(1)} %get-tuple-element.33), channel_id=1, source_target_pairs={{0,16},{4,20},{8,24},{12,28},{16,0},{20,4},{24,8},{28,12},{1,17},{... | collective-permute-start | bytes 1544 | tf_op jit(solution)/shard_map/ppermute | solution.py:483
  7.3 4.4 %collective-permute-start.3 = (f32[1,128]{1,0:T(1,128)S(1)}, f32[1,128]{1,0:T(1,128)S(1)}, u32[]{:S(2)}, u32[]{:S(2)}) collective-permute-start(f32[1,128]{1,0:T(1,128)S(1)} %get-tuple-element.34), channel_id=1, source_target_pairs={{0,24},{4,28},{8,16},{12,20},{16,8},{20,12},{24,0},{28,4},{1,25},{... | collective-permute-start | bytes 1544 | tf_op jit(solution)/shard_map/ppermute | solution.py:483
  11.7 9.1 %copy-start.5 = (f32[32,16]{0,1:T(8,128)S(1)}, f32[32,16]{0,1:T(8,128)}, u32[]{:S(2)}) copy-start(f32[32,16]{0,1:T(8,128)} %param.15) | copy-start | bytes 6148
  12.1 8.7 %copy-start.6 = (s32[16,6]{0,1:T(8,128)S(1)}, s32[16,6]{0,1:T(8,128)}, u32[]{:S(2)}) copy-start(s32[16,6]{0,1:T(8,128)} %param.18) | copy-start | bytes 1156
  12.1 8.7 %copy-start.7 = (f32[16,6]{0,1:T(8,128)S(1)}, f32[16,6]{0,1:T(8,128)}, u32[]{:S(2)}) copy-start(f32[16,6]{0,1:T(8,128)} %param.19) | copy-start | bytes 1156
  12.1 3.7 %collective-permute-start.4 = (f32[16,128]{1,0:T(8,128)S(1)}, f32[16,128]{1,0:T(8,128)S(1)}, u32[]{:S(2)}, u32[]{:S(2)}) collective-permute-start(f32[16,128]{1,0:T(8,128)S(1)} %get-tuple-element.35), channel_id=1, source_target_pairs={{0,4},{4,0},{8,12},{12,8},{16,20},{20,16},{24,28},{28,24},{1,5},{5... | collective-permute-start | bytes 24584 | tf_op jit(solution)/shard_map/ppermute | solution.py:478
  12.2 8.6 %copy-start.3 = (f32[2,32,16]{1,2,0:T(8,128)S(1)}, f32[2,32,16]{1,2,0:T(8,128)}, u32[]{:S(2)}) copy-start(f32[2,32,16]{1,2,0:T(8,128)} %param.14) | copy-start | bytes 12292
  12.2 9.8 %collective-permute-start.7 = (bf16[16,4096]{1,0:T(8,128)(2,1)S(1)}, bf16[16,4096]{1,0:T(8,128)(2,1)S(1)}, u32[]{:S(2)}, u32[]{:S(2)}) collective-permute-start(bf16[16,4096]{1,0:T(8,128)(2,1)S(1)} %get-tuple-element.38), channel_id=1, source_target_pairs={{0,8},{4,12},{8,0},{12,4},{16,24},{20,28},{24,16},{28,20},{1,9},{5... | collective-permute-start | bytes 393224 | tf_op jit(solution)/shard_map/ppermute | solution.py:483
  12.8 9.2 %collective-permute-start.8 = (bf16[16,4096]{1,0:T(8,128)(2,1)S(1)}, bf16[16,4096]{1,0:T(8,128)(2,1)S(1)}, u32[]{:S(2)}, u32[]{:S(2)}) collective-permute-start(bf16[16,4096]{1,0:T(8,128)(2,1)S(1)} %get-tuple-element.39), channel_id=1, source_target_pairs={{0,16},{4,20},{8,24},{12,28},{16,0},{20,4},{24,8},{28,12},{1,17},{... | collective-permute-start | bytes 393224 | tf_op jit(solution)/shard_map/ppermute | solution.py:483
  12.8 9.1 %collective-permute-start.9 = (bf16[16,4096]{1,0:T(8,128)(2,1)S(1)}, bf16[16,4096]{1,0:T(8,128)(2,1)S(1)}, u32[]{:S(2)}, u32[]{:S(2)}) collective-permute-start(bf16[16,4096]{1,0:T(8,128)(2,1)S(1)} %get-tuple-element.40), channel_id=1, source_target_pairs={{0,24},{4,28},{8,16},{12,20},{16,8},{20,12},{24,0},{28,4},{1,25},{... | collective-permute-start | bytes 393224 | tf_op jit(solution)/shard_map/ppermute | solution.py:483
  15.8 5.1 %copy-start.4 = (s32[32,16]{0,1:T(8,128)S(1)}, s32[32,16]{0,1:T(8,128)}, u32[]{:S(2)}) copy-start(s32[32,16]{0,1:T(8,128)} %param.17) | copy-start | bytes 6148
  15.8 5.0 %collective-permute-start.5 = (f32[32,128]{1,0:T(8,128)S(1)}, f32[32,128]{1,0:T(8,128)S(1)}, u32[]{:S(2)}, u32[]{:S(2)}) collective-permute-start(f32[32,128]{1,0:T(8,128)S(1)} %constant_dynamic-update-slice_fusion.message), channel_id=1, source_target_pairs={{0,1},{1,2},{2,3},{5,4},{6,5},{7,6},{8,9},{9,10},{10,11},{13,12},{... | collective-permute-start | bytes 49160 | tf_op jit(solution)/shard_map/ppermute | solution.py:518
  20.8 1.2 %collective-permute-start.6 = (f32[32,128]{1,0:T(8,128)S(1)}, f32[32,128]{1,0:T(8,128)S(1)}, u32[]{:S(2)}, u32[]{:S(2)}) collective-permute-start(f32[32,128]{1,0:T(8,128)S(1)} %collective-permute-done.5.mine), channel_id=1, source_target_pairs={{0,4},{4,0},{8,12},{12,8},{16,20},{20,16},{24,28},{28,24},{1,5},{5... | collective-permute-start | bytes 49160 | tf_op jit(solution)/shard_map/ppermute | solution.py:478
  20.8 0.7 %copy-start.8 = (s32[32]{0:T(128)S(1)}, s32[32]{0:T(128)}, u32[]{:S(2)}) copy-start(s32[32]{0:T(128)} %param.16) | copy-start | bytes 388
  22.9 1.6 %collective-permute-start.10 = (bf16[32,4096]{1,0:T(8,128)(2,1)S(1)}, bf16[32,4096]{1,0:T(8,128)(2,1)S(1)}, u32[]{:S(2)}, u32[]{:S(2)}) collective-permute-start(bf16[32,4096]{1,0:T(8,128)(2,1)S(1)} %get-tuple-element.41.second.own), channel_id=1, source_target_pairs={{0,4},{4,0},{8,12},{12,8},{16,20},{20,16},{24,28},{28,24},{1,5},{5... | collective-permute-start | bytes 786440 | tf_op jit(solution)/shard_map/ppermute | solution.py:478
  25.3 7.3 %collective-permute-start.11 = (bf16[16,5376]{1,0:T(8,128)(2,1)S(1)}, bf16[16,5376]{1,0:T(8,128)(2,1)S(1)}, u32[]{:S(2)}, u32[]{:S(2)}) collective-permute-start(bf16[16,5376]{1,0:T(8,128)(2,1)S(1)} %get-tuple-element.53), channel_id=1, source_target_pairs={{0,8},{4,12},{8,0},{12,4},{16,24},{20,28},{24,16},{28,20},{1,9},{5... | collective-permute-start | bytes 516104 | tf_op jit(solution)/shard_map/ppermute | solution.py:483
  26.0 9.6 %collective-permute-start.12 = (bf16[16,5376]{1,0:T(8,128)(2,1)S(1)}, bf16[16,5376]{1,0:T(8,128)(2,1)S(1)}, u32[]{:S(2)}, u32[]{:S(2)}) collective-permute-start(bf16[16,5376]{1,0:T(8,128)(2,1)S(1)} %get-tuple-element.54), channel_id=1, source_target_pairs={{0,24},{4,28},{8,16},{12,20},{16,8},{20,12},{24,0},{28,4},{1,25},{... | collective-permute-start | bytes 516104 | tf_op jit(solution)/shard_map/ppermute | solution.py:483
  27.3 9.6 %collective-permute-start.13 = (bf16[16,5376]{1,0:T(8,128)(2,1)S(1)}, bf16[16,5376]{1,0:T(8,128)(2,1)S(1)}, u32[]{:S(2)}, u32[]{:S(2)}) collective-permute-start(bf16[16,5376]{1,0:T(8,128)(2,1)S(1)} %get-tuple-element.55), channel_id=1, source_target_pairs={{0,16},{4,20},{8,24},{12,28},{16,0},{20,4},{24,8},{28,12},{1,17},{... | collective-permute-start | bytes 516104 | tf_op jit(solution)/shard_map/ppermute | solution.py:483

commit v14 on v12

--- a/solution.py
+++ b/solution.py
@@ -87,12 +87,16 @@
                 edge = jnp.where((lane >= to) & (lane < to + width), moved, edge)
         before = (iota((tiles, tiles), 0) < iota((tiles, tiles), 1)).astype(F32)
         asked = jnp.zeros((pairs, LANES), F32)
+        sources = [[am[c, p:p + 1, :] ^ m for p in range(parts)] for c in range(CYCLES)]
+        every = [(iota((members, tiles), 0) == x).astype(F32) for some in sources for x in some]
+        earlier_all = jnp.dot(jnp.concatenate(every, axis=0), before, preferred_element_type=F32)
         for c in range(CYCLES):
             seen = jnp.zeros((members, 1), F32)
             for p in range(parts):
-                source = am[c, p:p + 1, :] ^ m
-                named = (iota((members, tiles), 0) == source).astype(F32)
-                earlier = seen + jnp.dot(named, before, preferred_element_type=F32)
+                source = sources[c][p]
+                at = c * parts + p
+                named = every[at]
+                earlier = seen + earlier_all[at * members:(at + 1) * members, :]
                 rank = jnp.sum(named * earlier, axis=0, keepdims=True).astype(I32)
                 seen = seen + jnp.sum(named, axis=1, keepdims=True)
                 half = source % 2
@@ -305,6 +309,7 @@
 def make_send(pairs, rows):
     def kernel(own, other, trail, *refs):
         notes, sends, half = refs[:pairs], refs[pairs:2 * pairs], refs[2 * pairs]
+        sends = [sends[falling(pairs).index(k)] for k in range(pairs)]
         prior = jnp.concatenate([own[...], other[...]], axis=0)
         sent = requested([x[...] for x in notes], prior, 0, rows)
         for k in range(pairs):
@@ -350,6 +355,7 @@
 
     def kernel(keys, diff, pert, message, mine, theirs, after, *refs):
         got, prior, low_out, high_out = refs[:pairs], refs[pairs], refs[pairs + 1], refs[pairs + 2]
+        got = [got[falling(pairs).index(k)] for k in range(pairs)]
         below, above = halves(mine[...], theirs[...])
         low, high = edge_windows(message[...], below, above, size, parts)
         low_out[...] = low
@@ -500,7 +506,7 @@
         [prior, other, trail, *notes],
         name="send_first",
     )
-    got = exchange(sends, range(pairs))
+    got = exchange(sends, falling(pairs))
     message = jnp.concatenate([half, trade(half)], axis=0)
     steps = []
     for i in range(members):

time: 36.9 us -> 36.8 us (level)
  no operation moved by 1% of the time
where the time goes in v14:
time: 36.8 us; the launch traced here: 36.6 us
  starting transfers between devices  15.7 us (43%)
  waiting for transfers between devices  13.4 us (36%)
  Pallas kernels  5.98 us (16%)
  between operations  0.81 us (2%)
  local copies, waits for them, and re-layouts  0.69 us (2%)
    ppermute x9, waiting for transfers between devices, exchange(): lax.ppermute(x, 'member', [(i, i ^ 2 * k) for i in range(members)])  11.3 us
    ppermute x9, starting transfers between devices, exchange(): lax.ppermute(x, 'member', [(i, i ^ 2 * k) for i in range(members)])  11.2 us
    pallas_call x8, Pallas kernels, call(): pl.pallas_call(kernel, out_shape=[jax.ShapeDtypeStruct(s, d) for s, d in...  5.98 us
    ppermute x1, starting transfers between devices, body(): mine = lax.ppermute(message, ('member', 'region'), steps)  3.6 us
    ppermute x1, waiting for transfers between devices, body(): mine = lax.ppermute(message, ('member', 'region'), steps)  1.43 us
    ppermute x4, starting transfers between devices, trade(): return lax.ppermute(x, 'member', [(i, i ^ 1) for i in range(members)])  0.86 us
  transfers between devices with their start and end apart: 14, of which 7 were waited for; matrix products, arithmetic and copies ran while one was open for 0% of the time, Pallas kernels for 3%

profile of v14, /device:TPU:0, one launch (start us, length us, event | category | flops | bytes accessed | tf_op | source)
XLA Modules:
  0.0 36.6 jit_solution(1614434752376068920)
XLA Ops:
  0.6 0.0 copy-start
  0.6 0.0 copy-start.1
  0.7 0.0 copy-start.2
  0.7 1.2 %prepare.1 = (f32[1,128]{1,0:T(1,128)S(1)}, f32[1,128]{1,0:T(1,128)S(1)}, f32[1,128]{1,0:T(1,128)S(1)}, f32[1,128]{1,0:T(1,128)S(1)}, f32[8,128]{1,0:T(8,128)S(1)}, /*index=5*/s32[2,32,128]{2,1,0:T(8,128)S(1)}) custom-call(bf16[2,16,4096]{2,1,0:T(8,128)(2,1)} %state.1, bf16[2,16,4096]{2,1,0:T(8,128)(2,1)} %state.1, f32[16,4096]{1,0:T(8,128)} %diff.3, ...), custom_call_target="tpu_custom_call" | custom-call | tf_op jit(solution)/shard_map/prepare/pallas_call | solution.py:28
  1.9 0.0 copy-done
  1.9 0.0 copy-done.1
  1.9 0.0 copy-done.2
  1.9 0.6 %forecast_first.1.own = bf16[32,4096]{1,0:T(8,128)(2,1)S(1)} custom-call(bf16[2,16,4096]{2,1,0:T(8,128)(2,1)S(1)} %copy-done.2, f32[16,4096]{1,0:T(8,128)S(1)} %copy-done.1, bf16[2,2,16,4096]{3,2,1,0:T(8,128)(2,1)S(1)} %copy-done, f32[8,128]{1,0:T(8,128)S(1)} %get-tuple-element.30.after.trail), custom_call_target="tpu_custom_call" | custom-call | tf_op jit(solution)/shard_map/forecast_first/pallas_call | solution.py:28
  2.6 0.5 %collective-permute-start = (bf16[32,4096]{1,0:T(8,128)(2,1)S(1)}, bf16[32,4096]{1,0:T(8,128)(2,1)S(1)}, u32[]{:S(2)}, u32[]{:S(2)}) collective-permute-start(bf16[32,4096]{1,0:T(8,128)(2,1)S(1)} %forecast_first.1.own), channel_id=1, source_target_pairs={{0,4},{4,0},{8,12},{12,8},{16,20},{20,16},{24,28},{28,24},{1,5},{5... | collective-permute-start | bytes 786440 | tf_op jit(solution)/shard_map/ppermute | solution.py:475
  3.1 2.6 %collective-permute-start.1 = (f32[1,128]{1,0:T(1,128)S(1)}, f32[1,128]{1,0:T(1,128)S(1)}, u32[]{:S(2)}, u32[]{:S(2)}) collective-permute-start(f32[1,128]{1,0:T(1,128)S(1)} %get-tuple-element.32), channel_id=1, source_target_pairs={{0,8},{4,12},{8,0},{12,4},{16,24},{20,28},{24,16},{28,20},{1,9},{5... | collective-permute-start | bytes 1544 | tf_op jit(solution)/shard_map/ppermute | solution.py:480
  5.6 1.5 %collective-permute-start.2 = (f32[1,128]{1,0:T(1,128)S(1)}, f32[1,128]{1,0:T(1,128)S(1)}, u32[]{:S(2)}, u32[]{:S(2)}) collective-permute-start(f32[1,128]{1,0:T(1,128)S(1)} %get-tuple-element.33), channel_id=1, source_target_pairs={{0,16},{4,20},{8,24},{12,28},{16,0},{20,4},{24,8},{28,12},{1,17},{... | collective-permute-start | bytes 1544 | tf_op jit(solution)/shard_map/ppermute | solution.py:480
  7.2 0.0 collective-permute-start.3
  7.2 0.0 collective-permute-done.1.refs_1_
  7.2 2.0 %collective-permute-done.2.refs_2_ = f32[1,128]{1,0:T(1,128)S(1)} collective-permute-done((f32[1,128]{1,0:T(1,128)S(1)}, f32[1,128]{1,0:T(1,128)S(1)}, u32[]{:S(2)}, u32[]{:S(2)}) %collective-permute-start.2) | collective-permute-done | bytes 544 | tf_op jit(solution)/shard_map/ppermute | solution.py:480
  9.2 2.4 %collective-permute-done.3.refs_3_ = f32[1,128]{1,0:T(1,128)S(1)} collective-permute-done((f32[1,128]{1,0:T(1,128)S(1)}, f32[1,128]{1,0:T(1,128)S(1)}, u32[]{:S(2)}, u32[]{:S(2)}) %collective-permute-start.3) | collective-permute-done | bytes 544 | tf_op jit(solution)/shard_map/ppermute | solution.py:480
  11.6 0.0 collective-permute-done.other
  11.6 0.4 send_first.1
  12.0 0.0 copy-start.6
  12.0 0.0 copy-start.7
  12.0 0.1 collective-permute-start.4
  12.1 0.0 copy-start.3
  12.1 0.1 collective-permute-start.7
  12.2 2.0 %collective-permute-start.8 = (bf16[16,4096]{1,0:T(8,128)(2,1)S(1)}, bf16[16,4096]{1,0:T(8,128)(2,1)S(1)}, u32[]{:S(2)}, u32[]{:S(2)}) collective-permute-start(bf16[16,4096]{1,0:T(8,128)(2,1)S(1)} %get-tuple-element.39), channel_id=1, source_target_pairs={{0,16},{4,20},{8,24},{12,28},{16,0},{20,4},{24,8},{28,12},{1,17},{... | collective-permute-start | bytes 393224 | tf_op jit(solution)/shard_map/ppermute | solution.py:480
  14.2 1.5 %collective-permute-start.9 = (bf16[16,4096]{1,0:T(8,128)(2,1)S(1)}, bf16[16,4096]{1,0:T(8,128)(2,1)S(1)}, u32[]{:S(2)}, u32[]{:S(2)}) collective-permute-start(bf16[16,4096]{1,0:T(8,128)(2,1)S(1)} %get-tuple-element.40), channel_id=1, source_target_pairs={{0,8},{4,12},{8,0},{12,4},{16,24},{20,28},{24,16},{28,20},{1,9},{5... | collective-permute-start | bytes 393224 | tf_op jit(solution)/shard_map/ppermute | solution.py:480
  15.7 0.0 collective-permute-done.4
  15.7 3.6 %collective-permute-start.5 = (f32[32,128]{1,0:T(8,128)S(1)}, f32[32,128]{1,0:T(8,128)S(1)}, u32[]{:S(2)}, u32[]{:S(2)}) collective-permute-start(f32[32,128]{1,0:T(8,128)S(1)} %constant_dynamic-update-slice_fusion.message), channel_id=1, source_target_pairs={{0,1},{1,2},{2,3},{5,4},{6,5},{7,6},{8,9},{9,10},{10,11},{13,12},{... | collective-permute-start | bytes 49160 | tf_op jit(solution)/shard_map/ppermute | solution.py:515
  19.3 1.4 %collective-permute-done.5.mine = f32[32,128]{1,0:T(8,128)S(1)} collective-permute-done((f32[32,128]{1,0:T(8,128)S(1)}, f32[32,128]{1,0:T(8,128)S(1)}, u32[]{:S(2)}, u32[]{:S(2)}) %collective-permute-start.5) | collective-permute-done | bytes 16416 | tf_op jit(solution)/shard_map/ppermute | solution.py:515
  20.7 0.0 collective-permute-start.6
  20.7 0.0 copy-done.6
  20.7 0.0 copy-done.7
  20.7 0.6 %copy-done.8 = s32[32]{0:T(128)S(1)} copy-done((s32[32]{0:T(128)S(1)}, s32[32]{0:T(128)}, u32[]{:S(2)}) %copy-start.8) | copy-done | bytes 152
  21.4 0.2 observe.1
  21.5 0.3 collective-permute-done.6.theirs
  21.9 0.0 collective-permute-done.7.refs_1_
  21.9 0.0 collective-permute-done.8.refs_2_
  21.9 0.0 collective-permute-done.9.refs_3_
  21.9 0.9 %forecast_second.1 = (bf16[32,4096]{1,0:T(8,128)(2,1)S(1)}, f32[32,256]{1,0:T(8,128)S(1)}, f32[32,256]{1,0:T(8,128)S(1)}) custom-call(s32[2,32,128]{2,1,0:T(8,128)S(1)} %get-tuple-element.29.keys, f32[16,4096]{1,0:T(8,128)S(1)} %copy-done.1, bf16[2,2,16,4096]{3,2,1,0:T(8,128)(2,1)S(1)} %copy-done, f32[32,128]{1,0:T(8,128)S(1)} %constant_dynamic-update-slice_fusion.message, ...), custom_call_target="tpu_custom_call" | custom-call | tf_op jit(solution)/shard_map/forecast_second/pallas_call | solution.py:28
  22.8 0.3 collective-permute-start.10
  23.1 1.0 %assess_first.1 = (bf16[16,640]{1,0:T(8,128)(2,1)S(1)}, bf16[16,640]{1,0:T(8,128)(2,1)S(1)}, bf16[16,640]{1,0:T(8,128)(2,1)S(1)}, bf16[16,640]{1,0:T(8,128)(2,1)...) custom-call(bf16[32,4096]{1,0:T(8,128)(2,1)S(1)} %forecast_first.1.own, ...), custom_call_target="tpu_custom_call" | custom-call | tf_op jit(solution)/shard_map/assess_first/pallas_call | solution.py:28
  24.0 0.4 collective-permute-done.10.other
  24.4 0.8 %send_second.1 = (bf16[16,5376]{1,0:T(8,128)(2,1)S(1)}, bf16[16,5376]{1,0:T(8,128)(2,1)S(1)}, bf16[16,5376]{1,0:T(8,128)(2,1)S(1)}, bf16[16,5376]{1,0:T(8,128)(2,1)S(1)}) custom-call(bf16[32,4096]{1,0:T(8,128)(2,1)S(1)} %get-tuple-element.41.second.own, bf16[32,4096]{1,0:T(8,128)(2,1)S(1)} %collective-permute-done.10.other, ...), custom_call_target="tpu_custom_call" | custom-call | tf_op jit(solution)/shard_map/send_second/pallas_call | solution.py:28
  25.2 0.5 %collective-permute-start.11 = (bf16[16,5376]{1,0:T(8,128)(2,1)S(1)}, bf16[16,5376]{1,0:T(8,128)(2,1)S(1)}, u32[]{:S(2)}, u32[]{:S(2)}) collective-permute-start(bf16[16,5376]{1,0:T(8,128)(2,1)S(1)} %get-tuple-element.53), channel_id=1, source_target_pairs={{0,24},{4,28},{8,16},{12,20},{16,8},{20,12},{24,0},{28,4},{1,25},{... | collective-permute-start | bytes 516104 | tf_op jit(solution)/shard_map/ppermute | solution.py:480
  25.7 1.5 %collective-permute-start.12 = (bf16[16,5376]{1,0:T(8,128)(2,1)S(1)}, bf16[16,5376]{1,0:T(8,128)(2,1)S(1)}, u32[]{:S(2)}, u32[]{:S(2)}) collective-permute-start(bf16[16,5376]{1,0:T(8,128)(2,1)S(1)} %get-tuple-element.54), channel_id=1, source_target_pairs={{0,16},{4,20},{8,24},{12,28},{16,0},{20,4},{24,8},{28,12},{1,17},{... | collective-permute-start | bytes 516104 | tf_op jit(solution)/shard_map/ppermute | solution.py:480
  27.2 1.5 %collective-permute-start.13 = (bf16[16,5376]{1,0:T(8,128)(2,1)S(1)}, bf16[16,5376]{1,0:T(8,128)(2,1)S(1)}, u32[]{:S(2)}, u32[]{:S(2)}) collective-permute-start(bf16[16,5376]{1,0:T(8,128)(2,1)S(1)} %get-tuple-element.55), channel_id=1, source_target_pairs={{0,8},{4,12},{8,0},{12,4},{16,24},{20,28},{24,16},{28,20},{1,9},{5... | collective-permute-start | bytes 516104 | tf_op jit(solution)/shard_map/ppermute | solution.py:480
  28.8 4.7 %collective-permute-done.11.refs_1_ = bf16[16,5376]{1,0:T(8,128)(2,1)S(1)} collective-permute-done((bf16[16,5376]{1,0:T(8,128)(2,1)S(1)}, bf16[16,5376]{1,0:T(8,128)(2,1)S(1)}, u32[]{:S(2)}, u32[]{:S(2)}) %collective-permute-start.11) | collective-permute-done | bytes 172064 | tf_op jit(solution)/shard_map/ppermute | solution.py:480
  33.4 2.2 %collective-permute-done.12.refs_2_ = bf16[16,5376]{1,0:T(8,128)(2,1)S(1)} collective-permute-done((bf16[16,5376]{1,0:T(8,128)(2,1)S(1)}, bf16[16,5376]{1,0:T(8,128)(2,1)S(1)}, u32[]{:S(2)}, u32[]{:S(2)}) %collective-permute-start.12) | collective-permute-done | bytes 172064 | tf_op jit(solution)/shard_map/ppermute | solution.py:480
  35.6 0.0 collective-permute-done.13.refs_3_
  35.6 0.9 %finish.1 = (bf16[2,16,4096]{2,1,0:T(8,128)(2,1)}, f32[2,16,512]{2,1,0:T(8,128)}) custom-call(s32[2,32,128]{2,1,0:T(8,128)S(1)} %get-tuple-element.29.keys, bf16[16,5376]{1,0:T(8,128)(2,1)S(1)} %get-tuple-element.52.refs_0_, bf16[16,5376]{1,0:T(8,128)(2,1)S(1)} %collective-permute-done.11.refs_1_, bf16[16,5376]{1,0:T(8,128)(2,1)S(1)} %collective-permute-done.12.refs_2_, ...), custom_call_target="tpu_custom_call" | custom-call | tf_op jit(solution)/shard_map/finish/pallas_call | solution.py:28
  (8 shorter events, 0.0 us)
Async XLA Ops:
  0.6 1.2 %copy-start = (bf16[2,2,16,4096]{3,2,1,0:T(8,128)(2,1)S(1)}, bf16[2,2,16,4096]{3,2,1,0:T(8,128)(2,1)}, u32[]{:S(2)}) copy-start(bf16[2,2,16,4096]{3,2,1,0:T(8,128)(2,1)} %pert.3) | copy-start | bytes 1572868
  0.6 1.2 %copy-start.1 = (f32[16,4096]{1,0:T(8,128)S(1)}, f32[16,4096]{1,0:T(8,128)}, u32[]{:S(2)}) copy-start(f32[16,4096]{1,0:T(8,128)} %diff.3) | copy-start | bytes 786436
  0.7 1.3 %copy-start.2 = (bf16[2,16,4096]{2,1,0:T(8,128)(2,1)S(1)}, bf16[2,16,4096]{2,1,0:T(8,128)(2,1)}, u32[]{:S(2)}) copy-start(bf16[2,16,4096]{2,1,0:T(8,128)(2,1)} %state.1) | copy-start | bytes 786436
  2.6 9.0 %collective-permute-start = (bf16[32,4096]{1,0:T(8,128)(2,1)S(1)}, bf16[32,4096]{1,0:T(8,128)(2,1)S(1)}, u32[]{:S(2)}, u32[]{:S(2)}) collective-permute-start(bf16[32,4096]{1,0:T(8,128)(2,1)S(1)} %forecast_first.1.own), channel_id=1, source_target_pairs={{0,4},{4,0},{8,12},{12,8},{16,20},{20,16},{24,28},{28,24},{1,5},{5... | collective-permute-start | bytes 786440 | tf_op jit(solution)/shard_map/ppermute | solution.py:475
  3.1 4.1 %collective-permute-start.1 = (f32[1,128]{1,0:T(1,128)S(1)}, f32[1,128]{1,0:T(1,128)S(1)}, u32[]{:S(2)}, u32[]{:S(2)}) collective-permute-start(f32[1,128]{1,0:T(1,128)S(1)} %get-tuple-element.32), channel_id=1, source_target_pairs={{0,8},{4,12},{8,0},{12,4},{16,24},{20,28},{24,16},{28,20},{1,9},{5... | collective-permute-start | bytes 1544 | tf_op jit(solution)/shard_map/ppermute | solution.py:480
  5.6 3.5 %collective-permute-start.2 = (f32[1,128]{1,0:T(1,128)S(1)}, f32[1,128]{1,0:T(1,128)S(1)}, u32[]{:S(2)}, u32[]{:S(2)}) collective-permute-start(f32[1,128]{1,0:T(1,128)S(1)} %get-tuple-element.33), channel_id=1, source_target_pairs={{0,16},{4,20},{8,24},{12,28},{16,0},{20,4},{24,8},{28,12},{1,17},{... | collective-permute-start | bytes 1544 | tf_op jit(solution)/shard_map/ppermute | solution.py:480
  7.2 4.4 %collective-permute-start.3 = (f32[1,128]{1,0:T(1,128)S(1)}, f32[1,128]{1,0:T(1,128)S(1)}, u32[]{:S(2)}, u32[]{:S(2)}) collective-permute-start(f32[1,128]{1,0:T(1,128)S(1)} %get-tuple-element.34), channel_id=1, source_target_pairs={{0,24},{4,28},{8,16},{12,20},{16,8},{20,12},{24,0},{28,4},{1,25},{... | collective-permute-start | bytes 1544 | tf_op jit(solution)/shard_map/ppermute | solution.py:480
  11.6 9.1 %copy-start.5 = (f32[32,16]{0,1:T(8,128)S(1)}, f32[32,16]{0,1:T(8,128)}, u32[]{:S(2)}) copy-start(f32[32,16]{0,1:T(8,128)} %param.15) | copy-start | bytes 6148
  12.0 8.7 %copy-start.6 = (s32[16,6]{0,1:T(8,128)S(1)}, s32[16,6]{0,1:T(8,128)}, u32[]{:S(2)}) copy-start(s32[16,6]{0,1:T(8,128)} %param.18) | copy-start | bytes 1156
  12.0 8.7 %copy-start.7 = (f32[16,6]{0,1:T(8,128)S(1)}, f32[16,6]{0,1:T(8,128)}, u32[]{:S(2)}) copy-start(f32[16,6]{0,1:T(8,128)} %param.19) | copy-start | bytes 1156
  12.0 3.7 %collective-permute-start.4 = (f32[16,128]{1,0:T(8,128)S(1)}, f32[16,128]{1,0:T(8,128)S(1)}, u32[]{:S(2)}, u32[]{:S(2)}) collective-permute-start(f32[16,128]{1,0:T(8,128)S(1)} %get-tuple-element.35), channel_id=1, source_target_pairs={{0,4},{4,0},{8,12},{12,8},{16,20},{20,16},{24,28},{28,24},{1,5},{5... | collective-permute-start | bytes 24584 | tf_op jit(solution)/shard_map/ppermute | solution.py:475
  12.1 8.6 %copy-start.3 = (f32[2,32,16]{1,2,0:T(8,128)S(1)}, f32[2,32,16]{1,2,0:T(8,128)}, u32[]{:S(2)}) copy-start(f32[2,32,16]{1,2,0:T(8,128)} %param.14) | copy-start | bytes 12292
  12.1 9.8 %collective-permute-start.7 = (bf16[16,4096]{1,0:T(8,128)(2,1)S(1)}, bf16[16,4096]{1,0:T(8,128)(2,1)S(1)}, u32[]{:S(2)}, u32[]{:S(2)}) collective-permute-start(bf16[16,4096]{1,0:T(8,128)(2,1)S(1)} %get-tuple-element.38), channel_id=1, source_target_pairs={{0,24},{4,28},{8,16},{12,20},{16,8},{20,12},{24,0},{28,4},{1,25},{... | collective-permute-start | bytes 393224 | tf_op jit(solution)/shard_map/ppermute | solution.py:480
  12.2 9.7 %collective-permute-start.8 = (bf16[16,4096]{1,0:T(8,128)(2,1)S(1)}, bf16[16,4096]{1,0:T(8,128)(2,1)S(1)}, u32[]{:S(2)}, u32[]{:S(2)}) collective-permute-start(bf16[16,4096]{1,0:T(8,128)(2,1)S(1)} %get-tuple-element.39), channel_id=1, source_target_pairs={{0,16},{4,20},{8,24},{12,28},{16,0},{20,4},{24,8},{28,12},{1,17},{... | collective-permute-start | bytes 393224 | tf_op jit(solution)/shard_map/ppermute | solution.py:480
  14.2 7.7 %collective-permute-start.9 = (bf16[16,4096]{1,0:T(8,128)(2,1)S(1)}, bf16[16,4096]{1,0:T(8,128)(2,1)S(1)}, u32[]{:S(2)}, u32[]{:S(2)}) collective-permute-start(bf16[16,4096]{1,0:T(8,128)(2,1)S(1)} %get-tuple-element.40), channel_id=1, source_target_pairs={{0,8},{4,12},{8,0},{12,4},{16,24},{20,28},{24,16},{28,20},{1,9},{5... | collective-permute-start | bytes 393224 | tf_op jit(solution)/shard_map/ppermute | solution.py:480
  15.7 5.1 %copy-start.4 = (s32[32,16]{0,1:T(8,128)S(1)}, s32[32,16]{0,1:T(8,128)}, u32[]{:S(2)}) copy-start(s32[32,16]{0,1:T(8,128)} %param.17) | copy-start | bytes 6148
  15.7 5.0 %collective-permute-start.5 = (f32[32,128]{1,0:T(8,128)S(1)}, f32[32,128]{1,0:T(8,128)S(1)}, u32[]{:S(2)}, u32[]{:S(2)}) collective-permute-start(f32[32,128]{1,0:T(8,128)S(1)} %constant_dynamic-update-slice_fusion.message), channel_id=1, source_target_pairs={{0,1},{1,2},{2,3},{5,4},{6,5},{7,6},{8,9},{9,10},{10,11},{13,12},{... | collective-permute-start | bytes 49160 | tf_op jit(solution)/shard_map/ppermute | solution.py:515
  20.7 1.2 %collective-permute-start.6 = (f32[32,128]{1,0:T(8,128)S(1)}, f32[32,128]{1,0:T(8,128)S(1)}, u32[]{:S(2)}, u32[]{:S(2)}) collective-permute-start(f32[32,128]{1,0:T(8,128)S(1)} %collective-permute-done.5.mine), channel_id=1, source_target_pairs={{0,4},{4,0},{8,12},{12,8},{16,20},{20,16},{24,28},{28,24},{1,5},{5... | collective-permute-start | bytes 49160 | tf_op jit(solution)/shard_map/ppermute | solution.py:475
  20.7 0.7 %copy-start.8 = (s32[32]{0:T(128)S(1)}, s32[32]{0:T(128)}, u32[]{:S(2)}) copy-start(s32[32]{0:T(128)} %param.16) | copy-start | bytes 388
  22.8 1.6 %collective-permute-start.10 = (bf16[32,4096]{1,0:T(8,128)(2,1)S(1)}, bf16[32,4096]{1,0:T(8,128)(2,1)S(1)}, u32[]{:S(2)}, u32[]{:S(2)}) collective-permute-start(bf16[32,4096]{1,0:T(8,128)(2,1)S(1)} %get-tuple-element.41.second.own), channel_id=1, source_target_pairs={{0,4},{4,0},{8,12},{12,8},{16,20},{20,16},{24,28},{28,24},{1,5},{5... | collective-permute-start | bytes 786440 | tf_op jit(solution)/shard_map/ppermute | solution.py:475
  25.2 8.2 %collective-permute-start.11 = (bf16[16,5376]{1,0:T(8,128)(2,1)S(1)}, bf16[16,5376]{1,0:T(8,128)(2,1)S(1)}, u32[]{:S(2)}, u32[]{:S(2)}) collective-permute-start(bf16[16,5376]{1,0:T(8,128)(2,1)S(1)} %get-tuple-element.53), channel_id=1, source_target_pairs={{0,24},{4,28},{8,16},{12,20},{16,8},{20,12},{24,0},{28,4},{1,25},{... | collective-permute-start | bytes 516104 | tf_op jit(solution)/shard_map/ppermute | solution.py:480
  25.7 9.9 %collective-permute-start.12 = (bf16[16,5376]{1,0:T(8,128)(2,1)S(1)}, bf16[16,5376]{1,0:T(8,128)(2,1)S(1)}, u32[]{:S(2)}, u32[]{:S(2)}) collective-permute-start(bf16[16,5376]{1,0:T(8,128)(2,1)S(1)} %get-tuple-element.54), channel_id=1, source_target_pairs={{0,16},{4,20},{8,24},{12,28},{16,0},{20,4},{24,8},{28,12},{1,17},{... | collective-permute-start | bytes 516104 | tf_op jit(solution)/shard_map/ppermute | solution.py:480
  27.2 8.4 %collective-permute-start.13 = (bf16[16,5376]{1,0:T(8,128)(2,1)S(1)}, bf16[16,5376]{1,0:T(8,128)(2,1)S(1)}, u32[]{:S(2)}, u32[]{:S(2)}) collective-permute-start(bf16[16,5376]{1,0:T(8,128)(2,1)S(1)} %get-tuple-element.55), channel_id=1, source_target_pairs={{0,8},{4,12},{8,0},{12,4},{16,24},{20,28},{24,16},{28,20},{1,9},{5... | collective-permute-start | bytes 516104 | tf_op jit(solution)/shard_map/ppermute | solution.py:480

commit v15 on v14

--- a/solution.py
+++ b/solution.py
@@ -107,7 +107,7 @@
                 column = column_of(source * capacity + rank)
                 keys[c, p * tiles:(p + 1) * tiles, :] = jnp.broadcast_to(column, (tiles, LANES))
         for k in range(pairs):
-            notes[k][...] = jnp.where(lane < EDGE_AT, asked[k:k + 1, :] - 1.0, edge)
+            notes[falling(pairs).index(k)][...] = jnp.where(lane < EDGE_AT, asked[k:k + 1, :] - 1.0, edge)
 
     return kernel
 
@@ -309,7 +309,7 @@
 def make_send(pairs, rows):
     def kernel(own, other, trail, *refs):
         notes, sends, half = refs[:pairs], refs[pairs:2 * pairs], refs[2 * pairs]
-        sends = [sends[falling(pairs).index(k)] for k in range(pairs)]
+        notes, sends = [[x[falling(pairs).index(k)] for k in range(pairs)] for x in (notes, sends)]
         prior = jnp.concatenate([own[...], other[...]], axis=0)
         sent = requested([x[...] for x in notes], prior, 0, rows)
         for k in range(pairs):
@@ -382,7 +382,7 @@
 def make_send_second(pairs, rows, parts, tiles, cells, share):
     def kernel(own, other, where, terms, local, stats, own_sums, *refs):
         notes, kept, outs, sums = refs[:pairs], refs[pairs:2 * pairs], refs[2 * pairs:3 * pairs], refs[3 * pairs]
-        outs = [outs[falling(pairs).index(k)] for k in range(pairs)]
+        notes, outs = [[x[falling(pairs).index(k)] for k in range(pairs)] for x in (notes, outs)]
         prior = jnp.concatenate([own[...], other[...]], axis=0)
         sent = requested([x[...] for x in notes], prior, 1, rows)
         extra = kept[0].shape[1]
@@ -480,7 +480,7 @@
             got.append(lax.ppermute(x, "member", [(i, i ^ (2 * k)) for i in range(members)]))
         return got
 
-    notes = exchange(notes, range(pairs))
+    notes = exchange(notes, falling(pairs))
 
     where, terms, local = call(
         make_observe(blocks, per_block, tiles, near),

time: 36.8 us -> 36.6 us (level)
  transfers between devices with their start and end apart: 14 -> 14, of which waited for: 7 -> 9; matrix products, arithmetic and copies ran while one was open for 0% -> 0% of each run, Pallas kernels for 3% -> 3%
where the time goes in v15:
time: 36.6 us; the launch traced here: 36.4 us
  starting transfers between devices  15.7 us (43%)
  waiting for transfers between devices  13.2 us (36%)
  Pallas kernels  5.97 us (16%)
  between operations  0.81 us (2%)
  local copies, waits for them, and re-layouts  0.69 us (2%)
    ppermute x9, starting transfers between devices, exchange(): lax.ppermute(x, 'member', [(i, i ^ 2 * k) for i in range(members)])  11.3 us
    ppermute x9, waiting for transfers between devices, exchange(): lax.ppermute(x, 'member', [(i, i ^ 2 * k) for i in range(members)])  11.1 us
    pallas_call x8, Pallas kernels, call(): pl.pallas_call(kernel, out_shape=[jax.ShapeDtypeStruct(s, d) for s, d in...  5.97 us
    ppermute x1, starting transfers between devices, body(): mine = lax.ppermute(message, ('member', 'region'), steps)  3.6 us
    ppermute x1, waiting for transfers between devices, body(): mine = lax.ppermute(message, ('member', 'region'), steps)  1.43 us
    ppermute x4, starting transfers between devices, trade(): return lax.ppermute(x, 'member', [(i, i ^ 1) for i in range(members)])  0.86 us
  transfers between devices with their start and end apart: 14, of which 9 were waited for; matrix products, arithmetic and copies ran while one was open for 0% of the time, Pallas kernels for 3%

profile of v15, /device:TPU:0, one launch (start us, length us, event | category | flops | bytes accessed | tf_op | source)
XLA Modules:
  0.0 36.4 jit_solution(10179624449925596229)
XLA Ops:
  0.6 0.0 copy-start
  0.6 0.0 copy-start.1
  0.7 0.0 copy-start.2
  0.7 1.2 %prepare.1 = (f32[1,128]{1,0:T(1,128)S(1)}, f32[1,128]{1,0:T(1,128)S(1)}, f32[1,128]{1,0:T(1,128)S(1)}, f32[1,128]{1,0:T(1,128)S(1)}, f32[8,128]{1,0:T(8,128)S(1)}, /*index=5*/s32[2,32,128]{2,1,0:T(8,128)S(1)}) custom-call(bf16[2,16,4096]{2,1,0:T(8,128)(2,1)} %state.1, bf16[2,16,4096]{2,1,0:T(8,128)(2,1)} %state.1, f32[16,4096]{1,0:T(8,128)} %diff.3, ...), custom_call_target="tpu_custom_call" | custom-call | tf_op jit(solution)/shard_map/prepare/pallas_call | solution.py:28
  1.9 0.0 copy-done.1
  1.9 0.0 copy-done.2
  1.9 0.6 %forecast_first.1.own = bf16[32,4096]{1,0:T(8,128)(2,1)S(1)} custom-call(bf16[2,16,4096]{2,1,0:T(8,128)(2,1)S(1)} %copy-done.2, f32[16,4096]{1,0:T(8,128)S(1)} %copy-done.1, bf16[2,2,16,4096]{3,2,1,0:T(8,128)(2,1)S(1)} %copy-done, f32[8,128]{1,0:T(8,128)S(1)} %get-tuple-element.30.after.trail), custom_call_target="tpu_custom_call" | custom-call | tf_op jit(solution)/shard_map/forecast_first/pallas_call | solution.py:28
  2.6 0.5 %collective-permute-start = (bf16[32,4096]{1,0:T(8,128)(2,1)S(1)}, bf16[32,4096]{1,0:T(8,128)(2,1)S(1)}, u32[]{:S(2)}, u32[]{:S(2)}) collective-permute-start(bf16[32,4096]{1,0:T(8,128)(2,1)S(1)} %forecast_first.1.own), channel_id=1, source_target_pairs={{0,4},{4,0},{8,12},{12,8},{16,20},{20,16},{24,28},{28,24},{1,5},{5... | collective-permute-start | bytes 786440 | tf_op jit(solution)/shard_map/ppermute | solution.py:475
  3.1 3.5 %collective-permute-start.1 = (f32[1,128]{1,0:T(1,128)S(1)}, f32[1,128]{1,0:T(1,128)S(1)}, u32[]{:S(2)}, u32[]{:S(2)}) collective-permute-start(f32[1,128]{1,0:T(1,128)S(1)} %get-tuple-element.32), channel_id=1, source_target_pairs={{0,24},{4,28},{8,16},{12,20},{16,8},{20,12},{24,0},{28,4},{1,25},{... | collective-permute-start | bytes 1544 | tf_op jit(solution)/shard_map/ppermute | solution.py:480
  6.6 0.5 %collective-permute-start.2 = (f32[1,128]{1,0:T(1,128)S(1)}, f32[1,128]{1,0:T(1,128)S(1)}, u32[]{:S(2)}, u32[]{:S(2)}) collective-permute-start(f32[1,128]{1,0:T(1,128)S(1)} %get-tuple-element.33), channel_id=1, source_target_pairs={{0,16},{4,20},{8,24},{12,28},{16,0},{20,4},{24,8},{28,12},{1,17},{... | collective-permute-start | bytes 1544 | tf_op jit(solution)/shard_map/ppermute | solution.py:480
  7.1 0.1 collective-permute-start.3
  7.2 0.9 %collective-permute-done.1.refs_1_ = f32[1,128]{1,0:T(1,128)S(1)} collective-permute-done((f32[1,128]{1,0:T(1,128)S(1)}, f32[1,128]{1,0:T(1,128)S(1)}, u32[]{:S(2)}, u32[]{:S(2)}) %collective-permute-start.1) | collective-permute-done | bytes 544 | tf_op jit(solution)/shard_map/ppermute | solution.py:480
  8.1 2.0 %collective-permute-done.2.refs_2_ = f32[1,128]{1,0:T(1,128)S(1)} collective-permute-done((f32[1,128]{1,0:T(1,128)S(1)}, f32[1,128]{1,0:T(1,128)S(1)}, u32[]{:S(2)}, u32[]{:S(2)}) %collective-permute-start.2) | collective-permute-done | bytes 544 | tf_op jit(solution)/shard_map/ppermute | solution.py:480
  10.1 0.5 %collective-permute-done.3.refs_3_ = f32[1,128]{1,0:T(1,128)S(1)} collective-permute-done((f32[1,128]{1,0:T(1,128)S(1)}, f32[1,128]{1,0:T(1,128)S(1)}, u32[]{:S(2)}, u32[]{:S(2)}) %collective-permute-start.3) | collective-permute-done | bytes 544 | tf_op jit(solution)/shard_map/ppermute | solution.py:480
  10.6 0.0 collective-permute-done.other
  10.6 0.3 send_first.1
  11.0 0.0 copy-start.6
  11.0 0.0 copy-start.7
  11.0 0.1 collective-permute-start.4
  11.1 0.0 copy-start.3
  11.1 1.6 %collective-permute-start.7 = (bf16[16,4096]{1,0:T(8,128)(2,1)S(1)}, bf16[16,4096]{1,0:T(8,128)(2,1)S(1)}, u32[]{:S(2)}, u32[]{:S(2)}) collective-permute-start(bf16[16,4096]{1,0:T(8,128)(2,1)S(1)} %get-tuple-element.38), channel_id=1, source_target_pairs={{0,24},{4,28},{8,16},{12,20},{16,8},{20,12},{24,0},{28,4},{1,25},{... | collective-permute-start | bytes 393224 | tf_op jit(solution)/shard_map/ppermute | solution.py:480
  12.7 0.1 collective-permute-start.8
  12.8 1.9 %collective-permute-start.9 = (bf16[16,4096]{1,0:T(8,128)(2,1)S(1)}, bf16[16,4096]{1,0:T(8,128)(2,1)S(1)}, u32[]{:S(2)}, u32[]{:S(2)}) collective-permute-start(bf16[16,4096]{1,0:T(8,128)(2,1)S(1)} %get-tuple-element.40), channel_id=1, source_target_pairs={{0,8},{4,12},{8,0},{12,4},{16,24},{20,28},{24,16},{28,20},{1,9},{5... | collective-permute-start | bytes 393224 | tf_op jit(solution)/shard_map/ppermute | solution.py:480
  14.7 0.0 collective-permute-done.4
  14.7 3.6 %collective-permute-start.5 = (f32[32,128]{1,0:T(8,128)S(1)}, f32[32,128]{1,0:T(8,128)S(1)}, u32[]{:S(2)}, u32[]{:S(2)}) collective-permute-start(f32[32,128]{1,0:T(8,128)S(1)} %constant_dynamic-update-slice_fusion.message), channel_id=1, source_target_pairs={{0,1},{1,2},{2,3},{5,4},{6,5},{7,6},{8,9},{9,10},{10,11},{13,12},{... | collective-permute-start | bytes 49160 | tf_op jit(solution)/shard_map/ppermute | solution.py:515
  18.3 1.4 %collective-permute-done.5.mine = f32[32,128]{1,0:T(8,128)S(1)} collective-permute-done((f32[32,128]{1,0:T(8,128)S(1)}, f32[32,128]{1,0:T(8,128)S(1)}, u32[]{:S(2)}, u32[]{:S(2)}) %collective-permute-start.5) | collective-permute-done | bytes 16416 | tf_op jit(solution)/shard_map/ppermute | solution.py:515
  19.7 0.0 collective-permute-start.6
  19.7 0.0 copy-done.7
  19.7 0.0 copy-done.3
  19.8 0.0 copy-done.4
  19.8 0.6 %copy-done.8 = s32[32]{0:T(128)S(1)} copy-done((s32[32]{0:T(128)S(1)}, s32[32]{0:T(128)}, u32[]{:S(2)}) %copy-start.8) | copy-done | bytes 152
  20.4 0.2 observe.1
  20.6 0.3 collective-permute-done.6.theirs
  20.9 0.0 collective-permute-done.7.refs_1_
  20.9 0.0 collective-permute-done.8.refs_2_
  20.9 0.0 collective-permute-done.9.refs_3_
  20.9 0.9 %forecast_second.1 = (bf16[32,4096]{1,0:T(8,128)(2,1)S(1)}, f32[32,256]{1,0:T(8,128)S(1)}, f32[32,256]{1,0:T(8,128)S(1)}) custom-call(s32[2,32,128]{2,1,0:T(8,128)S(1)} %get-tuple-element.29.keys, f32[16,4096]{1,0:T(8,128)S(1)} %copy-done.1, bf16[2,2,16,4096]{3,2,1,0:T(8,128)(2,1)S(1)} %copy-done, f32[32,128]{1,0:T(8,128)S(1)} %constant_dynamic-update-slice_fusion.message, ...), custom_call_target="tpu_custom_call" | custom-call | tf_op jit(solution)/shard_map/forecast_second/pallas_call | solution.py:28
  21.8 0.3 collective-permute-start.10
  22.1 1.0 %assess_first.1 = (bf16[16,640]{1,0:T(8,128)(2,1)S(1)}, bf16[16,640]{1,0:T(8,128)(2,1)S(1)}, bf16[16,640]{1,0:T(8,128)(2,1)S(1)}, bf16[16,640]{1,0:T(8,128)(2,1)...) custom-call(bf16[32,4096]{1,0:T(8,128)(2,1)S(1)} %forecast_first.1.own, ...), custom_call_target="tpu_custom_call" | custom-call | tf_op jit(solution)/shard_map/assess_first/pallas_call | solution.py:28
  23.1 0.4 collective-permute-done.10.other
  23.4 0.8 %send_second.1 = (bf16[16,5376]{1,0:T(8,128)(2,1)S(1)}, bf16[16,5376]{1,0:T(8,128)(2,1)S(1)}, bf16[16,5376]{1,0:T(8,128)(2,1)S(1)}, bf16[16,5376]{1,0:T(8,128)(2,1)S(1)}) custom-call(bf16[32,4096]{1,0:T(8,128)(2,1)S(1)} %get-tuple-element.41.second.own, bf16[32,4096]{1,0:T(8,128)(2,1)S(1)} %collective-permute-done.10.other, ...), custom_call_target="tpu_custom_call" | custom-call | tf_op jit(solution)/shard_map/send_second/pallas_call | solution.py:28
  24.2 1.5 %collective-permute-start.11 = (bf16[16,5376]{1,0:T(8,128)(2,1)S(1)}, bf16[16,5376]{1,0:T(8,128)(2,1)S(1)}, u32[]{:S(2)}, u32[]{:S(2)}) collective-permute-start(bf16[16,5376]{1,0:T(8,128)(2,1)S(1)} %get-tuple-element.53), channel_id=1, source_target_pairs={{0,24},{4,28},{8,16},{12,20},{16,8},{20,12},{24,0},{28,4},{1,25},{... | collective-permute-start | bytes 516104 | tf_op jit(solution)/shard_map/ppermute | solution.py:480
  25.8 0.5 %collective-permute-start.12 = (bf16[16,5376]{1,0:T(8,128)(2,1)S(1)}, bf16[16,5376]{1,0:T(8,128)(2,1)S(1)}, u32[]{:S(2)}, u32[]{:S(2)}) collective-permute-start(bf16[16,5376]{1,0:T(8,128)(2,1)S(1)} %get-tuple-element.54), channel_id=1, source_target_pairs={{0,16},{4,20},{8,24},{12,28},{16,0},{20,4},{24,8},{28,12},{1,17},{... | collective-permute-start | bytes 516104 | tf_op jit(solution)/shard_map/ppermute | solution.py:480
  26.3 1.5 %collective-permute-start.13 = (bf16[16,5376]{1,0:T(8,128)(2,1)S(1)}, bf16[16,5376]{1,0:T(8,128)(2,1)S(1)}, u32[]{:S(2)}, u32[]{:S(2)}) collective-permute-start(bf16[16,5376]{1,0:T(8,128)(2,1)S(1)} %get-tuple-element.55), channel_id=1, source_target_pairs={{0,8},{4,12},{8,0},{12,4},{16,24},{20,28},{24,16},{28,20},{1,9},{5... | collective-permute-start | bytes 516104 | tf_op jit(solution)/shard_map/ppermute | solution.py:480
  27.8 4.7 %collective-permute-done.11.refs_1_ = bf16[16,5376]{1,0:T(8,128)(2,1)S(1)} collective-permute-done((bf16[16,5376]{1,0:T(8,128)(2,1)S(1)}, bf16[16,5376]{1,0:T(8,128)(2,1)S(1)}, u32[]{:S(2)}, u32[]{:S(2)}) %collective-permute-start.11) | collective-permute-done | bytes 172064 | tf_op jit(solution)/shard_map/ppermute | solution.py:480
  32.5 2.9 %collective-permute-done.12.refs_2_ = bf16[16,5376]{1,0:T(8,128)(2,1)S(1)} collective-permute-done((bf16[16,5376]{1,0:T(8,128)(2,1)S(1)}, bf16[16,5376]{1,0:T(8,128)(2,1)S(1)}, u32[]{:S(2)}, u32[]{:S(2)}) %collective-permute-start.12) | collective-permute-done | bytes 172064 | tf_op jit(solution)/shard_map/ppermute | solution.py:480
  35.4 0.1 collective-permute-done.13.refs_3_
  35.5 0.9 %finish.1 = (bf16[2,16,4096]{2,1,0:T(8,128)(2,1)}, f32[2,16,512]{2,1,0:T(8,128)}) custom-call(s32[2,32,128]{2,1,0:T(8,128)S(1)} %get-tuple-element.29.keys, bf16[16,5376]{1,0:T(8,128)(2,1)S(1)} %get-tuple-element.52.refs_0_, bf16[16,5376]{1,0:T(8,128)(2,1)S(1)} %collective-permute-done.11.refs_1_, bf16[16,5376]{1,0:T(8,128)(2,1)S(1)} %collective-permute-done.12.refs_2_, ...), custom_call_target="tpu_custom_call" | custom-call | tf_op jit(solution)/shard_map/finish/pallas_call | solution.py:28
  (8 shorter events, 0.0 us)
Async XLA Ops:
  0.6 1.2 %copy-start = (bf16[2,2,16,4096]{3,2,1,0:T(8,128)(2,1)S(1)}, bf16[2,2,16,4096]{3,2,1,0:T(8,128)(2,1)}, u32[]{:S(2)}) copy-start(bf16[2,2,16,4096]{3,2,1,0:T(8,128)(2,1)} %pert.3) | copy-start | bytes 1572868
  0.6 1.2 %copy-start.1 = (f32[16,4096]{1,0:T(8,128)S(1)}, f32[16,4096]{1,0:T(8,128)}, u32[]{:S(2)}) copy-start(f32[16,4096]{1,0:T(8,128)} %diff.3) | copy-start | bytes 786436
  0.7 1.3 %copy-start.2 = (bf16[2,16,4096]{2,1,0:T(8,128)(2,1)S(1)}, bf16[2,16,4096]{2,1,0:T(8,128)(2,1)}, u32[]{:S(2)}) copy-start(bf16[2,16,4096]{2,1,0:T(8,128)(2,1)} %state.1) | copy-start | bytes 786436
  2.6 8.1 %collective-permute-start = (bf16[32,4096]{1,0:T(8,128)(2,1)S(1)}, bf16[32,4096]{1,0:T(8,128)(2,1)S(1)}, u32[]{:S(2)}, u32[]{:S(2)}) collective-permute-start(bf16[32,4096]{1,0:T(8,128)(2,1)S(1)} %forecast_first.1.own), channel_id=1, source_target_pairs={{0,4},{4,0},{8,12},{12,8},{16,20},{20,16},{24,28},{28,24},{1,5},{5... | collective-permute-start | bytes 786440 | tf_op jit(solution)/shard_map/ppermute | solution.py:475
  3.1 5.0 %collective-permute-start.1 = (f32[1,128]{1,0:T(1,128)S(1)}, f32[1,128]{1,0:T(1,128)S(1)}, u32[]{:S(2)}, u32[]{:S(2)}) collective-permute-start(f32[1,128]{1,0:T(1,128)S(1)} %get-tuple-element.32), channel_id=1, source_target_pairs={{0,24},{4,28},{8,16},{12,20},{16,8},{20,12},{24,0},{28,4},{1,25},{... | collective-permute-start | bytes 1544 | tf_op jit(solution)/shard_map/ppermute | solution.py:480
  6.6 3.5 %collective-permute-start.2 = (f32[1,128]{1,0:T(1,128)S(1)}, f32[1,128]{1,0:T(1,128)S(1)}, u32[]{:S(2)}, u32[]{:S(2)}) collective-permute-start(f32[1,128]{1,0:T(1,128)S(1)} %get-tuple-element.33), channel_id=1, source_target_pairs={{0,16},{4,20},{8,24},{12,28},{16,0},{20,4},{24,8},{28,12},{1,17},{... | collective-permute-start | bytes 1544 | tf_op jit(solution)/shard_map/ppermute | solution.py:480
  7.1 3.5 %collective-permute-start.3 = (f32[1,128]{1,0:T(1,128)S(1)}, f32[1,128]{1,0:T(1,128)S(1)}, u32[]{:S(2)}, u32[]{:S(2)}) collective-permute-start(f32[1,128]{1,0:T(1,128)S(1)} %get-tuple-element.34), channel_id=1, source_target_pairs={{0,8},{4,12},{8,0},{12,4},{16,24},{20,28},{24,16},{28,20},{1,9},{5... | collective-permute-start | bytes 1544 | tf_op jit(solution)/shard_map/ppermute | solution.py:480
  10.6 9.1 %copy-start.5 = (f32[32,16]{0,1:T(8,128)S(1)}, f32[32,16]{0,1:T(8,128)}, u32[]{:S(2)}) copy-start(f32[32,16]{0,1:T(8,128)} %param.15) | copy-start | bytes 6148
  11.0 8.7 %copy-start.6 = (s32[16,6]{0,1:T(8,128)S(1)}, s32[16,6]{0,1:T(8,128)}, u32[]{:S(2)}) copy-start(s32[16,6]{0,1:T(8,128)} %param.18) | copy-start | bytes 1156
  11.0 8.7 %copy-start.7 = (f32[16,6]{0,1:T(8,128)S(1)}, f32[16,6]{0,1:T(8,128)}, u32[]{:S(2)}) copy-start(f32[16,6]{0,1:T(8,128)} %param.19) | copy-start | bytes 1156
  11.0 3.7 %collective-permute-start.4 = (f32[16,128]{1,0:T(8,128)S(1)}, f32[16,128]{1,0:T(8,128)S(1)}, u32[]{:S(2)}, u32[]{:S(2)}) collective-permute-start(f32[16,128]{1,0:T(8,128)S(1)} %get-tuple-element.35), channel_id=1, source_target_pairs={{0,4},{4,0},{8,12},{12,8},{16,20},{20,16},{24,28},{28,24},{1,5},{5... | collective-permute-start | bytes 24584 | tf_op jit(solution)/shard_map/ppermute | solution.py:475
  11.1 8.6 %copy-start.3 = (f32[2,32,16]{1,2,0:T(8,128)S(1)}, f32[2,32,16]{1,2,0:T(8,128)}, u32[]{:S(2)}) copy-start(f32[2,32,16]{1,2,0:T(8,128)} %param.14) | copy-start | bytes 12292
  11.1 9.8 %collective-permute-start.7 = (bf16[16,4096]{1,0:T(8,128)(2,1)S(1)}, bf16[16,4096]{1,0:T(8,128)(2,1)S(1)}, u32[]{:S(2)}, u32[]{:S(2)}) collective-permute-start(bf16[16,4096]{1,0:T(8,128)(2,1)S(1)} %get-tuple-element.38), channel_id=1, source_target_pairs={{0,24},{4,28},{8,16},{12,20},{16,8},{20,12},{24,0},{28,4},{1,25},{... | collective-permute-start | bytes 393224 | tf_op jit(solution)/shard_map/ppermute | solution.py:480
  12.7 8.2 %collective-permute-start.8 = (bf16[16,4096]{1,0:T(8,128)(2,1)S(1)}, bf16[16,4096]{1,0:T(8,128)(2,1)S(1)}, u32[]{:S(2)}, u32[]{:S(2)}) collective-permute-start(bf16[16,4096]{1,0:T(8,128)(2,1)S(1)} %get-tuple-element.39), channel_id=1, source_target_pairs={{0,16},{4,20},{8,24},{12,28},{16,0},{20,4},{24,8},{28,12},{1,17},{... | collective-permute-start | bytes 393224 | tf_op jit(solution)/shard_map/ppermute | solution.py:480
  12.8 8.1 %collective-permute-start.9 = (bf16[16,4096]{1,0:T(8,128)(2,1)S(1)}, bf16[16,4096]{1,0:T(8,128)(2,1)S(1)}, u32[]{:S(2)}, u32[]{:S(2)}) collective-permute-start(bf16[16,4096]{1,0:T(8,128)(2,1)S(1)} %get-tuple-element.40), channel_id=1, source_target_pairs={{0,8},{4,12},{8,0},{12,4},{16,24},{20,28},{24,16},{28,20},{1,9},{5... | collective-permute-start | bytes 393224 | tf_op jit(solution)/shard_map/ppermute | solution.py:480
  14.7 5.1 %copy-start.4 = (s32[32,16]{0,1:T(8,128)S(1)}, s32[32,16]{0,1:T(8,128)}, u32[]{:S(2)}) copy-start(s32[32,16]{0,1:T(8,128)} %param.17) | copy-start | bytes 6148
  14.7 5.0 %collective-permute-start.5 = (f32[32,128]{1,0:T(8,128)S(1)}, f32[32,128]{1,0:T(8,128)S(1)}, u32[]{:S(2)}, u32[]{:S(2)}) collective-permute-start(f32[32,128]{1,0:T(8,128)S(1)} %constant_dynamic-update-slice_fusion.message), channel_id=1, source_target_pairs={{0,1},{1,2},{2,3},{5,4},{6,5},{7,6},{8,9},{9,10},{10,11},{13,12},{... | collective-permute-start | bytes 49160 | tf_op jit(solution)/shard_map/ppermute | solution.py:515
  19.7 1.2 %collective-permute-start.6 = (f32[32,128]{1,0:T(8,128)S(1)}, f32[32,128]{1,0:T(8,128)S(1)}, u32[]{:S(2)}, u32[]{:S(2)}) collective-permute-start(f32[32,128]{1,0:T(8,128)S(1)} %collective-permute-done.5.mine), channel_id=1, source_target_pairs={{0,4},{4,0},{8,12},{12,8},{16,20},{20,16},{24,28},{28,24},{1,5},{5... | collective-permute-start | bytes 49160 | tf_op jit(solution)/shard_map/ppermute | solution.py:475
  19.7 0.7 %copy-start.8 = (s32[32]{0:T(128)S(1)}, s32[32]{0:T(128)}, u32[]{:S(2)}) copy-start(s32[32]{0:T(128)} %param.16) | copy-start | bytes 388
  21.8 1.6 %collective-permute-start.10 = (bf16[32,4096]{1,0:T(8,128)(2,1)S(1)}, bf16[32,4096]{1,0:T(8,128)(2,1)S(1)}, u32[]{:S(2)}, u32[]{:S(2)}) collective-permute-start(bf16[32,4096]{1,0:T(8,128)(2,1)S(1)} %get-tuple-element.41.second.own), channel_id=1, source_target_pairs={{0,4},{4,0},{8,12},{12,8},{16,20},{20,16},{24,28},{28,24},{1,5},{5... | collective-permute-start | bytes 786440 | tf_op jit(solution)/shard_map/ppermute | solution.py:475
  24.2 8.2 %collective-permute-start.11 = (bf16[16,5376]{1,0:T(8,128)(2,1)S(1)}, bf16[16,5376]{1,0:T(8,128)(2,1)S(1)}, u32[]{:S(2)}, u32[]{:S(2)}) collective-permute-start(bf16[16,5376]{1,0:T(8,128)(2,1)S(1)} %get-tuple-element.53), channel_id=1, source_target_pairs={{0,24},{4,28},{8,16},{12,20},{16,8},{20,12},{24,0},{28,4},{1,25},{... | collective-permute-start | bytes 516104 | tf_op jit(solution)/shard_map/ppermute | solution.py:480
  25.8 9.6 %collective-permute-start.12 = (bf16[16,5376]{1,0:T(8,128)(2,1)S(1)}, bf16[16,5376]{1,0:T(8,128)(2,1)S(1)}, u32[]{:S(2)}, u32[]{:S(2)}) collective-permute-start(bf16[16,5376]{1,0:T(8,128)(2,1)S(1)} %get-tuple-element.54), channel_id=1, source_target_pairs={{0,16},{4,20},{8,24},{12,28},{16,0},{20,4},{24,8},{28,12},{1,17},{... | collective-permute-start | bytes 516104 | tf_op jit(solution)/shard_map/ppermute | solution.py:480
  26.3 9.1 %collective-permute-start.13 = (bf16[16,5376]{1,0:T(8,128)(2,1)S(1)}, bf16[16,5376]{1,0:T(8,128)(2,1)S(1)}, u32[]{:S(2)}, u32[]{:S(2)}) collective-permute-start(bf16[16,5376]{1,0:T(8,128)(2,1)S(1)} %get-tuple-element.55), channel_id=1, source_target_pairs={{0,8},{4,12},{8,0},{12,4},{16,24},{20,28},{24,16},{28,20},{1,9},{5... | collective-permute-start | bytes 516104 | tf_op jit(solution)/shard_map/ppermute | solution.py:480

commit v16 on v14

--- a/solution.py
+++ b/solution.py
@@ -246,14 +246,14 @@
     return pltpu.roll(ref[...], ref.shape[1] - member * share, 1)[:, :share]
 
 
-def pack_mean(outs, at, least, total, sums, share):
+def pack_mean(outs, at, least, total, sums, share, cycle=0, before=None):
     rows = outs[0].shape[0]
     tiles = sums.shape[0]
     groups = tiles // rows
     m = here()
     lane = iota((rows, LANES), 1)
-    misc = jnp.zeros((rows, LANES), F32)
-    spot = 0
+    misc = jnp.zeros((rows, LANES), F32) if before is None else before
+    spot = 6 * groups * cycle
     for x in (least, total):
         for piece in pieces(x):
             for g in range(groups):
@@ -267,10 +267,9 @@
         out[:, end:end + LANES] = misc.astype(BF16)
 
 
-def unpack_mean(got, at, tiles, share):
+def unpack_mean(got, at, end, cycle, tiles, share):
     rows = got[0].shape[0]
     groups = tiles // rows
-    end = at + groups * share
     misc = [x[:, end:end + LANES].astype(F32) for x in got]
     means = []
     for g in range(groups):
@@ -278,7 +277,7 @@
         for x in misc:
             pair = []
             for kind in range(2):
-                spot = [(kind * 3 + piece) * groups + g for piece in range(3)]
+                spot = [((2 * cycle + kind) * 3 + piece) * groups + g for piece in range(3)]
                 high, middle, low = [x[:, i:i + 1] for i in spot]
                 pair.append(high + middle + low)
             stats.append(pair)
@@ -385,10 +384,10 @@
         outs = [outs[falling(pairs).index(k)] for k in range(pairs)]
         prior = jnp.concatenate([own[...], other[...]], axis=0)
         sent = requested([x[...] for x in notes], prior, 1, rows)
-        extra = kept[0].shape[1]
+        extra = kept[0].shape[1] - LANES
         for k in range(pairs):
             outs[k][:, :cells] = sent[k * rows:(k + 1) * rows, :].astype(BF16)
-            outs[k][:, cells:cells + extra] = kept[k][...]
+            outs[k][:, cells:cells + extra] = kept[k][:, :extra]
         least, total, weighted = assess(
             [other[p * tiles:(p + 1) * tiles, :] for p in range(parts)],
             where[...], terms[0:1, :], terms[2:3, :], local[...], parts, tiles, cells,
@@ -399,7 +398,8 @@
         total = scale * total + own_scale * stats[:, 1:2]
         sums[...] = scale * weighted + own_scale * own_sums[...]
         least = lower
-        pack_mean(outs, cells + extra, least, total, sums, share)
+        before = kept[0][:, extra:].astype(F32)
+        pack_mean(outs, cells + extra, least, total, sums, share, 1, before)
 
     return kernel
 
@@ -413,9 +413,10 @@
         for p in range(parts):
             analysis[p] = picked[p * tiles:(p + 1) * tiles, :].astype(BF16)
         share = mean.shape[2]
-        extra = tiles // rows * share + LANES
+        extra = tiles // rows * share
+        end = cells + CYCLES * extra
         for c in range(CYCLES):
-            for g, x in enumerate(unpack_mean(got, cells + c * extra, tiles, share)):
+            for g, x in enumerate(unpack_mean(got, cells + c * extra, end, c, tiles, share)):
                 mean[c, g * rows:(g + 1) * rows, :] = x
 
     return kernel
@@ -535,7 +536,7 @@
     )
     sends = call(
         make_send_second(pairs, rows, parts, tiles, cells, share),
-        [((rows, cells + CYCLES * extra), BF16)] * pairs,
+        [((rows, cells + CYCLES * (extra - LANES) + LANES), BF16)] * pairs,
         [second, trade(second), where, terms, local, stats, own_sums, *notes, *kept],
         scratch=sums,
         name="send_second",

time: 36.8 us -> 36.6 us (level)
  no operation moved by 1% of the time
where the time goes in v16:
time: 36.6 us; the launch traced here: 36.4 us
  starting transfers between devices  15.7 us (43%)
  waiting for transfers between devices  13.2 us (36%)
  Pallas kernels  5.98 us (16%)
  between operations  0.81 us (2%)
  local copies, waits for them, and re-layouts  0.69 us (2%)
    ppermute x9, starting transfers between devices, exchange(): lax.ppermute(x, 'member', [(i, i ^ 2 * k) for i in range(members)])  11.2 us
    ppermute x9, waiting for transfers between devices, exchange(): lax.ppermute(x, 'member', [(i, i ^ 2 * k) for i in range(members)])  11.1 us
    pallas_call x8, Pallas kernels, call(): pl.pallas_call(kernel, out_shape=[jax.ShapeDtypeStruct(s, d) for s, d in...  5.98 us
    ppermute x1, starting transfers between devices, body(): mine = lax.ppermute(message, ('member', 'region'), steps)  3.6 us
    ppermute x1, waiting for transfers between devices, body(): mine = lax.ppermute(message, ('member', 'region'), steps)  1.43 us
    ppermute x4, starting transfers between devices, trade(): return lax.ppermute(x, 'member', [(i, i ^ 1) for i in range(members)])  0.86 us
  transfers between devices with their start and end apart: 14, of which 7 were waited for; matrix products, arithmetic and copies ran while one was open for 0% of the time, Pallas kernels for 3%

profile of v16, /device:TPU:0, one launch (start us, length us, event | category | flops | bytes accessed | tf_op | source)
XLA Modules:
  0.0 36.4 jit_solution(14047738281533581861)
XLA Ops:
  0.6 0.0 copy-start
  0.6 0.0 copy-start.1
  0.7 0.0 copy-start.2
  0.7 1.2 %prepare.1 = (f32[1,128]{1,0:T(1,128)S(1)}, f32[1,128]{1,0:T(1,128)S(1)}, f32[1,128]{1,0:T(1,128)S(1)}, f32[1,128]{1,0:T(1,128)S(1)}, f32[8,128]{1,0:T(8,128)S(1)}, /*index=5*/s32[2,32,128]{2,1,0:T(8,128)S(1)}) custom-call(bf16[2,16,4096]{2,1,0:T(8,128)(2,1)} %state.1, bf16[2,16,4096]{2,1,0:T(8,128)(2,1)} %state.1, f32[16,4096]{1,0:T(8,128)} %diff.3, ...), custom_call_target="tpu_custom_call" | custom-call | tf_op jit(solution)/shard_map/prepare/pallas_call | solution.py:28
  1.9 0.0 copy-done
  1.9 0.0 copy-done.1
  1.9 0.0 copy-done.2
  1.9 0.6 %forecast_first.1.own = bf16[32,4096]{1,0:T(8,128)(2,1)S(1)} custom-call(bf16[2,16,4096]{2,1,0:T(8,128)(2,1)S(1)} %copy-done.2, f32[16,4096]{1,0:T(8,128)S(1)} %copy-done.1, bf16[2,2,16,4096]{3,2,1,0:T(8,128)(2,1)S(1)} %copy-done, f32[8,128]{1,0:T(8,128)S(1)} %get-tuple-element.30.after.trail), custom_call_target="tpu_custom_call" | custom-call | tf_op jit(solution)/shard_map/forecast_first/pallas_call | solution.py:28
  2.6 0.5 %collective-permute-start = (bf16[32,4096]{1,0:T(8,128)(2,1)S(1)}, bf16[32,4096]{1,0:T(8,128)(2,1)S(1)}, u32[]{:S(2)}, u32[]{:S(2)}) collective-permute-start(bf16[32,4096]{1,0:T(8,128)(2,1)S(1)} %forecast_first.1.own), channel_id=1, source_target_pairs={{0,4},{4,0},{8,12},{12,8},{16,20},{20,16},{24,28},{28,24},{1,5},{5... | collective-permute-start | bytes 786440 | tf_op jit(solution)/shard_map/ppermute | solution.py:476
  3.1 2.6 %collective-permute-start.1 = (f32[1,128]{1,0:T(1,128)S(1)}, f32[1,128]{1,0:T(1,128)S(1)}, u32[]{:S(2)}, u32[]{:S(2)}) collective-permute-start(f32[1,128]{1,0:T(1,128)S(1)} %get-tuple-element.32), channel_id=1, source_target_pairs={{0,8},{4,12},{8,0},{12,4},{16,24},{20,28},{24,16},{28,20},{1,9},{5... | collective-permute-start | bytes 1544 | tf_op jit(solution)/shard_map/ppermute | solution.py:481
  5.6 1.5 %collective-permute-start.2 = (f32[1,128]{1,0:T(1,128)S(1)}, f32[1,128]{1,0:T(1,128)S(1)}, u32[]{:S(2)}, u32[]{:S(2)}) collective-permute-start(f32[1,128]{1,0:T(1,128)S(1)} %get-tuple-element.33), channel_id=1, source_target_pairs={{0,16},{4,20},{8,24},{12,28},{16,0},{20,4},{24,8},{28,12},{1,17},{... | collective-permute-start | bytes 1544 | tf_op jit(solution)/shard_map/ppermute | solution.py:481
  7.2 0.0 collective-permute-start.3
  7.2 0.0 collective-permute-done.1.refs_1_
  7.2 2.0 %collective-permute-done.2.refs_2_ = f32[1,128]{1,0:T(1,128)S(1)} collective-permute-done((f32[1,128]{1,0:T(1,128)S(1)}, f32[1,128]{1,0:T(1,128)S(1)}, u32[]{:S(2)}, u32[]{:S(2)}) %collective-permute-start.2) | collective-permute-done | bytes 544 | tf_op jit(solution)/shard_map/ppermute | solution.py:481
  9.2 2.4 %collective-permute-done.3.refs_3_ = f32[1,128]{1,0:T(1,128)S(1)} collective-permute-done((f32[1,128]{1,0:T(1,128)S(1)}, f32[1,128]{1,0:T(1,128)S(1)}, u32[]{:S(2)}, u32[]{:S(2)}) %collective-permute-start.3) | collective-permute-done | bytes 544 | tf_op jit(solution)/shard_map/ppermute | solution.py:481
  11.6 0.0 collective-permute-done.other
  11.6 0.4 send_first.1
  12.0 0.0 copy-start.6
  12.0 0.0 copy-start.7
  12.0 0.1 collective-permute-start.4
  12.1 0.0 copy-start.3
  12.1 0.1 collective-permute-start.7
  12.2 2.0 %collective-permute-start.8 = (bf16[16,4096]{1,0:T(8,128)(2,1)S(1)}, bf16[16,4096]{1,0:T(8,128)(2,1)S(1)}, u32[]{:S(2)}, u32[]{:S(2)}) collective-permute-start(bf16[16,4096]{1,0:T(8,128)(2,1)S(1)} %get-tuple-element.39), channel_id=1, source_target_pairs={{0,16},{4,20},{8,24},{12,28},{16,0},{20,4},{24,8},{28,12},{1,17},{... | collective-permute-start | bytes 393224 | tf_op jit(solution)/shard_map/ppermute | solution.py:481
  14.2 1.5 %collective-permute-start.9 = (bf16[16,4096]{1,0:T(8,128)(2,1)S(1)}, bf16[16,4096]{1,0:T(8,128)(2,1)S(1)}, u32[]{:S(2)}, u32[]{:S(2)}) collective-permute-start(bf16[16,4096]{1,0:T(8,128)(2,1)S(1)} %get-tuple-element.40), channel_id=1, source_target_pairs={{0,8},{4,12},{8,0},{12,4},{16,24},{20,28},{24,16},{28,20},{1,9},{5... | collective-permute-start | bytes 393224 | tf_op jit(solution)/shard_map/ppermute | solution.py:481
  15.7 0.0 collective-permute-done.4
  15.7 3.6 %collective-permute-start.5 = (f32[32,128]{1,0:T(8,128)S(1)}, f32[32,128]{1,0:T(8,128)S(1)}, u32[]{:S(2)}, u32[]{:S(2)}) collective-permute-start(f32[32,128]{1,0:T(8,128)S(1)} %constant_dynamic-update-slice_fusion.message), channel_id=1, source_target_pairs={{0,1},{1,2},{2,3},{5,4},{6,5},{7,6},{8,9},{9,10},{10,11},{13,12},{... | collective-permute-start | bytes 49160 | tf_op jit(solution)/shard_map/ppermute | solution.py:516
  19.3 1.4 %collective-permute-done.5.mine = f32[32,128]{1,0:T(8,128)S(1)} collective-permute-done((f32[32,128]{1,0:T(8,128)S(1)}, f32[32,128]{1,0:T(8,128)S(1)}, u32[]{:S(2)}, u32[]{:S(2)}) %collective-permute-start.5) | collective-permute-done | bytes 16416 | tf_op jit(solution)/shard_map/ppermute | solution.py:516
  20.7 0.0 collective-permute-start.6
  20.7 0.0 copy-done.6
  20.7 0.0 copy-done.7
  20.7 0.6 %copy-done.8 = s32[32]{0:T(128)S(1)} copy-done((s32[32]{0:T(128)S(1)}, s32[32]{0:T(128)}, u32[]{:S(2)}) %copy-start.8) | copy-done | bytes 152
  21.4 0.2 observe.1
  21.5 0.3 collective-permute-done.6.theirs
  21.9 0.0 collective-permute-done.7.refs_1_
  21.9 0.0 collective-permute-done.8.refs_2_
  21.9 0.0 collective-permute-done.9.refs_3_
  21.9 0.9 %forecast_second.1 = (bf16[32,4096]{1,0:T(8,128)(2,1)S(1)}, f32[32,256]{1,0:T(8,128)S(1)}, f32[32,256]{1,0:T(8,128)S(1)}) custom-call(s32[2,32,128]{2,1,0:T(8,128)S(1)} %get-tuple-element.29.keys, f32[16,4096]{1,0:T(8,128)S(1)} %copy-done.1, bf16[2,2,16,4096]{3,2,1,0:T(8,128)(2,1)S(1)} %copy-done, f32[32,128]{1,0:T(8,128)S(1)} %constant_dynamic-update-slice_fusion.message, ...), custom_call_target="tpu_custom_call" | custom-call | tf_op jit(solution)/shard_map/forecast_second/pallas_call | solution.py:28
  22.8 0.3 collective-permute-start.10
  23.1 1.0 %assess_first.1 = (bf16[16,640]{1,0:T(8,128)(2,1)S(1)}, bf16[16,640]{1,0:T(8,128)(2,1)S(1)}, bf16[16,640]{1,0:T(8,128)(2,1)S(1)}, bf16[16,640]{1,0:T(8,128)(2,1)...) custom-call(bf16[32,4096]{1,0:T(8,128)(2,1)S(1)} %forecast_first.1.own, ...), custom_call_target="tpu_custom_call" | custom-call | tf_op jit(solution)/shard_map/assess_first/pallas_call | solution.py:28
  24.0 0.4 collective-permute-done.10.other
  24.4 0.8 %send_second.1 = (bf16[16,5248]{1,0:T(8,128)(2,1)S(1)}, bf16[16,5248]{1,0:T(8,128)(2,1)S(1)}, bf16[16,5248]{1,0:T(8,128)(2,1)S(1)}, bf16[16,5248]{1,0:T(8,128)(2,1)S(1)}) custom-call(bf16[32,4096]{1,0:T(8,128)(2,1)S(1)} %get-tuple-element.41.second.own, bf16[32,4096]{1,0:T(8,128)(2,1)S(1)} %collective-permute-done.10.other, ...), custom_call_target="tpu_custom_call" | custom-call | tf_op jit(solution)/shard_map/send_second/pallas_call | solution.py:28
  25.2 0.5 %collective-permute-start.11 = (bf16[16,5248]{1,0:T(8,128)(2,1)S(1)}, bf16[16,5248]{1,0:T(8,128)(2,1)S(1)}, u32[]{:S(2)}, u32[]{:S(2)}) collective-permute-start(bf16[16,5248]{1,0:T(8,128)(2,1)S(1)} %get-tuple-element.53), channel_id=1, source_target_pairs={{0,24},{4,28},{8,16},{12,20},{16,8},{20,12},{24,0},{28,4},{1,25},{... | collective-permute-start | bytes 503816 | tf_op jit(solution)/shard_map/ppermute | solution.py:481
  25.7 1.5 %collective-permute-start.12 = (bf16[16,5248]{1,0:T(8,128)(2,1)S(1)}, bf16[16,5248]{1,0:T(8,128)(2,1)S(1)}, u32[]{:S(2)}, u32[]{:S(2)}) collective-permute-start(bf16[16,5248]{1,0:T(8,128)(2,1)S(1)} %get-tuple-element.54), channel_id=1, source_target_pairs={{0,16},{4,20},{8,24},{12,28},{16,0},{20,4},{24,8},{28,12},{1,17},{... | collective-permute-start | bytes 503816 | tf_op jit(solution)/shard_map/ppermute | solution.py:481
  27.2 1.5 %collective-permute-start.13 = (bf16[16,5248]{1,0:T(8,128)(2,1)S(1)}, bf16[16,5248]{1,0:T(8,128)(2,1)S(1)}, u32[]{:S(2)}, u32[]{:S(2)}) collective-permute-start(bf16[16,5248]{1,0:T(8,128)(2,1)S(1)} %get-tuple-element.55), channel_id=1, source_target_pairs={{0,8},{4,12},{8,0},{12,4},{16,24},{20,28},{24,16},{28,20},{1,9},{5... | collective-permute-start | bytes 503816 | tf_op jit(solution)/shard_map/ppermute | solution.py:481
  28.8 4.6 %collective-permute-done.11.refs_1_ = bf16[16,5248]{1,0:T(8,128)(2,1)S(1)} collective-permute-done((bf16[16,5248]{1,0:T(8,128)(2,1)S(1)}, bf16[16,5248]{1,0:T(8,128)(2,1)S(1)}, u32[]{:S(2)}, u32[]{:S(2)}) %collective-permute-start.11) | collective-permute-done | bytes 167968 | tf_op jit(solution)/shard_map/ppermute | solution.py:481
  33.3 2.1 %collective-permute-done.12.refs_2_ = bf16[16,5248]{1,0:T(8,128)(2,1)S(1)} collective-permute-done((bf16[16,5248]{1,0:T(8,128)(2,1)S(1)}, bf16[16,5248]{1,0:T(8,128)(2,1)S(1)}, u32[]{:S(2)}, u32[]{:S(2)}) %collective-permute-start.12) | collective-permute-done | bytes 167968 | tf_op jit(solution)/shard_map/ppermute | solution.py:481
  35.4 0.0 collective-permute-done.13.refs_3_
  35.4 0.9 %finish.1 = (bf16[2,16,4096]{2,1,0:T(8,128)(2,1)}, f32[2,16,512]{2,1,0:T(8,128)}) custom-call(s32[2,32,128]{2,1,0:T(8,128)S(1)} %get-tuple-element.29.keys, bf16[16,5248]{1,0:T(8,128)(2,1)S(1)} %get-tuple-element.52.refs_0_, bf16[16,5248]{1,0:T(8,128)(2,1)S(1)} %collective-permute-done.11.refs_1_, bf16[16,5248]{1,0:T(8,128)(2,1)S(1)} %collective-permute-done.12.refs_2_, ...), custom_call_target="tpu_custom_call" | custom-call | tf_op jit(solution)/shard_map/finish/pallas_call | solution.py:28
  (8 shorter events, 0.0 us)
Async XLA Ops:
  0.6 1.2 %copy-start = (bf16[2,2,16,4096]{3,2,1,0:T(8,128)(2,1)S(1)}, bf16[2,2,16,4096]{3,2,1,0:T(8,128)(2,1)}, u32[]{:S(2)}) copy-start(bf16[2,2,16,4096]{3,2,1,0:T(8,128)(2,1)} %pert.3) | copy-start | bytes 1572868
  0.6 1.2 %copy-start.1 = (f32[16,4096]{1,0:T(8,128)S(1)}, f32[16,4096]{1,0:T(8,128)}, u32[]{:S(2)}) copy-start(f32[16,4096]{1,0:T(8,128)} %diff.3) | copy-start | bytes 786436
  0.7 1.3 %copy-start.2 = (bf16[2,16,4096]{2,1,0:T(8,128)(2,1)S(1)}, bf16[2,16,4096]{2,1,0:T(8,128)(2,1)}, u32[]{:S(2)}) copy-start(bf16[2,16,4096]{2,1,0:T(8,128)(2,1)} %state.1) | copy-start | bytes 786436
  2.6 9.0 %collective-permute-start = (bf16[32,4096]{1,0:T(8,128)(2,1)S(1)}, bf16[32,4096]{1,0:T(8,128)(2,1)S(1)}, u32[]{:S(2)}, u32[]{:S(2)}) collective-permute-start(bf16[32,4096]{1,0:T(8,128)(2,1)S(1)} %forecast_first.1.own), channel_id=1, source_target_pairs={{0,4},{4,0},{8,12},{12,8},{16,20},{20,16},{24,28},{28,24},{1,5},{5... | collective-permute-start | bytes 786440 | tf_op jit(solution)/shard_map/ppermute | solution.py:476
  3.1 4.1 %collective-permute-start.1 = (f32[1,128]{1,0:T(1,128)S(1)}, f32[1,128]{1,0:T(1,128)S(1)}, u32[]{:S(2)}, u32[]{:S(2)}) collective-permute-start(f32[1,128]{1,0:T(1,128)S(1)} %get-tuple-element.32), channel_id=1, source_target_pairs={{0,8},{4,12},{8,0},{12,4},{16,24},{20,28},{24,16},{28,20},{1,9},{5... | collective-permute-start | bytes 1544 | tf_op jit(solution)/shard_map/ppermute | solution.py:481
  5.6 3.5 %collective-permute-start.2 = (f32[1,128]{1,0:T(1,128)S(1)}, f32[1,128]{1,0:T(1,128)S(1)}, u32[]{:S(2)}, u32[]{:S(2)}) collective-permute-start(f32[1,128]{1,0:T(1,128)S(1)} %get-tuple-element.33), channel_id=1, source_target_pairs={{0,16},{4,20},{8,24},{12,28},{16,0},{20,4},{24,8},{28,12},{1,17},{... | collective-permute-start | bytes 1544 | tf_op jit(solution)/shard_map/ppermute | solution.py:481
  7.2 4.4 %collective-permute-start.3 = (f32[1,128]{1,0:T(1,128)S(1)}, f32[1,128]{1,0:T(1,128)S(1)}, u32[]{:S(2)}, u32[]{:S(2)}) collective-permute-start(f32[1,128]{1,0:T(1,128)S(1)} %get-tuple-element.34), channel_id=1, source_target_pairs={{0,24},{4,28},{8,16},{12,20},{16,8},{20,12},{24,0},{28,4},{1,25},{... | collective-permute-start | bytes 1544 | tf_op jit(solution)/shard_map/ppermute | solution.py:481
  11.6 9.1 %copy-start.5 = (f32[32,16]{0,1:T(8,128)S(1)}, f32[32,16]{0,1:T(8,128)}, u32[]{:S(2)}) copy-start(f32[32,16]{0,1:T(8,128)} %param.15) | copy-start | bytes 6148
  12.0 8.7 %copy-start.6 = (s32[16,6]{0,1:T(8,128)S(1)}, s32[16,6]{0,1:T(8,128)}, u32[]{:S(2)}) copy-start(s32[16,6]{0,1:T(8,128)} %param.18) | copy-start | bytes 1156
  12.0 8.7 %copy-start.7 = (f32[16,6]{0,1:T(8,128)S(1)}, f32[16,6]{0,1:T(8,128)}, u32[]{:S(2)}) copy-start(f32[16,6]{0,1:T(8,128)} %param.19) | copy-start | bytes 1156
  12.0 3.7 %collective-permute-start.4 = (f32[16,128]{1,0:T(8,128)S(1)}, f32[16,128]{1,0:T(8,128)S(1)}, u32[]{:S(2)}, u32[]{:S(2)}) collective-permute-start(f32[16,128]{1,0:T(8,128)S(1)} %get-tuple-element.35), channel_id=1, source_target_pairs={{0,4},{4,0},{8,12},{12,8},{16,20},{20,16},{24,28},{28,24},{1,5},{5... | collective-permute-start | bytes 24584 | tf_op jit(solution)/shard_map/ppermute | solution.py:476
  12.1 8.6 %copy-start.3 = (f32[2,32,16]{1,2,0:T(8,128)S(1)}, f32[2,32,16]{1,2,0:T(8,128)}, u32[]{:S(2)}) copy-start(f32[2,32,16]{1,2,0:T(8,128)} %param.14) | copy-start | bytes 12292
  12.1 9.8 %collective-permute-start.7 = (bf16[16,4096]{1,0:T(8,128)(2,1)S(1)}, bf16[16,4096]{1,0:T(8,128)(2,1)S(1)}, u32[]{:S(2)}, u32[]{:S(2)}) collective-permute-start(bf16[16,4096]{1,0:T(8,128)(2,1)S(1)} %get-tuple-element.38), channel_id=1, source_target_pairs={{0,24},{4,28},{8,16},{12,20},{16,8},{20,12},{24,0},{28,4},{1,25},{... | collective-permute-start | bytes 393224 | tf_op jit(solution)/shard_map/ppermute | solution.py:481
  12.2 9.7 %collective-permute-start.8 = (bf16[16,4096]{1,0:T(8,128)(2,1)S(1)}, bf16[16,4096]{1,0:T(8,128)(2,1)S(1)}, u32[]{:S(2)}, u32[]{:S(2)}) collective-permute-start(bf16[16,4096]{1,0:T(8,128)(2,1)S(1)} %get-tuple-element.39), channel_id=1, source_target_pairs={{0,16},{4,20},{8,24},{12,28},{16,0},{20,4},{24,8},{28,12},{1,17},{... | collective-permute-start | bytes 393224 | tf_op jit(solution)/shard_map/ppermute | solution.py:481
  14.2 7.7 %collective-permute-start.9 = (bf16[16,4096]{1,0:T(8,128)(2,1)S(1)}, bf16[16,4096]{1,0:T(8,128)(2,1)S(1)}, u32[]{:S(2)}, u32[]{:S(2)}) collective-permute-start(bf16[16,4096]{1,0:T(8,128)(2,1)S(1)} %get-tuple-element.40), channel_id=1, source_target_pairs={{0,8},{4,12},{8,0},{12,4},{16,24},{20,28},{24,16},{28,20},{1,9},{5... | collective-permute-start | bytes 393224 | tf_op jit(solution)/shard_map/ppermute | solution.py:481
  15.7 5.1 %copy-start.4 = (s32[32,16]{0,1:T(8,128)S(1)}, s32[32,16]{0,1:T(8,128)}, u32[]{:S(2)}) copy-start(s32[32,16]{0,1:T(8,128)} %param.17) | copy-start | bytes 6148
  15.7 5.0 %collective-permute-start.5 = (f32[32,128]{1,0:T(8,128)S(1)}, f32[32,128]{1,0:T(8,128)S(1)}, u32[]{:S(2)}, u32[]{:S(2)}) collective-permute-start(f32[32,128]{1,0:T(8,128)S(1)} %constant_dynamic-update-slice_fusion.message), channel_id=1, source_target_pairs={{0,1},{1,2},{2,3},{5,4},{6,5},{7,6},{8,9},{9,10},{10,11},{13,12},{... | collective-permute-start | bytes 49160 | tf_op jit(solution)/shard_map/ppermute | solution.py:516
  20.7 1.2 %collective-permute-start.6 = (f32[32,128]{1,0:T(8,128)S(1)}, f32[32,128]{1,0:T(8,128)S(1)}, u32[]{:S(2)}, u32[]{:S(2)}) collective-permute-start(f32[32,128]{1,0:T(8,128)S(1)} %collective-permute-done.5.mine), channel_id=1, source_target_pairs={{0,4},{4,0},{8,12},{12,8},{16,20},{20,16},{24,28},{28,24},{1,5},{5... | collective-permute-start | bytes 49160 | tf_op jit(solution)/shard_map/ppermute | solution.py:476
  20.7 0.7 %copy-start.8 = (s32[32]{0:T(128)S(1)}, s32[32]{0:T(128)}, u32[]{:S(2)}) copy-start(s32[32]{0:T(128)} %param.16) | copy-start | bytes 388
  22.8 1.6 %collective-permute-start.10 = (bf16[32,4096]{1,0:T(8,128)(2,1)S(1)}, bf16[32,4096]{1,0:T(8,128)(2,1)S(1)}, u32[]{:S(2)}, u32[]{:S(2)}) collective-permute-start(bf16[32,4096]{1,0:T(8,128)(2,1)S(1)} %get-tuple-element.41.second.own), channel_id=1, source_target_pairs={{0,4},{4,0},{8,12},{12,8},{16,20},{20,16},{24,28},{28,24},{1,5},{5... | collective-permute-start | bytes 786440 | tf_op jit(solution)/shard_map/ppermute | solution.py:476
  25.2 8.1 %collective-permute-start.11 = (bf16[16,5248]{1,0:T(8,128)(2,1)S(1)}, bf16[16,5248]{1,0:T(8,128)(2,1)S(1)}, u32[]{:S(2)}, u32[]{:S(2)}) collective-permute-start(bf16[16,5248]{1,0:T(8,128)(2,1)S(1)} %get-tuple-element.53), channel_id=1, source_target_pairs={{0,24},{4,28},{8,16},{12,20},{16,8},{20,12},{24,0},{28,4},{1,25},{... | collective-permute-start | bytes 503816 | tf_op jit(solution)/shard_map/ppermute | solution.py:481
  25.7 9.7 %collective-permute-start.12 = (bf16[16,5248]{1,0:T(8,128)(2,1)S(1)}, bf16[16,5248]{1,0:T(8,128)(2,1)S(1)}, u32[]{:S(2)}, u32[]{:S(2)}) collective-permute-start(bf16[16,5248]{1,0:T(8,128)(2,1)S(1)} %get-tuple-element.54), channel_id=1, source_target_pairs={{0,16},{4,20},{8,24},{12,28},{16,0},{20,4},{24,8},{28,12},{1,17},{... | collective-permute-start | bytes 503816 | tf_op jit(solution)/shard_map/ppermute | solution.py:481
  27.2 8.2 %collective-permute-start.13 = (bf16[16,5248]{1,0:T(8,128)(2,1)S(1)}, bf16[16,5248]{1,0:T(8,128)(2,1)S(1)}, u32[]{:S(2)}, u32[]{:S(2)}) collective-permute-start(bf16[16,5248]{1,0:T(8,128)(2,1)S(1)} %get-tuple-element.55), channel_id=1, source_target_pairs={{0,8},{4,12},{8,0},{12,4},{16,24},{20,28},{24,16},{28,20},{1,9},{5... | collective-permute-start | bytes 503816 | tf_op jit(solution)/shard_map/ppermute | solution.py:481
